TPU v7x, 32 devices: a whole 2x2x4 slice. The times are simulated.
32 devices in a mesh: seq: 4 (over x, core), batch: 8 (over z, y).
Axes of the slice: x: 2, y: 2, z: 4, core: 2. Of those that a mesh axis runs over, the one named last changes fastest.
Arguments:
- patches: bfloat16 [8, 1024, 768], P('batch', 'seq'), may hold values from -6 to 6
- specials: bfloat16 [8, 16, 768], P('batch', 'seq'), may hold values from -6 to 6
- segment_ids: int32 [8, 1024], P('batch', 'seq'), may hold values from 0 to 7, never falling along the last dimension, each value on 1 to 576 neighbouring positions
- special_order: int32 [8, 16], P('batch', 'seq'), may hold values from 0 to 15, each once within a row
- keep_mask: int32 [8, 16], P('batch'), may hold values 0 or 1
- norm_gains: float32 [2, 768], replicated, may hold values from 0.5 to 1.5
- norm_shifts: float32 [2, 768], replicated, may hold values from -3 to 3
- w_qkv: bfloat16 [768, 2304], replicated, may hold values from -0.21875 to 0.21875
- biases: float32 [4, 768], replicated, may hold values from -3 to 3
- w_out: bfloat16 [768, 768], replicated, may hold values from -0.875 to 0.875
- w_fc1: bfloat16 [768, 3072], replicated, may hold values from -0.21875 to 0.21875
- fc1_bias: float32 [3072], replicated, may hold values from -3 to 3
- w_fc2: bfloat16 [3072, 768], replicated, may hold values from -0.109375 to 0.109375
- cot_patches: bfloat16 [8, 1024, 768], P('batch', 'seq'), may hold values from -6 to 6
- cot_specials: bfloat16 [8, 16, 768], P('batch', 'seq'), may hold values from -6 to 6
Outputs:
- out_patches: bfloat16 [8, 1024, 768], P('batch', 'seq')
- out_specials: bfloat16 [8, 16, 768], P('batch', 'seq')
- grad_patches: float32 [8, 1024, 768], P('batch', 'seq')
- grad_specials: float32 [8, 16, 768], P('batch', 'seq')
- grad_gains: float32 [2, 768], P(None, ('seq', 'batch'))
- grad_shifts: float32 [2, 768], P(None, ('seq', 'batch'))
- grad_w_qkv: float32 [768, 2304], P(('seq', 'batch'))
- grad_biases: float32 [4, 768], P(None, ('seq', 'batch'))
- grad_w_out: float32 [768, 768], P(('seq', 'batch'))
- grad_w_fc1: float32 [768, 3072], P(('seq', 'batch'))
- grad_fc1_bias: float32 [3072], P(('seq', 'batch'))
- grad_w_fc2: float32 [3072, 768], P(('seq', 'batch'))
Inputs may be any that keep to these rules, and one draw needn't show every extreme that they name: `segment_ids`: within a row image ids never fall; every image of a row has 1 to 576 patches. `special_order`: each row holds every number once.
All inputs are finite; a program needn't handle non-finite values. No bound on the sum of `keep_mask` on one device may be relied on, other than what follows from the above.
Results may differ from a plain program's by a relative error of at most 0.011.
Values may be sent and summed in bfloat16 or wider, within the bound.
No kernel may reach another device: no remote copies, remote signals or barrier semaphores. Data moves between devices by JAX's collectives and lax.ppermute only.
A program may use at most 192 MiB of HBM per device.

v0:
```python
import jax
import jax.numpy as jnp
from jax import lax
from jax.sharding import PartitionSpec as P

HEADS = 12
HEAD = 64


def layer_norm(inputs, norm_gain, norm_shift):
    center = inputs - jnp.mean(inputs, axis=-1, keepdims=True)
    spread = jnp.mean(center * center, axis=-1, keepdims=True)
    return center * lax.rsqrt(spread + 1e-06) * norm_gain + norm_shift


def exact_gelu(inputs):
    return jax.nn.gelu(inputs, approximate=False)


def image_lookup(segments, keep_table):
    image_count = keep_table.shape[1]
    onehot = (segments[..., None] == jnp.arange(image_count, dtype=jnp.int32)).astype(jnp.float32)
    return jnp.sum(onehot * keep_table[:, None, :], axis=-1)


def split_heads(inputs):
    return inputs.reshape(inputs.shape[0], inputs.shape[1], HEADS, HEAD)


def masked_scores(query_heads, key_heads, query_segs, key_segs):
    scores = jnp.einsum(
        "rqhd,rkhd->rhqk", query_heads, key_heads, preferred_element_type=jnp.float32
    ) * HEAD ** (-0.5)
    same_image = query_segs[:, :, None] == key_segs[:, None, :]
    return jnp.where(same_image[:, None], scores, -1e30)


def body(
    patches,
    specials,
    segment_ids,
    special_order,
    keep_mask,
    norm_gains,
    norm_shifts,
    w_qkv,
    biases,
    w_out,
    w_fc1,
    fc1_bias,
    w_fc2,
    cot_patches,
    cot_specials,
):
    row_count, local_count, model_width = patches.shape
    image_count = keep_mask.shape[1] // 2
    tokens = jnp.concatenate([patches, specials], axis=1).astype(jnp.float32)
    seg_all = jnp.concatenate([segment_ids, special_order // 2], axis=1)
    keep_float = keep_mask.astype(jnp.float32) / 0.75
    keep_first = image_lookup(seg_all, keep_float[:, :image_count])
    keep_second = image_lookup(seg_all, keep_float[:, image_count:])
    normed = layer_norm(tokens, norm_gains[0], norm_shifts[0]).astype(jnp.bfloat16)
    qkv_proj = jnp.einsum("rnd,de->rne", normed, w_qkv, preferred_element_type=jnp.float32)
    query_proj = (qkv_proj[..., :model_width] + biases[0]).astype(jnp.bfloat16)
    key_proj = qkv_proj[..., model_width : 2 * model_width].astype(jnp.bfloat16)
    value_proj = (qkv_proj[..., 2 * model_width :] + biases[1]).astype(jnp.bfloat16)
    key_all, value_all, seg_keys = (
        lax.all_gather(key_proj, "seq", axis=1, tiled=True),
        lax.all_gather(value_proj, "seq", axis=1, tiled=True),
        lax.all_gather(seg_all, "seq", axis=1, tiled=True),
    )
    query_heads = split_heads(query_proj)
    scores = masked_scores(query_heads, split_heads(key_all), seg_all, seg_keys)
    row_top = jnp.max(scores, axis=-1, keepdims=True)
    row_total = jnp.sum(jnp.exp(scores - row_top), axis=-1, keepdims=True)
    attn_probs = (jnp.exp(scores - row_top) / row_total).astype(jnp.bfloat16)
    attended = jnp.einsum(
        "rhqk,rkhd->rqhd", attn_probs, split_heads(value_all), preferred_element_type=jnp.float32
    )
    attended = attended.reshape(row_count, -1, model_width).astype(jnp.bfloat16)
    branch = (
        jnp.einsum("rnd,de->rne", attended, w_out, preferred_element_type=jnp.float32) + biases[2]
    )
    middle = tokens + keep_first[..., None] * branch
    normed2 = layer_norm(middle, norm_gains[1], norm_shifts[1]).astype(jnp.bfloat16)
    hidden_pre = (
        jnp.einsum("rnd,df->rnf", normed2, w_fc1, preferred_element_type=jnp.float32) + fc1_bias
    )
    active = exact_gelu(hidden_pre).astype(jnp.bfloat16)
    branch2 = (
        jnp.einsum("rnf,fd->rnd", active, w_fc2, preferred_element_type=jnp.float32) + biases[3]
    )
    result = middle + keep_second[..., None] * branch2
    out_patches = result[:, :local_count].astype(jnp.bfloat16)
    out_specials = result[:, local_count:].astype(jnp.bfloat16)
    grad_out = jnp.concatenate([cot_patches, cot_specials], axis=1).astype(jnp.float32)
    grad_branch2 = (keep_second[..., None] * grad_out).astype(jnp.bfloat16)
    grad_w_fc2 = jnp.einsum("rnf,rnd->fd", active, grad_branch2, preferred_element_type=jnp.float32)
    grad_bias_feed = jnp.sum(grad_branch2.astype(jnp.float32), axis=(0, 1))
    grad_active = jnp.einsum("rnd,fd->rnf", grad_branch2, w_fc2, preferred_element_type=jnp.float32)
    gelu_unused, gelu_pull = jax.vjp(exact_gelu, hidden_pre)
    grad_hidden = gelu_pull(grad_active)[0].astype(jnp.bfloat16)
    grad_fc1_bias = jnp.sum(grad_hidden.astype(jnp.float32), axis=(0, 1))
    grad_w_fc1 = jnp.einsum("rnd,rnf->df", normed2, grad_hidden, preferred_element_type=jnp.float32)
    grad_normed2 = jnp.einsum("rnf,df->rnd", grad_hidden, w_fc1, preferred_element_type=jnp.float32)
    norm_unused, second_pull = jax.vjp(layer_norm, middle, norm_gains[1], norm_shifts[1])
    grad_mid_norm, grad_gain2, grad_shift2 = second_pull(grad_normed2)
    grad_middle = grad_out + grad_mid_norm
    feed_small = jnp.stack([grad_gain2, grad_shift2, grad_bias_feed])
    feed_sums = (
        lax.psum_scatter(grad_w_fc2, ("seq", "batch"), scatter_dimension=0, tiled=True),
        lax.psum_scatter(grad_w_fc1, ("seq", "batch"), scatter_dimension=0, tiled=True),
        lax.psum_scatter(grad_fc1_bias, ("seq", "batch"), scatter_dimension=0, tiled=True),
        lax.psum_scatter(feed_small, ("seq", "batch"), scatter_dimension=1, tiled=True),
    )
    grad_branch = (keep_first[..., None] * grad_middle).astype(jnp.bfloat16)
    grad_w_out = jnp.einsum(
        "rnd,rne->de", attended, grad_branch, preferred_element_type=jnp.float32
    )
    grad_bias_out = jnp.sum(grad_branch.astype(jnp.float32), axis=(0, 1))
    grad_attended = jnp.einsum(
        "rne,de->rnd", grad_branch, w_out, preferred_element_type=jnp.float32
    ).astype(jnp.bfloat16)
    key_heads = split_heads(key_all)
    value_heads = split_heads(value_all)
    scores_again = masked_scores(query_heads, key_heads, seg_all, seg_keys)
    probs_float = jnp.exp(scores_again - row_top) / row_total
    grad_heads = split_heads(grad_attended)
    grad_probs = jnp.einsum(
        "rqhd,rkhd->rhqk", grad_heads, value_heads, preferred_element_type=jnp.float32
    )
    inner_sum = jnp.sum(grad_probs * probs_float, axis=-1, keepdims=True)
    grad_scores = (probs_float * (grad_probs - inner_sum)).astype(jnp.bfloat16)
    score_scale = HEAD ** (-0.5)
    grad_query = (
        jnp.einsum("rhqk,rkhd->rqhd", grad_scores, key_heads, preferred_element_type=jnp.float32)
        * score_scale
    )
    grad_query = grad_query.reshape(row_count, -1, model_width).astype(jnp.bfloat16)
    query_every, grad_every = (
        lax.all_gather(query_proj, "seq", axis=1, tiled=True),
        lax.all_gather(grad_attended, "seq", axis=1, tiled=True),
    )
    top_every, total_every, inner_every = (
        lax.all_gather(row_top[..., 0], "seq", axis=2, tiled=True),
        lax.all_gather(row_total[..., 0], "seq", axis=2, tiled=True),
        lax.all_gather(inner_sum[..., 0], "seq", axis=2, tiled=True),
    )
    query_every = split_heads(query_every)
    grad_every = split_heads(grad_every)
    scores_keys = masked_scores(query_every, split_heads(key_proj), seg_keys, seg_all)
    probs_keys = jnp.exp(scores_keys - top_every[..., None]) / total_every[..., None]
    probs_grad = jnp.einsum(
        "rqhd,rkhd->rhqk", grad_every, split_heads(value_proj), preferred_element_type=jnp.float32
    )
    scores_grad = (probs_keys * (probs_grad - inner_every[..., None])).astype(jnp.bfloat16)
    key_part = (
        jnp.einsum("rhqk,rqhd->rkhd", scores_grad, query_every, preferred_element_type=jnp.float32)
        * score_scale
    )
    value_part = jnp.einsum(
        "rhqk,rqhd->rkhd",
        probs_keys.astype(jnp.bfloat16),
        grad_every,
        preferred_element_type=jnp.float32,
    )
    grad_key = key_part.reshape(row_count, -1, model_width)
    grad_value = value_part.reshape(row_count, -1, model_width)
    grad_key = grad_key.astype(jnp.bfloat16)
    grad_value = grad_value.astype(jnp.bfloat16)
    grad_bias_query = jnp.sum(grad_query.astype(jnp.float32), axis=(0, 1))
    grad_bias_value = jnp.sum(grad_value.astype(jnp.float32), axis=(0, 1))
    grad_mixed = jnp.concatenate([grad_query, grad_key, grad_value], axis=-1)
    grad_w_qkv = jnp.einsum("rnd,rne->de", normed, grad_mixed, preferred_element_type=jnp.float32)
    grad_normed = jnp.einsum("rne,de->rnd", grad_mixed, w_qkv, preferred_element_type=jnp.float32)
    first_unused, first_pull = jax.vjp(layer_norm, tokens, norm_gains[0], norm_shifts[0])
    grad_tok_norm, grad_gain1, grad_shift1 = first_pull(grad_normed)
    grad_tokens = grad_middle + grad_tok_norm
    mixer_small = jnp.stack(
        [grad_gain1, grad_shift1, grad_bias_query, grad_bias_value, grad_bias_out]
    )
    mixer_sums = (
        lax.psum_scatter(grad_w_qkv, ("seq", "batch"), scatter_dimension=0, tiled=True),
        lax.psum_scatter(grad_w_out, ("seq", "batch"), scatter_dimension=0, tiled=True),
        lax.psum_scatter(mixer_small, ("seq", "batch"), scatter_dimension=1, tiled=True),
    )
    sum_fc2, sum_fc1, sum_fc1_bias, sum_feed = feed_sums
    sum_qkv, sum_out, sum_mixer = mixer_sums
    grad_gains = jnp.stack([sum_mixer[0], sum_feed[0]])
    grad_shifts = jnp.stack([sum_mixer[1], sum_feed[1]])
    grad_biases = jnp.stack([sum_mixer[2], sum_mixer[3], sum_mixer[4], sum_feed[2]])
    return (
        out_patches,
        out_specials,
        grad_tokens[:, :local_count],
        grad_tokens[:, local_count:],
        grad_gains,
        grad_shifts,
        sum_qkv,
        grad_biases,
        sum_out,
        sum_fc1,
        sum_fc1_bias,
        sum_fc2,
    )


def solution(mesh):
    return jax.shard_map(
        body,
        mesh=mesh,
        in_specs=(
            P("batch", "seq", None),
            P("batch", "seq", None),
            P("batch", "seq"),
            P("batch", "seq"),
            P("batch", None),
            P(),
            P(),
            P(),
            P(),
            P(),
            P(),
            P(),
            P(),
            P("batch", "seq", None),
            P("batch", "seq", None),
        ),
        out_specs=(
            P("batch", "seq", None),
            P("batch", "seq", None),
            P("batch", "seq", None),
            P("batch", "seq", None),
            P(None, ("seq", "batch")),
            P(None, ("seq", "batch")),
            P(("seq", "batch"), None),
            P(None, ("seq", "batch")),
            P(("seq", "batch"), None),
            P(("seq", "batch"), None),
            P(("seq", "batch")),
            P(("seq", "batch"), None),
        ),
        check_vma=False,
    )
```

profile of v0, /device:TPU:0, one launch (start us, length us, event | category | flops | bytes accessed | tf_op | source)
XLA Modules:
  0.0 698.4 jit_solution(8245321264741629401)
XLA Ops:
  7.2 1.3 convert_reduce_fusion.3
  8.6 1.3 fusion.48
  9.9 0.8 slice_reduce_fusion.1
  11.3 2.2 convolution_bitcast_fusion
  13.6 1.4 copy-done.11
  15.8 1.5 copy.62
  17.4 1.5 slice_reduce_fusion
  18.9 2.3 fusion.50
  21.9 1.5 copy.59
  23.5 2.5 copy.65
  26.1 2.1 copy.61
  28.2 2.1 copy.67
  30.4 1.2 dynamic-slice
  32.9 1.4 dynamic-update-slice
  34.3 6.8 all-reduce
  41.1 1.6 broadcast_compare_fusion
  42.8 1.6 broadcast_compare_fusion.1
  44.4 2.1 copy.71
  47.2 1.4 select_reduce_fusion
  49.2 8.5 %copy.63 = bf16[1,1040,768]{1,2,0:T(8,128)(2,1)} copy(bf16[1,1040,768]{2,0,1:T(2,128)(2,1)} %all-gather.15.cloned.1.call-done) | data formatting | bytes 3194880 | tf_op jit(solution)/shard_map/all_gather | solution.py:68
  57.7 9.8 %fusion.75 = (f32[12,260]{1,0:T(8,128)S(1)}, f32[12,260,1040]{2,1,0:T(8,128)}) fusion(bf16[260,12,64]{0,2,1:T(8,128)(2,1)} %bitcast.121, bf16[1040,12,64]{0,2,1:T(8,128)(2,1)} %bitcast.107, pred[260,1040]{1,0:T(8,128)(4,1)} %broadcast_compare_fusion), kind=kOutput, calls=%fused_computation.145 | convolution fusion | flops 425065664 | bytes 15258880 | tf_op jit(solution)/shard_map/rqhd,rkhd->rhqk/dot_general | solution.py:31
  68.1 8.2 %fusion.8 = f32[12,260]{1,0:T(8,128)} fusion(f32[12,260,1040]{2,1,0:T(8,128)} %get-tuple-element.48, f32[12,260]{1,0:T(8,128)S(1)} %get-tuple-element.47), kind=kLoop, calls=%fused_computation.14 | loop fusion | flops 6486480 | bytes 13004160 | tf_op jit(solution)/shard_map/reduce_sum | solution.py:75
  76.3 3.3 all-gather.13.cloned.1.call-done
  79.6 8.6 %copy.60 = bf16[1,1040,768]{1,2,0:T(8,128)(2,1)} copy(bf16[1,1040,768]{2,0,1:T(2,128)(2,1)} %all-gather.13.cloned.1.call-done) | data formatting | bytes 3194880 | tf_op jit(solution)/shard_map/all_gather | solution.py:69
  88.2 8.0 %fusion.26 = bf16[12,64,260]{2,1,0:T(8,128)(2,1)S(1)} fusion(bf16[1040,12,64]{0,2,1:T(8,128)(2,1)} %bitcast.122, f32[12,260,1040]{2,1,0:T(8,128)} %get-tuple-element.48, f32[12,260]{1,0:T(8,128)} %fusion.8, f32[12,260]{1,0:T(8,128)} %copy-done.15), kind=kOutput, calls=%fused_computation.47 | convolution fusion | flops 425268480 | bytes 15000960 | tf_op jit(solution)/shard_map/rhqk,rkhd->rqhd/dot_general | solution.py:77
  97.3 10.7 %multiply_convert_fusion.2 = (bf16[260,3072]{1,0:T(8,128)(2,1)}, f32[260,3072]{1,0:T(8,128)S(1)}, f32[260,3072]{1,0:T(8,128)S(1)}) fusion(f32[3072]{0:T(1024)S(1)} %copy-done.38, bf16[768,3072]{1,0:T(8,128)(2,1)S(1)} %bitcast.147, f32[260,768]{1,0:T(8,128)S(1)} %get-tuple-element.50, f32[768]{0:T(1024)S(1)} %get-tuple-element.25, ...), kind=kOutput, calls=%fused_computation.27 | convolution fusion | flops 1280547840 | bytes 13525024 | tf_op jit(solution)/shard_map/rnd,df->rnf/dot_general | solution.py:87
  108.1 2.9 convert_reduce_fusion
  110.9 2.3 multiply_reduce_fusion.1
  113.7 0.9 copy-done.4
  114.6 0.8 convert_reduce_fusion.5
  116.2 1.3 convolution_convert_fusion
  117.4 2.1 copy.64
  119.5 10.9 %multiply_reduce_fusion = (f32[12,260]{1,0:T(8,128)S(1)}, f32[12,260,1040]{2,1,0:T(8,128)}) fusion(f32[12,260]{1,0:T(8,128)} %fusion.8, f32[12,260,1040]{2,1,0:T(8,128)} %get-tuple-element.48, f32[12,260]{1,0:T(8,128)} %copy-done.15, bf16[260,12,64]{0,2,1:T(8,128)(2,1)} %bitcast.129, bf16[1040,12,64]{0,2,1:T(8,128)(2,1)} %bitcast.123), kind=kOutput, calls=%fused_computation.10 | convolution fusion | flops 428310464 | bytes 27992640 | tf_op jit(solution)/shard_map/rqhd,rkhd->rhqk/dot_general | solution.py:129
  131.1 5.3 all-gather.7
  137.0 1.6 reshape.990
  138.6 5.5 all-gather.5
  144.8 1.6 reshape.986
  146.5 5.5 all-gather.4
  152.7 1.6 reshape.984
  154.3 3.3 fusion.77
  157.7 13.9 %convert_reduce_fusion.2 = (f32[12,64]{1,0:T(8,128)}, bf16[12,64,260]{2,1,0:T(8,128)(2,1)}) fusion(bf16[1040,12,64]{0,2,1:T(8,128)(2,1)} %bitcast.108, f32[12,260,1040]{2,1,0:T(8,128)} %get-tuple-element.54, f32[12,260]{1,0:T(8,128)} %copy-done.28, f32[12,260]{1,0:T(8,128)} %fusion.8, f32[12,260,1040]{2,1,0:T(8,128)} %get-tuple-element.48, ...), kind=kOutput, calls=%fused_computation.61 | convolution fusion | flops 432356352 | bytes 27995712 | tf_op jit(solution)/shard_map/rhqk,rkhd->rqhd/dot_general | solution.py:136
  171.7 8.5 %copy.66 = bf16[1,1040,768]{1,2,0:T(8,128)(2,1)} copy(bf16[1,1040,768]{2,0,1:T(2,128)(2,1)} %all-gather.17.cloned.1.call-done) | data formatting | bytes 3194880 | tf_op jit(solution)/shard_map/all_gather | solution.py:141
  180.2 10.9 %fusion.5 = f32[12,1040,260]{1,2,0:T(8,128)} fusion(bf16[1040,12,64]{0,2,1:T(8,128)(2,1)} %bitcast.109, bf16[260,12,64]{0,2,1:T(8,128)(2,1)} %bitcast.128, f32[12,1040]{1,0:T(8,128)} %bitcast.143, f32[12,1040]{1,0:T(8,128)} %bitcast.144, pred[1040,260]{0,1:T(8,128)(4,1)} %broadcast_compare_fusion.1), kind=kOutput, calls=%fused_computation.8 | convolution fusion | flops 428313600 | bytes 15346240 | tf_op jit(solution)/shard_map/rqhd,rkhd->rhqk/dot_general | solution.py:31
  191.1 5.2 copy.70
  196.3 4.8 reshape.968
  201.1 9.9 %convert_reduce_fusion.1 = (f32[12,64]{1,0:T(8,128)}, bf16[12,64,260]{2,1,0:T(8,128)(2,1)}) fusion(bf16[1040,12,64]{0,2,1:T(8,128)(2,1)} %reshape.968, f32[12,1040,260]{1,2,0:T(8,128)} %fusion.5), kind=kOutput, calls=%fused_computation.60 | convolution fusion | flops 419177472 | bytes 14979072 | tf_op jit(solution)/shard_map/rhqk,rqhd->rkhd/dot_general | solution.py:161
  211.0 12.0 %fusion.25 = bf16[12,64,260]{2,1,0:T(8,128)(2,1)} fusion(bf16[1040,12,64]{0,2,1:T(8,128)(2,1)} %bitcast.110, f32[12,1040,260]{1,2,0:T(8,128)} %fusion.5, bf16[1040,12,64]{0,2,1:T(8,128)(2,1)} %reshape.968, bf16[260,12,64]{0,2,1:T(8,128)(2,1)} %bitcast.120, f32[12,1040]{1,0:T(8,128)} %bitcast.130), kind=kOutput, calls=%fused_computation.46 | convolution fusion | flops 840802560 | bytes 17022720 | tf_op jit(solution)/shard_map/rhqk,rqhd->rkhd/dot_general | solution.py:158
  223.1 6.7 fusion.52
  229.8 8.2 %fusion.66 = f32[768,3072]{1,0:T(8,128)} fusion(bf16[260,3072]{1,0:T(8,128)(2,1)} %copy-done.12, f32[260,768]{1,0:T(8,128)} %copy-done.3, f32[768]{0:T(1024)S(1)} %get-tuple-element.25, f32[768]{0:T(1024)S(1)} %get-tuple-element.63, f32[260]{0:T(512)} %copy-done.25, f32[260]{0:T(512)} %copy-done.21), kind=kOutput, calls=%fused_computation.139 | convolution fusion | flops 1227832320 | bytes 11841568 | tf_op jit(solution)/shard_map/rnd,rnf->df/dot_general | solution.py:104
  238.7 7.9 %fusion.54 = f32[3072,768]{1,0:T(8,128)} fusion(bf16[260,3072]{1,0:T(8,128)(2,1)} %get-tuple-element.36, f32[260]{0:T(512)} %get-tuple-element.27, bf16[4,768]{1,0:T(4,128)(2,1)S(1)} %bitcast.141, bf16[256,768]{1,0:T(8,128)(2,1)} %bitcast.111), kind=kOutput, calls=%fused_computation.100 | convolution fusion | flops 1228032000 | bytes 11435024 | tf_op jit(solution)/shard_map/rnf,rnd->fd/dot_general | solution.py:98
  246.6 1.2 convert_reduce_fusion.4
  248.4 4.5 fusion.37
  254.2 1.4 stack.42
  255.6 1.3 stack.44
  258.2 1.3 pad_maximum_fusion.3
  259.6 3.4 fusion.70
  264.0 0.9 slice.111
  265.5 0.8 stack.43
  266.3 1.3 stack.45
  267.6 41.4 %all-reduce.4 = (f32[3,768]{1,0:T(4,128)S(1)}, f32[5,768]{1,0:T(8,128)}, f32[3072]{0:T(1024)}) all-reduce(f32[3,768]{1,0:T(4,128)} %pad_maximum_fusion.3, f32[5,768]{1,0:T(8,128)} %stack.45, f32[3072]{0:T(1024)} %get-tuple-element.60), channel_id=7, replica_groups=mesh['seq'=4,'batch'=8] {'seq','batch'}, use_global_device_ids=true, to_apply=%region_22.23.clone | all-reduce | flops 9216 | bytes 73728
  309.8 1.3 dynamic-slice.3
  312.9 95.1 %reduce-scatter.7.cloned.1.call-done = f32[24,2304]{1,0:T(8,128)} async-done(((f32[768,2304]{1,0:T(8,128)}), f32[24,2304]{1,0:T(8,128)}) %reduce-scatter.7.cloned.1.call-update) | async-done | bytes 221200 | tf_op jit(solution)/shard_map/reduce_scatter | solution.py:183
  408.0 141.3 %reduce-scatter.11.cloned.1.call-done = f32[24,3072]{1,0:T(8,128)} async-done(((f32[768,3072]{1,0:T(8,128)}), f32[24,3072]{1,0:T(8,128)}) %reduce-scatter.11.cloned.1.call-update) | async-done | bytes 294928 | tf_op jit(solution)/shard_map/reduce_scatter | solution.py:112
  549.4 141.9 %reduce-scatter.13.cloned.1.call-done = f32[96,768]{1,0:T(8,128)} async-done(((f32[3072,768]{1,0:T(8,128)}), f32[96,768]{1,0:T(8,128)}) %reduce-scatter.13.cloned.1.call-update) | async-done | bytes 294928 | tf_op jit(solution)/shard_map/reduce_scatter | solution.py:111
  (146 shorter events, 18.1 us)
Async XLA Ops:
  7.2 4.1 copy-start
  7.2 42.0 %all-gather.15.cloned.1.call-start = ((), (), s32[]{:S(2)}) async-start(), calls=%async_computation.5 | async-start | bytes 3993600 | tf_op jit(solution)/shard_map/all_gather | solution.py:68
  8.6 2.2 copy-start.23
  9.9 0.9 copy-start.30
  9.9 0.9 copy-start.26
  10.7 0.6 copy-start.19
  10.7 0.6 copy-start.34
  13.5 1.4 copy-start.11
  15.0 0.8 copy-start.10
  17.3 62.2 %all-gather.13.cloned.1.call-start = ((), (), s32[]{:S(2)}) async-start(), calls=%async_computation.4 | async-start | bytes 3993600 | tf_op jit(solution)/shard_map/all_gather | solution.py:69
  21.2 0.8 copy-start.8
  21.2 9.2 %copy-start.39 = (s32[1,4]{1,0:T(1,128)S(1)}, s32[1,4]{1,0:T(1,128)}, u32[]{:S(2)}) copy-start(s32[1,4]{1,0:T(1,128)} %param.18) | copy-start | bytes 52
  21.2 9.2 %copy-start.37 = (s32[1,256]{1,0:T(1,128)S(1)}, s32[1,256]{1,0:T(1,128)}, u32[]{:S(2)}) copy-start(s32[1,256]{1,0:T(1,128)} %param.17) | copy-start | bytes 3076
  23.4 148.2 %all-gather.17.cloned.1.call-start = ((), (), s32[]{:S(2)}) async-start(), calls=%async_computation.6 | async-start | bytes 3993600 | tf_op jit(solution)/shard_map/all_gather | solution.py:141
  26.0 165.0 %all-gather.19.cloned.1.call-start = ((), (), s32[]{:S(2)}) async-start(), calls=%async_computation.11 | async-start | bytes 2027520 | tf_op jit(solution)/shard_map/all_gather | solution.py:142
  30.4 2.5 copy-start.22
  67.5 0.6 copy-start.15
  88.1 9.1 %slice-start = ((s8[4718592]{0:T(1024)(128)(4,1)}), s8[4194304]{0:T(1024)(128)(4,1)S(1)}, s32[]{:S(2)}) async-start(s8[4718592]{0:T(1024)(128)(4,1)} %bitcast.146), calls=%async_computation.12 | async-start | bytes 8388608
  88.1 8.1 %copy-start.1 = (bf16[1,256,768]{2,1,0:T(8,128)(2,1)S(1)}, bf16[1,256,768]{2,1,0:T(8,128)(2,1)}, u32[]{:S(2)}) copy-start(bf16[1,256,768]{2,1,0:T(8,128)(2,1)} %param.15) | copy-start | bytes 1179652
  88.1 8.1 %copy-start.13 = (bf16[768,768]{1,0:T(8,128)(2,1)S(1)}, bf16[768,768]{1,0:T(8,128)(2,1)}, u32[]{:S(2)}) copy-start(bf16[768,768]{1,0:T(8,128)(2,1)} %param.24) | copy-start | bytes 3538948
  88.1 8.1 %copy-start.16 = (bf16[1,4,768]{2,1,0:T(4,128)(2,1)S(1)}, bf16[1,4,768]{2,1,0:T(4,128)(2,1)}, u32[]{:S(2)}) copy-start(bf16[1,4,768]{2,1,0:T(4,128)(2,1)} %param.16) | copy-start | bytes 18436
  88.1 8.1 %copy-start.35 = (f32[260]{0:T(512)S(1)}, f32[260]{0:T(512)}, u32[]{:S(2)}) copy-start(f32[260]{0:T(512)} %get-tuple-element.28) | copy-start | bytes 3124
  88.1 8.1 %copy-start.36 = (f32[768]{0:T(1024)S(1)}, f32[768]{0:T(1024)}, u32[]{:S(2)}) copy-start(f32[768]{0:T(1024)} %get-tuple-element.22) | copy-start | bytes 9220
  88.2 9.1 %slice-start.1 = ((s8[4718592]{0:T(1024)(128)(4,1)}), s8[524288]{0:T(1024)(128)(4,1)S(1)}, s32[]{:S(2)}) async-start(s8[4718592]{0:T(1024)(128)(4,1)} %bitcast.146), calls=%async_computation.13 | async-start | bytes 1048576
  96.2 11.8 %copy-start.14 = (bf16[12,64,260]{2,1,0:T(8,128)(2,1)}, bf16[12,64,260]{2,1,0:T(8,128)(2,1)S(1)}, u32[]{:S(2)}) copy-start(bf16[12,64,260]{2,1,0:T(8,128)(2,1)S(1)} %fusion.26) | copy-start | bytes 1198084
  96.2 1.1 copy-start.38
  96.2 11.8 %slice-start.2 = ((s8[4718592]{0:T(1024)(128)(4,1)}), s8[4194304]{0:T(1024)(128)(4,1)S(1)}, s32[]{:S(2)}) async-start(s8[4718592]{0:T(1024)(128)(4,1)} %bitcast.148), calls=%async_computation.14 | async-start | bytes 8388608
  96.9 16.3 %copy-start.3 = (f32[260,768]{1,0:T(8,128)}, f32[260,768]{1,0:T(8,128)S(1)}, u32[]{:S(2)}) copy-start(f32[260,768]{1,0:T(8,128)S(1)} %get-tuple-element.50) | copy-start | bytes 2396164
  96.9 16.3 %copy-start.21 = (f32[260]{0:T(512)}, f32[260]{0:T(512)S(1)}, u32[]{:S(2)}) copy-start(f32[260]{0:T(512)S(1)} %broadcast_multiply_fusion) | copy-start | bytes 3124
  97.2 16.0 %copy-start.25 = (f32[260]{0:T(512)}, f32[260]{0:T(512)S(1)}, u32[]{:S(2)}) copy-start(f32[260]{0:T(512)S(1)} %fusion.61) | copy-start | bytes 3124
  97.3 10.8 %copy-start.6 = (bf16[1,256,768]{2,1,0:T(8,128)(2,1)S(1)}, bf16[1,256,768]{2,1,0:T(8,128)(2,1)}, u32[]{:S(2)}) copy-start(bf16[1,256,768]{2,1,0:T(8,128)(2,1)} %param.28) | copy-start | bytes 1179652
  97.3 10.8 %copy-start.17 = (bf16[1,4,768]{2,1,0:T(4,128)(2,1)S(1)}, bf16[1,4,768]{2,1,0:T(4,128)(2,1)}, u32[]{:S(2)}) copy-start(bf16[1,4,768]{2,1,0:T(4,128)(2,1)} %param.29) | copy-start | bytes 18436
  97.3 10.8 %copy-start.29 = (f32[260]{0:T(512)S(1)}, f32[260]{0:T(512)}, u32[]{:S(2)}) copy-start(f32[260]{0:T(512)} %get-tuple-element.27) | copy-start | bytes 3124
  97.3 10.8 %slice-start.3 = ((s8[4718592]{0:T(1024)(128)(4,1)}), s8[524288]{0:T(1024)(128)(4,1)S(1)}, s32[]{:S(2)}) async-start(s8[4718592]{0:T(1024)(128)(4,1)} %bitcast.148), calls=%async_computation.15 | async-start | bytes 1048576
  110.9 2.3 copy-start.12
  113.6 0.9 copy-start.4
  113.6 1.8 copy-start.32
  115.4 0.8 copy-start.9
  130.4 0.6 copy-start.28
  157.6 155.3 %reduce-scatter.9.cloned.1.call-start = ((), (), s32[]{:S(2)}) async-start(), calls=%async_computation.8 | async-start | bytes 2433024 | tf_op jit(solution)/shard_map/reduce_scatter | solution.py:184
  171.6 236.4 %reduce-scatter.7.cloned.1.call-start = ((), (), s32[]{:S(2)}) async-start(), calls=%async_computation.7 | async-start | bytes 7299072 | tf_op jit(solution)/shard_map/reduce_scatter | solution.py:183
  229.8 319.6 %reduce-scatter.11.cloned.1.call-start = ((), (), s32[]{:S(2)}) async-start(), calls=%async_computation.9 | async-start | bytes 9732096 | tf_op jit(solution)/shard_map/reduce_scatter | solution.py:112
  238.0 0.7 copy-start.18
  238.0 453.3 %reduce-scatter.13.cloned.1.call-start = ((), (), s32[]{:S(2)}) async-start(), calls=%async_computation.10 | async-start | bytes 9732096 | tf_op jit(solution)/shard_map/reduce_scatter | solution.py:111
  259.5 3.5 copy-start.31
  259.5 3.5 copy-start.2
  259.5 3.5 copy-start.20
  259.5 3.5 copy-start.24
  259.5 3.5 copy-start.27
  259.5 4.0 copy-start.5
  259.5 4.0 copy-start.7
  259.6 4.0 copy-start.33
Sparse Core Ops, SparseCore 0:
  17.4 31.6 all-gather.14
  50.7 28.8 all-gather.12
  81.1 28.8 all-gather.16
  157.7 20.2 all-gather.18
  183.7 99.0 reduce-scatter.8
  289.8 118.1 reduce-scatter.6
  414.5 134.8 reduce-scatter.10
  556.8 134.4 reduce-scatter.12
where the time goes:
time: 705 us; the launch traced here: 698 us
  waiting for transfers between devices  382 us (54%)
  matrix products  129 us (18%)
  local copies, waits for them, and re-layouts  80.7 us (11%)
  blocking collectives  64.6 us (9%)
  other arithmetic  25 us (4%)
  between operations  15.7 us (2%)
    reduce_scatter x1, waiting for transfers between devices, body(): lax.psum_scatter(grad_w_fc2, ('seq', 'batch'), scatter_dimension=0, tiled...  142 us
    reduce_scatter x1, waiting for transfers between devices, body(): lax.psum_scatter(grad_w_fc1, ('seq', 'batch'), scatter_dimension=0, tiled...  141 us
    reduce_scatter x1, waiting for transfers between devices, body(): lax.psum_scatter(grad_w_qkv, ('seq', 'batch'), scatter_dimension=0, tiled...  95.1 us
    unnamed x1, blocking collectives  41.4 us
    dot_general x2, matrix products, masked_scores(): jnp.einsum('rqhd,rkhd->rhqk', query_heads, key_heads, preferred_element_t...  20.6 us
    unnamed x97, local copies, waits for them, and re-layouts  17.2 us
  transfers between devices with their start and end apart: 8, of which 5 were waited for; matrix products, arithmetic and copies ran while one was open for 32% of the time, Pallas kernels for 0%

commit v1 on v0

v1 whole, which is shorter than its diff:
```python
import jax
import jax.numpy as jnp
from jax import lax
from jax.sharding import PartitionSpec as P

HEADS = 12
HEAD = 64
PAD = 16
LANES = 128
FAR = -(2.0**100)
F32 = jnp.float32
BF16 = jnp.bfloat16


def dot(a, b):
    return jnp.dot(a, b, preferred_element_type=F32)


def dot_t(a, b):
    return lax.dot_general(a, b, (((1,), (1,)), ((), ())), preferred_element_type=F32)


def dot_lt(a, b):
    return lax.dot_general(a, b, (((0,), (0,)), ((), ())), preferred_element_type=F32)


def normalize(v):
    center = v - jnp.mean(v, axis=-1, keepdims=True)
    spread = jnp.mean(center * center, axis=-1, keepdims=True)
    scale = lax.rsqrt(spread + 1e-06)
    return center * scale, scale


def normalize_back(grad_hat, hat, scale):
    mean_g = jnp.mean(grad_hat, axis=-1, keepdims=True)
    mean_gh = jnp.mean(grad_hat * hat, axis=-1, keepdims=True)
    return scale * (grad_hat - mean_g - hat * mean_gh)


def gelu_pair(v):
    half = 0.5 * (1.0 + lax.erf(v * 0.5**0.5))
    slope = half + v * jnp.exp(-0.5 * v * v) * 0.3989422804014327
    return v * half, slope


def pick(arr, index, axis):
    return lax.dynamic_index_in_dim(arr, index, axis, keepdims=False)


def total(parts):
    out = parts[0].astype(F32)
    for part in parts[1:]:
        out = out + part.astype(F32)
    return out


def swap_seq(v, mask):
    return lax.ppermute(v, "seq", [(i, i ^ mask) for i in range(lax.axis_size("seq"))])


def swap_batch(v, mask):
    return lax.ppermute(v, "batch", [(i, i ^ mask) for i in range(lax.axis_size("batch"))])


def halve(parts, axis, bit, kind, dtype=BF16):
    own = (lax.axis_index(kind) >> bit) & 1
    send = total([pick(p, 1 - own, axis) for p in parts]).astype(dtype)
    swap = swap_seq if kind == "seq" else swap_batch
    return [pick(p, own, axis) for p in parts] + [swap(send, 1 << bit)]


def bits_of(kind):
    return lax.axis_size(kind).bit_length() - 1


def split_bits(arr, axis, count):
    shape = arr.shape
    return arr.reshape(shape[:axis] + (2,) * count + shape[axis + 1 :])


def halve_batch(parts, axis, dtype=BF16, skip=()):
    left = [b for b in range(bits_of("batch")) if b not in skip]
    while left:
        bit = left.pop(0)
        parts = halve(parts, axis + len(left), bit, "batch", dtype)
    return parts


def body(
    patches,
    specials,
    segment_ids,
    special_order,
    keep_mask,
    norm_gains,
    norm_shifts,
    w_qkv,
    biases,
    w_out,
    w_fc1,
    fc1_bias,
    w_fc2,
    cot_patches,
    cot_specials,
):
    rows, count, width = patches.shape
    extra = specials.shape[1]
    images = keep_mask.shape[1] // 2
    block = count + PAD
    own_heads = HEADS // 4
    cols = own_heads * HEAD
    hidden = w_fc1.shape[1] // 4
    s = lax.axis_index("seq")
    nb = lax.axis_size("batch")
    nbits = bits_of("batch")

    zeros = jnp.zeros((PAD - extra, width), BF16)
    mine = jnp.concatenate([patches[0], specials[0], zeros], axis=0)
    segs = jnp.concatenate([segment_ids[0], special_order[0] // 2, jnp.full((PAD - extra,), -1, jnp.int32)])
    onehot = (segs[:, None] == jnp.arange(LANES, dtype=jnp.int32)).astype(BF16)
    pay = jnp.concatenate([mine, onehot], axis=1)
    cot = jnp.concatenate([cot_patches[0], cot_specials[0], zeros], axis=0)
    pay_c = swap_seq(pay, 1)
    pay_x = swap_seq(pay, 2)
    pay_d = swap_seq(pay_x, 1)
    cot_c = swap_seq(cot, 1)
    allpay = jnp.concatenate([pay, pay_c, pay_x, pay_d], axis=0)
    cots = jnp.concatenate([cot, cot_c], axis=0)
    tok = allpay[:, :width].astype(F32)
    hot = allpay[:, width:]
    hot_chip = hot[: 2 * block].astype(F32)
    keep = keep_mask[0].astype(F32) / 0.75
    keep_a = hot_chip[:, :images] @ keep[:images, None]
    keep_m = hot_chip[:, :images] @ keep[images:, None]

    hat1, scale1 = normalize(tok)
    normed = (hat1 * norm_gains[0] + norm_shifts[0]).astype(BF16)
    w_own = [lax.dynamic_slice(w_qkv, (0, j * width + s * cols), (width, cols)) for j in range(3)]
    bias_own = [lax.dynamic_slice(biases, (j, s * cols), (1, cols)) for j in range(2)]
    query = ((dot(normed, w_own[0]) + bias_own[0]).astype(BF16).astype(F32) * HEAD**-0.5).astype(BF16)
    key = dot(normed, w_own[1]).astype(BF16)
    value = (dot(normed, w_own[2]) + bias_own[1]).astype(BF16)
    far = jnp.where(hot[:, :images] > 0, 0.0, FAR).astype(BF16)

    def head(v, h):
        return v[:, h * HEAD : (h + 1) * HEAD]

    attended, tops = [], []
    for h in range(own_heads):
        q = jnp.concatenate([head(query, h), hot[:, :images]], axis=1)
        k = jnp.concatenate([head(key, h), far], axis=1)
        sc = dot_t(q, k)
        top = jnp.max(sc, axis=-1, keepdims=True)
        e = jnp.exp(sc - top)
        tot = jnp.sum(e, axis=-1, keepdims=True)
        attended.append(dot((e / tot).astype(BF16), head(value, h)))
        tops.append((top, tot))
    attended = jnp.concatenate(attended, axis=1).astype(BF16)

    chip = 2 * block
    att_x = swap_seq(attended[chip:], 2)
    six = jnp.concatenate([attended[:chip], att_x], axis=1)
    six_c = swap_seq(six, 1)
    six_c = jnp.concatenate([six_c[block:], six_c[:block]], axis=0)
    w_out_own = jnp.concatenate(
        [lax.dynamic_slice(w_out, ((s ^ j) * cols, 0), (cols, width)) for j in (0, 2)], axis=0
    )
    w_out_oth = jnp.concatenate(
        [lax.dynamic_slice(w_out, ((s ^ j) * cols, 0), (cols, width)) for j in (1, 3)], axis=0
    )
    branch = dot(six, w_out_own) + dot(six_c, w_out_oth) + biases[2]
    middle = tok[:chip] + keep_a * branch
    hat2, scale2 = normalize(middle)
    normed2 = (hat2 * norm_gains[1] + norm_shifts[1]).astype(BF16)
    gout = cots.astype(F32)
    gb2 = (keep_m * gout).astype(BF16)

    fc1 = [lax.dynamic_slice(w_fc1, (0, (s ^ j) * hidden), (width, hidden)) for j in (0, 2)]
    fc2 = [lax.dynamic_slice(w_fc2, ((s ^ j) * hidden, 0), (hidden, width)) for j in (0, 2)]
    f_bias = [lax.dynamic_slice(fc1_bias, ((s ^ j) * hidden,), (hidden,)) for j in (0, 2)]
    g_fc2, g_fc1, g_fb = [], [], []
    branch2 = 0.0
    gn2 = 0.0
    for j in range(2):
        pre = dot(normed2, fc1[j]) + f_bias[j]
        act, slope = gelu_pair(pre)
        act = act.astype(BF16)
        g_fc2.append(dot_lt(act, gb2).astype(BF16))
        gh = (dot_t(gb2, fc2[j]) * slope).astype(BF16)
        g_fc1.append(dot_lt(normed2, gh).astype(BF16))
        g_fb.append(jnp.sum(gh.astype(F32), axis=0))
        branch2 = branch2 + dot(act, fc2[j])
        gn2 = gn2 + dot_t(gh, fc1[j])

    keep2 = g_fc2[0].reshape(nb, -1, width)
    got2 = swap_seq(g_fc2[1], 2).reshape(nb, -1, width)
    parts2 = [split_bits(p, 0, nbits) for p in (keep2, got2)]
    out_fc2 = total(halve_batch(parts2, 0))

    arr = jnp.stack(g_fc1, axis=1).reshape(2, 2, nb, -1, 2, hidden)
    parts1 = [split_bits(arr, 2, nbits)]
    parts1 = halve(parts1, 2 + nbits - 1, 0, "batch")
    parts1 = halve(parts1, 0, 1, "seq")
    parts1[-1] = jnp.flip(parts1[-1], axis=-2)
    parts1 = halve_batch(parts1, 1, skip=(0,))
    sum1 = total(parts1)
    own_c = s & 1
    sent = pick(sum1, 1 - own_c, 0).astype(BF16)
    kept = pick(sum1, own_c, 0)
    got = swap_seq(sent, 1).astype(F32)
    rel = jnp.stack([kept[:, 0], got[:, 0], kept[:, 1], got[:, 1]], axis=0)
    out_fc1 = jnp.concatenate([pick(rel, s ^ a, 0) for a in range(4)], axis=1)

    b2_c = swap_seq(branch2[block:].astype(BF16), 1).astype(F32)
    result = middle[:block] + keep_m[:block] * (branch2[:block] + b2_c + biases[3])

    gn2_c = swap_seq(gn2.astype(BF16), 1).astype(F32)
    gn2 = gn2 + jnp.concatenate([gn2_c[block:], gn2_c[:block]], axis=0)
    gmid = gout + normalize_back(gn2 * norm_gains[1], hat2, scale2)
    gbr = (keep_a * gmid).astype(BF16)
    own = slice(0, block)
    small = [
        jnp.sum(gn2[own] * hat2[own], axis=0),
        jnp.sum(gn2[own], axis=0),
        jnp.sum(gb2[own].astype(F32), axis=0),
        jnp.sum(gbr[own].astype(F32), axis=0),
    ]
    g_out = [dot_lt(six[:, j * cols : (j + 1) * cols], gbr).astype(BF16) for j in range(2)]
    keep_o = g_out[0].reshape(nb, -1, width)
    got_o = swap_seq(g_out[1], 2).reshape(nb, -1, width)
    out_out = total(halve_batch([split_bits(p, 0, nbits) for p in (keep_o, got_o)], 0))

    gatt6 = dot_t(gbr, w_out_own).astype(BF16)
    gatt_x = swap_seq(gatt6[:, cols:], 2)
    gatt = jnp.concatenate([gatt6[:, :cols], gatt_x], axis=0)

    gq, gk, gv = [], [], []
    for h in range(own_heads):
        q = jnp.concatenate([head(query, h), hot[:, :images]], axis=1)
        k = jnp.concatenate([head(key, h), far], axis=1)
        top, tot = tops[h]
        prob = jnp.exp(dot_t(q, k) - top) / tot
        go = head(gatt, h)
        gp = dot_t(go, head(value, h))
        inner = jnp.sum(gp * prob, axis=-1, keepdims=True)
        gs = (prob * (gp - inner)).astype(BF16)
        gq.append(dot(gs, head(key, h)) * HEAD**-0.5)
        gk.append(dot_lt(gs, head(query, h)))
        gv.append(dot_lt(prob.astype(BF16), go))
    gq, gk, gv = [jnp.concatenate(v, axis=1).astype(BF16) for v in (gq, gk, gv)]
    gqkv = jnp.concatenate([gq, gk, gv], axis=1)
    w_cat = jnp.concatenate(w_own, axis=1)
    gn1 = dot_t(gqkv, w_cat)
    g_qkv = dot_lt(normed, gqkv).astype(BF16)
    small = small + [jnp.sum(gn1 * hat1, axis=0), jnp.sum(gn1, axis=0)]
    own_small = jnp.stack([jnp.sum(gq.astype(F32), axis=0), jnp.sum(gv.astype(F32), axis=0)])

    blocks = gn1.reshape(2, 2, block, width)
    got_n = swap_seq(blocks[:, 1].astype(BF16), 1)
    half_n = blocks[:, 0] + got_n.astype(F32)
    fin = half_n[0] + swap_seq(half_n[1].astype(BF16), 2).astype(F32)
    gtok = gmid[:block] + normalize_back(fin * norm_gains[0], hat1[:block], scale1[:block])

    arr = g_qkv.reshape(4, nb, -1, 3 * cols)
    sum_q = total(halve_batch([split_bits(arr, 1, nbits)], 1))
    pieces = [pick(sum_q, s, 0)] + [
        swap_seq(pick(sum_q, s ^ j, 0).astype(BF16), j).astype(F32) for j in (1, 2, 3)
    ]
    rel = jnp.stack(pieces, axis=0)
    absolute = jnp.stack([pick(rel, s ^ a, 0) for a in range(4)], axis=1)
    out_qkv = absolute.reshape(-1, 4, 3, cols).transpose(0, 2, 1, 3).reshape(-1, 3 * width)

    sm = jnp.stack(small).reshape(6, 2, 2, nb, -1)
    parts = [split_bits(sm, 3, nbits)]
    parts = halve(parts, 1, 1, "seq", F32)
    parts = halve(parts, 1, 0, "seq", F32)
    sums = total(halve_batch(parts, 1, F32))
    sums_own = total(halve_batch([split_bits(own_small.reshape(2, nb, -1), 1, nbits)], 1, F32))
    fb_keep = g_fb[0].reshape(nb, -1)
    fb_got = swap_seq(g_fb[1], 2).reshape(nb, -1)
    out_fb = total(halve_batch([split_bits(p, 0, nbits) for p in (fb_keep, fb_got)], 0, F32))

    grad_gains = jnp.stack([sums[4], sums[0]])
    grad_shifts = jnp.stack([sums[5], sums[1]])
    grad_biases = jnp.stack([sums_own[0], sums_own[1], sums[3], sums[2]])
    return (
        result[None, :count].astype(BF16),
        result[None, count : count + extra].astype(BF16),
        gtok[None, :count],
        gtok[None, count : count + extra],
        grad_gains,
        grad_shifts,
        out_qkv,
        grad_biases,
        out_out,
        out_fc1,
        out_fb,
        out_fc2,
    )


def solution(mesh):
    tok = P("batch", "seq", None)
    ids = P("batch", "seq")
    split = P(None, ("seq", "batch"))
    rows = P(("seq", "batch"), None)
    return jax.shard_map(
        body,
        mesh=mesh,
        in_specs=(tok, tok, ids, ids, P("batch", None)) + (P(),) * 8 + (tok, tok),
        out_specs=(tok, tok, tok, tok, split, split, rows, split, rows, rows, P(("seq", "batch")), rows),
        check_vma=False,
    )
```

time: 705 us -> 281 us (0.40)
  waiting for transfers between devices: 382 us -> 57.4 us
  blocking collectives: 64.6 us -> 0 us
  matrix products: 129 us -> 77.6 us
  local copies, waits for them, and re-layouts: 80.7 us -> 35.2 us
  starting transfers between devices: 0.54 us -> 43.8 us
  other arithmetic: 25 us -> 59.5 us
  between operations: 15.7 us -> 2.36 us
    reduce_scatter x4 -> x0, waiting for transfers between devices: 378 us -> none  [the longest x1 142 us: body(): lax.psum_scatter(grad_w_fc2, ('seq', 'batch'), scatter_dimension=0, tiled...]
    ppermute x0 -> x42, waiting for transfers between devices: none -> 57.4 us  [the longest x21 34.4 us: swap_batch(): lax.ppermute(v, 'batch', [(i, i ^ mask) for i in range(lax.axis_size('bat...]
    dot_general x19 -> x42, matrix products: 129 us -> 77.6 us  [the longest x12 30.7 us: dot_t(): lax.dot_general(a, b, (((1,), (1,)), ((), ())), preferred_element_type=F32)]
    ppermute x0 -> x42, starting transfers between devices: none -> 43.8 us  [the longest x21 25.5 us: swap_batch(): lax.ppermute(v, 'batch', [(i, i ^ mask) for i in range(lax.axis_size('bat...]
    unnamed x1 -> x0, blocking collectives: 41.4 us -> none
    all_gather x7 -> x0, local copies, waits for them, and re-layouts: 32.8 us -> none  [the longest x1 8.55 us: body(): lax.all_gather(value_proj, 'seq', axis=1, tiled=True)]
    convert_element_type x1 -> x21, other arithmetic: 2.29 us -> 29.1 us  [the longest x11 14.1 us: halve(): send = total([pick(p, 1 - own, axis) for p in parts]).astype(dtype)]
    all_gather x4 -> x0, blocking collectives: 23.2 us -> none  [the longest x1 6.8 us: body(): lax.all_gather(seg_all, 'seq', axis=1, tiled=True)]
  transfers between devices with their start and end apart: 8 -> 42, of which waited for: 5 -> 20; matrix products, arithmetic and copies ran while one was open for 32% -> 54% of each run, Pallas kernels for 0% -> 0%
where the time goes in v1:
time: 281 us; the launch traced here: 276 us
  matrix products  77.6 us (28%)
  other arithmetic  59.5 us (21%)
  waiting for transfers between devices  57.4 us (20%)
  starting transfers between devices  43.8 us (16%)
  local copies, waits for them, and re-layouts  35.2 us (13%)
    ppermute x21, waiting for transfers between devices, swap_batch(): lax.ppermute(v, 'batch', [(i, i ^ mask) for i in range(lax.axis_size('bat...  34.4 us
    dot_general x12, matrix products, dot_t(): lax.dot_general(a, b, (((1,), (1,)), ((), ())), preferred_element_type=F32)  30.7 us
    dot_general x13, matrix products, dot_lt(): lax.dot_general(a, b, (((0,), (0,)), ((), ())), preferred_element_type=F32)  26.8 us
    ppermute x21, starting transfers between devices, swap_batch(): lax.ppermute(v, 'batch', [(i, i ^ mask) for i in range(lax.axis_size('bat...  25.5 us
    ppermute x21, waiting for transfers between devices, swap_seq(): lax.ppermute(v, 'seq', [(i, i ^ mask) for i in range(lax.axis_size('seq'))])  22.9 us
    dot_general x15, matrix products, dot(): return jnp.dot(a, b, preferred_element_type=F32)  19.7 us
    ppermute x21, starting transfers between devices, swap_seq(): lax.ppermute(v, 'seq', [(i, i ^ mask) for i in range(lax.axis_size('seq'))])  18.3 us
    convert_element_type x11, other arithmetic, halve(): send = total([pick(p, 1 - own, axis) for p in parts]).astype(dtype)  14.1 us
  transfers between devices with their start and end apart: 42, of which 20 were waited for; matrix products, arithmetic and copies ran while one was open for 54% of the time, Pallas kernels for 0%

profile of v1, /device:TPU:0, one launch (start us, length us, event | category | flops | bytes accessed | tf_op | source)
XLA Modules:
  0.0 275.9 jit_solution(6121105057747643825)
XLA Ops:
  3.4 3.0 %collective-permute-start.1 = (bf16[272,896]{1,0:T(8,128)(2,1)S(1)}, bf16[272,896]{1,0:T(8,128)(2,1)S(1)}, u32[]{:S(2)}, u32[]{:S(2)}) collective-permute-start(bf16[272,896]{1,0:T(8,128)(2,1)S(1)} %pad_maximum_fusion.4), channel_id=1, source_target_pairs={{0,16},{8,24},{16,0},{24,8},{1,17},{9,25},{17,1},{25,9},{2,18},{10... | collective-permute-start | bytes 1462280 | tf_op jit(solution)/shard_map/ppermute | solution.py:58
  6.4 1.8 pad_maximum_fusion.6
  12.3 5.2 %collective-permute-done.1 = bf16[272,896]{1,0:T(8,128)(2,1)S(1)} collective-permute-done((bf16[272,896]{1,0:T(8,128)(2,1)S(1)}, bf16[272,896]{1,0:T(8,128)(2,1)S(1)}, u32[]{:S(2)}, u32[]{:S(2)}) %collective-permute-start.1) | collective-permute-done | bytes 487456 | tf_op jit(solution)/shard_map/ppermute | solution.py:58
  17.7 3.1 %constant_dynamic-slice_fusion.55 = (bf16[768,192]{1,0:T(8,128)(2,1)}, bf16[768,192]{1,0:T(8,128)(2,1)}, bf16[768,192]{1,0:T(8,128)(2,1)}) fusion(bf16[768,2304]{1,0:T(8,128)(2,1)} %param.22, s32[]{:T(128)S(6)} %select_n.266, s32[]{:T(128)S(6)} %select_n.264, s32[]{:T(128)S(6)} %select_n.268), kind=kLoop, calls=%fused_computation.338 | loop fusion | bytes 1769484 | tf_op jit(solution)/shard_map/dynamic_slice | solution.py:138
  22.2 5.2 %pad_maximum_fusion = bf16[1088,896]{1,0:T(8,128)(2,1)S(1)} fusion(bf16[272,896]{1,0:T(8,128)(2,1)} %copy-done.25, bf16[272,896]{1,0:T(8,128)(2,1)} %copy-done.24, bf16[272,896]{1,0:T(8,128)(2,1)S(1)} %collective-permute-done, bf16[272,128]{1,0:T(8,128)(2,1)S(1)} %fusion.98, bf16[12,768]{1,0:T(8,128)(2,1)S(1)} %broadcast_in_dim.14, ...), kind=kLoop, calls=%fused_computation.60 | loop fusion | flops 13647872 | bytes 3899392 | tf_op jit(solution)/shard_map/concatenate | solution.py:127
  37.9 1.6 copy-done
  44.9 1.8 collective-permute-start.3
  47.2 6.1 %collective-permute-done.3 = bf16[544,192]{0,1:T(8,128)(2,1)S(1)} collective-permute-done((bf16[544,192]{0,1:T(8,128)(2,1)S(1)}, bf16[544,192]{0,1:T(8,128)(2,1)S(1)}, u32[]{:S(2)}, u32[]{:S(2)}) %collective-permute-start.3) | collective-permute-done | bytes 208928 | tf_op jit(solution)/shard_map/ppermute | solution.py:58
  53.7 1.6 collective-permute-done.4
  59.9 1.9 multiply_convert_fusion.5
  61.8 2.3 convert_reduce_fusion.2
  65.2 2.0 fusion.46
  68.2 2.6 convert_reduce_fusion.1
  70.8 1.8 collective-permute-start.34
  72.6 2.2 convolution_convert_fusion.12
  74.7 3.3 %convolution_convert_fusion.10 = bf16[768,768]{1,0:T(8,128)(2,1)} fusion(bf16[544,768]{1,0:T(8,128)(2,1)S(1)} %get-tuple-element.162, f32[544]{0:T(1024)S(1)} %convolution_reduce_fusion, bf16[272,768]{1,0:T(8,128)(2,1)} %collective-permute-done.6, bf16[12,768]{1,0:T(8,128)(2,1)S(1)} %broadcast_in_dim.14, bf16[4,768]{1,0:T(4,128)(2,1)S(1)} %bitcast.466, ...), kind=kOutput, calls=%fused_computation.90 | convolution fusion | flops 646496256 | bytes 2852992 | tf_op jit(solution)/shard_map/dot_general | solution.py:24
  78.5 4.4 %fusion.226 = (bf16[544,768]{1,0:T(8,128)(2,1)}, f32[544,768]{1,0:T(8,128)}) fusion(f32[544,768]{1,0:T(8,128)} %fusion.46, bf16[544,768]{1,0:T(8,128)(2,1)} %copy-done.40, bf16[768,3072]{1,0:T(8,128)(2,1)} %param.25, s32[]{:T(128)S(6)} %select_n.273), kind=kOutput, calls=%fused_computation.472 | convolution fusion | flops 642564096 | bytes 6193156 | tf_op jit(solution)/shard_map/dot_general | solution.py:20
  82.9 2.2 fusion.44
  85.1 2.1 convolution_add_fusion.3
  89.8 1.8 collective-permute-start.35
  91.7 1.8 collective-permute-done.35
  93.5 2.1 collective-permute-start.36
  95.6 2.3 copy_bitcast_fusion
  99.5 2.7 collective-permute-start.37
  102.1 3.2 %convolution_convert_fusion.11 = bf16[768,768]{1,0:T(8,128)(2,1)} fusion(bf16[544,768]{1,0:T(8,128)(2,1)S(1)} %copy-done.87, f32[544]{0:T(1024)S(1)} %copy-done.70, bf16[272,768]{1,0:T(8,128)(2,1)} %collective-permute-done.6, bf16[12,768]{1,0:T(8,128)(2,1)S(1)} %broadcast_in_dim.14, bf16[4,768]{1,0:T(4,128)(2,1)S(1)} %bitcast.467, ...), kind=kOutput, calls=%fused_computation.91 | convolution fusion | flops 646496256 | bytes 2852992 | tf_op jit(solution)/shard_map/dot_general | solution.py:24
  111.9 2.8 %multiply_convert_fusion.3 = (bf16[544,768]{1,0:T(8,128)(2,1)S(1)}, f32[544,768]{1,0:T(8,128)}, bf16[544,768]{1,0:T(8,128)(2,1)S(1)}) fusion(f32[544]{0:T(1024)S(1)} %copy-done.62, f32[544,768]{1,0:T(8,128)S(1)} %copy-done.5, f32[544]{0:T(1024)S(1)} %broadcast_multiply_fusion.1, f32[544]{0:T(1024)S(1)} %broadcast_multiply_fusion.2, ...), kind=kLoop, calls=%fused_computation.81 | loop fusion | flops 7520256 | bytes 7534208 | tf_op jit(solution)/shard_map/convert_element_type | solution.py:220
  120.1 2.4 convolution_convert_fusion.16
  124.3 3.6 %collective-permute-done.8 = bf16[544,192]{1,0:T(8,128)(2,1)S(1)} collective-permute-done((bf16[544,192]{1,0:T(8,128)(2,1)S(1)}, bf16[544,192]{1,0:T(8,128)(2,1)S(1)}, u32[]{:S(2)}, u32[]{:S(2)}) %collective-permute-start.8) | collective-permute-done | bytes 208928 | tf_op jit(solution)/shard_map/ppermute | solution.py:58
  127.8 3.7 %multiply_reduce_fusion.2 = (f32[1088]{0:T(1024)S(1)}, f32[1088,1088]{0,1:T(8,128)S(1)}) fusion(f32[1088]{0:T(1024)S(1)} %copy-done.66, f32[1088,1088]{0,1:T(8,128)} %copy-done.1, f32[1088]{0:T(1024)S(1)} %copy-done.52, bf16[1088,192]{0,1:T(8,128)(2,1)S(1)} %copy-done.85, bf16[544,192]{1,0:T(8,128)(2,1)S(1)} %get-tuple-element.103, ...), kind=kOutput, calls=%fused_computation.5 | convolution fusion | flops 156531648 | bytes 10195200 | tf_op jit(solution)/shard_map/dot_general | solution.py:20
  134.1 3.5 %multiply_reduce_fusion = (f32[1088]{0:T(1024)S(1)}, f32[1088,1088]{0,1:T(8,128)}) fusion(f32[1088]{0:T(1024)S(1)} %copy-done.64, f32[1088,1088]{0,1:T(8,128)S(1)} %bitcast.416, f32[1088]{0:T(1024)S(1)} %get-tuple-element.131, bf16[1088,192]{0,1:T(8,128)(2,1)S(1)} %copy-done.85, bf16[544,192]{1,0:T(8,128)(2,1)S(1)} %collective-permute-done.8, ...), kind=kOutput, calls=%fused_computation.1 | convolution fusion | flops 156531648 | bytes 10473728 | tf_op jit(solution)/shard_map/dot_general | solution.py:20
  137.5 3.5 %multiply_convert_fusion = bf16[1088,1088]{0,1:T(8,128)(2,1)S(1)} fusion(f32[1088,1088]{0,1:T(8,128)} %get-tuple-element.150, f32[1088]{0:T(1024)S(1)} %get-tuple-element.149, f32[1088]{0:T(1024)S(1)} %copy-done.64, f32[1088,1088]{0,1:T(8,128)S(1)} %bitcast.416, f32[1088]{0:T(1024)S(1)} %get-tuple-element.131), kind=kLoop, calls=%fused_computation | loop fusion | flops 5918720 | bytes 11850496 | tf_op jit(solution)/shard_map/convert_element_type | solution.py:246
  141.1 3.5 %multiply_reduce_fusion.1 = (f32[1088]{0:T(1024)S(1)}, f32[1088,1088]{0,1:T(8,128)}) fusion(f32[1088]{0:T(1024)S(1)} %copy-done.68, f32[1088,1088]{0,1:T(8,128)S(1)} %bitcast.420, f32[1088]{0:T(1024)S(1)} %copy-done.54, bf16[1088,192]{0,1:T(8,128)(2,1)S(1)} %copy-done.85, bf16[544,192]{1,0:T(8,128)(2,1)S(1)} %get-tuple-element.103, ...), kind=kOutput, calls=%fused_computation.3 | convolution fusion | flops 156531648 | bytes 10473728 | tf_op jit(solution)/shard_map/dot_general | solution.py:20
  144.6 5.0 %multiply_convert_fusion.1 = bf16[1088,1088]{0,1:T(8,128)(2,1)} fusion(f32[1088,1088]{0,1:T(8,128)} %get-tuple-element.146, f32[1088]{0:T(1024)S(1)} %get-tuple-element.145, f32[1088]{0:T(1024)S(1)} %copy-done.68, f32[1088,1088]{0,1:T(8,128)S(1)} %bitcast.420, f32[1088]{0:T(1024)S(1)} %copy-done.54), kind=kLoop, calls=%fused_computation.2 | loop fusion | flops 5918720 | bytes 11850496 | tf_op jit(solution)/shard_map/convert_element_type | solution.py:246
  149.6 2.9 %constant_dynamic-update-slice_fusion.4 = (bf16[1088,576]{0,1:T(8,128)(2,1)}, bf16[1088,64]{0,1:T(8,128)(2,1)S(1)}) fusion(bf16[1088,576]{0,1:T(8,128)(2,1)} %get-tuple-element.143, bf16[1088,1088]{0,1:T(8,128)(2,1)} %multiply_convert_fusion.1, bf16[1088,192]{0,1:T(8,128)(2,1)S(1)} %copy-done.17), kind=kOutput, calls=%fused_computation.351 | convolution fusion | flops 151658496 | bytes 2940928 | tf_op jit(solution)/shard_map/dot_general | solution.py:16
  158.5 1.8 constant_dynamic-update-slice_fusion.2
  160.4 1.7 constant_dynamic-update-slice_fusion.1
  162.0 1.6 constant_dynamic-update-slice_fusion
  163.7 3.8 %convolution_convert_fusion.14 = bf16[768,576]{0,1:T(8,128)(2,1)} fusion(bf16[1088,576]{0,1:T(8,128)(2,1)} %get-tuple-element.157, bf16[1088,768]{1,0:T(8,128)(2,1)S(1)} %copy-done.14), kind=kOutput, calls=%fused_computation.99 | convolution fusion | flops 963035136 | bytes 3809280 | tf_op jit(solution)/shard_map/dot_general | solution.py:24
  167.5 4.7 %fusion.213 = (f32[768]{0:T(1024)S(1)}, f32[768]{0:T(1024)S(1)}, f32[1088,768]{1,0:T(8,128)}, f32[1088,768]{1,0:T(8,128)}) fusion(f32[1088]{0:T(1024)S(1)} %copy-done.60, f32[1088]{0:T(1024)S(1)} %broadcast_multiply_fusion, bf16[1088,896]{1,0:T(8,128)(2,1)S(1)} %pad_maximum_fusion, bf16[1088,576]{0,1:T(8,128)(2,1)S(1)} %copy-done.73, ...), kind=kOutput, calls=%fused_computation.459 | convolution fusion | flops 970258944 | bytes 10508800 | tf_op jit(solution)/shard_map/dot_general | solution.py:20
  178.4 2.4 fusion.55
  180.9 2.0 collective-permute-start.11
  182.9 2.4 collective-permute-done.11
  186.9 3.1 %collective-permute-done.23 = f32[2,2,24]{2,1,0:T(2,128)S(1)} collective-permute-done((f32[2,2,24]{2,1,0:T(2,128)S(1)}, f32[2,2,24]{2,1,0:T(2,128)S(1)}, u32[]{:S(2)}, u32[]{:S(2)}) %collective-permute-start.23) | collective-permute-done | bytes 416 | tf_op jit(solution)/shard_map/ppermute | solution.py:62
  190.6 3.2 %collective-permute-done.13 = f32[6,2,2,24]{3,0,2,1:T(8,128)S(1)} collective-permute-done((f32[6,2,2,24]{3,0,2,1:T(8,128)S(1)}, f32[6,2,2,24]{3,0,2,1:T(8,128)S(1)}, u32[]{:S(2)}, u32[]{:S(2)}) %collective-permute-start.13) | collective-permute-done | bytes 2336 | tf_op jit(solution)/shard_map/ppermute | solution.py:62
  194.3 3.2 %collective-permute-done.14 = f32[6,2,24]{2,0,1:T(8,128)S(1)} collective-permute-done((f32[6,2,24]{2,0,1:T(8,128)S(1)}, f32[6,2,24]{2,0,1:T(8,128)S(1)}, u32[]{:S(2)}, u32[]{:S(2)}) %collective-permute-start.14) | collective-permute-done | bytes 1184 | tf_op jit(solution)/shard_map/ppermute | solution.py:62
  198.5 3.4 %collective-permute-done.24 = f32[2,24]{1,0:T(2,128)S(1)} collective-permute-done((f32[2,24]{1,0:T(2,128)S(1)}, f32[2,24]{1,0:T(2,128)S(1)}, u32[]{:S(2)}, u32[]{:S(2)}) %collective-permute-start.24) | collective-permute-done | bytes 224 | tf_op jit(solution)/shard_map/ppermute | solution.py:62
  203.0 3.4 %collective-permute-done.15 = f32[6,24]{1,0:T(8,128)S(1)} collective-permute-done((f32[6,24]{1,0:T(8,128)S(1)}, f32[6,24]{1,0:T(8,128)S(1)}, u32[]{:S(2)}, u32[]{:S(2)}) %collective-permute-start.15) | collective-permute-done | bytes 608 | tf_op jit(solution)/shard_map/ppermute | solution.py:62
  211.2 1.5 collective-permute-start.39
  212.7 2.6 collective-permute-done.26
  218.0 1.9 collective-permute-start.30
  224.5 2.0 collective-permute-done.28
  227.9 2.2 collective-permute-done.17
  230.2 1.7 fusion.83
  231.9 1.8 collective-permute-start.18
  234.5 1.9 fusion.69
  238.4 2.0 rev.4
  240.4 1.9 fusion.70
  244.3 2.0 collective-permute-start.21
  247.9 2.3 collective-permute-done.20
  251.8 1.9 fusion.30
  258.3 2.0 collective-permute-start.41
  260.2 7.0 %collective-permute-done.32 = bf16[2,24,2,768]{3,1,0,2:T(8,128)(2,1)S(1)} collective-permute-done((bf16[2,24,2,768]{3,1,0,2:T(8,128)(2,1)S(1)}, bf16[2,24,2,768]{3,1,0,2:T(8,128)(2,1)S(1)}, u32[]{:S(2)}, u32[]{:S(2)}) %collective-permute-start.32) | collective-permute-done | bytes 147488 | tf_op jit(solution)/shard_map/ppermute | solution.py:62
  268.5 1.8 collective-permute-done.41
  270.3 1.9 fusion.78
  (408 shorter events, 99.5 us)
Async XLA Ops:
  0.6 8.1 %copy-start.76 = (f32[2,768]{1,0:T(2,128)S(1)}, f32[2,768]{1,0:T(2,128)}, u32[]{:S(2)}) copy-start(f32[2,768]{1,0:T(2,128)} %param.20) | copy-start | bytes 18436
  0.7 8.7 %copy-start.77 = (f32[2,768]{1,0:T(2,128)S(1)}, f32[2,768]{1,0:T(2,128)}, u32[]{:S(2)}) copy-start(f32[2,768]{1,0:T(2,128)} %param.21) | copy-start | bytes 18436
  0.7 9.3 %copy-start.78 = (f32[4,768]{1,0:T(4,128)S(1)}, f32[4,768]{1,0:T(4,128)}, u32[]{:S(2)}) copy-start(f32[4,768]{1,0:T(4,128)} %param.23) | copy-start | bytes 36868
  0.7 9.9 %copy-start.32 = (bf16[768,768]{1,0:T(8,128)(2,1)S(1)}, bf16[768,768]{1,0:T(8,128)(2,1)}, u32[]{:S(2)}) copy-start(bf16[768,768]{1,0:T(8,128)(2,1)} %param.24) | copy-start | bytes 3538948
  3.4 8.2 %copy-start.79 = (f32[3072]{0:T(1024)S(1)}, f32[3072]{0:T(1024)}, u32[]{:S(2)}) copy-start(f32[3072]{0:T(1024)} %param.26) | copy-start | bytes 36868
  3.4 14.1 %collective-permute-start.1 = (bf16[272,896]{1,0:T(8,128)(2,1)S(1)}, bf16[272,896]{1,0:T(8,128)(2,1)S(1)}, u32[]{:S(2)}, u32[]{:S(2)}) collective-permute-start(bf16[272,896]{1,0:T(8,128)(2,1)S(1)} %pad_maximum_fusion.4), channel_id=1, source_target_pairs={{0,16},{8,24},{16,0},{24,8},{1,17},{9,25},{17,1},{25,9},{2,18},{10... | collective-permute-start | bytes 1462280 | tf_op jit(solution)/shard_map/ppermute | solution.py:58
  6.4 14.9 %collective-permute-start = (bf16[272,896]{1,0:T(8,128)(2,1)S(1)}, bf16[272,896]{1,0:T(8,128)(2,1)S(1)}, u32[]{:S(2)}, u32[]{:S(2)}) collective-permute-start(bf16[272,896]{1,0:T(8,128)(2,1)S(1)} %pad_maximum_fusion.4), channel_id=1, source_target_pairs={{0,8},{8,0},{16,24},{24,16},{1,9},{9,1},{17,25},{25,17},{2,10},{10... | collective-permute-start | bytes 1462280 | tf_op jit(solution)/shard_map/ppermute | solution.py:58
  8.2 53.5 %collective-permute-start.6 = (bf16[272,768]{1,0:T(8,128)(2,1)}, bf16[272,768]{1,0:T(8,128)(2,1)}, u32[]{:S(2)}, u32[]{:S(2)}) collective-permute-start(bf16[272,768]{1,0:T(8,128)(2,1)} %pad_maximum_fusion.6), channel_id=1, source_target_pairs={{0,8},{8,0},{16,24},{24,16},{1,9},{9,1},{17,25},{25,17},{2,10},{10... | collective-permute-start | bytes 1253384 | tf_op jit(solution)/shard_map/ppermute | solution.py:58
  9.4 19.1 %copy-start.55 = (f32[768]{0:T(1024)}, f32[768]{0:T(1024)S(1)}, u32[]{:S(2)}) copy-start(f32[768]{0:T(1024)S(1)} %get-tuple-element.71) | copy-start | bytes 9220
  11.6 9.1 %copy-start.83 = (s32[1,16]{1,0:T(1,128)S(1)}, s32[1,16]{1,0:T(1,128)}, u32[]{:S(2)}) copy-start(s32[1,16]{1,0:T(1,128)} %param.19) | copy-start | bytes 196
  11.6 9.7 %copy-start.15 = (bf16[1,256,768]{2,1,0:T(8,128)(2,1)S(1)}, bf16[1,256,768]{2,1,0:T(8,128)(2,1)}, u32[]{:S(2)}) copy-start(bf16[1,256,768]{2,1,0:T(8,128)(2,1)} %param.15) | copy-start | bytes 1179652
  11.6 9.7 %copy-start.50 = (bf16[1,4,768]{2,1,0:T(4,128)(2,1)S(1)}, bf16[1,4,768]{2,1,0:T(4,128)(2,1)}, u32[]{:S(2)}) copy-start(bf16[1,4,768]{2,1,0:T(4,128)(2,1)} %param.16) | copy-start | bytes 18436
  17.5 3.8 %collective-permute-start.2 = (bf16[272,896]{1,0:T(8,128)(2,1)S(1)}, bf16[272,896]{1,0:T(8,128)(2,1)S(1)}, u32[]{:S(2)}, u32[]{:S(2)}) collective-permute-start(bf16[272,896]{1,0:T(8,128)(2,1)S(1)} %collective-permute-done.1), channel_id=1, source_target_pairs={{0,8},{8,0},{16,24},{24,16},{1,9},{9,1},{17,25},{25,17},{2,10},{10... | collective-permute-start | bytes 1462280 | tf_op jit(solution)/shard_map/ppermute | solution.py:58
  28.4 18.8 %copy-start.59 = (f32[1088]{0:T(1024)}, f32[1088]{0:T(1024)S(1)}, u32[]{:S(2)}) copy-start(f32[1088]{0:T(1024)S(1)} %add_rsqrt_fusion) | copy-start | bytes 13060
  31.2 11.0 %copy-start.84 = (bf16[1088,192]{0,1:T(8,128)(2,1)}, bf16[1088,192]{0,1:T(8,128)(2,1)S(1)}, u32[]{:S(2)}) copy-start(bf16[1088,192]{0,1:T(8,128)(2,1)S(1)} %fusion.10) | copy-start | bytes 1253380
  44.8 8.6 %copy-start.19 = (bf16[1088,192]{0,1:T(8,128)(2,1)}, bf16[1088,192]{0,1:T(8,128)(2,1)S(1)}, u32[]{:S(2)}) copy-start(bf16[1088,192]{0,1:T(8,128)(2,1)S(1)} %pad_maximum_fusion.5) | copy-start | bytes 1253380
  44.9 8.4 %collective-permute-start.3 = (bf16[544,192]{0,1:T(8,128)(2,1)S(1)}, bf16[544,192]{0,1:T(8,128)(2,1)S(1)}, u32[]{:S(2)}, u32[]{:S(2)}) collective-permute-start(bf16[544,192]{0,1:T(8,128)(2,1)S(1)} %get-tuple-element.95), channel_id=1, source_target_pairs={{0,16},{8,24},{16,0},{24,8},{1,17},{9,25},{17,1},{25,9},{2,18},{10... | collective-permute-start | bytes 626696 | tf_op jit(solution)/shard_map/ppermute | solution.py:58
  47.0 27.8 %copy-start.69 = (f32[544]{0:T(1024)}, f32[544]{0:T(1024)S(1)}, u32[]{:S(2)}) copy-start(f32[544]{0:T(1024)S(1)} %convolution_reduce_fusion) | copy-start | bytes 6532
  47.2 9.6 %copy-start.61 = (f32[544]{0:T(1024)}, f32[544]{0:T(1024)S(1)}, u32[]{:S(2)}) copy-start(f32[544]{0:T(1024)S(1)} %convolution_reduce_fusion.1) | copy-start | bytes 6532
  53.4 1.9 collective-permute-start.4
  70.8 18.9 %collective-permute-start.34 = (f32[768]{0:T(1024)S(1)}, f32[768]{0:T(1024)S(1)}, u32[]{:S(2)}, u32[]{:S(2)}) collective-permute-start(f32[768]{0:T(1024)S(1)} %get-tuple-element.166), channel_id=1, source_target_pairs={{0,16},{8,24},{16,0},{24,8},{1,17},{9,25},{17,1},{25,9},{2,18},{10... | collective-permute-start | bytes 9224 | tf_op jit(solution)/shard_map/ppermute | solution.py:58
  78.1 131.8 %collective-permute-start.38 = (bf16[768,768]{1,0:T(8,128)(2,1)}, bf16[768,768]{1,0:T(8,128)(2,1)}, u32[]{:S(2)}, u32[]{:S(2)}) collective-permute-start(bf16[768,768]{1,0:T(8,128)(2,1)} %convolution_convert_fusion.10), channel_id=1, source_target_pairs={{0,16},{8,24},{16,0},{24,8},{1,17},{9,25},{17,1},{25,9},{2,18},{10... | collective-permute-start | bytes 3538952 | tf_op jit(solution)/shard_map/ppermute | solution.py:58
  82.9 25.6 %collective-permute-start.7 = (bf16[544,768]{1,0:T(8,128)(2,1)}, bf16[544,768]{1,0:T(8,128)(2,1)}, u32[]{:S(2)}, u32[]{:S(2)}) collective-permute-start(bf16[544,768]{1,0:T(8,128)(2,1)} %get-tuple-element.139), channel_id=1, source_target_pairs={{0,8},{8,0},{16,24},{24,16},{1,9},{9,1},{17,25},{25,17},{2,10},{10... | collective-permute-start | bytes 2506760 | tf_op jit(solution)/shard_map/ppermute | solution.py:58
  89.3 16.7 %collective-permute-start.5 = (bf16[272,768]{1,0:T(8,128)(2,1)}, bf16[272,768]{1,0:T(8,128)(2,1)}, u32[]{:S(2)}, u32[]{:S(2)}) collective-permute-start(bf16[272,768]{1,0:T(8,128)(2,1)} %slice.456), channel_id=1, source_target_pairs={{0,8},{8,0},{16,24},{24,16},{1,9},{9,1},{17,25},{25,17},{2,10},{10... | collective-permute-start | bytes 1253384 | tf_op jit(solution)/shard_map/ppermute | solution.py:58
  89.8 3.7 %collective-permute-start.35 = (f32[2,2,96]{2,1,0:T(2,128)S(1)}, f32[2,2,96]{2,1,0:T(2,128)S(1)}, u32[]{:S(2)}, u32[]{:S(2)}) collective-permute-start(f32[2,2,96]{2,1,0:T(2,128)S(1)} %bitcast.473), channel_id=1, source_target_pairs={{0,1},{1,0},{2,3},{3,2},{4,5},{5,4},{6,7},{7,6},{8,9},{9,8},{10,11... | collective-permute-start | bytes 4616 | tf_op jit(solution)/shard_map/ppermute | solution.py:62
  93.5 5.9 %collective-permute-start.36 = (f32[2,96]{1,0:T(2,128)S(1)}, f32[2,96]{1,0:T(2,128)S(1)}, u32[]{:S(2)}, u32[]{:S(2)}) collective-permute-start(f32[2,96]{1,0:T(2,128)S(1)} %add.1154), channel_id=1, source_target_pairs={{0,2},{1,3},{2,0},{3,1},{4,6},{5,7},{6,4},{7,5},{8,10},{9,11},{10,... | collective-permute-start | bytes 2312 | tf_op jit(solution)/shard_map/ppermute | solution.py:62
  97.9 118.9 %collective-permute-start.29 = (bf16[2,2,2,2,24,2,768]{6,4,1,5,3,2,0:T(8,128)(2,1)}, bf16[2,2,2,2,24,2,768]{6,4,1,5,3,2,0:T(8,128)(2,1)}, u32[]{:S(2)}, u32[]{:S(2)}) collective-permute-start(bf16[2,2,2,2,24,2,768]{6,4,1,5,3,2,0:T(8,128)(2,1)} %copy_bitcast_fusion), channel_id=1, source_target_pairs={{0,1},{1,0},{2,3},{3,2},{4,5},{5,4},{6,7},{7,6},{8,9},{9,8},{10,11... | collective-permute-start | bytes 3538952 | tf_op jit(solution)/shard_map/ppermute | solution.py:62
  99.5 5.9 %collective-permute-start.37 = (f32[96]{0:T(128)S(1)}, f32[96]{0:T(128)S(1)}, u32[]{:S(2)}, u32[]{:S(2)}) collective-permute-start(f32[96]{0:T(128)S(1)} %fusion.172), channel_id=1, source_target_pairs={{0,4},{1,5},{2,6},{3,7},{4,0},{5,1},{6,2},{7,3},{8,12},{9,13},{10,... | collective-permute-start | bytes 1160 | tf_op jit(solution)/shard_map/ppermute | solution.py:62
  117.3 10.5 %copy-start.52 = (f32[1088]{0:T(1024)S(1)}, f32[1088]{0:T(1024)}, u32[]{:S(2)}) copy-start(f32[1088]{0:T(1024)} %copy-done.51) | copy-start | bytes 13060
  117.3 10.5 %copy-start.66 = (f32[1088]{0:T(1024)S(1)}, f32[1088]{0:T(1024)}, u32[]{:S(2)}) copy-start(f32[1088]{0:T(1024)} %copy-done.65) | copy-start | bytes 13060
  117.3 10.5 %copy-start.85 = (bf16[1088,192]{0,1:T(8,128)(2,1)S(1)}, bf16[1088,192]{0,1:T(8,128)(2,1)}, u32[]{:S(2)}) copy-start(bf16[1088,192]{0,1:T(8,128)(2,1)} %copy-done.84) | copy-start | bytes 1253380
  118.6 9.2 %collective-permute-start.8 = (bf16[544,192]{1,0:T(8,128)(2,1)S(1)}, bf16[544,192]{1,0:T(8,128)(2,1)S(1)}, u32[]{:S(2)}, u32[]{:S(2)}) collective-permute-start(bf16[544,192]{1,0:T(8,128)(2,1)S(1)} %get-tuple-element.102), channel_id=1, source_target_pairs={{0,16},{8,24},{16,0},{24,8},{1,17},{9,25},{17,1},{25,9},{2,18},{10... | collective-permute-start | bytes 626696 | tf_op jit(solution)/shard_map/ppermute | solution.py:58
  120.1 13.9 %slice-start = ((s8[5013504]{0:T(1024)(128)(4,1)}), s8[4194304]{0:T(1024)(128)(4,1)S(1)}, s32[]{:S(2)}) async-start(s8[5013504]{0:T(1024)(128)(4,1)} %bitcast.415), calls=%async_computation | async-start | bytes 8388608
  122.5 85.1 %collective-permute-start.25 = (bf16[192,768]{1,0:T(8,128)(2,1)}, bf16[192,768]{1,0:T(8,128)(2,1)}, u32[]{:S(2)}, u32[]{:S(2)}) collective-permute-start(bf16[192,768]{1,0:T(8,128)(2,1)} %convolution_convert_fusion.16), channel_id=1, source_target_pairs={{0,16},{8,24},{16,0},{24,8},{1,17},{9,25},{17,1},{25,9},{2,18},{10... | collective-permute-start | bytes 884744 | tf_op jit(solution)/shard_map/ppermute | solution.py:58
  132.8 8.2 %slice-start.4 = ((s8[5013504]{0:T(1024)(128)(4,1)}), s8[4194304]{0:T(1024)(128)(4,1)S(1)}, s32[]{:S(2)}) async-start(s8[5013504]{0:T(1024)(128)(4,1)} %bitcast.419), calls=%async_computation.4 | async-start | bytes 8388608
  134.1 7.0 %slice-start.5 = ((s8[5013504]{0:T(1024)(128)(4,1)}), s8[819200]{0:T(1024)(128)(4,1)S(1)}, s32[]{:S(2)}) async-start(s8[5013504]{0:T(1024)(128)(4,1)} %bitcast.419), calls=%async_computation.5 | async-start | bytes 1638400
  173.6 7.3 %collective-permute-start.22 = (f32[2,2,2,24]{3,0,2,1:T(2,128)S(1)}, f32[2,2,2,24]{3,0,2,1:T(2,128)S(1)}, u32[]{:S(2)}, u32[]{:S(2)}) collective-permute-start(f32[2,2,2,24]{3,0,2,1:T(2,128)S(1)} %fusion.155), channel_id=1, source_target_pairs={{0,1},{1,0},{2,3},{3,2},{4,5},{5,4},{6,7},{7,6},{8,9},{9,8},{10,11... | collective-permute-start | bytes 2312 | tf_op jit(solution)/shard_map/ppermute | solution.py:62
  176.6 46.1 %collective-permute-start.16 = (bf16[4,2,2,24,576]{4,3,0,1,2:T(8,128)(2,1)}, bf16[4,2,2,24,576]{4,3,0,1,2:T(8,128)(2,1)}, u32[]{:S(2)}, u32[]{:S(2)}) collective-permute-start(bf16[4,2,2,24,576]{4,3,0,1,2:T(8,128)(2,1)} %copy_bitcast_fusion.2), channel_id=1, source_target_pairs={{0,1},{1,0},{2,3},{3,2},{4,5},{5,4},{6,7},{7,6},{8,9},{9,8},{10,11... | collective-permute-start | bytes 1327112 | tf_op jit(solution)/shard_map/ppermute | solution.py:62
  180.9 34.5 %copy-start.33 = (bf16[192,768]{1,0:T(8,128)(2,1)S(1)}, bf16[192,768]{1,0:T(8,128)(2,1)}, u32[]{:S(2)}) copy-start(bf16[192,768]{1,0:T(8,128)(2,1)} %convolution_convert_fusion.17) | copy-start | bytes 884740
  180.9 35.9 %copy-start.4 = (bf16[768,768]{1,0:T(8,128)(2,1)S(1)}, bf16[768,768]{1,0:T(8,128)(2,1)}, u32[]{:S(2)}) copy-start(bf16[768,768]{1,0:T(8,128)(2,1)} %convolution_convert_fusion.12) | copy-start | bytes 3538948
  180.9 4.3 %collective-permute-start.11 = (f32[6,2,2,2,2,24]{5,0,4,3,2,1:T(8,128)S(1)}, f32[6,2,2,2,2,24]{5,0,4,3,2,1:T(8,128)S(1)}, u32[]{:S(2)}, u32[]{:S(2)}) collective-permute-start(f32[6,2,2,2,2,24]{5,0,4,3,2,1:T(8,128)S(1)} %dynamic-slice_bitcast_fusion.5), channel_id=1, source_target_pairs={{0,16},{8,24},{16,0},{24,8},{1,17},{9,25},{17,1},{25,9},{2,18},{10... | collective-permute-start | bytes 27656 | tf_op jit(solution)/shard_map/ppermute | solution.py:58
  185.2 1.2 collective-permute-start.12
  186.5 3.6 %collective-permute-start.23 = (f32[2,2,24]{2,1,0:T(2,128)S(1)}, f32[2,2,24]{2,1,0:T(2,128)S(1)}, u32[]{:S(2)}, u32[]{:S(2)}) collective-permute-start(f32[2,2,24]{2,1,0:T(2,128)S(1)} %bitcast_add_fusion.1), channel_id=1, source_target_pairs={{0,2},{1,3},{2,0},{3,1},{4,6},{5,7},{6,4},{7,5},{8,10},{9,11},{10,... | collective-permute-start | bytes 1160 | tf_op jit(solution)/shard_map/ppermute | solution.py:62
  190.0 3.7 %collective-permute-start.13 = (f32[6,2,2,24]{3,0,2,1:T(8,128)S(1)}, f32[6,2,2,24]{3,0,2,1:T(8,128)S(1)}, u32[]{:S(2)}, u32[]{:S(2)}) collective-permute-start(f32[6,2,2,24]{3,0,2,1:T(8,128)S(1)} %fusion.125), channel_id=1, source_target_pairs={{0,1},{1,0},{2,3},{3,2},{4,5},{5,4},{6,7},{7,6},{8,9},{9,8},{10,11... | collective-permute-start | bytes 6920 | tf_op jit(solution)/shard_map/ppermute | solution.py:62
  193.8 3.7 %collective-permute-start.14 = (f32[6,2,24]{2,0,1:T(8,128)S(1)}, f32[6,2,24]{2,0,1:T(8,128)S(1)}, u32[]{:S(2)}, u32[]{:S(2)}) collective-permute-start(f32[6,2,24]{2,0,1:T(8,128)S(1)} %fusion.131), channel_id=1, source_target_pairs={{0,2},{1,3},{2,0},{3,1},{4,6},{5,7},{6,4},{7,5},{8,10},{9,11},{10,... | collective-permute-start | bytes 3464 | tf_op jit(solution)/shard_map/ppermute | solution.py:62
  197.4 4.5 %collective-permute-start.24 = (f32[2,24]{1,0:T(2,128)S(1)}, f32[2,24]{1,0:T(2,128)S(1)}, u32[]{:S(2)}, u32[]{:S(2)}) collective-permute-start(f32[2,24]{1,0:T(2,128)S(1)} %fusion.164), channel_id=1, source_target_pairs={{0,4},{1,5},{2,6},{3,7},{4,0},{5,1},{6,2},{7,3},{8,12},{9,13},{10,... | collective-permute-start | bytes 584 | tf_op jit(solution)/shard_map/ppermute | solution.py:62
  201.9 4.5 %collective-permute-start.15 = (f32[6,24]{1,0:T(8,128)S(1)}, f32[6,24]{1,0:T(8,128)S(1)}, u32[]{:S(2)}, u32[]{:S(2)}) collective-permute-start(f32[6,24]{1,0:T(8,128)S(1)} %fusion.149), channel_id=1, source_target_pairs={{0,4},{1,5},{2,6},{3,7},{4,0},{5,1},{6,2},{7,3},{8,12},{9,13},{10,... | collective-permute-start | bytes 1736 | tf_op jit(solution)/shard_map/ppermute | solution.py:62
  206.4 45.4 %collective-permute-start.9 = (bf16[2,272,768]{2,1,0:T(8,128)(2,1)}, bf16[2,272,768]{2,1,0:T(8,128)(2,1)}, u32[]{:S(2)}, u32[]{:S(2)}) collective-permute-start(bf16[2,272,768]{2,1,0:T(8,128)(2,1)} %fusion.55), channel_id=1, source_target_pairs={{0,8},{8,0},{16,24},{24,16},{1,9},{9,1},{17,25},{25,17},{2,10},{10... | collective-permute-start | bytes 2506760 | tf_op jit(solution)/shard_map/ppermute | solution.py:58
  208.6 6.7 %collective-permute-start.26 = (bf16[2,2,24,768]{3,2,1,0:T(8,128)(2,1)S(1)}, bf16[2,2,24,768]{3,2,1,0:T(8,128)(2,1)S(1)}, u32[]{:S(2)}, u32[]{:S(2)}) collective-permute-start(bf16[2,2,24,768]{3,2,1,0:T(8,128)(2,1)S(1)} %fusion.96), channel_id=1, source_target_pairs={{0,1},{1,0},{2,3},{3,2},{4,5},{5,4},{6,7},{7,6},{8,9},{9,8},{10,11... | collective-permute-start | bytes 442376 | tf_op jit(solution)/shard_map/ppermute | solution.py:62
  211.2 22.5 %collective-permute-start.39 = (bf16[2,2,96,768]{3,2,1,0:T(8,128)(2,1)S(1)}, bf16[2,2,96,768]{3,2,1,0:T(8,128)(2,1)S(1)}, u32[]{:S(2)}, u32[]{:S(2)}) collective-permute-start(bf16[2,2,96,768]{3,2,1,0:T(8,128)(2,1)S(1)} %fusion.63), channel_id=1, source_target_pairs={{0,1},{1,0},{2,3},{3,2},{4,5},{5,4},{6,7},{7,6},{8,9},{9,8},{10,11... | collective-permute-start | bytes 1769480 | tf_op jit(solution)/shard_map/ppermute | solution.py:62
  216.3 4.4 %collective-permute-start.27 = (bf16[2,24,768]{2,1,0:T(8,128)(2,1)S(1)}, bf16[2,24,768]{2,1,0:T(8,128)(2,1)S(1)}, u32[]{:S(2)}, u32[]{:S(2)}) collective-permute-start(bf16[2,24,768]{2,1,0:T(8,128)(2,1)S(1)} %fusion.97), channel_id=1, source_target_pairs={{0,2},{1,3},{2,0},{3,1},{4,6},{5,7},{6,4},{7,5},{8,10},{9,11},{10,... | collective-permute-start | bytes 221192 | tf_op jit(solution)/shard_map/ppermute | solution.py:62
  218.0 19.5 %collective-permute-start.30 = (bf16[2,2,2,24,2,768]{5,3,0,4,2,1:T(8,128)(2,1)S(1)}, bf16[2,2,2,24,2,768]{5,3,0,4,2,1:T(8,128)(2,1)S(1)}, u32[]{:S(2)}, u32[]{:S(2)}) collective-permute-start(bf16[2,2,2,24,2,768]{5,3,0,4,2,1:T(8,128)(2,1)S(1)} %fusion.38), channel_id=1, source_target_pairs={{0,16},{8,24},{16,0},{24,8},{1,17},{9,25},{17,1},{25,9},{2,18},{10... | collective-permute-start | bytes 1769480 | tf_op jit(solution)/shard_map/ppermute | solution.py:58
  221.5 5.0 %collective-permute-start.28 = (bf16[24,768]{1,0:T(8,128)(2,1)S(1)}, bf16[24,768]{1,0:T(8,128)(2,1)S(1)}, u32[]{:S(2)}, u32[]{:S(2)}) collective-permute-start(bf16[24,768]{1,0:T(8,128)(2,1)S(1)} %fusion.110), channel_id=1, source_target_pairs={{0,4},{1,5},{2,6},{3,7},{4,0},{5,1},{6,2},{7,3},{8,12},{9,13},{10,... | collective-permute-start | bytes 110600 | tf_op jit(solution)/shard_map/ppermute | solution.py:62
  223.7 6.5 %collective-permute-start.17 = (bf16[4,2,24,576]{3,2,0,1:T(8,128)(2,1)S(1)}, bf16[4,2,24,576]{3,2,0,1:T(8,128)(2,1)S(1)}, u32[]{:S(2)}, u32[]{:S(2)}) collective-permute-start(bf16[4,2,24,576]{3,2,0,1:T(8,128)(2,1)S(1)} %fusion.74), channel_id=1, source_target_pairs={{0,2},{1,3},{2,0},{3,1},{4,6},{5,7},{6,4},{7,5},{8,10},{9,11},{10,... | collective-permute-start | bytes 663560 | tf_op jit(solution)/shard_map/ppermute | solution.py:62
  231.9 11.3 %collective-permute-start.18 = (bf16[4,24,576]{2,1,0:T(8,128)(2,1)}, bf16[4,24,576]{2,1,0:T(8,128)(2,1)S(1)}, u32[]{:S(2)}, u32[]{:S(2)}) collective-permute-start(bf16[4,24,576]{2,1,0:T(8,128)(2,1)} %fusion.83), channel_id=1, source_target_pairs={{0,4},{1,5},{2,6},{3,7},{4,0},{5,1},{6,2},{7,3},{8,12},{9,13},{10,... | collective-permute-start | bytes 331784 | tf_op jit(solution)/shard_map/ppermute | solution.py:62
  236.4 20.7 %collective-permute-start.40 = (bf16[2,96,768]{2,1,0:T(8,128)(2,1)}, bf16[2,96,768]{2,1,0:T(8,128)(2,1)}, u32[]{:S(2)}, u32[]{:S(2)}) collective-permute-start(bf16[2,96,768]{2,1,0:T(8,128)(2,1)} %fusion.69), channel_id=1, source_target_pairs={{0,2},{1,3},{2,0},{3,1},{4,6},{5,7},{6,4},{7,5},{8,10},{9,11},{10,... | collective-permute-start | bytes 884744 | tf_op jit(solution)/shard_map/ppermute | solution.py:62
  242.3 11.4 %collective-permute-start.31 = (bf16[2,2,24,2,768]{4,2,0,3,1:T(8,128)(2,1)}, bf16[2,2,24,2,768]{4,2,0,3,1:T(8,128)(2,1)}, u32[]{:S(2)}, u32[]{:S(2)}) collective-permute-start(bf16[2,2,24,2,768]{4,2,0,3,1:T(8,128)(2,1)} %fusion.70), channel_id=1, source_target_pairs={{0,2},{1,3},{2,0},{3,1},{4,6},{5,7},{6,4},{7,5},{8,10},{9,11},{10,... | collective-permute-start | bytes 884744 | tf_op jit(solution)/shard_map/ppermute | solution.py:62
  244.2 2.1 collective-permute-start.19
  244.3 3.6 %collective-permute-start.21 = (bf16[24,576]{1,0:T(8,128)(2,1)S(1)}, bf16[24,576]{1,0:T(8,128)(2,1)S(1)}, u32[]{:S(2)}, u32[]{:S(2)}) collective-permute-start(bf16[24,576]{1,0:T(8,128)(2,1)S(1)} %get-tuple-element.113), channel_id=1, source_target_pairs={{0,24},{8,16},{16,8},{24,0},{1,25},{9,17},{17,9},{25,1},{2,26},{10... | collective-permute-start | bytes 82952 | tf_op jit(solution)/shard_map/ppermute | solution.py:58
  246.3 3.9 %collective-permute-start.20 = (bf16[24,576]{1,0:T(8,128)(2,1)S(1)}, bf16[24,576]{1,0:T(8,128)(2,1)S(1)}, u32[]{:S(2)}, u32[]{:S(2)}) collective-permute-start(bf16[24,576]{1,0:T(8,128)(2,1)S(1)} %get-tuple-element.114), channel_id=1, source_target_pairs={{0,16},{8,24},{16,0},{24,8},{1,17},{9,25},{17,1},{25,9},{2,18},{10... | collective-permute-start | bytes 82952 | tf_op jit(solution)/shard_map/ppermute | solution.py:58
  254.9 12.4 %collective-permute-start.32 = (bf16[2,24,2,768]{3,1,0,2:T(8,128)(2,1)S(1)}, bf16[2,24,2,768]{3,1,0,2:T(8,128)(2,1)S(1)}, u32[]{:S(2)}, u32[]{:S(2)}) collective-permute-start(bf16[2,24,2,768]{3,1,0,2:T(8,128)(2,1)S(1)} %fusion.79), channel_id=1, source_target_pairs={{0,4},{1,5},{2,6},{3,7},{4,0},{5,1},{6,2},{7,3},{8,12},{9,13},{10,... | collective-permute-start | bytes 442376 | tf_op jit(solution)/shard_map/ppermute | solution.py:62
  256.0 17.1 %collective-permute-start.10 = (bf16[272,768]{1,0:T(8,128)(2,1)S(1)}, bf16[272,768]{1,0:T(8,128)(2,1)S(1)}, u32[]{:S(2)}, u32[]{:S(2)}) collective-permute-start(bf16[272,768]{1,0:T(8,128)(2,1)S(1)} %fusion.75), channel_id=1, source_target_pairs={{0,16},{8,24},{16,0},{24,8},{1,17},{9,25},{17,1},{25,9},{2,18},{10... | collective-permute-start | bytes 1253384 | tf_op jit(solution)/shard_map/ppermute | solution.py:58
  258.3 12.0 %collective-permute-start.41 = (bf16[96,768]{1,0:T(8,128)(2,1)S(1)}, bf16[96,768]{1,0:T(8,128)(2,1)S(1)}, u32[]{:S(2)}, u32[]{:S(2)}) collective-permute-start(bf16[96,768]{1,0:T(8,128)(2,1)S(1)} %fusion.77), channel_id=1, source_target_pairs={{0,4},{1,5},{2,6},{3,7},{4,0},{5,1},{6,2},{7,3},{8,12},{9,13},{10,... | collective-permute-start | bytes 442376 | tf_op jit(solution)/shard_map/ppermute | solution.py:62
  268.3 3.8 %collective-permute-start.33 = (bf16[24,2,768]{2,0,1:T(8,128)(2,1)S(1)}, bf16[24,2,768]{2,0,1:T(8,128)(2,1)S(1)}, u32[]{:S(2)}, u32[]{:S(2)}) collective-permute-start(bf16[24,2,768]{2,0,1:T(8,128)(2,1)S(1)} %fusion.109), channel_id=1, source_target_pairs={{0,8},{8,0},{16,24},{24,16},{1,9},{9,1},{17,25},{25,17},{2,10},{10... | collective-permute-start | bytes 221192 | tf_op jit(solution)/shard_map/ppermute | solution.py:58
  (78 other events, 233.5 us)

commit v2 on v1

v2 whole, which is shorter than its diff:
```python
import functools

import jax
import jax.numpy as jnp
from jax import lax
from jax.experimental import pallas as pl
from jax.experimental.pallas import tpu as pltpu
from jax.sharding import PartitionSpec as P

HEADS = 12
HEAD = 64
PAD = 32
LANES = 128
OWN = 3
FAR = -(2.0**100)
F32 = jnp.float32
BF16 = jnp.bfloat16
SDS = jax.ShapeDtypeStruct


def dot(a, b):
    return jnp.dot(a, b, preferred_element_type=F32)


def dot_t(a, b):
    return lax.dot_general(a, b, (((1,), (1,)), ((), ())), preferred_element_type=F32)


def dot_lt(a, b):
    return lax.dot_general(a, b, (((0,), (0,)), ((), ())), preferred_element_type=F32)


def normalize(v):
    center = v - jnp.mean(v, axis=-1, keepdims=True)
    spread = jnp.mean(center * center, axis=-1, keepdims=True)
    scale = lax.rsqrt(spread + 1e-06)
    return center * scale, scale


def normalize_back(grad_hat, hat, scale):
    mean_g = jnp.mean(grad_hat, axis=-1, keepdims=True)
    mean_gh = jnp.mean(grad_hat * hat, axis=-1, keepdims=True)
    return scale * (grad_hat - mean_g - hat * mean_gh)


def gelu_pair(v):
    half = 0.5 * (1.0 + lax.erf(v * 0.5**0.5))
    slope = half + v * jnp.exp(-0.5 * v * v) * 0.3989422804014327
    return v * half, slope


def lane_of(rows):
    return lax.broadcasted_iota(jnp.int32, (rows, LANES), 1)


def unpack_head(tiles, e):
    tile = tiles[:, (e // 2) * LANES : (e // 2 + 1) * LANES]
    return tile if e % 2 == 0 else pltpu.roll(tile, HEAD, 1)


def pack_pair(low, high):
    return jnp.where(lane_of(low.shape[0]) < HEAD, low, pltpu.roll(high, HEAD, 1))


def vmem():
    return pl.BlockSpec(memory_space=pltpu.VMEM)


def smem():
    return pl.BlockSpec(memory_space=pltpu.SMEM)


def call(kernel, outs, args, scratch=(), flops=0, scalars=0):
    nbytes = sum(a.size * a.dtype.itemsize for a in args)
    nbytes += sum(o.size * o.dtype.itemsize for o in outs)
    return pl.pallas_call(
        kernel,
        out_shape=outs,
        in_specs=[smem()] * scalars + [vmem()] * (len(args) - scalars),
        out_specs=[vmem()] * len(outs),
        scratch_shapes=list(scratch),
        cost_estimate=pl.CostEstimate(flops=flops, bytes_accessed=nbytes, transcendentals=0),
    )(*args)


def attend_kernel(p0, p1, p2, p3, gain, shift, w, bias, qa, ka, va, lse, keep, send, normed, oacc):
    rows = p0.shape[0]
    width = gain.shape[1]
    whole = 4 * rows
    lane = lane_of(rows)
    for i, p in enumerate((p0, p1, p2, p3)):
        at = pl.ds(i * rows, rows)
        hat, _ = normalize(p[:, :width].astype(F32))
        nrm = (hat * gain[...] + shift[...]).astype(BF16)
        normed[at, :] = nrm
        qkv = dot(nrm, w[...]) + bias[...]
        hot = p[:, width:].astype(F32)
        far = jnp.where((lane >= HEAD) & (lane < HEAD + 8) & (hot == 0.0), FAR, 0.0)
        one = jnp.where(lane == HEAD, 1.0, 0.0)
        for h in range(OWN):
            q = unpack_head(qkv, 3 * h) * HEAD**-0.5
            qa[h, at, :] = jnp.where(lane < HEAD, q, hot).astype(BF16)
            ka[h, at, :] = jnp.where(lane < HEAD, unpack_head(qkv, 3 * h + 1), far).astype(BF16)
            va[h, at, :] = jnp.where(lane < HEAD, unpack_head(qkv, 3 * h + 2), one).astype(BF16)
    step = whole // 3

    def block(i, carry):
        h, b = i // 3, i % 3
        at = pl.ds(pl.multiple_of(b * step, step), step)
        sc = dot_t(qa[h, at, :], ka[h])
        top = jnp.max(sc, axis=-1, keepdims=True)
        e = jnp.exp(sc - top).astype(BF16)
        o = dot(e, va[h])
        tot = o[:, HEAD : HEAD + 1]
        oacc[h, at, :] = o * (1.0 / tot)
        col = jnp.broadcast_to(top + jnp.log(tot), (step, LANES))
        lse[h, b] = col.T[:8]
        return carry

    lax.fori_loop(0, 3 * OWN, block, 0)
    for out, start in ((keep, 0), (send, 2 * rows)):
        at = pl.ds(start, 2 * rows)
        out[:, :LANES] = pack_pair(oacc[0, at, :], oacc[1, at, :]).astype(BF16)
        out[:, LANES:] = oacc[2, at, :HEAD].astype(BF16)


def keep_column(p0, p1, table, width):
    hot = jnp.concatenate([p0[:, width:], p1[:, width:]], axis=0).astype(F32)
    return jnp.sum(hot * table, axis=-1, keepdims=True)


def middle_kernel(sref, a0, a1, a2, a3, p0, p1, c0, c1, table, w_out, bias, gain, shift, middle, normed2, gb2):
    s = sref[0]
    rows, width = c0.shape
    cols = a0.shape[1]
    acc = jnp.zeros((2 * rows, width), F32) + bias[...]
    for j, a in ((0, a0), (2, a2)):
        w = w_out[pl.ds(pl.multiple_of((s ^ j) * cols, HEAD), cols), :]
        acc = acc + dot(a[...], w)
    for j, a in ((1, a1), (3, a3)):
        w = w_out[pl.ds(pl.multiple_of((s ^ j) * cols, HEAD), cols), :]
        part = dot(a[...], w)
        acc = acc + jnp.concatenate([part[rows:], part[:rows]], axis=0)
    keep_a = keep_column(p0, p1, table[0:1, :], width)
    keep_m = keep_column(p0, p1, table[1:2, :], width)
    tok = jnp.concatenate([p0[:, :width], p1[:, :width]], axis=0).astype(F32)
    mid = tok + keep_a * acc
    middle[...] = mid
    hat, _ = normalize(mid)
    normed2[...] = (hat * gain[...] + shift[...]).astype(BF16)
    gout = jnp.concatenate([c0[...], c1[...]], axis=0).astype(F32)
    gb2[...] = (keep_m * gout).astype(BF16)


def feed_kernel(last, sref, bref, normed2, gb2, fc1, bias, fc2, *refs):
    if last:
        b2_in, gn_in, g2, g1_send, g1_keep, gb, b2_keep, b2_send, gn_keep, gn_send, wide, b2, gn = refs
    else:
        g2a, g2b, g1_send, g1_keep, gb, b2, gn, wide = refs
    i = pl.program_id(0)
    half = b2.shape[0] // 2
    pre = dot(normed2[...], fc1[...]) + bias[...]
    gact = dot_t(gb2[...], fc2[...])
    act, slope = gelu_pair(pre)
    act = act.astype(BF16)
    gh = (gact * slope).astype(BF16)
    grad2 = dot_lt(act, gb2[...]).astype(BF16)
    if last:
        g2[...] = grad2
    else:

        @pl.when(i == 0)
        def _():
            g2a[...] = grad2

        @pl.when(i == 1)
        def _():
            g2b[...] = grad2

    split_rows(dot_lt(normed2[...], gh), wide, bref[0] & 1, g1_send, g1_keep)
    gb[...] = jnp.sum(gh.astype(F32), axis=0, keepdims=True)
    part2 = dot(act, fc2[...])
    partn = dot_t(gh, fc1[...])

    @pl.when(i == 0)
    def _():
        if last:
            b2[...] = b2_in[...] + part2
            gn[...] = gn_in[...] + partn
        else:
            b2[...] = part2
            gn[...] = partn

    @pl.when(i > 0)
    def _():
        b2[...] += part2
        gn[...] += partn

    if last:

        @pl.when(i == pl.num_programs(0) - 1)
        def _():
            b2_keep[...] = b2[:half]
            b2_send[...] = b2[half:].astype(BF16)
            gn_keep[...] = gn[...]
            gn_send[:half] = gn[half:].astype(BF16)
            gn_send[half:] = gn[:half].astype(BF16)


def split_rows(value, wide, bit, send, keep):
    if len(send.shape) == 2:
        rows = value.shape[0] // 2
        send[...] = value[:rows].astype(BF16)
        keep[...] = value[rows:].astype(BF16)
        return
    wide[...] = value
    rows = send.shape[1]
    for m in range(send.shape[0]):
        base = 2 * m * rows
        send[m] = wide[pl.ds(pl.multiple_of(base + (1 - bit) * rows, 8), rows), :].astype(BF16)
        keep[m] = wide[pl.ds(pl.multiple_of(base + bit * rows, 8), rows), :].astype(BF16)


def feed(last, pick, per, sidx, bidx, normed2, gb2, w_fc1, bias, w_fc2, prev=()):
    tokens, width = normed2.shape
    hidden = w_fc1.shape[1] // 4
    chunk = hidden // 2
    steps = 2
    const = lambda i, s, b: (0, 0)
    full = pl.BlockSpec((tokens, width), const)
    half = pl.BlockSpec((tokens // 2, width), const)
    in_specs = [
        full,
        full,
        pl.BlockSpec((width, chunk), lambda i, s, b: (0, (s[0] ^ pick) * steps + i)),
        pl.BlockSpec((1, chunk), lambda i, s, b: (0, (s[0] ^ pick) * steps + i)),
        pl.BlockSpec((chunk, width), lambda i, s, b: ((s[0] ^ pick) * steps + i, 0)),
    ] + [full] * len(prev)
    if last:
        out_specs = [pl.BlockSpec((chunk, width), lambda i, s, b: (i, 0))]
        outs = [SDS((hidden, width), BF16)]
    else:
        out_specs = [pl.BlockSpec((chunk, width), const)] * 2
        outs = [SDS((chunk, width), BF16)] * 2
    if per % 8 == 0:
        pairs = width // (2 * per)
        out_specs += [pl.BlockSpec((pairs, per, chunk), lambda i, s, b: (0, 0, i))] * 2
        outs += [SDS((pairs, per, hidden), BF16)] * 2
    else:
        out_specs += [pl.BlockSpec((width // 2, chunk), lambda i, s, b: (0, i))] * 2
        outs += [SDS((width // 2, hidden), BF16)] * 2
    out_specs += [pl.BlockSpec((1, chunk), lambda i, s, b: (0, i))]
    outs += [SDS((1, hidden), F32)]
    scratch = [pltpu.VMEM((width, chunk), F32)]
    if last:
        out_specs += [half, half, full, full]
        outs += [SDS((tokens // 2, width), F32), SDS((tokens // 2, width), BF16)]
        outs += [SDS((tokens, width), F32), SDS((tokens, width), BF16)]
        scratch += [pltpu.VMEM((tokens, width), F32)] * 2
    else:
        out_specs += [full, full]
        outs += [SDS((tokens, width), F32)] * 2
    out = pl.pallas_call(
        functools.partial(feed_kernel, last),
        grid_spec=pltpu.PrefetchScalarGridSpec(
            num_scalar_prefetch=2,
            grid=(steps,),
            in_specs=in_specs,
            out_specs=out_specs,
            scratch_shapes=scratch,
        ),
        out_shape=outs,
        cost_estimate=pl.CostEstimate(
            flops=12 * tokens * width * hidden, bytes_accessed=10 * width * hidden, transcendentals=0
        ),
    )(sidx, bidx, normed2, gb2, w_fc1, bias, w_fc2, *prev)
    at = 1 if last else 2
    out = list(out)
    if per % 8:
        out[at : at + 2] = by_batch_bit(jnp.concatenate(out[at : at + 2], axis=0), per)
    return out


def by_batch_bit(arr, per):
    arr = arr.reshape(-1, 2, per, arr.shape[-1])
    own = lax.axis_index("batch") & 1
    return [pick(arr, 1 - own, 1), pick(arr, own, 1)]


def branch_back_kernel(
    sref, gn_keep, gn_got, middle, p0, p1, c0, c1, table, w_out, gain, shift, a0, a2, gb2,
    b2_keep, b2_got, bias, gain1, shift1, fb_own, fb_oth,
    gmid_own, gatt, gatt_send, go_keep, go_send, early, opat, ospe, fcol,
):
    s = sref[0]
    rows, width = c0.shape
    cols = a0.shape[1]
    mid = middle[...]
    hat, scale = normalize(mid)
    g = gn_keep[...] + gn_got[...].astype(F32)
    gout = jnp.concatenate([c0[...], c1[...]], axis=0).astype(F32)
    gmid = gout + normalize_back(g * gain[...], hat, scale)
    gmid_own[...] = gmid[:rows]
    keep_a = keep_column(p0, p1, table[0:1, :], width)
    gbr = (keep_a * gmid).astype(BF16)
    w_own = w_out[pl.ds(pl.multiple_of(s * cols, HEAD), cols), :]
    w_oth = w_out[pl.ds(pl.multiple_of((s ^ 2) * cols, HEAD), cols), :]
    gatt_send[...] = dot_t(gbr, w_oth).astype(BF16)
    gatt[...] = dot_t(gbr, w_own).astype(BF16)
    go_send[...] = dot_lt(a2[...], gbr).astype(BF16)
    go_keep[...] = dot_lt(a0[...], gbr).astype(BF16)

    hot = p0[:, width:].astype(F32)
    keep_m = jnp.sum(hot * table[1:2, :], axis=-1, keepdims=True)
    res = (mid[:rows] + keep_m * (b2_keep[...] + b2_got[...].astype(F32) + bias[...])).astype(BF16)
    opat[...] = res[: opat.shape[0]]
    ospe[...] = res[opat.shape[0] : opat.shape[0] + ospe.shape[0]]

    own = slice(0, rows)
    blank = functools.partial(jnp.zeros, dtype=F32)
    lines = [
        gain1[...],
        shift1[...],
        blank((HEAD + 2, width)),
        jnp.sum(g[own] * hat[own], axis=0, keepdims=True),
        jnp.sum(g[own], axis=0, keepdims=True),
        jnp.sum(gb2[own, :].astype(F32), axis=0, keepdims=True),
        jnp.sum(gbr[own].astype(F32), axis=0, keepdims=True),
        blank((LANES - HEAD - 8, width)),
    ]
    early[...] = jnp.concatenate(lines, axis=0).T
    lane = lane_of(cols)
    for j, ref in ((0, fb_own), (2, fb_oth)):
        fcol[...] = jnp.broadcast_to(ref[...], (LANES, ref.shape[1])).T
        at = pl.ds(pl.multiple_of((s ^ j) * cols, HEAD), cols)
        val = early[at, :]
        for k in range(4):
            val = jnp.where(lane == HEAD + 8 + k, fcol[pl.ds(k, cols, stride=4), :], val)
        early[at, :] = val


def attend_back_kernel(first, heads, qa, ka, va, lse, ga, gx, out, sums, goa, dq, dk, dv):
    whole = qa.shape[1]
    half = ga.shape[0]
    lane = lane_of(half)
    for i in range(heads):
        h = first + i
        for ref, start in ((ga, 0), (gx, half)):
            if h < 2:
                t = ref[:, :LANES].astype(F32)
                t = jnp.where(lane < HEAD, t if h == 0 else pltpu.roll(t, HEAD, 1), 0.0)
            else:
                t = ref[:, LANES:].astype(F32)
                t = jnp.concatenate([t, jnp.zeros_like(t)], axis=1)
            goa[i, pl.ds(start, half), :] = t.astype(BF16)
    step = whole // 3

    def block(n, carry):
        i, b = n // 3, n % 3
        h = first + i
        at = pl.ds(pl.multiple_of(b * step, step), step)
        q, go = qa[h, at, :], goa[i, at, :]
        prob = jnp.exp(dot_t(ka[h], q) - lse[h, b][0:1, :])
        gp = dot_t(va[h], go)
        inner = jnp.sum(gp * prob, axis=0, keepdims=True)
        gs = (prob * (gp - inner)).astype(BF16)
        pv = dot(prob.astype(BF16), go)
        pk = dot(gs, q)
        dq[i, at, :] = dot_lt(gs, ka[h])

        @pl.when(b == 0)
        def _():
            dv[i] = pv
            dk[i] = pk

        @pl.when(b > 0)
        def _():
            dv[i] += pv
            dk[i] += pk

        return carry

    lax.fori_loop(0, 3 * heads, block, 0)
    for i in range(heads):
        out[i, :, :LANES] = pack_pair(dq[i] * HEAD**-0.5, dk[i]).astype(BF16)
        out[i, :, LANES:] = dv[i, :, :HEAD].astype(BF16)
        sums[i] = jnp.sum(out[i].astype(F32), axis=0, keepdims=True)


def attend_back(first, heads, qa, ka, va, lse, ga, gx):
    whole = qa.shape[1]
    return call(
        functools.partial(attend_back_kernel, first, heads),
        [SDS((heads, whole, 3 * HEAD), BF16), SDS((heads, 1, 3 * HEAD), F32)],
        (qa, ka, va, lse, ga, gx),
        [pltpu.VMEM((heads, whole, LANES), BF16)] + [pltpu.VMEM((heads, whole, LANES), F32)] * 3,
        flops=10 * heads * whole * whole * LANES,
    )


def norm1_kernel(g0, g12, w, keep, send):
    rows = keep.shape[0] // 2
    cols = g0.shape[2]
    for i in range(4):
        at = pl.ds(i * rows, rows)
        part = dot_t(g0[0, at, :], w[:, :cols])
        part = part + dot_t(g12[0, at, :], w[:, cols : 2 * cols])
        part = part + dot_t(g12[1, at, :], w[:, 2 * cols : 3 * cols])
        to = pl.ds((i // 2) * rows, rows)
        if i % 2 == 0:
            keep[to, :] = part
        else:
            send[to, :] = part.astype(BF16)


def qkv_grad_kernel(sref, bref, normed, g0, g12, s0, s12, w, early, send, keep, tile, wide):
    width, cols = w.shape[0], g0.shape[2]
    every = (g0[0], g12[0], g12[1])
    parts = [dot_lt(normed[...], g) for g in every]
    g = jnp.concatenate(parts, axis=1)
    w32 = w[:, : 3 * cols].astype(F32)
    rows = jnp.concatenate([s0[0], s12[0], s12[1]], axis=1)
    both = jnp.sum(g * w32, axis=-1, keepdims=True)
    gshift = jnp.sum(w32 * rows, axis=-1, keepdims=True)
    ggain = (both - early[:, 1:2] * gshift) / early[:, 0:1]
    lane = lane_of(width)
    tail = jnp.concatenate([g[:, 4 * LANES :], jnp.zeros((width, LANES - HEAD), F32)], axis=1)
    tail = jnp.where(lane == HEAD, ggain, tail)
    tail = jnp.where(lane == HEAD + 1, gshift, tail)
    tile[...] = jnp.where(lane >= HEAD + 4, early[...], tail)
    ones = jnp.ones((g0.shape[1], LANES), BF16)
    at = pl.multiple_of(sref[0] * cols, HEAD)
    for h, part in enumerate(every):
        col = dot_lt(part, ones)
        here = pl.ds(at + h * HEAD, HEAD)
        lanes = lane_of(HEAD)
        row = tile[here, :]
        row = jnp.where(lanes == HEAD + 2, col[:HEAD], row)
        tile[here, :] = jnp.where(lanes == HEAD + 3, col[2 * HEAD :], row)
    split_rows(jnp.concatenate([g[:, : 4 * LANES], tile[...]], axis=1), wide, bref[0] & 1, send, keep)


def wide_sum(*parts):
    return sum(p.astype(F32) for p in parts[1:]) + parts[0].astype(F32)


def stage1_kernel(sref, keep_own, got_own, keep_oth, got_oth, send):
    x = sref[0] >> 1
    n, _, width = send.shape
    width = width // 2
    for i in range(n):
        m = (1 - x) * n + i
        send[i, :, :width] = wide_sum(keep_own[m], got_own[m]).astype(BF16)
        send[i, :, width:] = wide_sum(keep_oth[m], got_oth[m]).astype(BF16)


def stage2_kernel(
    sref, bref, keep_own, got_own, keep_oth, got_oth, got_b, fc2, got2a, got2b, out, got_o,
    send_a, zb1, zb2, zb3, keep_b,
):
    x, y, q = sref[0] >> 1, bref[0] & 1, bref[0] >> 1
    n = got_b.shape[0] // 4
    width = keep_own.shape[2]
    deep = fc2.shape[1]
    for c in range(2):
        for k, ref in enumerate((keep_b, zb1, zb2, zb3)):
            i = c * 4 + (q ^ k)
            m = x * 8 + i
            ref[c, :, :width] = wide_sum(keep_own[m], got_own[m], got_b[i, :, width:]).astype(ref.dtype)
            ref[c, :, width:] = wide_sum(keep_oth[m], got_oth[m], got_b[i, :, :width]).astype(ref.dtype)
    for j in range(4):
        b = 2 * j + 1 - y
        got = got2a if j < 2 else got2b
        send_a[j, :deep] = wide_sum(fc2[b], got[b - 4 * (j // 2)]).astype(BF16)
        send_a[j, deep:] = wide_sum(out[b], got_o[b]).astype(BF16)


def stage3_kernel(
    sref, bref, fc2, got2, out, got_o, got_a, keep_b, zb1, zb2, zb3, gn_keep, gn_got,
    za1, za2, za3, keep_a, swap_send, swap_keep, xsend,
):
    c, y, q = sref[0] & 1, bref[0] & 1, bref[0] >> 1
    deep = fc2.shape[1]
    for k, ref in enumerate((keep_a, za1, za2, za3)):
        j = q ^ k
        b = 2 * j + y
        ref[:deep] = wide_sum(fc2[b], got2[b], got_a[j, :deep]).astype(ref.dtype)
        ref[deep:] = wide_sum(out[b], got_o[b], got_a[j, deep:]).astype(ref.dtype)
    swap_send[...] = wide_sum(keep_b[1 - c], zb1[1 - c], zb2[1 - c], zb3[1 - c]).astype(BF16)
    swap_keep[...] = wide_sum(keep_b[c], zb1[c], zb2[c], zb3[c])
    rows = xsend.shape[0]
    xsend[...] = wide_sum(gn_keep[rows:], gn_got[rows:]).astype(BF16)


def final_kernel(
    sref, k0, c0, x0, p0, gmid, gain, keep_a, za1, za2, za3, swap_keep, swap_got,
    gpat, gspe, fc2, out, fc1,
):
    s = sref[0]
    rows, width = x0.shape
    count = gpat.shape[0]
    extra = gspe.shape[0]
    hat, scale = normalize(p0[:, :width].astype(F32))
    g = wide_sum(k0[:rows], c0[:rows], x0[...])
    res = gmid[...] + normalize_back(g * gain[...], hat, scale)
    gpat[...] = res[:count]
    gspe[...] = res[count : count + extra]
    sums = wide_sum(keep_a[...], za1[...], za2[...], za3[...])
    deep = fc2.shape[0]
    fc2[...] = sums[:deep]
    out[...] = sums[deep:]
    hidden = swap_keep.shape[1] // 2

    def place(j, value):
        fc1[:, pl.ds(pl.multiple_of((s ^ j) * hidden, LANES), hidden)] = value

    place(0, swap_keep[:, :hidden])
    place(2, swap_keep[:, hidden:])
    place(1, swap_got[:, :hidden].astype(F32))
    place(3, swap_got[:, hidden:].astype(F32))


def norm_only_kernel(k0, c0, x0, p0, gmid, gain, gpat, gspe):
    rows, width = x0.shape
    count = gpat.shape[0]
    hat, scale = normalize(p0[:, :width].astype(F32))
    g = wide_sum(k0[:rows], c0[:rows], x0[...])
    res = gmid[...] + normalize_back(g * gain[...], hat, scale)
    gpat[...] = res[:count]
    gspe[...] = res[count : count + gspe.shape[0]]


def quarter_kernel(bref, keep, got, z1, z2, z3, kept):
    q = bref[0] >> 1
    for r in range(4):
        for k, ref in enumerate((kept, z1, z2, z3)):
            m = r * 4 + (q ^ k)
            ref[r] = wide_sum(keep[m], got[m]).astype(ref.dtype)


def owner_kernel(sref, kept, z1, z2, z3, s1, s2, s3, own):
    s = sref[0]
    for k, ref in enumerate((own, s1, s2, s3)):
        m = s ^ k
        ref[...] = wide_sum(kept[m], z1[m], z2[m], z3[m]).astype(ref.dtype)


def collect_kernel(sref, own, g1, g2, g3, out, vec, every):
    s = sref[0]
    for k, ref in enumerate((own, g1, g2, g3)):
        every[k] = ref[...].astype(F32)
    pieces = [every[s ^ a] for a in range(4)]

    def part(u):
        j, a, h = u // 12, (u // 3) % 4, u % 3
        e = 3 * h + j
        return pieces[a][:, (e // 2) * LANES : (e // 2 + 1) * LANES], e % 2

    lane = lane_of(out.shape[0])
    for t in range(out.shape[1] // LANES):
        (low, lo), (high, hi) = part(2 * t), part(2 * t + 1)
        low = pltpu.roll(low, HEAD, 1) if lo else low
        high = high if hi else pltpu.roll(high, HEAD, 1)
        out[:, t * LANES : (t + 1) * LANES] = jnp.where(lane < HEAD, low, high)
    tail = 4 * LANES
    vec[...] = wide_sum(*[every[k, :, tail:] for k in range(4)])


def pick(arr, index, axis):
    return lax.dynamic_index_in_dim(arr, index, axis, keepdims=False)


def total(parts):
    out = parts[0].astype(F32)
    for part in parts[1:]:
        out = out + part.astype(F32)
    return out


def swap(kind, v, mask):
    return lax.ppermute(v, kind, [(i, i ^ mask) for i in range(lax.axis_size(kind))])


def swap_seq(v, mask):
    return swap("seq", v, mask)


def after(value, *first):
    return lax.optimization_barrier((value, first))[0]


def bits_of(kind):
    return lax.axis_size(kind).bit_length() - 1


def split_bits(arr, axis, count):
    shape = arr.shape
    return arr.reshape(shape[:axis] + (2,) * count + shape[axis + 1 :])


def to_send(parts, axis, bit, kind):
    own = (lax.axis_index(kind) >> bit) & 1
    send = total([pick(p, 1 - own, axis) for p in parts]).astype(BF16)
    return send, [pick(p, own, axis) for p in parts]


def send_four(parts, axis, low):
    own = (lax.axis_index("batch") >> low) & 3

    def quarter(p, k):
        return pick(pick(p, k >> 1, axis), k & 1, axis)

    sends = [total([quarter(p, own ^ k) for p in parts]).astype(BF16) for k in (1, 2, 3)]
    return sends, [quarter(p, own) for p in parts]


def swap_four(sends, low):
    return [swap("batch", v, k << low) for k, v in zip((1, 2, 3), sends)]


def sum_rest(parts, axis, low):
    top = bits_of("batch")
    while low < top:
        if low + 1 < top:
            sends, kept = send_four(parts, axis + top - low - 2, low)
            parts, low = kept + swap_four(sends, low), low + 2
        else:
            send, kept = to_send(parts, axis, low, "batch")
            parts, low = kept + [swap("batch", send, 1 << low)], low + 1
    return total(parts)


def body(
    patches,
    specials,
    segment_ids,
    special_order,
    keep_mask,
    norm_gains,
    norm_shifts,
    w_qkv,
    biases,
    w_out,
    w_fc1,
    fc1_bias,
    w_fc2,
    cot_patches,
    cot_specials,
):
    count, width = patches.shape[1:]
    extra = specials.shape[1]
    images = keep_mask.shape[1] // 2
    block = count + PAD
    chip = 2 * block
    whole = 4 * block
    cols = OWN * HEAD
    hidden = w_fc1.shape[1] // 4
    s = lax.axis_index("seq")
    sidx = s.astype(jnp.int32).reshape(1)
    bidx = lax.axis_index("batch").astype(jnp.int32).reshape(1)
    nb = lax.axis_size("batch")
    nbits = bits_of("batch")

    zeros = jnp.zeros((PAD - extra, width), BF16)
    mine = jnp.concatenate([patches[0], specials[0], zeros], axis=0)
    segs = jnp.concatenate(
        [segment_ids[0], special_order[0] // 2, jnp.full((PAD - extra,), -1, jnp.int32)]
    )
    marks = jnp.arange(LANES, dtype=jnp.int32) - HEAD
    hot = ((segs[:, None] == marks) & (marks >= 0)).astype(BF16)
    pay = jnp.concatenate([mine, hot], axis=1)
    cot = jnp.concatenate([cot_patches[0], cot_specials[0], zeros], axis=0)
    pay_c = swap_seq(pay, 1)
    pay_x = swap_seq(pay, 2)
    cot_c = swap_seq(cot, 1)
    keep = keep_mask[0].astype(F32).reshape(2, images) / 0.75
    table = jnp.pad(keep, ((0, 6), (HEAD, LANES - HEAD - images)))

    order = [(h, j) for h in range(OWN) for j in range(3)]
    w_own = [lax.dynamic_slice(w_qkv, (0, j * width + s * cols + h * HEAD), (width, HEAD)) for h, j in order]
    w_own = jnp.concatenate(w_own + [jnp.zeros((width, HEAD), BF16)], axis=1)
    sides = {0: biases[0], 1: jnp.zeros((width,), F32), 2: biases[1]}
    bias_own = [lax.dynamic_slice(sides[j], (s * cols + h * HEAD,), (HEAD,)) for h, j in order]
    bias_own = jnp.concatenate(bias_own + [jnp.zeros((HEAD,), F32)])[None]
    pay_x, w_own, bias_own, table = lax.optimization_barrier((pay_x, w_own, bias_own, table))
    pay_d = swap_seq(pay_x, 1)
    gain1, gain2 = norm_gains[0:1], norm_gains[1:2]
    shift1, shift2 = norm_shifts[0:1], norm_shifts[1:2]
    fb = fc1_bias.reshape(1, -1)

    headed = SDS((OWN, whole, LANES), BF16)
    qa, ka, va, lse, a0, att_send, normed = call(
        attend_kernel,
        [headed] * 3
        + [SDS((OWN, 3, 8, whole // 3), F32), SDS((chip, cols), BF16), SDS((chip, cols), BF16)]
        + [SDS((whole, width), BF16)],
        (pay, pay_c, pay_x, pay_d, gain1, shift1, w_own, bias_own),
        [pltpu.VMEM((OWN, whole, LANES), F32)],
        flops=2 * whole * width * 3 * cols + 4 * OWN * whole * whole * LANES,
    )
    a2 = swap_seq(att_send, 2)
    a1 = swap_seq(a0, 1)
    a3 = swap_seq(a2, 1)

    middle, normed2, gb2 = call(
        middle_kernel,
        [SDS((chip, width), F32), SDS((chip, width), BF16), SDS((chip, width), BF16)],
        (sidx, a0, a1, a2, a3, pay, pay_c, cot, cot_c, table, w_out, biases[2:3], gain2, shift2),
        flops=2 * chip * width * width,
        scalars=1,
    )
    per = width // (4 * nb)
    fc2_a, fc2_b, oth_y, keep_oth, fb_oth, b2, gn = feed(
        False, 2, per, sidx, bidx, normed2, gb2, w_fc1, fb, w_fc2
    )
    got2a = swap_seq(fc2_a, 2)
    got_oth = swap("batch", oth_y, 1)
    fc2_keep, own_y, keep_own, fb_own, b2_keep, b2_send, gn_keep, gn_send = feed(
        True, 0, per, sidx, bidx, normed2, gb2, w_fc1, fb, w_fc2, (b2, gn)
    )
    gn_send, b2_send, fc2_b, own_y, got2a, got_oth = lax.optimization_barrier(
        (gn_send, b2_send, fc2_b, own_y, got2a, got_oth)
    )
    gn_got = swap_seq(gn_send, 1)
    b2_got = swap_seq(b2_send, 1)
    got2b = swap_seq(fc2_b, 2)
    got_own = swap("batch", own_y, 1)

    gmid, gatt, gatt_send, go_keep, go_send, early, opat, ospe = call(
        branch_back_kernel,
        [SDS((block, width), F32), SDS((chip, cols), BF16), SDS((chip, cols), BF16)]
        + [SDS((cols, width), BF16), SDS((cols, width), BF16), SDS((width, LANES), F32)]
        + [SDS((count, width), BF16), SDS((extra, width), BF16)],
        (sidx, gn_keep, gn_got, middle, pay, pay_c, cot, cot_c, table, w_out, gain2, shift2, a0, a2, gb2)
        + (b2_keep, b2_got, biases[3:4], gain1, shift1, fb_own, fb_oth),
        [pltpu.VMEM((hidden, LANES), F32)],
        flops=8 * chip * width * cols,
        scalars=1,
    )
    gatt_x = swap_seq(gatt_send, 2)
    got_own = after(got_own, gatt_send)
    pairs = (keep_own, got_own, keep_oth, got_oth)

    def head_grads(first, heads, lse):
        return attend_back(first, heads, qa, ka, va, lse, gatt, gatt_x)

    def norm_part(g0, g12):
        return call(
            norm1_kernel,
            [SDS((chip, width), F32), SDS((chip, width), BF16)],
            (g0, g12, w_own),
            flops=2 * whole * width * 5 * LANES,
        )

    def qkv_part(g0, s0, g12, s12, early):
        wide = 5 * LANES
        if per % 8 == 0:
            outs = [SDS((width // (2 * per), per, wide), BF16)] * 2
        else:
            outs = [SDS((width // 2, wide), BF16)] * 2
        out = call(
            qkv_grad_kernel,
            outs,
            (sidx, bidx, normed, g0, g12, s0, s12, w_own, early),
            [pltpu.VMEM((width, LANES), F32), pltpu.VMEM((width, wide), F32)],
            flops=2 * whole * width * wide,
            scalars=2,
        )
        return out if per % 8 == 0 else by_batch_bit(jnp.concatenate(out, axis=0), per)

    rest = (sidx, bidx, per, block, chip, hidden, cols, count, extra, width)
    reduce_all = reduce_eight if nb == 8 else reduce_any
    out_fc2, out_out, out_fc1, out_qkv, vec, gpat, gspe = reduce_all(
        rest, pairs, (fc2_keep, got2a, got2b), (go_keep, go_send), lse, gatt_x, early,
        head_grads, norm_part, qkv_part, pay, gmid, gain1,
    )
    grad_gains = jnp.stack([vec[:, 0], vec[:, 4]])
    grad_shifts = jnp.stack([vec[:, 1], vec[:, 5]])
    grad_biases = jnp.stack([vec[:, 2], vec[:, 3], vec[:, 7], vec[:, 6]])
    return (
        opat[None],
        ospe[None],
        gpat[None],
        gspe[None],
        grad_gains,
        grad_shifts,
        out_qkv,
        grad_biases,
        out_out,
        out_fc1,
        vec[:, 8:12].reshape(-1),
        out_fc2,
    )


def reduce_eight(
    rest, pairs, twos, outs, lse, gatt_x, early, head_grads, norm_part, qkv_part, pay, gmid, gain1
):
    sidx, bidx, per, block, chip, hidden, cols, count, extra, width = rest
    fc2_keep, got2a, got2b = twos
    go_keep, go_send = outs
    wide = 5 * LANES
    deep = hidden // 8
    (send_b,) = call(stage1_kernel, [SDS((8, per, 2 * hidden), BF16)], (sidx,) + pairs, scalars=1)
    go_send, send_b, lse, got2b = lax.optimization_barrier((go_send, send_b, after(lse, gatt_x), got2b))
    got_b = swap_seq(send_b, 2)
    got_o = swap_seq(go_send, 2)
    g0, s0 = head_grads(0, 1, lse)
    g0, got_b, got_o = lax.optimization_barrier((g0, got_b, got_o))

    fc2_keep = fc2_keep.reshape(8, deep, width)
    got2a = got2a.reshape(4, deep, width)
    got2b = got2b.reshape(4, deep, width)
    go_keep = go_keep.reshape(8, per, width)
    got_o = got_o.reshape(8, per, width)
    quarter = SDS((2, per, 2 * hidden), BF16)
    send_a, zb1, zb2, zb3, keep_b = call(
        stage2_kernel,
        [SDS((4, deep + per, width), BF16), quarter, quarter, quarter, SDS(quarter.shape, F32)],
        (sidx, bidx) + pairs + (got_b, fc2_keep, got2a, got2b, go_keep, got_o),
        scalars=2,
    )
    send_a, zb, lse = lax.optimization_barrier((send_a, (zb1, zb2, zb3), after(lse, g0)))
    got_a = swap("batch", send_a, 1)
    got_zb = swap_four(zb, 1)
    g12, s12 = head_grads(1, 2, lse)
    g12, got_a, got_zb = lax.optimization_barrier((g12, got_a, got_zb))

    gn1_keep, gn1_send = norm_part(g0, g12)
    gn1_c = swap_seq(gn1_send, 1)
    got2 = jnp.concatenate([got2a, got2b], axis=0)
    quarter = SDS((deep + per, width), BF16)
    za1, za2, za3, keep_a, swap_send, swap_keep, xsend = call(
        stage3_kernel,
        [quarter, quarter, quarter, SDS(quarter.shape, F32)]
        + [SDS((per, 2 * hidden), BF16), SDS((per, 2 * hidden), F32), SDS((block, width), BF16)],
        (sidx, bidx, fc2_keep, got2, go_keep, got_o, got_a, keep_b, *got_zb, gn1_keep, gn1_c),
        scalars=2,
    )
    xsend, za, swap_send, early = lax.optimization_barrier((xsend, (za1, za2, za3), swap_send, early))
    gn1_x = swap_seq(xsend, 2)
    got_za = swap_four(za, 1)
    swap_got = swap_seq(swap_send, 1)
    q_send, q_keep = qkv_part(g0, s0, g12, s12, early)
    q_send, gn1_x, got_za, swap_got = lax.optimization_barrier((q_send, gn1_x, got_za, swap_got))
    got_q = swap("batch", q_send, 1)
    gpat, gspe, out_fc2, out_out, out_fc1 = call(
        final_kernel,
        [SDS((count, width), F32), SDS((extra, width), F32), SDS((deep, width), F32)]
        + [SDS((per, width), F32), SDS((per, 4 * hidden), F32)],
        (sidx, gn1_keep, gn1_c, gn1_x, pay, gmid, gain1, keep_a, *got_za, swap_keep, swap_got),
        scalars=1,
    )
    got_q = after(got_q, gpat)
    quarter = SDS((4, per, wide), BF16)
    z1, z2, z3, kept = call(
        quarter_kernel, [quarter, quarter, quarter, SDS(quarter.shape, F32)], (bidx, q_keep, got_q), scalars=1
    )
    got_z = swap_four((z1, z2, z3), 1)
    row = SDS((per, wide), BF16)
    s1, s2, s3, own = call(
        owner_kernel, [row, row, row, SDS(row.shape, F32)], (sidx, kept, *got_z), scalars=1
    )
    gots = [swap_seq(v, k) for k, v in ((1, s1), (2, s2), (3, s3))]
    out_qkv, vec = call(
        collect_kernel,
        [SDS((per, 3 * width), F32), SDS((per, LANES), F32)],
        (sidx, own, *gots),
        [pltpu.VMEM((4, per, wide), F32)],
        scalars=1,
    )
    return out_fc2, out_out, out_fc1, out_qkv, vec[:, HEAD:], gpat, gspe


def reduce_any(
    rest, pairs, twos, outs, lse, gatt_x, early, head_grads, norm_part, qkv_part, pay, gmid, gain1
):
    sidx, bidx, per, block, chip, hidden, cols, count, extra, width = rest
    s = lax.axis_index("seq")
    nb = lax.axis_size("batch")
    nbits = bits_of("batch")
    low = nbits - 1
    fc2_keep, got2a, got2b = twos
    go_keep, go_send = outs
    keep_own, got_own, keep_oth, got_oth = [
        split_bits(p.reshape(2, 2, nb // 2, per, hidden), 2, low) for p in pairs
    ]
    g0, s0 = head_grads(0, 1, lse)
    g12, s12 = head_grads(1, 2, lse)
    send_own, parts_own = to_send([keep_own, got_own], 0, 1, "seq")
    send_oth, parts_oth = to_send([keep_oth, got_oth], 0, 1, "seq")
    got_b = swap_seq(jnp.concatenate([send_own, send_oth], axis=-1), 2)
    sum_own = sum_rest(parts_own + [got_b[..., hidden:]], 1, 1)
    sum_oth = sum_rest(parts_oth + [got_b[..., :hidden]], 1, 1)
    own_c = s & 1
    other = jnp.concatenate([pick(sum_own, 1 - own_c, 0), pick(sum_oth, 1 - own_c, 0)], axis=-1)
    got = swap_seq(other.astype(BF16), 1).astype(F32)
    rel = jnp.stack([pick(sum_own, own_c, 0), got[:, :hidden], pick(sum_oth, own_c, 0), got[:, hidden:]])
    out_fc1 = jnp.concatenate([pick(rel, s ^ a, 0) for a in range(4)], axis=1)
    got2 = jnp.concatenate([got2a, got2b], axis=0)
    got_o = swap_seq(go_send, 2)
    both = []
    for keep, got in ((fc2_keep, got2), (go_keep, got_o)):
        parts = [split_bits(p.reshape(nb, -1, width), 0, nbits) for p in (keep, got)]
        both.append(sum_rest(parts, 0, 0))
    gn1_keep, gn1_send = norm_part(g0, g12)
    gn1_c = swap_seq(gn1_send, 1)
    gn1_x = swap_seq((gn1_keep[block:] + gn1_c[block:].astype(F32)).astype(BF16), 2)
    gpat, gspe = call(
        norm_only_kernel,
        [SDS((count, width), F32), SDS((extra, width), F32)],
        (gn1_keep, gn1_c, gn1_x, pay, gmid, gain1),
    )
    q_send, q_keep = qkv_part(g0, s0, g12, s12, early)
    wide = 5 * LANES
    parts = [split_bits(p.reshape(4, nb // 2, per, wide), 1, low) for p in (q_keep, swap("batch", q_send, 1))]
    sum_q = sum_rest(parts, 1, 1)
    pieces = [pick(sum_q, s, 0)] + [
        swap_seq(pick(sum_q, s ^ j, 0).astype(BF16), j).astype(F32) for j in (1, 2, 3)
    ]
    rel = jnp.stack([p[:, : 3 * cols] for p in pieces])
    absolute = jnp.stack([pick(rel, s ^ a, 0) for a in range(4)], axis=1)
    out_qkv = absolute.reshape(-1, 4, OWN, 3, HEAD).transpose(0, 3, 1, 2, 4).reshape(-1, 3 * width)
    vec = total([p[:, 3 * cols :] for p in pieces])
    return both[0], both[1], out_fc1, out_qkv, vec, gpat, gspe


def solution(mesh):
    tok = P("batch", "seq", None)
    ids = P("batch", "seq")
    split = P(None, ("seq", "batch"))
    rows = P(("seq", "batch"), None)
    return jax.shard_map(
        body,
        mesh=mesh,
        in_specs=(tok, tok, ids, ids, P("batch", None)) + (P(),) * 8 + (tok, tok),
        out_specs=(tok, tok, tok, tok, split, split, rows, split, rows, rows, P(("seq", "batch")), rows),
        check_vma=False,
    )
```

time: 281 us -> 230 us (0.82); the launches traced: 276 us -> 229 us
  Pallas kernels: 0 us -> 111 us
  matrix products: 77.6 us -> 0 us
  other arithmetic: 59.5 us -> 6.18 us
  local copies, waits for them, and re-layouts: 35.2 us -> 18.7 us
  starting transfers between devices: 43.8 us -> 34.4 us
    pallas_call x0 -> x16, Pallas kernels: none -> 111 us  [the longest x14 84.9 us: call(): pl.pallas_call(kernel, out_shape=outs, in_specs=[smem()] * scalars + [vme...]
    dot_general x42 -> x0, matrix products: 77.6 us -> none  [the longest x12 30.7 us: dot_t(): lax.dot_general(a, b, (((1,), (1,)), ((), ())), preferred_element_type=F32)]
    convert_element_type x21 -> x1, other arithmetic: 29.1 us -> 0.11 us  [body(): hot = ((segs[:, None] == marks) & (marks >= 0)).astype(BF16)]
    ppermute x42 -> x33, starting transfers between devices: 43.8 us -> 34.4 us  [swap(): lax.ppermute(v, kind, [(i, i ^ mask) for i in range(lax.axis_size(kind))])]
    add x19 -> x0, other arithmetic: 8.12 us -> none  [the longest x17 5.96 us: total(): out = out + part.astype(F32)]
    reduce_sum x13 -> x0, other arithmetic: 5.83 us -> none  [the longest x3 2.24 us: body(): tot = jnp.sum(e, axis=-1, keepdims=True)]
    convert_element_type x8 -> x0, local copies, waits for them, and re-layouts: 5.56 us -> none  [the longest x1 2.44 us: body(): got_n = swap_seq(blocks[:, 1].astype(BF16), 1)]
    concatenate x6 -> x2, other arithmetic: 7.1 us -> 2.21 us  [the longest x1 1.15 us: reduce_eight(): got2 = jnp.concatenate([got2a, got2b], axis=0)]
  transfers between devices with their start and end apart: 42 -> 33, of which waited for: 20 -> 16; matrix products, arithmetic and copies ran while one was open for 54% -> 4% of each run, Pallas kernels for 0% -> 32%
where the time goes in v2:
time: 230 us; the launch traced here: 229 us
  Pallas kernels  111 us (48%)
  waiting for transfers between devices  58.3 us (25%)
  starting transfers between devices  34.4 us (15%)
  local copies, waits for them, and re-layouts  18.7 us (8%)
  other arithmetic  6.18 us (3%)
    pallas_call x14, Pallas kernels, call(): pl.pallas_call(kernel, out_shape=outs, in_specs=[smem()] * scalars + [vme...  84.9 us
    ppermute x33, waiting for transfers between devices, swap(): lax.ppermute(v, kind, [(i, i ^ mask) for i in range(lax.axis_size(kind))])  58.3 us
    ppermute x33, starting transfers between devices, swap(): lax.ppermute(v, kind, [(i, i ^ mask) for i in range(lax.axis_size(kind))])  34.4 us
    pallas_call x2, Pallas kernels, feed(): pl.pallas_call(functools.partial(feed_kernel, last), grid_spec=pltpu.Pref...  26 us
    unnamed x82, local copies, waits for them, and re-layouts  8.26 us
  transfers between devices with their start and end apart: 33, of which 16 were waited for; matrix products, arithmetic and copies ran while one was open for 4% of the time, Pallas kernels for 32%

profile of v2, /device:TPU:0, one launch (start us, length us, event | category | flops | bytes accessed | tf_op | source)
XLA Modules:
  0.0 229.5 jit_solution(3791911047028735769)
XLA Ops:
  1.3 0.8 pad_add_fusion
  2.2 1.1 pad_maximum_fusion.1.p0
  3.3 3.0 %collective-permute-start.1 = (bf16[288,896]{1,0:T(8,128)(2,1)S(1)}, bf16[288,896]{1,0:T(8,128)(2,1)}, u32[]{:S(2)}, u32[]{:S(2)}) collective-permute-start(bf16[288,896]{1,0:T(8,128)(2,1)S(1)} %pad_maximum_fusion.1.p0), channel_id=1, source_target_pairs={{0,16},{8,24},{16,0},{24,8},{1,17},{9,25},{17,1},{25,9},{2,18},{10... | collective-permute-start | bytes 1548296 | tf_op jit(solution)/shard_map/ppermute | solution.py:581
  7.7 1.5 fusion.6
  9.9 2.1 constant_dynamic-slice_fusion.6
  12.1 2.0 concatenate.24.w
  14.1 4.0 %collective-permute-done.1.p2 = bf16[288,896]{1,0:T(8,128)(2,1)} collective-permute-done((bf16[288,896]{1,0:T(8,128)(2,1)S(1)}, bf16[288,896]{1,0:T(8,128)(2,1)}, u32[]{:S(2)}, u32[]{:S(2)}) %collective-permute-start.1) | collective-permute-done | bytes 516128 | tf_op jit(solution)/shard_map/ppermute | solution.py:581
  19.4 0.9 collective-permute-done.2.p3
  20.3 0.8 copy-done.38
  21.0 17.5 %shard_map.238 = (bf16[3,1152,128]{2,1,0:T(8,128)(2,1)}, bf16[3,1152,128]{2,1,0:T(8,128)(2,1)}, bf16[3,1152,128]{2,1,0:T(8,128)(2,1)}, f32[3,3,8,384]{3,2,1,0:T(...) custom-call(bf16[288,896]{1,0:T(8,128)(2,1)} %copy-done, ...), custom_call_target="tpu_custom_call" | custom-call | flops 3057647616 | bytes 8032768 | tf_op jit(solution)/shard_map/pallas_call | solution.py:76
  38.5 1.8 collective-permute-start.4
  40.3 7.5 %collective-permute-done.4.a2 = bf16[576,192]{1,0:T(8,128)(2,1)S(1)} collective-permute-done((bf16[576,192]{1,0:T(8,128)(2,1)}, bf16[576,192]{1,0:T(8,128)(2,1)S(1)}, u32[]{:S(2)}, u32[]{:S(2)}) %collective-permute-start.4) | collective-permute-done | bytes 221216 | tf_op jit(solution)/shard_map/ppermute | solution.py:581
  47.9 1.5 collective-permute-done.5.a3
  49.4 0.7 copy-done.21
  50.2 5.3 %shard_map.239 = (f32[576,768]{1,0:T(8,128)}, bf16[576,768]{1,0:T(8,128)(2,1)}, bf16[576,768]{1,0:T(8,128)(2,1)}) custom-call(s32[1]{0:T(128)} %bitcast.sref, bf16[576,192]{1,0:T(8,128)(2,1)} %get-tuple-element.126.a0, bf16[576,192]{1,0:T(8,128)(2,1)} %copy-done.20, bf16[576,192]{1,0:T(8,128)(2,1)} %copy-done.11, bf16[576,192]{1,0:T(8,128)(2,1)} %copy-done.21, ...), custom_call_target="tpu_custom_call" | custom-call | flops 679477248 | bytes 7533572 | tf_op jit(solution)/shard_map/pallas_call | solution.py:76
  55.5 12.7 %shard_map.240 = (bf16[384,768]{1,0:T(8,128)(2,1)}, bf16[384,768]{1,0:T(8,128)(2,1)}, bf16[16,24,768]{2,1,0:T(8,128)(2,1)}, bf16[16,24,768]{2,1,0:T(8,128)(2,1)}...) custom-call(s32[1]{0:T(128)} %bitcast.sref, s32[1]{0:T(128)} %bitcast.1.bref, ...), custom_call_target="tpu_custom_call" | custom-call | flops 4076863488 | bytes 5898240 | tf_op jit(solution)/shard_map/pallas_call | solution.py:263
  68.2 1.8 collective-permute-start.7
  70.0 1.5 collective-permute-start.8
  71.5 13.3 %shard_map.241 = (bf16[768,768]{1,0:T(8,128)(2,1)}, bf16[16,24,768]{2,1,0:T(8,128)(2,1)}, bf16[16,24,768]{2,1,0:T(8,128)(2,1)}, f32[1,768]{1,0:T(1,128)}, f32[28...) custom-call(s32[1]{0:T(128)} %bitcast.sref, s32[1]{0:T(128)} %bitcast.1.bref, ...), custom_call_target="tpu_custom_call" | custom-call | flops 4076863488 | bytes 5898240 | tf_op jit(solution)/shard_map/pallas_call | solution.py:263
  85.8 1.5 collective-permute-start.11
  87.9 0.7 collective-permute-done.10.b2_got
  88.6 0.8 copy-done.18
  89.3 1.0 copy-done.13
  90.4 7.4 %shard_map.242 = (f32[288,768]{1,0:T(8,128)}, bf16[576,192]{1,0:T(8,128)(2,1)}, bf16[576,192]{1,0:T(8,128)(2,1)}, bf16[192,768]{1,0:T(8,128)(2,1)}, bf16[192,768...) custom-call(s32[1]{0:T(128)} %bitcast.sref, ...), custom_call_target="tpu_custom_call" | custom-call | flops 679477248 | bytes 12909572 | tf_op jit(solution)/shard_map/pallas_call | solution.py:76
  97.8 0.8 collective-permute-start.12
  98.6 2.7 %collective-permute-done.11.got_own = bf16[16,24,768]{2,1,0:T(8,128)(2,1)S(1)} collective-permute-done((bf16[16,24,768]{2,1,0:T(8,128)(2,1)}, bf16[16,24,768]{2,1,0:T(8,128)(2,1)S(1)}, u32[]{:S(2)}, u32[]{:S(2)}) %collective-permute-start.11) | collective-permute-done | bytes 589856 | tf_op jit(solution)/shard_map/ppermute | solution.py:581
  101.3 0.9 copy-done.8
  102.1 2.5 %shard_map.243 = bf16[8,24,1536]{2,1,0:T(8,128)(2,1)} custom-call(s32[1]{0:T(128)} %bitcast.sref, bf16[16,24,768]{2,1,0:T(8,128)(2,1)} %get-tuple-element.152.keep_own, bf16[16,24,768]{2,1,0:T(8,128)(2,1)} %copy-done.8, bf16[16,24,768]{2,1,0:T(8,128)(2,1)} %get-tuple-element.156.keep_oth, bf16[16,24,768]{2,1,0:T(8,128)(2,1)} %copy-done.7), custom_call_target="tpu_custom_call" | custom-call | bytes 2949124 | tf_op jit(solution)/shard_map/pallas_call | solution.py:76
  104.7 4.1 %collective-permute-done.12.gx = bf16[576,192]{1,0:T(8,128)(2,1)S(1)} collective-permute-done((bf16[576,192]{1,0:T(8,128)(2,1)}, bf16[576,192]{1,0:T(8,128)(2,1)S(1)}, u32[]{:S(2)}, u32[]{:S(2)}) %collective-permute-start.12) | collective-permute-done | bytes 221216 | tf_op jit(solution)/shard_map/ppermute | solution.py:581
  109.4 1.5 collective-permute-start.15
  110.9 8.1 %shard_map.244 = (bf16[1,1152,192]{2,1,0:T(8,128)(2,1)}, f32[1,1,192]{2,1,0:T(1,128)}) custom-call(bf16[3,1152,128]{2,1,0:T(8,128)(2,1)} %get-tuple-element.148.qa, bf16[3,1152,128]{2,1,0:T(8,128)(2,1)} %get-tuple-element.149.ka, bf16[3,1152,128]{2,1,0:T(8,128)(2,1)} %get-tuple-element.150.va, f32[3,3,8,384]{3,2,1,0:T(8,128)} %get-tuple-element.178.lse, ...), custom_call_target="tpu_custom_call" | custom-call | flops 1698693120 | bytes 3650304 | tf_op jit(solution)/shard_map/pallas_call | solution.py:76
  119.0 10.5 %collective-permute-done.15 = bf16[192,768]{1,0:T(8,128)(2,1)S(1)} collective-permute-done((bf16[192,768]{1,0:T(8,128)(2,1)S(1)}, bf16[192,768]{1,0:T(8,128)(2,1)S(1)}, u32[]{:S(2)}, u32[]{:S(2)}) %collective-permute-start.15) | collective-permute-done | bytes 294944 | tf_op jit(solution)/shard_map/ppermute | solution.py:581
  129.5 0.7 copy-done.12
  130.4 4.0 %shard_map.245 = (bf16[4,120,768]{2,1,0:T(8,128)(2,1)}, bf16[2,24,1536]{2,1,0:T(8,128)(2,1)}, bf16[2,24,1536]{2,1,0:T(8,128)(2,1)}, bf16[2,24,1536]{2,1,0:T(8,128)(2,1)}, f32[2,24,1536]{2,1,0:T(8,128)}) custom-call(s32[1]{0:T(128)} %bitcast.sref, s32[1]{0:T(128)} %bitcast.1.bref, bf16[16,24,768]{2,1,0:T(8,128)(2,1)} %get-tuple-element.152.keep_own, ...), custom_call_target="tpu_custom_call" | custom-call | bytes 7372808 | tf_op jit(solution)/shard_map/pallas_call | solution.py:76
  134.4 1.1 collective-permute-start.16
  135.5 1.6 collective-permute-start.17
  137.1 2.6 %collective-permute-start.18 = (bf16[2,24,1536]{2,1,0:T(8,128)(2,1)}, bf16[2,24,1536]{2,1,0:T(8,128)(2,1)S(1)}, u32[]{:S(2)}, u32[]{:S(2)}) collective-permute-start(bf16[2,24,1536]{2,1,0:T(8,128)(2,1)} %get-tuple-element.182), channel_id=1, source_target_pairs={{0,4},{1,5},{2,6},{3,7},{4,0},{5,1},{6,2},{7,3},{8,12},{9,13},{10,... | collective-permute-start | bytes 442376 | tf_op jit(solution)/shard_map/ppermute | solution.py:581
  139.9 13.9 %shard_map.246 = (bf16[2,1152,192]{2,1,0:T(8,128)(2,1)}, f32[2,1,192]{2,1,0:T(1,128)}) custom-call(bf16[3,1152,128]{2,1,0:T(8,128)(2,1)} %get-tuple-element.148.qa, bf16[3,1152,128]{2,1,0:T(8,128)(2,1)} %get-tuple-element.149.ka, bf16[3,1152,128]{2,1,0:T(8,128)(2,1)} %get-tuple-element.150.va, f32[3,3,8,384]{3,2,1,0:T(8,128)} %get-tuple-element.178.lse, ...), custom_call_target="tpu_custom_call" | custom-call | flops 3397386240 | bytes 4093440 | tf_op jit(solution)/shard_map/pallas_call | solution.py:76
  153.9 5.4 %shard_map.247 = (f32[576,768]{1,0:T(8,128)}, bf16[576,768]{1,0:T(8,128)(2,1)}) custom-call(bf16[1,1152,192]{2,1,0:T(8,128)(2,1)} %get-tuple-element.166.g0, bf16[2,1152,192]{2,1,0:T(8,128)(2,1)} %get-tuple-element.184.g12, bf16[768,640]{1,0:T(8,128)(2,1)} %concatenate.24.w), custom_call_target="tpu_custom_call" | custom-call | flops 1132462080 | bytes 4964352 | tf_op jit(solution)/shard_map/pallas_call | solution.py:76
  159.4 1.1 pad_maximum_fusion.got2
  160.5 1.5 collective-permute-done.20.gn_got.c0
  162.0 1.0 copy-done.2
  163.0 4.3 %shard_map.248 = (bf16[120,768]{1,0:T(8,128)(2,1)}, bf16[120,768]{1,0:T(8,128)(2,1)}, bf16[120,768]{1,0:T(8,128)(2,1)}, f32[120,768]{1,0:T(8,128)}, bf16[24,1536...) custom-call(s32[1]{0:T(128)} %bitcast.sref, s32[1]{0:T(128)} %bitcast.1.bref, ...), custom_call_target="tpu_custom_call" | custom-call | bytes 8663048 | tf_op jit(solution)/shard_map/pallas_call | solution.py:76
  167.9 0.7 collective-permute-start.22
  168.6 3.5 %collective-permute-start.23 = (bf16[120,768]{1,0:T(8,128)(2,1)}, bf16[120,768]{1,0:T(8,128)(2,1)S(1)}, u32[]{:S(2)}, u32[]{:S(2)}) collective-permute-start(bf16[120,768]{1,0:T(8,128)(2,1)} %get-tuple-element.205), channel_id=1, source_target_pairs={{0,4},{1,5},{2,6},{3,7},{4,0},{5,1},{6,2},{7,3},{8,12},{9,13},{10,... | collective-permute-start | bytes 552968 | tf_op jit(solution)/shard_map/ppermute | solution.py:581
  172.3 6.6 %shard_map.249 = (bf16[16,24,640]{2,1,0:T(8,128)(2,1)}, bf16[16,24,640]{2,1,0:T(8,128)(2,1)}) custom-call(s32[1]{0:T(128)} %bitcast.sref, s32[1]{0:T(128)} %bitcast.1.bref, bf16[1152,768]{1,0:T(8,128)(2,1)} %get-tuple-element.187.normed, bf16[1,1152,192]{2,1,0:T(8,128)(2,1)} %get-tuple-element.166.g0, bf16[2,1152,192]{2,1,0:T(8,128)(2,1)} %get-tuple-element.184.g12, ...), custom_call_target="tpu_custom_call" | custom-call | flops 1132462080 | bytes 5458184 | tf_op jit(solution)/shard_map/pallas_call | solution.py:76
  178.9 6.7 %collective-permute-done.23.za2 = bf16[120,768]{1,0:T(8,128)(2,1)S(1)} collective-permute-done((bf16[120,768]{1,0:T(8,128)(2,1)}, bf16[120,768]{1,0:T(8,128)(2,1)S(1)}, u32[]{:S(2)}, u32[]{:S(2)}) %collective-permute-start.23) | collective-permute-done | bytes 184352 | tf_op jit(solution)/shard_map/ppermute | solution.py:581
  185.7 1.0 collective-permute-start.26
  186.7 4.3 %shard_map.250 = (f32[256,768]{1,0:T(8,128)}, f32[4,768]{1,0:T(4,128)}, f32[96,768]{1,0:T(8,128)}, f32[24,768]{1,0:T(8,128)}, f32[24,3072]{1,0:T(8,128)}) custom-call(s32[1]{0:T(128)} %bitcast.sref, f32[576,768]{1,0:T(8,128)} %get-tuple-element.185.gn_keep.k0, bf16[576,768]{1,0:T(8,128)(2,1)} %copy-done.2, bf16[288,768]{1,0:T(8,128)(2,1)} %copy-done.17, ...), custom_call_target="tpu_custom_call" | custom-call | bytes 7105540 | tf_op jit(solution)/shard_map/pallas_call | solution.py:76
  191.0 6.1 %collective-permute-done.26.got = bf16[16,24,640]{2,1,0:T(8,128)(2,1)S(1)} collective-permute-done((bf16[16,24,640]{2,1,0:T(8,128)(2,1)}, bf16[16,24,640]{2,1,0:T(8,128)(2,1)S(1)}, u32[]{:S(2)}, u32[]{:S(2)}) %collective-permute-start.26) | collective-permute-done | bytes 491552 | tf_op jit(solution)/shard_map/ppermute | solution.py:581
  197.0 0.8 copy-done.16
  197.8 2.0 shard_map.251
  199.9 4.5 %collective-permute-start.27 = (bf16[4,24,640]{2,1,0:T(8,128)(2,1)}, bf16[4,24,640]{2,1,0:T(8,128)(2,1)S(1)}, u32[]{:S(2)}, u32[]{:S(2)}) collective-permute-start(bf16[4,24,640]{2,1,0:T(8,128)(2,1)} %get-tuple-element.222), channel_id=1, source_target_pairs={{0,2},{1,3},{2,0},{3,1},{4,6},{5,7},{6,4},{7,5},{8,10},{9,11},{10,... | collective-permute-start | bytes 368648 | tf_op jit(solution)/shard_map/ppermute | solution.py:581
  204.4 0.9 collective-permute-start.28
  205.3 1.5 collective-permute-start.29
  206.8 1.6 collective-permute-done.27.z1
  208.4 6.8 %collective-permute-done.28.z2 = bf16[4,24,640]{2,1,0:T(8,128)(2,1)S(1)} collective-permute-done((bf16[4,24,640]{2,1,0:T(8,128)(2,1)}, bf16[4,24,640]{2,1,0:T(8,128)(2,1)S(1)}, u32[]{:S(2)}, u32[]{:S(2)}) %collective-permute-start.28) | collective-permute-done | bytes 122912 | tf_op jit(solution)/shard_map/ppermute | solution.py:581
  215.9 1.8 shard_map.252
  217.7 1.5 collective-permute-start.31
  219.6 2.3 collective-permute-done.31.g2
  221.9 0.9 collective-permute-done.32.g3
  223.4 1.7 shard_map.253
  225.0 1.3 slice_reduce_fusion.3
  226.4 0.8 slice.77
  (128 shorter events, 11.7 us)
Async XLA Ops:
  3.3 8.8 %copy-start = (bf16[288,896]{1,0:T(8,128)(2,1)}, bf16[288,896]{1,0:T(8,128)(2,1)S(1)}, u32[]{:S(2)}) copy-start(bf16[288,896]{1,0:T(8,128)(2,1)S(1)} %pad_maximum_fusion.1.p0) | copy-start | bytes 1548292
  3.3 14.9 %collective-permute-start.1 = (bf16[288,896]{1,0:T(8,128)(2,1)S(1)}, bf16[288,896]{1,0:T(8,128)(2,1)}, u32[]{:S(2)}, u32[]{:S(2)}) collective-permute-start(bf16[288,896]{1,0:T(8,128)(2,1)S(1)} %pad_maximum_fusion.1.p0), channel_id=1, source_target_pairs={{0,16},{8,24},{16,0},{24,8},{1,17},{9,25},{17,1},{25,9},{2,18},{10... | collective-permute-start | bytes 1548296 | tf_op jit(solution)/shard_map/ppermute | solution.py:581
  6.3 13.1 %collective-permute-start = (bf16[288,896]{1,0:T(8,128)(2,1)S(1)}, bf16[288,896]{1,0:T(8,128)(2,1)S(1)}, u32[]{:S(2)}, u32[]{:S(2)}) collective-permute-start(bf16[288,896]{1,0:T(8,128)(2,1)S(1)} %pad_maximum_fusion.1.p0), channel_id=1, source_target_pairs={{0,8},{8,0},{16,24},{24,16},{1,9},{9,1},{17,25},{25,17},{2,10},{10... | collective-permute-start | bytes 1548296 | tf_op jit(solution)/shard_map/ppermute | solution.py:581
  12.1 6.1 %copy-start.19 = (bf16[1,256,768]{2,1,0:T(8,128)(2,1)S(1)}, bf16[1,256,768]{2,1,0:T(8,128)(2,1)}, u32[]{:S(2)}) copy-start(bf16[1,256,768]{2,1,0:T(8,128)(2,1)} %param.28) | copy-start | bytes 1179652
  12.1 6.1 %copy-start.35 = (bf16[1,4,768]{2,1,0:T(4,128)(2,1)S(1)}, bf16[1,4,768]{2,1,0:T(4,128)(2,1)}, u32[]{:S(2)}) copy-start(bf16[1,4,768]{2,1,0:T(4,128)(2,1)} %param.29) | copy-start | bytes 18436
  12.1 6.7 %copy-start.36 = (f32[2,768]{1,0:T(2,128)S(1)}, f32[2,768]{1,0:T(2,128)}, u32[]{:S(2)}) copy-start(f32[2,768]{1,0:T(2,128)} %param.21) | copy-start | bytes 18436
  12.1 6.6 %copy-start.37 = (f32[2,768]{1,0:T(2,128)S(1)}, f32[2,768]{1,0:T(2,128)}, u32[]{:S(2)}) copy-start(f32[2,768]{1,0:T(2,128)} %param.20) | copy-start | bytes 18436
  18.1 2.1 collective-permute-start.2
  18.2 20.3 %copy-start.1 = (bf16[288,768]{1,0:T(8,128)(2,1)}, bf16[288,768]{1,0:T(8,128)(2,1)S(1)}, u32[]{:S(2)}) copy-start(bf16[288,768]{1,0:T(8,128)(2,1)S(1)} %pad_maximum_fusion.2.c0) | copy-start | bytes 1327108
  18.2 29.7 %collective-permute-start.6 = (bf16[288,768]{1,0:T(8,128)(2,1)S(1)}, bf16[288,768]{1,0:T(8,128)(2,1)S(1)}, u32[]{:S(2)}, u32[]{:S(2)}) collective-permute-start(bf16[288,768]{1,0:T(8,128)(2,1)S(1)} %pad_maximum_fusion.2.c0), channel_id=1, source_target_pairs={{0,8},{8,0},{16,24},{24,16},{1,9},{9,1},{17,25},{25,17},{2,10},{10... | collective-permute-start | bytes 1327112 | tf_op jit(solution)/shard_map/ppermute | solution.py:581
  38.5 9.3 %collective-permute-start.4 = (bf16[576,192]{1,0:T(8,128)(2,1)}, bf16[576,192]{1,0:T(8,128)(2,1)S(1)}, u32[]{:S(2)}, u32[]{:S(2)}) collective-permute-start(bf16[576,192]{1,0:T(8,128)(2,1)} %get-tuple-element.127), channel_id=1, source_target_pairs={{0,16},{8,24},{16,0},{24,8},{1,17},{9,25},{17,1},{25,9},{2,18},{10... | collective-permute-start | bytes 663560 | tf_op jit(solution)/shard_map/ppermute | solution.py:581
  40.3 7.5 %collective-permute-start.3 = (bf16[576,192]{1,0:T(8,128)(2,1)}, bf16[576,192]{1,0:T(8,128)(2,1)S(1)}, u32[]{:S(2)}, u32[]{:S(2)}) collective-permute-start(bf16[576,192]{1,0:T(8,128)(2,1)} %get-tuple-element.126.a0), channel_id=1, source_target_pairs={{0,8},{8,0},{16,24},{24,16},{1,9},{9,1},{17,25},{25,17},{2,10},{10... | collective-permute-start | bytes 663560 | tf_op jit(solution)/shard_map/ppermute | solution.py:581
  47.9 1.6 copy-start.11
  47.9 1.6 collective-permute-start.5
  47.9 1.6 copy-start.10
  47.9 1.6 copy-start.20
  68.2 16.6 %collective-permute-start.7 = (bf16[384,768]{1,0:T(8,128)(2,1)}, bf16[384,768]{1,0:T(8,128)(2,1)S(1)}, u32[]{:S(2)}, u32[]{:S(2)}) collective-permute-start(bf16[384,768]{1,0:T(8,128)(2,1)} %get-tuple-element.138), channel_id=1, source_target_pairs={{0,16},{8,24},{16,0},{24,8},{1,17},{9,25},{17,1},{25,9},{2,18},{10... | collective-permute-start | bytes 1769480 | tf_op jit(solution)/shard_map/ppermute | solution.py:581
  70.0 15.3 %collective-permute-start.8 = (bf16[16,24,768]{2,1,0:T(8,128)(2,1)}, bf16[16,24,768]{2,1,0:T(8,128)(2,1)S(1)}, u32[]{:S(2)}, u32[]{:S(2)}) collective-permute-start(bf16[16,24,768]{2,1,0:T(8,128)(2,1)} %get-tuple-element.139), channel_id=1, source_target_pairs={{0,1},{1,0},{2,3},{3,2},{4,5},{5,4},{6,7},{7,6},{8,9},{9,8},{10,11... | collective-permute-start | bytes 1769480 | tf_op jit(solution)/shard_map/ppermute | solution.py:581
  84.8 12.9 %copy-start.3 = (bf16[384,768]{1,0:T(8,128)(2,1)}, bf16[384,768]{1,0:T(8,128)(2,1)S(1)}, u32[]{:S(2)}) copy-start(bf16[384,768]{1,0:T(8,128)(2,1)S(1)} %collective-permute-done.7) | copy-start | bytes 1769476
  85.3 12.4 %copy-start.7 = (bf16[16,24,768]{2,1,0:T(8,128)(2,1)}, bf16[16,24,768]{2,1,0:T(8,128)(2,1)S(1)}, u32[]{:S(2)}) copy-start(bf16[16,24,768]{2,1,0:T(8,128)(2,1)S(1)} %collective-permute-done.8.got_oth) | copy-start | bytes 1769476
  85.3 3.3 %collective-permute-start.9 = (bf16[576,768]{1,0:T(8,128)(2,1)}, bf16[576,768]{1,0:T(8,128)(2,1)S(1)}, u32[]{:S(2)}, u32[]{:S(2)}) collective-permute-start(bf16[576,768]{1,0:T(8,128)(2,1)} %get-tuple-element.140), channel_id=1, source_target_pairs={{0,8},{8,0},{16,24},{24,16},{1,9},{9,1},{17,25},{25,17},{2,10},{10... | collective-permute-start | bytes 2654216 | tf_op jit(solution)/shard_map/ppermute | solution.py:581
  85.3 3.3 %collective-permute-start.10 = (bf16[288,768]{1,0:T(8,128)(2,1)}, bf16[288,768]{1,0:T(8,128)(2,1)S(1)}, u32[]{:S(2)}, u32[]{:S(2)}) collective-permute-start(bf16[288,768]{1,0:T(8,128)(2,1)} %get-tuple-element.143), channel_id=1, source_target_pairs={{0,8},{8,0},{16,24},{24,16},{1,9},{9,1},{17,25},{25,17},{2,10},{10... | collective-permute-start | bytes 1327112 | tf_op jit(solution)/shard_map/ppermute | solution.py:581
  85.8 15.4 %collective-permute-start.11 = (bf16[16,24,768]{2,1,0:T(8,128)(2,1)}, bf16[16,24,768]{2,1,0:T(8,128)(2,1)S(1)}, u32[]{:S(2)}, u32[]{:S(2)}) collective-permute-start(bf16[16,24,768]{2,1,0:T(8,128)(2,1)} %get-tuple-element.153), channel_id=1, source_target_pairs={{0,1},{1,0},{2,3},{3,2},{4,5},{5,4},{6,7},{7,6},{8,9},{9,8},{10,11... | collective-permute-start | bytes 1769480 | tf_op jit(solution)/shard_map/ppermute | solution.py:581
  87.3 21.5 %collective-permute-start.13 = (bf16[384,768]{1,0:T(8,128)(2,1)}, bf16[384,768]{1,0:T(8,128)(2,1)S(1)}, u32[]{:S(2)}, u32[]{:S(2)}) collective-permute-start(bf16[384,768]{1,0:T(8,128)(2,1)} %get-tuple-element.160), channel_id=1, source_target_pairs={{0,16},{8,24},{16,0},{24,8},{1,17},{9,25},{17,1},{25,9},{2,18},{10... | collective-permute-start | bytes 1769480 | tf_op jit(solution)/shard_map/ppermute | solution.py:581
  89.3 1.0 copy-start.13
  97.8 11.7 %copy-start.40 = (bf16[192,768]{1,0:T(8,128)(2,1)S(1)}, bf16[192,768]{1,0:T(8,128)(2,1)}, u32[]{:S(2)}) copy-start(bf16[192,768]{1,0:T(8,128)(2,1)} %get-tuple-element.165) | copy-start | bytes 884740
  97.8 11.0 %collective-permute-start.12 = (bf16[576,192]{1,0:T(8,128)(2,1)}, bf16[576,192]{1,0:T(8,128)(2,1)S(1)}, u32[]{:S(2)}, u32[]{:S(2)}) collective-permute-start(bf16[576,192]{1,0:T(8,128)(2,1)} %get-tuple-element.154), channel_id=1, source_target_pairs={{0,16},{8,24},{16,0},{24,8},{1,17},{9,25},{17,1},{25,9},{2,18},{10... | collective-permute-start | bytes 663560 | tf_op jit(solution)/shard_map/ppermute | solution.py:581
  108.8 2.1 copy-start.39
  108.8 10.2 %copy-start.5 = (bf16[384,768]{1,0:T(8,128)(2,1)}, bf16[384,768]{1,0:T(8,128)(2,1)S(1)}, u32[]{:S(2)}) copy-start(bf16[384,768]{1,0:T(8,128)(2,1)S(1)} %collective-permute-done.13) | copy-start | bytes 1769476
  108.8 20.7 %collective-permute-start.14 = (bf16[8,24,1536]{2,1,0:T(8,128)(2,1)}, bf16[8,24,1536]{2,1,0:T(8,128)(2,1)S(1)}, u32[]{:S(2)}, u32[]{:S(2)}) collective-permute-start(bf16[8,24,1536]{2,1,0:T(8,128)(2,1)} %shard_map.243), channel_id=1, source_target_pairs={{0,16},{8,24},{16,0},{24,8},{1,17},{9,25},{17,1},{25,9},{2,18},{10... | collective-permute-start | bytes 1769480 | tf_op jit(solution)/shard_map/ppermute | solution.py:581
  109.4 20.1 %collective-permute-start.15 = (bf16[192,768]{1,0:T(8,128)(2,1)S(1)}, bf16[192,768]{1,0:T(8,128)(2,1)S(1)}, u32[]{:S(2)}, u32[]{:S(2)}) collective-permute-start(bf16[192,768]{1,0:T(8,128)(2,1)S(1)} %copy-done.40), channel_id=1, source_target_pairs={{0,16},{8,24},{16,0},{24,8},{1,17},{9,25},{17,1},{25,9},{2,18},{10... | collective-permute-start | bytes 884744 | tf_op jit(solution)/shard_map/ppermute | solution.py:581
  129.5 0.9 copy-start.15
  134.4 19.5 %collective-permute-start.16 = (bf16[4,120,768]{2,1,0:T(8,128)(2,1)}, bf16[4,120,768]{2,1,0:T(8,128)(2,1)S(1)}, u32[]{:S(2)}, u32[]{:S(2)}) collective-permute-start(bf16[4,120,768]{2,1,0:T(8,128)(2,1)} %get-tuple-element.180), channel_id=1, source_target_pairs={{0,1},{1,0},{2,3},{3,2},{4,5},{5,4},{6,7},{7,6},{8,9},{9,8},{10,11... | collective-permute-start | bytes 2211848 | tf_op jit(solution)/shard_map/ppermute | solution.py:581
  135.5 18.3 %collective-permute-start.17 = (bf16[2,24,1536]{2,1,0:T(8,128)(2,1)}, bf16[2,24,1536]{2,1,0:T(8,128)(2,1)S(1)}, u32[]{:S(2)}, u32[]{:S(2)}) collective-permute-start(bf16[2,24,1536]{2,1,0:T(8,128)(2,1)} %get-tuple-element.181), channel_id=1, source_target_pairs={{0,2},{1,3},{2,0},{3,1},{4,6},{5,7},{6,4},{7,5},{8,10},{9,11},{10,... | collective-permute-start | bytes 442376 | tf_op jit(solution)/shard_map/ppermute | solution.py:581
  137.1 16.8 %collective-permute-start.18 = (bf16[2,24,1536]{2,1,0:T(8,128)(2,1)}, bf16[2,24,1536]{2,1,0:T(8,128)(2,1)S(1)}, u32[]{:S(2)}, u32[]{:S(2)}) collective-permute-start(bf16[2,24,1536]{2,1,0:T(8,128)(2,1)} %get-tuple-element.182), channel_id=1, source_target_pairs={{0,4},{1,5},{2,6},{3,7},{4,0},{5,1},{6,2},{7,3},{8,12},{9,13},{10,... | collective-permute-start | bytes 442376 | tf_op jit(solution)/shard_map/ppermute | solution.py:581
  139.7 14.2 %collective-permute-start.19 = (bf16[2,24,1536]{2,1,0:T(8,128)(2,1)}, bf16[2,24,1536]{2,1,0:T(8,128)(2,1)S(1)}, u32[]{:S(2)}, u32[]{:S(2)}) collective-permute-start(bf16[2,24,1536]{2,1,0:T(8,128)(2,1)} %get-tuple-element.183), channel_id=1, source_target_pairs={{0,6},{1,7},{2,4},{3,5},{4,2},{5,3},{6,0},{7,1},{8,14},{9,15},{10,... | collective-permute-start | bytes 442376 | tf_op jit(solution)/shard_map/ppermute | solution.py:581
  153.8 5.4 %copy-start.25 = (bf16[2,24,1536]{2,1,0:T(8,128)(2,1)}, bf16[2,24,1536]{2,1,0:T(8,128)(2,1)S(1)}, u32[]{:S(2)}) copy-start(bf16[2,24,1536]{2,1,0:T(8,128)(2,1)S(1)} %collective-permute-done.17.zb1) | copy-start | bytes 442372
  153.9 5.4 %copy-start.26 = (bf16[2,24,1536]{2,1,0:T(8,128)(2,1)}, bf16[2,24,1536]{2,1,0:T(8,128)(2,1)S(1)}, u32[]{:S(2)}) copy-start(bf16[2,24,1536]{2,1,0:T(8,128)(2,1)S(1)} %collective-permute-done.18.zb2) | copy-start | bytes 442372
  153.9 5.4 %copy-start.27 = (bf16[2,24,1536]{2,1,0:T(8,128)(2,1)}, bf16[2,24,1536]{2,1,0:T(8,128)(2,1)S(1)}, u32[]{:S(2)}) copy-start(bf16[2,24,1536]{2,1,0:T(8,128)(2,1)S(1)} %collective-permute-done.19.zb3) | copy-start | bytes 442372
  153.9 5.4 %copy-start.14 = (bf16[4,120,768]{2,1,0:T(8,128)(2,1)}, bf16[4,120,768]{2,1,0:T(8,128)(2,1)S(1)}, u32[]{:S(2)}) copy-start(bf16[4,120,768]{2,1,0:T(8,128)(2,1)S(1)} %collective-permute-done.16.got_a) | copy-start | bytes 2211844
  153.9 5.5 %copy-start.4 = (bf16[384,768]{1,0:T(8,128)(2,1)S(1)}, bf16[384,768]{1,0:T(8,128)(2,1)}, u32[]{:S(2)}) copy-start(bf16[384,768]{1,0:T(8,128)(2,1)} %copy-done.3) | copy-start | bytes 1769476
  153.9 5.5 %copy-start.6 = (bf16[384,768]{1,0:T(8,128)(2,1)S(1)}, bf16[384,768]{1,0:T(8,128)(2,1)}, u32[]{:S(2)}) copy-start(bf16[384,768]{1,0:T(8,128)(2,1)} %copy-done.5) | copy-start | bytes 1769476
  159.3 2.7 %collective-permute-start.20 = (bf16[576,768]{1,0:T(8,128)(2,1)}, bf16[576,768]{1,0:T(8,128)(2,1)S(1)}, u32[]{:S(2)}, u32[]{:S(2)}) collective-permute-start(bf16[576,768]{1,0:T(8,128)(2,1)} %get-tuple-element.186), channel_id=1, source_target_pairs={{0,8},{8,0},{16,24},{24,16},{1,9},{9,1},{17,25},{25,17},{2,10},{10... | collective-permute-start | bytes 2654216 | tf_op jit(solution)/shard_map/ppermute | solution.py:581
  162.0 1.0 copy-start.2
  167.4 18.3 %collective-permute-start.21 = (bf16[288,768]{1,0:T(8,128)(2,1)}, bf16[288,768]{1,0:T(8,128)(2,1)S(1)}, u32[]{:S(2)}, u32[]{:S(2)}) collective-permute-start(bf16[288,768]{1,0:T(8,128)(2,1)} %get-tuple-element.203), channel_id=1, source_target_pairs={{0,16},{8,24},{16,0},{24,8},{1,17},{9,25},{17,1},{25,9},{2,18},{10... | collective-permute-start | bytes 1327112 | tf_op jit(solution)/shard_map/ppermute | solution.py:581
  167.9 11.0 %collective-permute-start.22 = (bf16[120,768]{1,0:T(8,128)(2,1)}, bf16[120,768]{1,0:T(8,128)(2,1)S(1)}, u32[]{:S(2)}, u32[]{:S(2)}) collective-permute-start(bf16[120,768]{1,0:T(8,128)(2,1)} %get-tuple-element.204), channel_id=1, source_target_pairs={{0,2},{1,3},{2,0},{3,1},{4,6},{5,7},{6,4},{7,5},{8,10},{9,11},{10,... | collective-permute-start | bytes 552968 | tf_op jit(solution)/shard_map/ppermute | solution.py:581
  168.6 17.1 %collective-permute-start.23 = (bf16[120,768]{1,0:T(8,128)(2,1)}, bf16[120,768]{1,0:T(8,128)(2,1)S(1)}, u32[]{:S(2)}, u32[]{:S(2)}) collective-permute-start(bf16[120,768]{1,0:T(8,128)(2,1)} %get-tuple-element.205), channel_id=1, source_target_pairs={{0,4},{1,5},{2,6},{3,7},{4,0},{5,1},{6,2},{7,3},{8,12},{9,13},{10,... | collective-permute-start | bytes 552968 | tf_op jit(solution)/shard_map/ppermute | solution.py:581
  172.1 13.6 %collective-permute-start.24 = (bf16[120,768]{1,0:T(8,128)(2,1)}, bf16[120,768]{1,0:T(8,128)(2,1)S(1)}, u32[]{:S(2)}, u32[]{:S(2)}) collective-permute-start(bf16[120,768]{1,0:T(8,128)(2,1)} %get-tuple-element.206), channel_id=1, source_target_pairs={{0,6},{1,7},{2,4},{3,5},{4,2},{5,3},{6,0},{7,1},{8,14},{9,15},{10,... | collective-permute-start | bytes 552968 | tf_op jit(solution)/shard_map/ppermute | solution.py:581
  172.3 6.6 %collective-permute-start.25 = (bf16[24,1536]{1,0:T(8,128)(2,1)}, bf16[24,1536]{1,0:T(8,128)(2,1)S(1)}, u32[]{:S(2)}, u32[]{:S(2)}) collective-permute-start(bf16[24,1536]{1,0:T(8,128)(2,1)} %get-tuple-element.207), channel_id=1, source_target_pairs={{0,8},{8,0},{16,24},{24,16},{1,9},{9,1},{17,25},{25,17},{2,10},{10... | collective-permute-start | bytes 221192 | tf_op jit(solution)/shard_map/ppermute | solution.py:581
  178.9 7.8 %copy-start.31 = (bf16[24,1536]{1,0:T(8,128)(2,1)}, bf16[24,1536]{1,0:T(8,128)(2,1)S(1)}, u32[]{:S(2)}) copy-start(bf16[24,1536]{1,0:T(8,128)(2,1)S(1)} %collective-permute-done.25.swap_got) | copy-start | bytes 221188
  178.9 7.8 %copy-start.22 = (bf16[120,768]{1,0:T(8,128)(2,1)}, bf16[120,768]{1,0:T(8,128)(2,1)S(1)}, u32[]{:S(2)}) copy-start(bf16[120,768]{1,0:T(8,128)(2,1)S(1)} %collective-permute-done.22.za1) | copy-start | bytes 552964
  185.7 1.0 copy-start.23
  185.7 1.0 copy-start.24
  185.7 1.0 copy-start.17
  185.7 11.3 %collective-permute-start.26 = (bf16[16,24,640]{2,1,0:T(8,128)(2,1)}, bf16[16,24,640]{2,1,0:T(8,128)(2,1)S(1)}, u32[]{:S(2)}, u32[]{:S(2)}) collective-permute-start(bf16[16,24,640]{2,1,0:T(8,128)(2,1)} %get-tuple-element.219), channel_id=1, source_target_pairs={{0,1},{1,0},{2,3},{3,2},{4,5},{5,4},{6,7},{7,6},{8,9},{9,8},{10,11... | collective-permute-start | bytes 1474568 | tf_op jit(solution)/shard_map/ppermute | solution.py:581
  199.9 8.5 %collective-permute-start.27 = (bf16[4,24,640]{2,1,0:T(8,128)(2,1)}, bf16[4,24,640]{2,1,0:T(8,128)(2,1)S(1)}, u32[]{:S(2)}, u32[]{:S(2)}) collective-permute-start(bf16[4,24,640]{2,1,0:T(8,128)(2,1)} %get-tuple-element.222), channel_id=1, source_target_pairs={{0,2},{1,3},{2,0},{3,1},{4,6},{5,7},{6,4},{7,5},{8,10},{9,11},{10,... | collective-permute-start | bytes 368648 | tf_op jit(solution)/shard_map/ppermute | solution.py:581
  204.4 10.8 %collective-permute-start.28 = (bf16[4,24,640]{2,1,0:T(8,128)(2,1)}, bf16[4,24,640]{2,1,0:T(8,128)(2,1)S(1)}, u32[]{:S(2)}, u32[]{:S(2)}) collective-permute-start(bf16[4,24,640]{2,1,0:T(8,128)(2,1)} %get-tuple-element.223), channel_id=1, source_target_pairs={{0,4},{1,5},{2,6},{3,7},{4,0},{5,1},{6,2},{7,3},{8,12},{9,13},{10,... | collective-permute-start | bytes 368648 | tf_op jit(solution)/shard_map/ppermute | solution.py:581
  205.3 9.9 %collective-permute-start.29 = (bf16[4,24,640]{2,1,0:T(8,128)(2,1)}, bf16[4,24,640]{2,1,0:T(8,128)(2,1)S(1)}, u32[]{:S(2)}, u32[]{:S(2)}) collective-permute-start(bf16[4,24,640]{2,1,0:T(8,128)(2,1)} %get-tuple-element.224), channel_id=1, source_target_pairs={{0,6},{1,7},{2,4},{3,5},{4,2},{5,3},{6,0},{7,1},{8,14},{9,15},{10,... | collective-permute-start | bytes 368648 | tf_op jit(solution)/shard_map/ppermute | solution.py:581
  208.4 6.8 %copy-start.28 = (bf16[4,24,640]{2,1,0:T(8,128)(2,1)}, bf16[4,24,640]{2,1,0:T(8,128)(2,1)S(1)}, u32[]{:S(2)}) copy-start(bf16[4,24,640]{2,1,0:T(8,128)(2,1)S(1)} %collective-permute-done.27.z1) | copy-start | bytes 368644
  217.7 1.9 collective-permute-start.30
  217.7 4.2 %collective-permute-start.31 = (bf16[24,640]{1,0:T(8,128)(2,1)}, bf16[24,640]{1,0:T(8,128)(2,1)S(1)}, u32[]{:S(2)}, u32[]{:S(2)}) collective-permute-start(bf16[24,640]{1,0:T(8,128)(2,1)} %get-tuple-element.227), channel_id=1, source_target_pairs={{0,16},{8,24},{16,0},{24,8},{1,17},{9,25},{17,1},{25,9},{2,18},{10... | collective-permute-start | bytes 92168 | tf_op jit(solution)/shard_map/ppermute | solution.py:581
  219.2 3.5 %collective-permute-start.32 = (bf16[24,640]{1,0:T(8,128)(2,1)}, bf16[24,640]{1,0:T(8,128)(2,1)S(1)}, u32[]{:S(2)}, u32[]{:S(2)}) collective-permute-start(bf16[24,640]{1,0:T(8,128)(2,1)} %get-tuple-element.228), channel_id=1, source_target_pairs={{0,24},{8,16},{16,8},{24,0},{1,25},{9,17},{17,9},{25,1},{2,26},{10... | collective-permute-start | bytes 92168 | tf_op jit(solution)/shard_map/ppermute | solution.py:581
  219.6 3.2 %copy-start.32 = (bf16[24,640]{1,0:T(8,128)(2,1)}, bf16[24,640]{1,0:T(8,128)(2,1)S(1)}, u32[]{:S(2)}) copy-start(bf16[24,640]{1,0:T(8,128)(2,1)S(1)} %collective-permute-done.30.g1) | copy-start | bytes 92164
  221.9 0.9 copy-start.33
  (10 other events, 7.5 us)

commit v3 on v2

--- a/solution.py
+++ b/solution.py
@@ -70,7 +70,7 @@
     return pl.BlockSpec(memory_space=pltpu.SMEM)
 
 
-def call(kernel, outs, args, scratch=(), flops=0, scalars=0):
+def call(kernel, outs, args, scratch=(), flops=0, scalars=0, room=24):
     nbytes = sum(a.size * a.dtype.itemsize for a in args)
     nbytes += sum(o.size * o.dtype.itemsize for o in outs)
     return pl.pallas_call(
@@ -79,14 +79,27 @@
         in_specs=[smem()] * scalars + [vmem()] * (len(args) - scalars),
         out_specs=[vmem()] * len(outs),
         scratch_shapes=list(scratch),
+        compiler_params=pltpu.CompilerParams(vmem_limit_bytes=room << 20),
         cost_estimate=pl.CostEstimate(flops=flops, bytes_accessed=nbytes, transcendentals=0),
     )(*args)
 
 
-def attend_kernel(p0, p1, p2, p3, gain, shift, w, bias, qa, ka, va, lse, keep, send, normed, oacc):
+def attend_block(h, b, step, qa, ka, va, lse, oacc):
+    at = pl.ds(pl.multiple_of(b * step, step), step)
+    sc = dot_t(qa[h, at, :], ka[h])
+    top = jnp.max(sc, axis=-1, keepdims=True)
+    e = jnp.exp(sc - top).astype(BF16)
+    o = dot(e, va[h])
+    tot = o[:, HEAD : HEAD + 1]
+    oacc[h, at, :] = o * (1.0 / tot)
+    col = jnp.broadcast_to(top + jnp.log(tot), (step, LANES))
+    lse[h, b] = col.T[:8]
+
+
+def attend_first_kernel(p0, p1, p2, p3, gain, shift, w, bias, qa, ka, va, lse, part, send, normed, oacc):
     rows = p0.shape[0]
     width = gain.shape[1]
-    whole = 4 * rows
+    step = 4 * rows // 3
     lane = lane_of(rows)
     for i, p in enumerate((p0, p1, p2, p3)):
         at = pl.ds(i * rows, rows)
@@ -102,26 +115,33 @@
             qa[h, at, :] = jnp.where(lane < HEAD, q, hot).astype(BF16)
             ka[h, at, :] = jnp.where(lane < HEAD, unpack_head(qkv, 3 * h + 1), far).astype(BF16)
             va[h, at, :] = jnp.where(lane < HEAD, unpack_head(qkv, 3 * h + 2), one).astype(BF16)
-    step = whole // 3
 
     def block(i, carry):
-        h, b = i // 3, i % 3
-        at = pl.ds(pl.multiple_of(b * step, step), step)
-        sc = dot_t(qa[h, at, :], ka[h])
-        top = jnp.max(sc, axis=-1, keepdims=True)
-        e = jnp.exp(sc - top).astype(BF16)
-        o = dot(e, va[h])
-        tot = o[:, HEAD : HEAD + 1]
-        oacc[h, at, :] = o * (1.0 / tot)
-        col = jnp.broadcast_to(top + jnp.log(tot), (step, LANES))
-        lse[h, b] = col.T[:8]
+        attend_block(i // 2, 1 + i % 2, step, qa, ka, va, lse, oacc)
         return carry
 
-    lax.fori_loop(0, 3 * OWN, block, 0)
-    for out, start in ((keep, 0), (send, 2 * rows)):
-        at = pl.ds(start, 2 * rows)
-        out[:, :LANES] = pack_pair(oacc[0, at, :], oacc[1, at, :]).astype(BF16)
-        out[:, LANES:] = oacc[2, at, :HEAD].astype(BF16)
+    lax.fori_loop(0, 2 * OWN, block, 0)
+    gather_heads(oacc, step, 2 * rows - step, part, 0)
+    gather_heads(oacc, 2 * rows, 2 * rows, send, 0)
+
+
+def gather_heads(oacc, start, size, out, to):
+    at, dst = pl.ds(start, size), pl.ds(to, size)
+    out[dst, :LANES] = pack_pair(oacc[0, at, :], oacc[1, at, :]).astype(BF16)
+    out[dst, LANES:] = oacc[2, at, :HEAD].astype(BF16)
+
+
+def attend_second_kernel(qa, ka, va, lse_in, part, keep, lse, oacc):
+    step = oacc.shape[1]
+    lse[...] = lse_in[...]
+
+    def block(h, carry):
+        attend_block(h, 0, step, qa, ka, va, lse, oacc)
+        return carry
+
+    lax.fori_loop(0, OWN, block, 0)
+    gather_heads(oacc, 0, step, keep, 0)
+    keep[pl.ds(step, part.shape[0]), :] = part[...]
 
 
 def keep_column(p0, p1, table, width):
@@ -152,59 +172,64 @@
     gb2[...] = (keep_m * gout).astype(BF16)
 
 
-def feed_kernel(last, sref, bref, normed2, gb2, fc1, bias, fc2, *refs):
+def feed_kernel(last, fast, sref, bref, normed2, gb2, fc1, bias, fc2, *refs):
     if last:
-        b2_in, gn_in, g2, g1_send, g1_keep, gb, b2_keep, b2_send, gn_keep, gn_send, wide, b2, gn = refs
+        b2_in, gn_in, y_in, g2, y_send, g1_keep, gb, b2_keep, b2_send, gn_keep, gn_send, wide = refs
     else:
-        g2a, g2b, g1_send, g1_keep, gb, b2, gn, wide = refs
-    i = pl.program_id(0)
-    half = b2.shape[0] // 2
+        g2a, g2b, y_first, y_second, g1_keep, gb, b2, gn, wide = refs
+    tokens = normed2.shape[0]
+    half = tokens // 2
     pre = dot(normed2[...], fc1[...]) + bias[...]
     gact = dot_t(gb2[...], fc2[...])
     act, slope = gelu_pair(pre)
     act = act.astype(BF16)
     gh = (gact * slope).astype(BF16)
-    grad2 = dot_lt(act, gb2[...]).astype(BF16)
+    grad1 = dot_lt(normed2[...], gh)
+    if not fast:
+        rows = grad1.shape[0] // 2
+        if last:
+            y_send[...] = grad1[:rows].astype(BF16)
+            g1_keep[...] = grad1[rows:].astype(BF16)
+        else:
+            y_first[...] = grad1[:rows].astype(BF16)
+            g1_keep[...] = grad1[rows:].astype(BF16)
+    else:
+        x, y = sref[0] >> 1, bref[0] & 1
+        wide[...] = grad1
+        n, rows = g1_keep.shape[:2]
+        n = n // 2
+        for m in range(2 * n):
+            base = 2 * rows * (((1 - x) if m < n else x) * n + m % n)
+            piece = wide[pl.ds(pl.multiple_of(base + (1 - y) * rows, 8), rows), :].astype(BF16)
+            if last:
+                y_send[n + m] = piece
+            elif m < n:
+                y_first[m] = piece
+            else:
+                y_second[m - n] = piece
+            g1_keep[m] = wide[pl.ds(pl.multiple_of(base + y * rows, 8), rows), :].astype(BF16)
+        if last:
+            for m in range(n):
+                y_send[m] = y_in[m]
+    gb[...] = jnp.sum(gh.astype(F32), axis=0, keepdims=True)
+    partn = dot_t(gh, fc1[...])
+    part2 = dot(act, fc2[...])
     if last:
-        g2[...] = grad2
+        partn = partn + gn_in[...]
+        part2 = part2 + b2_in[...]
+        b2_keep[...] = part2[:half]
+        b2_send[...] = part2[half:].astype(BF16)
+        gn_keep[...] = partn
+        gn_send[:half] = partn[half:].astype(BF16)
+        gn_send[half:] = partn[:half].astype(BF16)
+        g2[...] = dot_lt(act, gb2[...]).astype(BF16)
     else:
-
-        @pl.when(i == 0)
-        def _():
-            g2a[...] = grad2
-
-        @pl.when(i == 1)
-        def _():
-            g2b[...] = grad2
-
-    split_rows(dot_lt(normed2[...], gh), wide, bref[0] & 1, g1_send, g1_keep)
-    gb[...] = jnp.sum(gh.astype(F32), axis=0, keepdims=True)
-    part2 = dot(act, fc2[...])
-    partn = dot_t(gh, fc1[...])
-
-    @pl.when(i == 0)
-    def _():
-        if last:
-            b2[...] = b2_in[...] + part2
-            gn[...] = gn_in[...] + partn
-        else:
-            b2[...] = part2
-            gn[...] = partn
-
-    @pl.when(i > 0)
-    def _():
-        b2[...] += part2
-        gn[...] += partn
-
-    if last:
-
-        @pl.when(i == pl.num_programs(0) - 1)
-        def _():
-            b2_keep[...] = b2[:half]
-            b2_send[...] = b2[half:].astype(BF16)
-            gn_keep[...] = gn[...]
-            gn_send[:half] = gn[half:].astype(BF16)
-            gn_send[half:] = gn[:half].astype(BF16)
+        b2[...] = part2
+        gn[...] = partn
+        grad2 = dot_lt(act, gb2[...]).astype(BF16)
+        rows = g2a.shape[0]
+        g2a[...] = grad2[:rows]
+        g2b[...] = grad2[rows:]
 
 
 def split_rows(value, wide, bit, send, keep):
@@ -221,64 +246,34 @@
         keep[m] = wide[pl.ds(pl.multiple_of(base + bit * rows, 8), rows), :].astype(BF16)
 
 
-def feed(last, pick, per, sidx, bidx, normed2, gb2, w_fc1, bias, w_fc2, prev=()):
+def feed(last, fast, per, sidx, bidx, normed2, gb2, fc1, bias, fc2, prev=()):
     tokens, width = normed2.shape
-    hidden = w_fc1.shape[1] // 4
-    chunk = hidden // 2
-    steps = 2
-    const = lambda i, s, b: (0, 0)
-    full = pl.BlockSpec((tokens, width), const)
-    half = pl.BlockSpec((tokens // 2, width), const)
-    in_specs = [
-        full,
-        full,
-        pl.BlockSpec((width, chunk), lambda i, s, b: (0, (s[0] ^ pick) * steps + i)),
-        pl.BlockSpec((1, chunk), lambda i, s, b: (0, (s[0] ^ pick) * steps + i)),
-        pl.BlockSpec((chunk, width), lambda i, s, b: ((s[0] ^ pick) * steps + i, 0)),
-    ] + [full] * len(prev)
+    hidden = fc1.shape[1]
+    pairs = width // (2 * per)
     if last:
-        out_specs = [pl.BlockSpec((chunk, width), lambda i, s, b: (i, 0))]
         outs = [SDS((hidden, width), BF16)]
+        send = [SDS((3 * pairs // 2, per, hidden), BF16)]
     else:
-        out_specs = [pl.BlockSpec((chunk, width), const)] * 2
-        outs = [SDS((chunk, width), BF16)] * 2
-    if per % 8 == 0:
-        pairs = width // (2 * per)
-        out_specs += [pl.BlockSpec((pairs, per, chunk), lambda i, s, b: (0, 0, i))] * 2
-        outs += [SDS((pairs, per, hidden), BF16)] * 2
-    else:
-        out_specs += [pl.BlockSpec((width // 2, chunk), lambda i, s, b: (0, i))] * 2
-        outs += [SDS((width // 2, hidden), BF16)] * 2
-    out_specs += [pl.BlockSpec((1, chunk), lambda i, s, b: (0, i))]
-    outs += [SDS((1, hidden), F32)]
-    scratch = [pltpu.VMEM((width, chunk), F32)]
+        outs = [SDS((hidden // 4, width), BF16), SDS((3 * hidden // 4, width), BF16)]
+        send = [SDS((pairs // 2, per, hidden), BF16)] * 2
+    keep = SDS((pairs, per, hidden), BF16)
+    if not fast:
+        keep = SDS((width // 2, hidden), BF16)
+        send = [keep] if last else [keep, SDS((8, LANES), BF16)]
+    outs += send + [keep, SDS((1, hidden), F32)]
     if last:
-        out_specs += [half, half, full, full]
         outs += [SDS((tokens // 2, width), F32), SDS((tokens // 2, width), BF16)]
         outs += [SDS((tokens, width), F32), SDS((tokens, width), BF16)]
-        scratch += [pltpu.VMEM((tokens, width), F32)] * 2
     else:
-        out_specs += [full, full]
         outs += [SDS((tokens, width), F32)] * 2
-    out = pl.pallas_call(
-        functools.partial(feed_kernel, last),
-        grid_spec=pltpu.PrefetchScalarGridSpec(
-            num_scalar_prefetch=2,
-            grid=(steps,),
-            in_specs=in_specs,
-            out_specs=out_specs,
-            scratch_shapes=scratch,
-        ),
-        out_shape=outs,
-        cost_estimate=pl.CostEstimate(
-            flops=12 * tokens * width * hidden, bytes_accessed=10 * width * hidden, transcendentals=0
-        ),
-    )(sidx, bidx, normed2, gb2, w_fc1, bias, w_fc2, *prev)
-    at = 1 if last else 2
-    out = list(out)
-    if per % 8:
-        out[at : at + 2] = by_batch_bit(jnp.concatenate(out[at : at + 2], axis=0), per)
-    return out
+    return call(
+        functools.partial(feed_kernel, last, fast),
+        outs,
+        (sidx, bidx, normed2, gb2, fc1, bias, fc2) + tuple(prev),
+        [pltpu.VMEM((width, hidden), F32)],
+        flops=12 * tokens * width * hidden,
+        scalars=2,
+    )
 
 
 def by_batch_bit(arr, per):
@@ -287,47 +282,52 @@
     return [pick(arr, 1 - own, 1), pick(arr, own, 1)]
 
 
-def branch_back_kernel(
-    sref, gn_keep, gn_got, middle, p0, p1, c0, c1, table, w_out, gain, shift, a0, a2, gb2,
-    b2_keep, b2_got, bias, gain1, shift1, fb_own, fb_oth,
-    gmid_own, gatt, gatt_send, go_keep, go_send, early, opat, ospe, fcol,
+def middle_back_kernel(
+    sref, gn_keep, gn_got, middle, p0, p1, c0, c1, table, w_out, gain, gb2, gmid_own, gbr_out, gatt_send, sums
 ):
     s = sref[0]
     rows, width = c0.shape
-    cols = a0.shape[1]
-    mid = middle[...]
-    hat, scale = normalize(mid)
+    cols = gatt_send.shape[1]
+    hat, scale = normalize(middle[...])
     g = gn_keep[...] + gn_got[...].astype(F32)
     gout = jnp.concatenate([c0[...], c1[...]], axis=0).astype(F32)
     gmid = gout + normalize_back(g * gain[...], hat, scale)
-    gmid_own[...] = gmid[:rows]
     keep_a = keep_column(p0, p1, table[0:1, :], width)
     gbr = (keep_a * gmid).astype(BF16)
-    w_own = w_out[pl.ds(pl.multiple_of(s * cols, HEAD), cols), :]
+    gbr_out[...] = gbr
     w_oth = w_out[pl.ds(pl.multiple_of((s ^ 2) * cols, HEAD), cols), :]
     gatt_send[...] = dot_t(gbr, w_oth).astype(BF16)
-    gatt[...] = dot_t(gbr, w_own).astype(BF16)
-    go_send[...] = dot_lt(a2[...], gbr).astype(BF16)
-    go_keep[...] = dot_lt(a0[...], gbr).astype(BF16)
-
-    hot = p0[:, width:].astype(F32)
-    keep_m = jnp.sum(hot * table[1:2, :], axis=-1, keepdims=True)
-    res = (mid[:rows] + keep_m * (b2_keep[...] + b2_got[...].astype(F32) + bias[...])).astype(BF16)
-    opat[...] = res[: opat.shape[0]]
-    ospe[...] = res[opat.shape[0] : opat.shape[0] + ospe.shape[0]]
-
+    gmid_own[...] = gmid[:rows]
     own = slice(0, rows)
-    blank = functools.partial(jnp.zeros, dtype=F32)
     lines = [
-        gain1[...],
-        shift1[...],
-        blank((HEAD + 2, width)),
         jnp.sum(g[own] * hat[own], axis=0, keepdims=True),
         jnp.sum(g[own], axis=0, keepdims=True),
         jnp.sum(gb2[own, :].astype(F32), axis=0, keepdims=True),
         jnp.sum(gbr[own].astype(F32), axis=0, keepdims=True),
-        blank((LANES - HEAD - 8, width)),
+        jnp.zeros((4, width), F32),
     ]
+    sums[...] = jnp.concatenate(lines, axis=0)
+
+
+def branch_back_kernel(
+    sref, bref, gbr, w_out, a0, a2, middle, p0, table, b2_keep, b2_got, bias, gain1, shift1, sums, fb_own, fb_oth,
+    gatt, go_send, go_keep, early, opat, ospe, fcol, wide,
+):
+    s = sref[0]
+    cols = a0.shape[1]
+    rows, width = b2_keep.shape
+    w_own = w_out[pl.ds(pl.multiple_of(s * cols, HEAD), cols), :]
+    gatt[...] = dot_t(gbr[...], w_own).astype(BF16)
+    for j, a in enumerate((a0, a2)):
+        split_rows(dot_lt(a[...], gbr[...]), wide, bref[0] & 1, go_send.at[j], go_keep.at[j])
+    hot = p0[:, width:].astype(F32)
+    keep_m = jnp.sum(hot * table[1:2, :], axis=-1, keepdims=True)
+    res = middle[:rows, :] + keep_m * (b2_keep[...] + b2_got[...].astype(F32) + bias[...])
+    res = res.astype(BF16)
+    opat[...] = res[: opat.shape[0]]
+    ospe[...] = res[opat.shape[0] : opat.shape[0] + ospe.shape[0]]
+    blank = functools.partial(jnp.zeros, dtype=F32)
+    lines = [gain1[...], shift1[...], blank((HEAD + 2, width)), sums[:4, :], blank((LANES - HEAD - 8, width))]
     early[...] = jnp.concatenate(lines, axis=0).T
     lane = lane_of(cols)
     for j, ref in ((0, fb_own), (2, fb_oth)):
@@ -444,83 +444,73 @@
     return sum(p.astype(F32) for p in parts[1:]) + parts[0].astype(F32)
 
 
-def stage1_kernel(sref, keep_own, got_own, keep_oth, got_oth, send):
-    x = sref[0] >> 1
-    n, _, width = send.shape
-    width = width // 2
+def stage1_kernel(
+    bref, keep_own, keep_oth, y1, y2, fc2, got2a, got2b, out, y3, msg_x, msg_a, part_b, part_o, part_a
+):
+    y = bref[0] & 1
+    n = keep_own.shape[0] // 2
     for i in range(n):
-        m = (1 - x) * n + i
-        send[i, :, :width] = wide_sum(keep_own[m], got_own[m]).astype(BF16)
-        send[i, :, width:] = wide_sum(keep_oth[m], got_oth[m]).astype(BF16)
-
-
-def stage2_kernel(
-    sref, bref, keep_own, got_own, keep_oth, got_oth, got_b, fc2, got2a, got2b, out, got_o,
-    send_a, zb1, zb2, zb3, keep_b,
-):
-    x, y, q = sref[0] >> 1, bref[0] & 1, bref[0] >> 1
-    n = got_b.shape[0] // 4
-    width = keep_own.shape[2]
-    deep = fc2.shape[1]
-    for c in range(2):
-        for k, ref in enumerate((keep_b, zb1, zb2, zb3)):
-            i = c * 4 + (q ^ k)
-            m = x * 8 + i
-            ref[c, :, :width] = wide_sum(keep_own[m], got_own[m], got_b[i, :, width:]).astype(ref.dtype)
-            ref[c, :, width:] = wide_sum(keep_oth[m], got_oth[m], got_b[i, :, :width]).astype(ref.dtype)
+        msg_x[2 * i] = wide_sum(keep_own[i], y2[n + i]).astype(BF16)
+        msg_x[2 * i + 1] = wide_sum(keep_oth[i], y1[i]).astype(BF16)
+        part_b[2 * i] = wide_sum(keep_own[n + i], y2[2 * n + i])
+        part_b[2 * i + 1] = wide_sum(keep_oth[n + i], y2[i])
     for j in range(4):
-        b = 2 * j + 1 - y
-        got = got2a if j < 2 else got2b
-        send_a[j, :deep] = wide_sum(fc2[b], got[b - 4 * (j // 2)]).astype(BF16)
-        send_a[j, deep:] = wide_sum(out[b], got_o[b]).astype(BF16)
-
-
-def stage3_kernel(
-    sref, bref, fc2, got2, out, got_o, got_a, keep_b, zb1, zb2, zb3, gn_keep, gn_got,
-    za1, za2, za3, keep_a, swap_send, swap_keep, xsend,
-):
-    c, y, q = sref[0] & 1, bref[0] & 1, bref[0] >> 1
-    deep = fc2.shape[1]
-    for k, ref in enumerate((keep_a, za1, za2, za3)):
+        msg_x[2 * n + j] = wide_sum(out[1, j], y3[1, j]).astype(BF16)
+        part_o[j] = wide_sum(out[0, j], y3[0, j])
+        for bit, ref in ((1 - y, msg_a), (y, part_a)):
+            got = got2a[bit] if j == 0 else got2b[2 * j - 2 + bit]
+            ref[j] = wide_sum(fc2[2 * j + bit], got).astype(ref.dtype)
+
+
+def stage2_kernel(bref, part_b, part_o, part_a, got_x, got_a, z1, z2, z3, kept):
+    q = bref[0] >> 1
+    per = part_o.shape[1]
+    n = part_b.shape[0]
+    deep = part_a.shape[1]
+    for k, ref in enumerate((kept, z1, z2, z3)):
         j = q ^ k
-        b = 2 * j + y
-        ref[:deep] = wide_sum(fc2[b], got2[b], got_a[j, :deep]).astype(ref.dtype)
-        ref[deep:] = wide_sum(out[b], got_o[b], got_a[j, deep:]).astype(ref.dtype)
-    swap_send[...] = wide_sum(keep_b[1 - c], zb1[1 - c], zb2[1 - c], zb3[1 - c]).astype(BF16)
-    swap_keep[...] = wide_sum(keep_b[c], zb1[c], zb2[c], zb3[c])
-    rows = xsend.shape[0]
-    xsend[...] = wide_sum(gn_keep[rows:], gn_got[rows:]).astype(BF16)
-
-
-def final_kernel(
-    sref, k0, c0, x0, p0, gmid, gain, keep_a, za1, za2, za3, swap_keep, swap_got,
-    gpat, gspe, fc2, out, fc1,
-):
+        for c in range(2):
+            i = 2 * (c * 4 + j)
+            for half in range(2):
+                at = pl.ds((2 * c + half) * per, per)
+                ref[at, :] = wide_sum(part_b[i + half], got_x[i + 1 - half]).astype(ref.dtype)
+        ref[pl.ds(4 * per, deep), :] = wide_sum(part_a[j], got_a[j]).astype(ref.dtype)
+        ref[pl.ds(4 * per + deep, per), :] = wide_sum(part_o[j], got_x[n + j]).astype(ref.dtype)
+
+
+def shift_kernel(keep, got, send):
+    rows = send.shape[0]
+    send[...] = wide_sum(keep[rows:, :], got[rows:, :]).astype(BF16)
+
+
+def quarter_kernel(bref, keep, got, z1, z2, z3, kept):
+    q = bref[0] >> 1
+    for r in range(4):
+        for k, ref in enumerate((kept, z1, z2, z3)):
+            m = r * 4 + (q ^ k)
+            ref[r] = wide_sum(keep[m], got[m]).astype(ref.dtype)
+
+
+def sums_kernel(sref, kept, z1, z2, z3, swap_send, swap_keep, fc2, out):
+    c = sref[0] & 1
+    rows = swap_send.shape[0]
+    deep = fc2.shape[0]
+    for pos, ref in ((1 - c, swap_send), (c, swap_keep)):
+        at = pl.ds(pl.multiple_of(pos * rows, 8), rows)
+        ref[...] = wide_sum(kept[at, :], z1[at, :], z2[at, :], z3[at, :]).astype(ref.dtype)
+    for lo, ref in ((2 * rows, fc2), (2 * rows + deep, out)):
+        at = pl.ds(lo, ref.shape[0])
+        ref[...] = wide_sum(kept[at, :], z1[at, :], z2[at, :], z3[at, :])
+
+
+def owner_kernel(sref, kept, z1, z2, z3, s1, s2, s3, own):
     s = sref[0]
-    rows, width = x0.shape
-    count = gpat.shape[0]
-    extra = gspe.shape[0]
-    hat, scale = normalize(p0[:, :width].astype(F32))
-    g = wide_sum(k0[:rows], c0[:rows], x0[...])
-    res = gmid[...] + normalize_back(g * gain[...], hat, scale)
-    gpat[...] = res[:count]
-    gspe[...] = res[count : count + extra]
-    sums = wide_sum(keep_a[...], za1[...], za2[...], za3[...])
-    deep = fc2.shape[0]
-    fc2[...] = sums[:deep]
-    out[...] = sums[deep:]
-    hidden = swap_keep.shape[1] // 2
-
-    def place(j, value):
-        fc1[:, pl.ds(pl.multiple_of((s ^ j) * hidden, LANES), hidden)] = value
-
-    place(0, swap_keep[:, :hidden])
-    place(2, swap_keep[:, hidden:])
-    place(1, swap_got[:, :hidden].astype(F32))
-    place(3, swap_got[:, hidden:].astype(F32))
-
-
-def norm_only_kernel(k0, c0, x0, p0, gmid, gain, gpat, gspe):
+    for k, ref in enumerate((own, s1, s2, s3)):
+        m = s ^ k
+        ref[...] = wide_sum(kept[m], z1[m], z2[m], z3[m]).astype(ref.dtype)
+
+
+def final_kernel(k0, c0, x0, p0, gmid, gain, gpat, gspe):
     rows, width = x0.shape
     count = gpat.shape[0]
     hat, scale = normalize(p0[:, :width].astype(F32))
@@ -530,23 +520,11 @@
     gspe[...] = res[count : count + gspe.shape[0]]
 
 
-def quarter_kernel(bref, keep, got, z1, z2, z3, kept):
-    q = bref[0] >> 1
-    for r in range(4):
-        for k, ref in enumerate((kept, z1, z2, z3)):
-            m = r * 4 + (q ^ k)
-            ref[r] = wide_sum(keep[m], got[m]).astype(ref.dtype)
-
-
-def owner_kernel(sref, kept, z1, z2, z3, s1, s2, s3, own):
+def collect_kernel(sref, own, g1, g2, g3, swap_keep, swap_got, out, vec, fc1, every):
     s = sref[0]
-    for k, ref in enumerate((own, s1, s2, s3)):
-        m = s ^ k
-        ref[...] = wide_sum(kept[m], z1[m], z2[m], z3[m]).astype(ref.dtype)
-
-
-def collect_kernel(sref, own, g1, g2, g3, out, vec, every):
-    s = sref[0]
+    per, hidden = swap_keep.shape[0] // 2, swap_keep.shape[1]
+    for j, value in ((0, swap_keep[:per]), (2, swap_keep[per:]), (1, swap_got[:per]), (3, swap_got[per:])):
+        fc1[:, pl.ds(pl.multiple_of((s ^ j) * hidden, LANES), hidden)] = value.astype(F32)
     for k, ref in enumerate((own, g1, g2, g3)):
         every[k] = ref[...].astype(F32)
     pieces = [every[s ^ a] for a in range(4)]
@@ -682,23 +660,35 @@
     sides = {0: biases[0], 1: jnp.zeros((width,), F32), 2: biases[1]}
     bias_own = [lax.dynamic_slice(sides[j], (s * cols + h * HEAD,), (HEAD,)) for h, j in order]
     bias_own = jnp.concatenate(bias_own + [jnp.zeros((HEAD,), F32)])[None]
-    pay_x, w_own, bias_own, table = lax.optimization_barrier((pay_x, w_own, bias_own, table))
+    w1 = [lax.dynamic_slice(w_fc1, (0, (s ^ j) * hidden), (width, hidden)) for j in (2, 0)]
+    w2 = [lax.dynamic_slice(w_fc2, ((s ^ j) * hidden, 0), (hidden, width)) for j in (2, 0)]
+    fb = [lax.dynamic_slice(fc1_bias, ((s ^ j) * hidden,), (hidden,))[None] for j in (2, 0)]
+    pay_x, w_own, bias_own, table, w1, w2, fb = lax.optimization_barrier(
+        (pay_x, w_own, bias_own, table, w1, w2, fb)
+    )
     pay_d = swap_seq(pay_x, 1)
     gain1, gain2 = norm_gains[0:1], norm_gains[1:2]
     shift1, shift2 = norm_shifts[0:1], norm_shifts[1:2]
-    fb = fc1_bias.reshape(1, -1)
 
     headed = SDS((OWN, whole, LANES), BF16)
-    qa, ka, va, lse, a0, att_send, normed = call(
-        attend_kernel,
+    tops = SDS((OWN, 3, 8, whole // 3), F32)
+    step = whole // 3
+    qa, ka, va, lse, part, att_send, normed = call(
+        attend_first_kernel,
         [headed] * 3
-        + [SDS((OWN, 3, 8, whole // 3), F32), SDS((chip, cols), BF16), SDS((chip, cols), BF16)]
-        + [SDS((whole, width), BF16)],
+        + [tops, SDS((chip - step, cols), BF16), SDS((chip, cols), BF16), SDS((whole, width), BF16)],
         (pay, pay_c, pay_x, pay_d, gain1, shift1, w_own, bias_own),
         [pltpu.VMEM((OWN, whole, LANES), F32)],
-        flops=2 * whole * width * 3 * cols + 4 * OWN * whole * whole * LANES,
+        flops=2 * whole * width * 3 * cols + 3 * OWN * whole * whole * LANES,
     )
     a2 = swap_seq(att_send, 2)
+    a0, lse = call(
+        attend_second_kernel,
+        [SDS((chip, cols), BF16), tops],
+        (qa, ka, va, lse, part),
+        [pltpu.VMEM((OWN, step, LANES), F32)],
+        flops=OWN * whole * whole * LANES,
+    )
     a1 = swap_seq(a0, 1)
     a3 = swap_seq(a2, 1)
 
@@ -710,36 +700,58 @@
         scalars=1,
     )
     per = width // (4 * nb)
-    fc2_a, fc2_b, oth_y, keep_oth, fb_oth, b2, gn = feed(
-        False, 2, per, sidx, bidx, normed2, gb2, w_fc1, fb, w_fc2
+    fast = nb == 8
+    fc2_a, fc2_b, y1, y_rest, keep_oth, fb_oth, b2, gn = feed(
+        False, fast, per, sidx, bidx, normed2, gb2, w1[0], fb[0], w2[0]
     )
     got2a = swap_seq(fc2_a, 2)
-    got_oth = swap("batch", oth_y, 1)
-    fc2_keep, own_y, keep_own, fb_own, b2_keep, b2_send, gn_keep, gn_send = feed(
-        True, 0, per, sidx, bidx, normed2, gb2, w_fc1, fb, w_fc2, (b2, gn)
-    )
-    gn_send, b2_send, fc2_b, own_y, got2a, got_oth = lax.optimization_barrier(
-        (gn_send, b2_send, fc2_b, own_y, got2a, got_oth)
-    )
+    if fast:
+        got_y1 = swap("batch", y1, 1)
+        ahead = (got2a, got_y1)
+    else:
+        y1, keep_oth = by_batch_bit(jnp.concatenate([y1, keep_oth], axis=0), per)
+        got_y1 = swap("batch", y1, 1)
+        ahead = (got2a, got_y1)
+    fc2_keep, y2, keep_own, fb_own, b2_keep, b2_send, gn_keep, gn_send = feed(
+        True, fast, per, sidx, bidx, normed2, gb2, w1[1], fb[1], w2[1], (b2, gn, y_rest)
+    )
+    if not fast:
+        y2, keep_own = by_batch_bit(jnp.concatenate([y2, keep_own], axis=0), per)
+    gn_send, b2_send, fc2_b, y2, (got2a, got_y1) = lax.optimization_barrier((gn_send, b2_send, fc2_b, y2, ahead))
     gn_got = swap_seq(gn_send, 1)
     b2_got = swap_seq(b2_send, 1)
     got2b = swap_seq(fc2_b, 2)
-    got_own = swap("batch", own_y, 1)
-
-    gmid, gatt, gatt_send, go_keep, go_send, early, opat, ospe = call(
+    got_y2 = swap("batch", y2, 1)
+
+    gmid, gbr, gatt_send, line_sums = call(
+        middle_back_kernel,
+        [SDS((block, width), F32), SDS((chip, width), BF16), SDS((chip, cols), BF16), SDS((8, width), F32)],
+        (sidx, gn_keep, gn_got, middle, pay, pay_c, cot, cot_c, table, w_out, gain2, gb2),
+        flops=2 * chip * width * cols,
+        scalars=1,
+    )
+    gatt_x = swap_seq(gatt_send, 2)
+    if fast:
+        split = SDS((2, cols // (2 * per), per, width), BF16)
+    else:
+        split = SDS((2, cols // 2, width), BF16)
+    gatt, go_send, go_keep, early, opat, ospe = call(
         branch_back_kernel,
-        [SDS((block, width), F32), SDS((chip, cols), BF16), SDS((chip, cols), BF16)]
-        + [SDS((cols, width), BF16), SDS((cols, width), BF16), SDS((width, LANES), F32)]
+        [SDS((chip, cols), BF16), split, split, SDS((width, LANES), F32)]
         + [SDS((count, width), BF16), SDS((extra, width), BF16)],
-        (sidx, gn_keep, gn_got, middle, pay, pay_c, cot, cot_c, table, w_out, gain2, shift2, a0, a2, gb2)
-        + (b2_keep, b2_got, biases[3:4], gain1, shift1, fb_own, fb_oth),
-        [pltpu.VMEM((hidden, LANES), F32)],
-        flops=8 * chip * width * cols,
-        scalars=1,
-    )
-    gatt_x = swap_seq(gatt_send, 2)
-    got_own = after(got_own, gatt_send)
-    pairs = (keep_own, got_own, keep_oth, got_oth)
+        (sidx, bidx, gbr, w_out, a0, a2, middle, pay, table, b2_keep, b2_got, biases[3:4], gain1, shift1)
+        + (line_sums, fb_own, fb_oth),
+        [pltpu.VMEM((hidden, LANES), F32), pltpu.VMEM((cols, width), F32)],
+        flops=6 * chip * width * cols,
+        scalars=2,
+    )
+    if not fast:
+        halves = [by_batch_bit(jnp.concatenate([go_send[j], go_keep[j]], axis=0), per) for j in range(2)]
+        go_send, go_keep = [jnp.stack([halves[j][k] for j in range(2)]) for k in range(2)]
+    got_o = swap("batch", go_send, 1)
+    got_y2, got2b = after((got_y2, got2b), gatt_send)
+    gatt_x = after(gatt_x, go_send)
+    pairs = (keep_own, keep_oth, got_y1, got_y2)
 
     def head_grads(first, heads, lse):
         return attend_back(first, heads, qa, ka, va, lse, gatt, gatt_x)
@@ -754,7 +766,7 @@
 
     def qkv_part(g0, s0, g12, s12, early):
         wide = 5 * LANES
-        if per % 8 == 0:
+        if fast:
             outs = [SDS((width // (2 * per), per, wide), BF16)] * 2
         else:
             outs = [SDS((width // 2, wide), BF16)] * 2
@@ -766,12 +778,12 @@
             flops=2 * whole * width * wide,
             scalars=2,
         )
-        return out if per % 8 == 0 else by_batch_bit(jnp.concatenate(out, axis=0), per)
+        return out if fast else by_batch_bit(jnp.concatenate(out, axis=0), per)
 
     rest = (sidx, bidx, per, block, chip, hidden, cols, count, extra, width)
-    reduce_all = reduce_eight if nb == 8 else reduce_any
+    reduce_all = reduce_eight if fast else reduce_any
     out_fc2, out_out, out_fc1, out_qkv, vec, gpat, gspe = reduce_all(
-        rest, pairs, (fc2_keep, got2a, got2b), (go_keep, go_send), lse, gatt_x, early,
+        rest, pairs, (fc2_keep, got2a, got2b), (go_keep, got_o), lse, gatt_x, early,
         head_grads, norm_part, qkv_part, pay, gmid, gain1,
     )
     grad_gains = jnp.stack([vec[:, 0], vec[:, 4]])
@@ -798,74 +810,71 @@
 ):
     sidx, bidx, per, block, chip, hidden, cols, count, extra, width = rest
     fc2_keep, got2a, got2b = twos
-    go_keep, go_send = outs
+    go_keep, got_o = outs
     wide = 5 * LANES
     deep = hidden // 8
-    (send_b,) = call(stage1_kernel, [SDS((8, per, 2 * hidden), BF16)], (sidx,) + pairs, scalars=1)
-    go_send, send_b, lse, got2b = lax.optimization_barrier((go_send, send_b, after(lse, gatt_x), got2b))
-    got_b = swap_seq(send_b, 2)
-    got_o = swap_seq(go_send, 2)
-    g0, s0 = head_grads(0, 1, lse)
-    g0, got_b, got_o = lax.optimization_barrier((g0, got_b, got_o))
-
     fc2_keep = fc2_keep.reshape(8, deep, width)
-    got2a = got2a.reshape(4, deep, width)
-    got2b = got2b.reshape(4, deep, width)
-    go_keep = go_keep.reshape(8, per, width)
-    got_o = got_o.reshape(8, per, width)
-    quarter = SDS((2, per, 2 * hidden), BF16)
-    send_a, zb1, zb2, zb3, keep_b = call(
-        stage2_kernel,
-        [SDS((4, deep + per, width), BF16), quarter, quarter, quarter, SDS(quarter.shape, F32)],
-        (sidx, bidx) + pairs + (got_b, fc2_keep, got2a, got2b, go_keep, got_o),
-        scalars=2,
-    )
-    send_a, zb, lse = lax.optimization_barrier((send_a, (zb1, zb2, zb3), after(lse, g0)))
-    got_a = swap("batch", send_a, 1)
-    got_zb = swap_four(zb, 1)
+    got2a = got2a.reshape(2, deep, width)
+    got2b = got2b.reshape(6, deep, width)
+    g0, s0 = head_grads(0, 1, after(lse, gatt_x))
+    g0, got_y2, got2b, got_o = lax.optimization_barrier((g0, pairs[3], got2b, got_o))
+    keep_own, keep_oth, got_y1 = pairs[:3]
+    msg_x, msg_a, part_b, part_o, part_a = call(
+        stage1_kernel,
+        [SDS((20, per, width), BF16), SDS((4, deep, width), BF16)]
+        + [SDS((16, per, width), F32), SDS((4, per, width), F32), SDS((4, deep, width), F32)],
+        (bidx, keep_own, keep_oth, got_y1, got_y2, fc2_keep, got2a, got2b, go_keep, got_o),
+        scalars=1,
+    )
+    msg_x, msg_a, lse = lax.optimization_barrier((msg_x, msg_a, after(lse, g0)))
+    got_x = swap_seq(msg_x, 2)
+    got_a = swap("batch", msg_a, 1)
     g12, s12 = head_grads(1, 2, lse)
-    g12, got_a, got_zb = lax.optimization_barrier((g12, got_a, got_zb))
+    g12, got_x, got_a = lax.optimization_barrier((g12, got_x, got_a))
 
     gn1_keep, gn1_send = norm_part(g0, g12)
     gn1_c = swap_seq(gn1_send, 1)
-    got2 = jnp.concatenate([got2a, got2b], axis=0)
-    quarter = SDS((deep + per, width), BF16)
-    za1, za2, za3, keep_a, swap_send, swap_keep, xsend = call(
-        stage3_kernel,
-        [quarter, quarter, quarter, SDS(quarter.shape, F32)]
-        + [SDS((per, 2 * hidden), BF16), SDS((per, 2 * hidden), F32), SDS((block, width), BF16)],
-        (sidx, bidx, fc2_keep, got2, go_keep, got_o, got_a, keep_b, *got_zb, gn1_keep, gn1_c),
-        scalars=2,
-    )
-    xsend, za, swap_send, early = lax.optimization_barrier((xsend, (za1, za2, za3), swap_send, early))
+    q_send, q_keep = qkv_part(g0, s0, g12, s12, after(early, gn1_send))
+    q_send, gn1_c, got_x, got_a = lax.optimization_barrier((q_send, gn1_c, got_x, got_a))
+    got_q = swap("batch", q_send, 1)
+    (xsend,) = call(shift_kernel, [SDS((block, width), BF16)], (gn1_keep, gn1_c))
     gn1_x = swap_seq(xsend, 2)
-    got_za = swap_four(za, 1)
-    swap_got = swap_seq(swap_send, 1)
-    q_send, q_keep = qkv_part(g0, s0, g12, s12, early)
-    q_send, gn1_x, got_za, swap_got = lax.optimization_barrier((q_send, gn1_x, got_za, swap_got))
-    got_q = swap("batch", q_send, 1)
-    gpat, gspe, out_fc2, out_out, out_fc1 = call(
+    quarter = SDS((5 * per + deep, width), BF16)
+    z1, z2, z3, kept = call(
+        stage2_kernel,
+        [quarter, quarter, quarter, SDS(quarter.shape, F32)],
+        (bidx, part_b, part_o, part_a, got_x, got_a),
+        scalars=1,
+    )
+    got_z = swap_four((z1, z2, z3), 1)
+    gpat, gspe = call(
         final_kernel,
-        [SDS((count, width), F32), SDS((extra, width), F32), SDS((deep, width), F32)]
-        + [SDS((per, width), F32), SDS((per, 4 * hidden), F32)],
-        (sidx, gn1_keep, gn1_c, gn1_x, pay, gmid, gain1, keep_a, *got_za, swap_keep, swap_got),
-        scalars=1,
+        [SDS((count, width), F32), SDS((extra, width), F32)],
+        (gn1_keep, gn1_c, after(gn1_x, z1), pay, gmid, gain1),
     )
     got_q = after(got_q, gpat)
     quarter = SDS((4, per, wide), BF16)
-    z1, z2, z3, kept = call(
+    q1, q2, q3, q_kept = call(
         quarter_kernel, [quarter, quarter, quarter, SDS(quarter.shape, F32)], (bidx, q_keep, got_q), scalars=1
     )
-    got_z = swap_four((z1, z2, z3), 1)
+    (q1, q2, q3), got_z = lax.optimization_barrier(((q1, q2, q3), got_z))
+    got_qz = swap_four((q1, q2, q3), 1)
+    swap_send, swap_keep, out_fc2, out_out = call(
+        sums_kernel,
+        [SDS((2 * per, width), BF16), SDS((2 * per, width), F32), SDS((deep, width), F32), SDS((per, width), F32)],
+        (sidx, kept, *got_z),
+        scalars=1,
+    )
+    swap_got = swap_seq(swap_send, 1)
     row = SDS((per, wide), BF16)
     s1, s2, s3, own = call(
-        owner_kernel, [row, row, row, SDS(row.shape, F32)], (sidx, kept, *got_z), scalars=1
+        owner_kernel, [row, row, row, SDS(row.shape, F32)], (sidx, q_kept, *after(got_qz, out_out)), scalars=1
     )
     gots = [swap_seq(v, k) for k, v in ((1, s1), (2, s2), (3, s3))]
-    out_qkv, vec = call(
+    out_qkv, vec, out_fc1 = call(
         collect_kernel,
-        [SDS((per, 3 * width), F32), SDS((per, LANES), F32)],
-        (sidx, own, *gots),
+        [SDS((per, 3 * width), F32), SDS((per, LANES), F32), SDS((per, 4 * hidden), F32)],
+        (sidx, own, *gots, swap_keep, swap_got),
         [pltpu.VMEM((4, per, wide), F32)],
         scalars=1,
     )
@@ -881,8 +890,8 @@
     nbits = bits_of("batch")
     low = nbits - 1
     fc2_keep, got2a, got2b = twos
-    go_keep, go_send = outs
-    keep_own, got_own, keep_oth, got_oth = [
+    go_keep, got_o = outs
+    keep_own, keep_oth, got_oth, got_own = [
         split_bits(p.reshape(2, 2, nb // 2, per, hidden), 2, low) for p in pairs
     ]
     g0, s0 = head_grads(0, 1, lse)
@@ -898,16 +907,16 @@
     rel = jnp.stack([pick(sum_own, own_c, 0), got[:, :hidden], pick(sum_oth, own_c, 0), got[:, hidden:]])
     out_fc1 = jnp.concatenate([pick(rel, s ^ a, 0) for a in range(4)], axis=1)
     got2 = jnp.concatenate([got2a, got2b], axis=0)
-    got_o = swap_seq(go_send, 2)
-    both = []
-    for keep, got in ((fc2_keep, got2), (go_keep, got_o)):
-        parts = [split_bits(p.reshape(nb, -1, width), 0, nbits) for p in (keep, got)]
-        both.append(sum_rest(parts, 0, 0))
+    parts = [split_bits(p.reshape(nb, -1, width), 0, nbits) for p in (fc2_keep, got2)]
+    out_fc2 = sum_rest(parts, 0, 0)
+    parts = [split_bits(p.reshape(2, nb // 2, per, width), 1, low) for p in (go_keep, got_o)]
+    parts = [p[0] for p in parts] + [swap_seq(total([p[1] for p in parts]).astype(BF16), 2)]
+    out_out = sum_rest(parts, 0, 1)
     gn1_keep, gn1_send = norm_part(g0, g12)
     gn1_c = swap_seq(gn1_send, 1)
     gn1_x = swap_seq((gn1_keep[block:] + gn1_c[block:].astype(F32)).astype(BF16), 2)
     gpat, gspe = call(
-        norm_only_kernel,
+        final_kernel,
         [SDS((count, width), F32), SDS((extra, width), F32)],
         (gn1_keep, gn1_c, gn1_x, pay, gmid, gain1),
     )
@@ -922,7 +931,7 @@
     absolute = jnp.stack([pick(rel, s ^ a, 0) for a in range(4)], axis=1)
     out_qkv = absolute.reshape(-1, 4, OWN, 3, HEAD).transpose(0, 3, 1, 2, 4).reshape(-1, 3 * width)
     vec = total([p[:, 3 * cols :] for p in pieces])
-    return both[0], both[1], out_fc1, out_qkv, vec, gpat, gspe
+    return out_fc2, out_out, out_fc1, out_qkv, vec, gpat, gspe
 
 
 def solution(mesh):

time: 230 us -> 175 us (0.76)
  Pallas kernels: 111 us -> 60.1 us
  local copies, waits for them, and re-layouts: 18.7 us -> 15.9 us
  waiting for transfers between devices: 58.3 us -> 60.8 us
    pallas_call x2 -> x0, Pallas kernels: 26 us -> none  [feed(): pl.pallas_call(functools.partial(feed_kernel, last), grid_spec=pltpu.Pref...]
    pallas_call x14 -> x19, Pallas kernels: 84.9 us -> 60.1 us  [call(): pl.pallas_call(kernel, out_shape=outs, in_specs=[smem()] * scalars + [vme...]
    dynamic_slice x0 -> x2, local copies, waits for them, and re-layouts: none -> 4.71 us  [the longest x1 4.63 us: body(): lax.dynamic_slice(w_fc2, ((s ^ j) * hidden, 0), (hidden, width))]
    unnamed x82 -> x50, local copies, waits for them, and re-layouts: 8.26 us -> 3.69 us
    ppermute x33 -> x30, waiting for transfers between devices: 58.3 us -> 60.8 us  [swap(): lax.ppermute(v, kind, [(i, i ^ mask) for i in range(lax.axis_size(kind))])]
    ppermute x33 -> x30, starting transfers between devices: 34.4 us -> 32.2 us  [swap(): lax.ppermute(v, kind, [(i, i ^ mask) for i in range(lax.axis_size(kind))])]
  transfers between devices with their start and end apart: 33 -> 30, of which waited for: 16 -> 19; matrix products, arithmetic and copies ran while one was open for 4% -> 6% of each run, Pallas kernels for 32% -> 28%
where the time goes in v3:
time: 175 us; the launch traced here: 174 us
  waiting for transfers between devices  60.8 us (35%)
  Pallas kernels  60.1 us (34%)
  starting transfers between devices  32.2 us (18%)
  local copies, waits for them, and re-layouts  15.9 us (9%)
  other arithmetic  4.37 us (2%)
    ppermute x30, waiting for transfers between devices, swap(): lax.ppermute(v, kind, [(i, i ^ mask) for i in range(lax.axis_size(kind))])  60.8 us
    pallas_call x19, Pallas kernels, call(): pl.pallas_call(kernel, out_shape=outs, in_specs=[smem()] * scalars + [vme...  60.1 us
    ppermute x30, starting transfers between devices, swap(): lax.ppermute(v, kind, [(i, i ^ mask) for i in range(lax.axis_size(kind))])  32.2 us
    dynamic_slice x1, local copies, waits for them, and re-layouts, body(): lax.dynamic_slice(w_fc2, ((s ^ j) * hidden, 0), (hidden, width))  4.63 us
    unnamed x50, local copies, waits for them, and re-layouts  3.69 us
  transfers between devices with their start and end apart: 30, of which 19 were waited for; matrix products, arithmetic and copies ran while one was open for 6% of the time, Pallas kernels for 28%

profile of v3, /device:TPU:0, one launch (start us, length us, event | category | flops | bytes accessed | tf_op | source)
XLA Modules:
  0.0 174.5 jit_solution(2118416359811121884)
XLA Ops:
  0.7 0.7 and_select_fusion
  1.4 0.8 pad_add_fusion
  2.2 1.1 pad_maximum_fusion.p0
  3.3 3.0 %collective-permute-start.1 = (bf16[288,896]{1,0:T(8,128)(2,1)S(1)}, bf16[288,896]{1,0:T(8,128)(2,1)S(1)}, u32[]{:S(2)}, u32[]{:S(2)}) collective-permute-start(bf16[288,896]{1,0:T(8,128)(2,1)S(1)} %pad_maximum_fusion.p0), channel_id=1, source_target_pairs={{0,16},{8,24},{16,0},{24,8},{1,17},{9,25},{17,1},{25,9},{2,18},{10... | collective-permute-start | bytes 1548296 | tf_op jit(solution)/shard_map/ppermute | solution.py:559
  6.8 3.0 %constant_dynamic-slice_fusion.10 = (bf16[768,64]{1,0:T(8,128)(2,1)S(1)}, bf16[768,64]{1,0:T(8,128)(2,1)S(1)}, bf16[768,64]{1,0:T(8,128)(2,1)S(1)}, bf16[768,64]...) fusion(bf16[768,2304]{1,0:T(8,128)(2,1)} %param.22, ...), kind=kLoop, calls=%fused_computation.21 | loop fusion | bytes 1769508 | tf_op jit(solution)/shard_map/dynamic_slice | solution.py:658
  9.8 0.7 broadcast_in_dim.31
  10.5 2.4 %concatenate.21.w = bf16[768,640]{1,0:T(8,128)(2,1)S(1)} concatenate(bf16[768,64]{1,0:T(8,128)(2,1)} %get-tuple-element.269, bf16[768,64]{1,0:T(8,128)(2,1)} %get-tuple-element.268, bf16[768,64]{1,0:T(8,128)(2,1)} %get-tuple-element.267, bf16[768,64]{1,0:T(8,128)(2,1)} %get-tuple-element.266, bf16[768,64]{1,0:T(8,128)(2,1)S(1)} %get-tuple-element.265, ...), dimensions={1} | concatenate | bytes 1966080 | tf_op jit(solution)/shard_map/concatenate | solution.py:659
  13.0 4.6 %constant_dynamic-slice_fusion = (bf16[768,768]{1,0:T(8,128)(2,1)}, bf16[768,768]{1,0:T(8,128)(2,1)}, bf16[768,768]{1,0:T(8,128)(2,1)}, bf16[768,768]{1,0:T(8,128)(2,1)}) fusion(bf16[3072,768]{1,0:T(8,128)(2,1)} %param.27, s32[]{:T(128)S(6)} %select_n.68, s32[]{:T(128)S(6)} %select_n.67, bf16[768,3072]{1,0:T(8,128)(2,1)} %param.25), kind=kLoop, calls=%fused_computation.11 | loop fusion | bytes 9437192 | tf_op jit(solution)/shard_map/dynamic_slice | solution.py:664
  18.7 1.2 collective-permute-done.2.p3
  20.0 10.3 %shard_map.238 = (bf16[3,1152,128]{2,1,0:T(8,128)(2,1)S(1)}, bf16[3,1152,128]{2,1,0:T(8,128)(2,1)S(1)}, bf16[3,1152,128]{2,1,0:T(8,128)(2,1)S(1)}, f32[3,3,8,384...) custom-call(bf16[288,896]{1,0:T(8,128)(2,1)S(1)} %pad_maximum_fusion, ...), custom_call_target="tpu_custom_call" | custom-call | flops 2548039680 | bytes 7885312 | tf_op jit(solution)/shard_map/pallas_call | solution.py:76
  30.3 1.8 %collective-permute-start.4 = (bf16[576,192]{1,0:T(8,128)(2,1)S(1)}, bf16[576,192]{1,0:T(8,128)(2,1)S(1)}, u32[]{:S(2)}, u32[]{:S(2)}) collective-permute-start(bf16[576,192]{1,0:T(8,128)(2,1)S(1)} %get-tuple-element.140), channel_id=1, source_target_pairs={{0,16},{8,24},{16,0},{24,8},{1,17},{9,25},{17,1},{25,9},{2,18},{10... | collective-permute-start | bytes 663560 | tf_op jit(solution)/shard_map/ppermute | solution.py:559
  32.1 4.9 %shard_map.239 = (bf16[576,192]{1,0:T(8,128)(2,1)}, f32[3,3,8,384]{3,2,1,0:T(8,128)S(1)}) custom-call(bf16[3,1152,128]{2,1,0:T(8,128)(2,1)S(1)} %get-tuple-element.134.qa, bf16[3,1152,128]{2,1,0:T(8,128)(2,1)S(1)} %get-tuple-element.135.ka, bf16[3,1152,128]{2,1,0:T(8,128)(2,1)S(1)} %get-tuple-element.136.va, f32[3,3,8,384]{3,2,1,0:T(8,128)S(1)} %get-tuple-element.137.lse_in, ...), custom_call_target="tpu_custom_call" | custom-call | flops 509607936 | bytes 3170304 | tf_op jit(solution)/shard_map/pallas_call | solution.py:76
  36.9 1.0 copy-done.12
  37.9 0.9 copy-done.14
  38.8 0.6 copy-done.16
  40.0 1.8 %collective-permute-done.3.a1 = bf16[576,192]{1,0:T(8,128)(2,1)} collective-permute-done((bf16[576,192]{1,0:T(8,128)(2,1)}, bf16[576,192]{1,0:T(8,128)(2,1)}, u32[]{:S(2)}, u32[]{:S(2)}) %collective-permute-start.3) | collective-permute-done | bytes 221216 | tf_op jit(solution)/shard_map/ppermute | solution.py:559
  41.8 1.0 copy-done.2
  42.8 3.2 %shard_map.240 = (f32[576,768]{1,0:T(8,128)S(1)}, bf16[576,768]{1,0:T(8,128)(2,1)S(1)}, bf16[576,768]{1,0:T(8,128)(2,1)S(1)}) custom-call(s32[1]{0:T(128)} %bitcast.sref, bf16[576,192]{1,0:T(8,128)(2,1)} %get-tuple-element.139.a0, bf16[576,192]{1,0:T(8,128)(2,1)} %collective-permute-done.3.a1, bf16[576,192]{1,0:T(8,128)(2,1)S(1)} %collective-permute-done.4.a2, ...), custom_call_target="tpu_custom_call" | custom-call | flops 679477248 | bytes 7533572 | tf_op jit(solution)/shard_map/pallas_call | solution.py:76
  46.1 5.1 %shard_map.241 = (bf16[192,768]{1,0:T(8,128)(2,1)S(1)}, bf16[576,768]{1,0:T(8,128)(2,1)S(1)}, bf16[8,24,768]{2,1,0:T(8,128)(2,1)S(1)}, bf16[8,24,768]{2,1,0:T(8,...) custom-call(s32[1]{0:T(128)} %bitcast.sref, ...), custom_call_target="tpu_custom_call" | custom-call | flops 4076863488 | bytes 10033160 | tf_op jit(solution)/shard_map/pallas_call | solution.py:76
  51.2 1.1 collective-permute-start.7
  52.3 1.5 collective-permute-start.8
  53.9 5.2 %shard_map.242 = (bf16[768,768]{1,0:T(8,128)(2,1)S(1)}, bf16[24,24,768]{2,1,0:T(8,128)(2,1)S(1)}, bf16[16,24,768]{2,1,0:T(8,128)(2,1)S(1)}, f32[1,768]{1,0:T(1,1...) custom-call(s32[1]{0:T(128)} %bitcast.sref, ...), custom_call_target="tpu_custom_call" | custom-call | flops 4076863488 | bytes 14604296 | tf_op jit(solution)/shard_map/pallas_call | solution.py:76
  59.0 1.3 collective-permute-done.7
  60.3 0.8 collective-permute-done.8.y1
  61.1 1.5 collective-permute-start.12
  62.6 0.8 collective-permute-start.13
  63.5 3.0 %shard_map.243 = (f32[288,768]{1,0:T(8,128)S(1)}, bf16[576,768]{1,0:T(8,128)(2,1)S(1)}, bf16[576,192]{1,0:T(8,128)(2,1)S(1)}, f32[8,768]{1,0:T(8,128)S(1)}) custom-call(s32[1]{0:T(128)} %bitcast.sref, f32[576,768]{1,0:T(8,128)S(1)} %get-tuple-element.153.gn_keep, bf16[576,768]{1,0:T(8,128)(2,1)S(1)} %collective-permute-done.9.gn_got, ...), custom_call_target="tpu_custom_call" | custom-call | flops 169869312 | bytes 10427396 | tf_op jit(solution)/shard_map/pallas_call | solution.py:76
  66.5 1.2 collective-permute-start.11
  67.8 2.8 %shard_map.244 = (bf16[576,192]{1,0:T(8,128)(2,1)S(1)}, bf16[2,4,24,768]{3,2,1,0:T(8,128)(2,1)S(1)}, bf16[2,4,24,768]{3,2,1,0:T(8,128)(2,1)S(1)}, f32[768,128]{1...) custom-call(s32[1]{0:T(128)} %bitcast.sref, s32[1]{0:T(128)} %bitcast.1.bref, ...), custom_call_target="tpu_custom_call" | custom-call | flops 509607936 | bytes 7767048 | tf_op jit(solution)/shard_map/pallas_call | solution.py:76
  70.5 1.2 collective-permute-start.14
  71.7 11.8 %collective-permute-done.12.y2 = bf16[24,24,768]{2,1,0:T(8,128)(2,1)S(1)} collective-permute-done((bf16[24,24,768]{2,1,0:T(8,128)(2,1)S(1)}, bf16[24,24,768]{2,1,0:T(8,128)(2,1)S(1)}, u32[]{:S(2)}, u32[]{:S(2)}) %collective-permute-start.12) | collective-permute-done | bytes 884768 | tf_op jit(solution)/shard_map/ppermute | solution.py:559
  83.6 1.5 collective-permute-done.13
  85.1 5.6 %collective-permute-done.11.gx = bf16[576,192]{1,0:T(8,128)(2,1)S(1)} collective-permute-done((bf16[576,192]{1,0:T(8,128)(2,1)S(1)}, bf16[576,192]{1,0:T(8,128)(2,1)S(1)}, u32[]{:S(2)}, u32[]{:S(2)}) %collective-permute-start.11) | collective-permute-done | bytes 221216 | tf_op jit(solution)/shard_map/ppermute | solution.py:559
  90.7 5.3 %shard_map.245 = (bf16[1,1152,192]{2,1,0:T(8,128)(2,1)S(1)}, f32[1,1,192]{2,1,0:T(1,128)S(1)}) custom-call(bf16[3,1152,128]{2,1,0:T(8,128)(2,1)S(1)} %copy-done.11, bf16[3,1152,128]{2,1,0:T(8,128)(2,1)S(1)} %copy-done.13, bf16[3,1152,128]{2,1,0:T(8,128)(2,1)S(1)} %copy-done.15, f32[3,3,8,384]{3,2,1,0:T(8,128)S(1)} %copy-done.17, ...), custom_call_target="tpu_custom_call" | custom-call | flops 1698693120 | bytes 3650304 | tf_op jit(solution)/shard_map/pallas_call | solution.py:76
  96.1 0.6 shard_map.246
  96.7 0.9 collective-permute-start.15
  97.6 0.7 collective-permute-start.16
  98.2 11.0 %shard_map.247 = (bf16[2,1152,192]{2,1,0:T(8,128)(2,1)S(1)}, f32[2,1,192]{2,1,0:T(1,128)S(1)}) custom-call(bf16[3,1152,128]{2,1,0:T(8,128)(2,1)S(1)} %copy-done.11, bf16[3,1152,128]{2,1,0:T(8,128)(2,1)S(1)} %copy-done.13, bf16[3,1152,128]{2,1,0:T(8,128)(2,1)S(1)} %copy-done.15, f32[3,3,8,384]{3,2,1,0:T(8,128)S(1)} %copy-done.17, ...), custom_call_target="tpu_custom_call" | custom-call | flops 3397386240 | bytes 4093440 | tf_op jit(solution)/shard_map/pallas_call | solution.py:76
  109.2 2.7 %collective-permute-done.16.got_a = bf16[4,96,768]{2,1,0:T(8,128)(2,1)S(1)} collective-permute-done((bf16[4,96,768]{2,1,0:T(8,128)(2,1)S(1)}, bf16[4,96,768]{2,1,0:T(8,128)(2,1)S(1)}, u32[]{:S(2)}, u32[]{:S(2)}) %collective-permute-start.16) | collective-permute-done | bytes 589856 | tf_op jit(solution)/shard_map/ppermute | solution.py:559
  111.9 2.6 %collective-permute-done.15.got_x = bf16[20,24,768]{2,1,0:T(8,128)(2,1)S(1)} collective-permute-done((bf16[20,24,768]{2,1,0:T(8,128)(2,1)S(1)}, bf16[20,24,768]{2,1,0:T(8,128)(2,1)S(1)}, u32[]{:S(2)}, u32[]{:S(2)}) %collective-permute-start.15) | collective-permute-done | bytes 737312 | tf_op jit(solution)/shard_map/ppermute | solution.py:559
  114.5 1.7 shard_map.248
  116.3 3.4 %shard_map.249 = (bf16[16,24,640]{2,1,0:T(8,128)(2,1)S(1)}, bf16[16,24,640]{2,1,0:T(8,128)(2,1)S(1)}) custom-call(s32[1]{0:T(128)} %bitcast.sref, s32[1]{0:T(128)} %bitcast.1.bref, bf16[1152,768]{1,0:T(8,128)(2,1)S(1)} %copy-done.5, bf16[1,1152,192]{2,1,0:T(8,128)(2,1)S(1)} %get-tuple-element.181.g0, bf16[2,1152,192]{2,1,0:T(8,128)(2,1)S(1)} %get-tuple-element.198.g12, ...), custom_call_target="tpu_custom_call" | custom-call | flops 1132462080 | bytes 5458184 | tf_op jit(solution)/shard_map/pallas_call | solution.py:76
  120.4 1.0 collective-permute-start.18
  121.7 2.5 %collective-permute-start.21 = (bf16[216,768]{1,0:T(8,128)(2,1)S(1)}, bf16[216,768]{1,0:T(8,128)(2,1)S(1)}, u32[]{:S(2)}, u32[]{:S(2)}) collective-permute-start(bf16[216,768]{1,0:T(8,128)(2,1)S(1)} %get-tuple-element.227), channel_id=1, source_target_pairs={{0,4},{1,5},{2,6},{3,7},{4,0},{5,1},{6,2},{7,3},{8,12},{9,13},{10,... | collective-permute-start | bytes 995336 | tf_op jit(solution)/shard_map/ppermute | solution.py:559
  124.2 1.4 collective-permute-start.22
  125.8 6.9 %collective-permute-done.18.x0 = bf16[288,768]{1,0:T(8,128)(2,1)S(1)} collective-permute-done((bf16[288,768]{1,0:T(8,128)(2,1)S(1)}, bf16[288,768]{1,0:T(8,128)(2,1)S(1)}, u32[]{:S(2)}, u32[]{:S(2)}) %collective-permute-start.18) | collective-permute-done | bytes 442400 | tf_op jit(solution)/shard_map/ppermute | solution.py:559
  132.7 1.5 shard_map.252
  134.4 13.2 %collective-permute-done.21.z2 = bf16[216,768]{1,0:T(8,128)(2,1)S(1)} collective-permute-done((bf16[216,768]{1,0:T(8,128)(2,1)S(1)}, bf16[216,768]{1,0:T(8,128)(2,1)S(1)}, u32[]{:S(2)}, u32[]{:S(2)}) %collective-permute-start.21) | collective-permute-done | bytes 331808 | tf_op jit(solution)/shard_map/ppermute | solution.py:559
  147.9 6.3 %collective-permute-start.23 = (bf16[4,24,640]{2,1,0:T(8,128)(2,1)S(1)}, bf16[4,24,640]{2,1,0:T(8,128)(2,1)S(1)}, u32[]{:S(2)}, u32[]{:S(2)}) collective-permute-start(bf16[4,24,640]{2,1,0:T(8,128)(2,1)S(1)} %get-tuple-element.229), channel_id=1, source_target_pairs={{0,2},{1,3},{2,0},{3,1},{4,6},{5,7},{6,4},{7,5},{8,10},{9,11},{10,... | collective-permute-start | bytes 368648 | tf_op jit(solution)/shard_map/ppermute | solution.py:559
  154.2 1.9 %collective-permute-start.24 = (bf16[4,24,640]{2,1,0:T(8,128)(2,1)S(1)}, bf16[4,24,640]{2,1,0:T(8,128)(2,1)S(1)}, u32[]{:S(2)}, u32[]{:S(2)}) collective-permute-start(bf16[4,24,640]{2,1,0:T(8,128)(2,1)S(1)} %get-tuple-element.230), channel_id=1, source_target_pairs={{0,4},{1,5},{2,6},{3,7},{4,0},{5,1},{6,2},{7,3},{8,12},{9,13},{10,... | collective-permute-start | bytes 368648 | tf_op jit(solution)/shard_map/ppermute | solution.py:559
  156.1 1.5 collective-permute-start.25
  157.6 0.8 shard_map.254
  158.4 1.6 collective-permute-done.23.z1
  160.0 1.3 collective-permute-done.24.z2
  161.3 4.8 %collective-permute-done.25.z3 = bf16[4,24,640]{2,1,0:T(8,128)(2,1)S(1)} collective-permute-done((bf16[4,24,640]{2,1,0:T(8,128)(2,1)S(1)}, bf16[4,24,640]{2,1,0:T(8,128)(2,1)S(1)}, u32[]{:S(2)}, u32[]{:S(2)}) %collective-permute-start.25) | collective-permute-done | bytes 122912 | tf_op jit(solution)/shard_map/ppermute | solution.py:559
  166.3 1.3 collective-permute-start.27
  167.6 0.6 collective-permute-start.28
  168.2 2.1 %collective-permute-done.27.g2 = bf16[24,640]{1,0:T(8,128)(2,1)S(1)} collective-permute-done((bf16[24,640]{1,0:T(8,128)(2,1)S(1)}, bf16[24,640]{1,0:T(8,128)(2,1)S(1)}, u32[]{:S(2)}, u32[]{:S(2)}) %collective-permute-start.27) | collective-permute-done | bytes 30752 | tf_op jit(solution)/shard_map/ppermute | solution.py:559
  170.3 0.6 collective-permute-done.28.g3
  170.9 0.9 shard_map.256
  172.1 0.6 reshape.66
  172.8 0.6 pad_maximum_fusion.4
  173.3 0.6 pad_maximum_fusion.3
  173.9 0.6 pad_maximum_fusion.2
  (96 shorter events, 4.6 us)
Async XLA Ops:
  0.6 5.7 %copy-start.19 = (f32[4,768]{1,0:T(4,128)S(1)}, f32[4,768]{1,0:T(4,128)}, u32[]{:S(2)}) copy-start(f32[4,768]{1,0:T(4,128)} %param.23) | copy-start | bytes 36868
  0.7 5.7 %copy-start.23 = (f32[3072]{0:T(1024)S(1)}, f32[3072]{0:T(1024)}, u32[]{:S(2)}) copy-start(f32[3072]{0:T(1024)} %param.26) | copy-start | bytes 36868
  0.7 5.8 %copy-start.24 = (s32[1,16]{1,0:T(1,128)S(1)}, s32[1,16]{1,0:T(1,128)}, u32[]{:S(2)}) copy-start(s32[1,16]{1,0:T(1,128)} %param.19) | copy-start | bytes 196
  3.3 14.8 %collective-permute-start.1 = (bf16[288,896]{1,0:T(8,128)(2,1)S(1)}, bf16[288,896]{1,0:T(8,128)(2,1)S(1)}, u32[]{:S(2)}, u32[]{:S(2)}) collective-permute-start(bf16[288,896]{1,0:T(8,128)(2,1)S(1)} %pad_maximum_fusion.p0), channel_id=1, source_target_pairs={{0,16},{8,24},{16,0},{24,8},{1,17},{9,25},{17,1},{25,9},{2,18},{10... | collective-permute-start | bytes 1548296 | tf_op jit(solution)/shard_map/ppermute | solution.py:559
  6.3 12.4 %collective-permute-start = (bf16[288,896]{1,0:T(8,128)(2,1)S(1)}, bf16[288,896]{1,0:T(8,128)(2,1)S(1)}, u32[]{:S(2)}, u32[]{:S(2)}) collective-permute-start(bf16[288,896]{1,0:T(8,128)(2,1)S(1)} %pad_maximum_fusion.p0), channel_id=1, source_target_pairs={{0,8},{8,0},{16,24},{24,16},{1,9},{9,1},{17,25},{25,17},{2,10},{10... | collective-permute-start | bytes 1548296 | tf_op jit(solution)/shard_map/ppermute | solution.py:559
  13.0 5.2 %copy-start.18 = (bf16[1,256,768]{2,1,0:T(8,128)(2,1)S(1)}, bf16[1,256,768]{2,1,0:T(8,128)(2,1)}, u32[]{:S(2)}) copy-start(bf16[1,256,768]{2,1,0:T(8,128)(2,1)} %param.28) | copy-start | bytes 1179652
  13.0 5.2 %copy-start.20 = (bf16[1,4,768]{2,1,0:T(4,128)(2,1)S(1)}, bf16[1,4,768]{2,1,0:T(4,128)(2,1)}, u32[]{:S(2)}) copy-start(bf16[1,4,768]{2,1,0:T(4,128)(2,1)} %param.29) | copy-start | bytes 18436
  13.0 5.7 %copy-start.21 = (f32[2,768]{1,0:T(2,128)S(1)}, f32[2,768]{1,0:T(2,128)}, u32[]{:S(2)}) copy-start(f32[2,768]{1,0:T(2,128)} %param.21) | copy-start | bytes 18436
  13.0 5.7 %copy-start.22 = (f32[2,768]{1,0:T(2,128)S(1)}, f32[2,768]{1,0:T(2,128)}, u32[]{:S(2)}) copy-start(f32[2,768]{1,0:T(2,128)} %param.20) | copy-start | bytes 18436
  18.1 1.9 %collective-permute-start.2 = (bf16[288,896]{1,0:T(8,128)(2,1)S(1)}, bf16[288,896]{1,0:T(8,128)(2,1)S(1)}, u32[]{:S(2)}, u32[]{:S(2)}) collective-permute-start(bf16[288,896]{1,0:T(8,128)(2,1)S(1)} %collective-permute-done.1.p2), channel_id=1, source_target_pairs={{0,8},{8,0},{16,24},{24,16},{1,9},{9,1},{17,25},{25,17},{2,10},{10... | collective-permute-start | bytes 1548296 | tf_op jit(solution)/shard_map/ppermute | solution.py:559
  18.2 21.8 %collective-permute-start.6 = (bf16[288,768]{1,0:T(8,128)(2,1)S(1)}, bf16[288,768]{1,0:T(8,128)(2,1)}, u32[]{:S(2)}, u32[]{:S(2)}) collective-permute-start(bf16[288,768]{1,0:T(8,128)(2,1)S(1)} %pad_maximum_fusion.1.c0), channel_id=1, source_target_pairs={{0,8},{8,0},{16,24},{24,16},{1,9},{9,1},{17,25},{25,17},{2,10},{10... | collective-permute-start | bytes 1327112 | tf_op jit(solution)/shard_map/ppermute | solution.py:559
  18.7 11.5 %copy-start.1 = (bf16[288,896]{1,0:T(8,128)(2,1)}, bf16[288,896]{1,0:T(8,128)(2,1)S(1)}, u32[]{:S(2)}) copy-start(bf16[288,896]{1,0:T(8,128)(2,1)S(1)} %collective-permute-done.p1) | copy-start | bytes 1548292
  30.2 6.7 %copy-start.4 = (bf16[1152,768]{1,0:T(8,128)(2,1)}, bf16[1152,768]{1,0:T(8,128)(2,1)S(1)}, u32[]{:S(2)}) copy-start(bf16[1152,768]{1,0:T(8,128)(2,1)S(1)} %get-tuple-element.200.normed) | copy-start | bytes 5308420
  30.3 6.7 %copy-start.10 = (bf16[3,1152,128]{2,1,0:T(8,128)(2,1)}, bf16[3,1152,128]{2,1,0:T(8,128)(2,1)S(1)}, u32[]{:S(2)}) copy-start(bf16[3,1152,128]{2,1,0:T(8,128)(2,1)S(1)} %get-tuple-element.134.qa) | copy-start | bytes 2654212
  30.3 9.2 %collective-permute-start.4 = (bf16[576,192]{1,0:T(8,128)(2,1)S(1)}, bf16[576,192]{1,0:T(8,128)(2,1)S(1)}, u32[]{:S(2)}, u32[]{:S(2)}) collective-permute-start(bf16[576,192]{1,0:T(8,128)(2,1)S(1)} %get-tuple-element.140), channel_id=1, source_target_pairs={{0,16},{8,24},{16,0},{24,8},{1,17},{9,25},{17,1},{25,9},{2,18},{10... | collective-permute-start | bytes 663560 | tf_op jit(solution)/shard_map/ppermute | solution.py:559
  32.1 9.7 %copy-start = (bf16[768,768]{1,0:T(8,128)(2,1)S(1)}, bf16[768,768]{1,0:T(8,128)(2,1)}, u32[]{:S(2)}) copy-start(bf16[768,768]{1,0:T(8,128)(2,1)} %w_out.5) | copy-start | bytes 3538948
  36.9 1.0 copy-start.12
  37.9 0.9 copy-start.14
  38.8 0.6 copy-start.16
  39.5 2.3 %collective-permute-start.3 = (bf16[576,192]{1,0:T(8,128)(2,1)}, bf16[576,192]{1,0:T(8,128)(2,1)}, u32[]{:S(2)}, u32[]{:S(2)}) collective-permute-start(bf16[576,192]{1,0:T(8,128)(2,1)} %get-tuple-element.139.a0), channel_id=1, source_target_pairs={{0,8},{8,0},{16,24},{24,16},{1,9},{9,1},{17,25},{25,17},{2,10},{10... | collective-permute-start | bytes 663560 | tf_op jit(solution)/shard_map/ppermute | solution.py:559
  39.5 2.3 %collective-permute-start.5 = (bf16[576,192]{1,0:T(8,128)(2,1)S(1)}, bf16[576,192]{1,0:T(8,128)(2,1)}, u32[]{:S(2)}, u32[]{:S(2)}) collective-permute-start(bf16[576,192]{1,0:T(8,128)(2,1)S(1)} %collective-permute-done.4.a2), channel_id=1, source_target_pairs={{0,8},{8,0},{16,24},{24,16},{1,9},{9,1},{17,25},{25,17},{2,10},{10... | collective-permute-start | bytes 663560 | tf_op jit(solution)/shard_map/ppermute | solution.py:559
  41.8 1.0 copy-start.2
  42.8 3.2 %copy-start.8 = (bf16[768,768]{1,0:T(8,128)(2,1)S(1)}, bf16[768,768]{1,0:T(8,128)(2,1)}, u32[]{:S(2)}) copy-start(bf16[768,768]{1,0:T(8,128)(2,1)} %get-tuple-element.149.fc2) | copy-start | bytes 3538948
  42.8 3.2 %copy-start.9 = (bf16[768,768]{1,0:T(8,128)(2,1)S(1)}, bf16[768,768]{1,0:T(8,128)(2,1)}, u32[]{:S(2)}) copy-start(bf16[768,768]{1,0:T(8,128)(2,1)} %get-tuple-element.147.fc1) | copy-start | bytes 3538948
  46.1 7.8 %copy-start.6 = (bf16[768,768]{1,0:T(8,128)(2,1)S(1)}, bf16[768,768]{1,0:T(8,128)(2,1)}, u32[]{:S(2)}) copy-start(bf16[768,768]{1,0:T(8,128)(2,1)} %get-tuple-element.146.fc2) | copy-start | bytes 3538948
  46.1 7.8 %copy-start.7 = (bf16[768,768]{1,0:T(8,128)(2,1)S(1)}, bf16[768,768]{1,0:T(8,128)(2,1)}, u32[]{:S(2)}) copy-start(bf16[768,768]{1,0:T(8,128)(2,1)} %get-tuple-element.144.fc1) | copy-start | bytes 3538948
  51.2 9.1 %collective-permute-start.7 = (bf16[192,768]{1,0:T(8,128)(2,1)S(1)}, bf16[192,768]{1,0:T(8,128)(2,1)S(1)}, u32[]{:S(2)}, u32[]{:S(2)}) collective-permute-start(bf16[192,768]{1,0:T(8,128)(2,1)S(1)} %get-tuple-element.158), channel_id=1, source_target_pairs={{0,16},{8,24},{16,0},{24,8},{1,17},{9,25},{17,1},{25,9},{2,18},{10... | collective-permute-start | bytes 884744 | tf_op jit(solution)/shard_map/ppermute | solution.py:559
  52.3 8.8 %collective-permute-start.8 = (bf16[8,24,768]{2,1,0:T(8,128)(2,1)S(1)}, bf16[8,24,768]{2,1,0:T(8,128)(2,1)S(1)}, u32[]{:S(2)}, u32[]{:S(2)}) collective-permute-start(bf16[8,24,768]{2,1,0:T(8,128)(2,1)S(1)} %get-tuple-element.159), channel_id=1, source_target_pairs={{0,1},{1,0},{2,3},{3,2},{4,5},{5,4},{6,7},{7,6},{8,9},{9,8},{10,11... | collective-permute-start | bytes 884744 | tf_op jit(solution)/shard_map/ppermute | solution.py:559
  53.9 9.7 %copy-start.3 = (bf16[288,896]{1,0:T(8,128)(2,1)S(1)}, bf16[288,896]{1,0:T(8,128)(2,1)}, u32[]{:S(2)}) copy-start(bf16[288,896]{1,0:T(8,128)(2,1)} %copy-done.1) | copy-start | bytes 1548292
  61.1 2.4 %collective-permute-start.9 = (bf16[576,768]{1,0:T(8,128)(2,1)S(1)}, bf16[576,768]{1,0:T(8,128)(2,1)S(1)}, u32[]{:S(2)}, u32[]{:S(2)}) collective-permute-start(bf16[576,768]{1,0:T(8,128)(2,1)S(1)} %get-tuple-element.160), channel_id=1, source_target_pairs={{0,8},{8,0},{16,24},{24,16},{1,9},{9,1},{17,25},{25,17},{2,10},{10... | collective-permute-start | bytes 2654216 | tf_op jit(solution)/shard_map/ppermute | solution.py:559
  61.1 22.4 %collective-permute-start.12 = (bf16[24,24,768]{2,1,0:T(8,128)(2,1)S(1)}, bf16[24,24,768]{2,1,0:T(8,128)(2,1)S(1)}, u32[]{:S(2)}, u32[]{:S(2)}) collective-permute-start(bf16[24,24,768]{2,1,0:T(8,128)(2,1)S(1)} %get-tuple-element.177), channel_id=1, source_target_pairs={{0,1},{1,0},{2,3},{3,2},{4,5},{5,4},{6,7},{7,6},{8,9},{9,8},{10,11... | collective-permute-start | bytes 2654216 | tf_op jit(solution)/shard_map/ppermute | solution.py:559
  62.6 22.5 %collective-permute-start.13 = (bf16[576,768]{1,0:T(8,128)(2,1)S(1)}, bf16[576,768]{1,0:T(8,128)(2,1)S(1)}, u32[]{:S(2)}, u32[]{:S(2)}) collective-permute-start(bf16[576,768]{1,0:T(8,128)(2,1)S(1)} %get-tuple-element.178), channel_id=1, source_target_pairs={{0,16},{8,24},{16,0},{24,8},{1,17},{9,25},{17,1},{25,9},{2,18},{10... | collective-permute-start | bytes 2654216 | tf_op jit(solution)/shard_map/ppermute | solution.py:559
  63.4 4.3 %collective-permute-start.10 = (bf16[288,768]{1,0:T(8,128)(2,1)S(1)}, bf16[288,768]{1,0:T(8,128)(2,1)S(1)}, u32[]{:S(2)}, u32[]{:S(2)}) collective-permute-start(bf16[288,768]{1,0:T(8,128)(2,1)S(1)} %get-tuple-element.164), channel_id=1, source_target_pairs={{0,8},{8,0},{16,24},{24,16},{1,9},{9,1},{17,25},{25,17},{2,10},{10... | collective-permute-start | bytes 1327112 | tf_op jit(solution)/shard_map/ppermute | solution.py:559
  66.5 24.2 %collective-permute-start.11 = (bf16[576,192]{1,0:T(8,128)(2,1)S(1)}, bf16[576,192]{1,0:T(8,128)(2,1)S(1)}, u32[]{:S(2)}, u32[]{:S(2)}) collective-permute-start(bf16[576,192]{1,0:T(8,128)(2,1)S(1)} %get-tuple-element.171), channel_id=1, source_target_pairs={{0,16},{8,24},{16,0},{24,8},{1,17},{9,25},{17,1},{25,9},{2,18},{10... | collective-permute-start | bytes 663560 | tf_op jit(solution)/shard_map/ppermute | solution.py:559
  67.7 23.0 %copy-start.11 = (bf16[3,1152,128]{2,1,0:T(8,128)(2,1)S(1)}, bf16[3,1152,128]{2,1,0:T(8,128)(2,1)}, u32[]{:S(2)}) copy-start(bf16[3,1152,128]{2,1,0:T(8,128)(2,1)} %copy-done.10) | copy-start | bytes 2654212
  67.7 23.0 %copy-start.13 = (bf16[3,1152,128]{2,1,0:T(8,128)(2,1)S(1)}, bf16[3,1152,128]{2,1,0:T(8,128)(2,1)}, u32[]{:S(2)}) copy-start(bf16[3,1152,128]{2,1,0:T(8,128)(2,1)} %copy-done.12) | copy-start | bytes 2654212
  67.7 23.0 %copy-start.15 = (bf16[3,1152,128]{2,1,0:T(8,128)(2,1)S(1)}, bf16[3,1152,128]{2,1,0:T(8,128)(2,1)}, u32[]{:S(2)}) copy-start(bf16[3,1152,128]{2,1,0:T(8,128)(2,1)} %copy-done.14) | copy-start | bytes 2654212
  67.7 23.0 %copy-start.17 = (f32[3,3,8,384]{3,2,1,0:T(8,128)S(1)}, f32[3,3,8,384]{3,2,1,0:T(8,128)}, u32[]{:S(2)}) copy-start(f32[3,3,8,384]{3,2,1,0:T(8,128)} %copy-done.16) | copy-start | bytes 331780
  70.5 25.5 %collective-permute-start.14 = (bf16[2,4,24,768]{3,2,1,0:T(8,128)(2,1)S(1)}, bf16[2,4,24,768]{3,2,1,0:T(8,128)(2,1)S(1)}, u32[]{:S(2)}, u32[]{:S(2)}) collective-permute-start(bf16[2,4,24,768]{3,2,1,0:T(8,128)(2,1)S(1)} %get-tuple-element.172), channel_id=1, source_target_pairs={{0,1},{1,0},{2,3},{3,2},{4,5},{5,4},{6,7},{7,6},{8,9},{9,8},{10,11... | collective-permute-start | bytes 884744 | tf_op jit(solution)/shard_map/ppermute | solution.py:559
  96.7 17.9 %collective-permute-start.15 = (bf16[20,24,768]{2,1,0:T(8,128)(2,1)S(1)}, bf16[20,24,768]{2,1,0:T(8,128)(2,1)S(1)}, u32[]{:S(2)}, u32[]{:S(2)}) collective-permute-start(bf16[20,24,768]{2,1,0:T(8,128)(2,1)S(1)} %get-tuple-element.196), channel_id=1, source_target_pairs={{0,16},{8,24},{16,0},{24,8},{1,17},{9,25},{17,1},{25,9},{2,18},{10... | collective-permute-start | bytes 2211848 | tf_op jit(solution)/shard_map/ppermute | solution.py:559
  97.6 14.4 %collective-permute-start.16 = (bf16[4,96,768]{2,1,0:T(8,128)(2,1)S(1)}, bf16[4,96,768]{2,1,0:T(8,128)(2,1)S(1)}, u32[]{:S(2)}, u32[]{:S(2)}) collective-permute-start(bf16[4,96,768]{2,1,0:T(8,128)(2,1)S(1)} %get-tuple-element.197), channel_id=1, source_target_pairs={{0,1},{1,0},{2,3},{3,2},{4,5},{5,4},{6,7},{7,6},{8,9},{9,8},{10,11... | collective-permute-start | bytes 1769480 | tf_op jit(solution)/shard_map/ppermute | solution.py:559
  114.5 1.8 %copy-start.5 = (bf16[1152,768]{1,0:T(8,128)(2,1)S(1)}, bf16[1152,768]{1,0:T(8,128)(2,1)}, u32[]{:S(2)}) copy-start(bf16[1152,768]{1,0:T(8,128)(2,1)} %copy-done.4) | copy-start | bytes 5308420
  116.2 3.5 %collective-permute-start.17 = (bf16[576,768]{1,0:T(8,128)(2,1)S(1)}, bf16[576,768]{1,0:T(8,128)(2,1)S(1)}, u32[]{:S(2)}, u32[]{:S(2)}) collective-permute-start(bf16[576,768]{1,0:T(8,128)(2,1)S(1)} %get-tuple-element.204), channel_id=1, source_target_pairs={{0,8},{8,0},{16,24},{24,16},{1,9},{9,1},{17,25},{25,17},{2,10},{10... | collective-permute-start | bytes 2654216 | tf_op jit(solution)/shard_map/ppermute | solution.py:559
  119.7 14.5 %collective-permute-start.19 = (bf16[16,24,640]{2,1,0:T(8,128)(2,1)S(1)}, bf16[16,24,640]{2,1,0:T(8,128)(2,1)S(1)}, u32[]{:S(2)}, u32[]{:S(2)}) collective-permute-start(bf16[16,24,640]{2,1,0:T(8,128)(2,1)S(1)} %get-tuple-element.221), channel_id=1, source_target_pairs={{0,1},{1,0},{2,3},{3,2},{4,5},{5,4},{6,7},{7,6},{8,9},{9,8},{10,11... | collective-permute-start | bytes 1474568 | tf_op jit(solution)/shard_map/ppermute | solution.py:559
  120.4 12.3 %collective-permute-start.18 = (bf16[288,768]{1,0:T(8,128)(2,1)S(1)}, bf16[288,768]{1,0:T(8,128)(2,1)S(1)}, u32[]{:S(2)}, u32[]{:S(2)}) collective-permute-start(bf16[288,768]{1,0:T(8,128)(2,1)S(1)} %shard_map.250), channel_id=1, source_target_pairs={{0,16},{8,24},{16,0},{24,8},{1,17},{9,25},{17,1},{25,9},{2,18},{10... | collective-permute-start | bytes 1327112 | tf_op jit(solution)/shard_map/ppermute | solution.py:559
  121.7 25.8 %collective-permute-start.21 = (bf16[216,768]{1,0:T(8,128)(2,1)S(1)}, bf16[216,768]{1,0:T(8,128)(2,1)S(1)}, u32[]{:S(2)}, u32[]{:S(2)}) collective-permute-start(bf16[216,768]{1,0:T(8,128)(2,1)S(1)} %get-tuple-element.227), channel_id=1, source_target_pairs={{0,4},{1,5},{2,6},{3,7},{4,0},{5,1},{6,2},{7,3},{8,12},{9,13},{10,... | collective-permute-start | bytes 995336 | tf_op jit(solution)/shard_map/ppermute | solution.py:559
  124.2 23.3 %collective-permute-start.22 = (bf16[216,768]{1,0:T(8,128)(2,1)S(1)}, bf16[216,768]{1,0:T(8,128)(2,1)S(1)}, u32[]{:S(2)}, u32[]{:S(2)}) collective-permute-start(bf16[216,768]{1,0:T(8,128)(2,1)S(1)} %get-tuple-element.228), channel_id=1, source_target_pairs={{0,6},{1,7},{2,4},{3,5},{4,2},{5,3},{6,0},{7,1},{8,14},{9,15},{10,... | collective-permute-start | bytes 995336 | tf_op jit(solution)/shard_map/ppermute | solution.py:559
  125.6 22.3 %collective-permute-start.20 = (bf16[216,768]{1,0:T(8,128)(2,1)S(1)}, bf16[216,768]{1,0:T(8,128)(2,1)S(1)}, u32[]{:S(2)}, u32[]{:S(2)}) collective-permute-start(bf16[216,768]{1,0:T(8,128)(2,1)S(1)} %get-tuple-element.215), channel_id=1, source_target_pairs={{0,2},{1,3},{2,0},{3,1},{4,6},{5,7},{6,4},{7,5},{8,10},{9,11},{10,... | collective-permute-start | bytes 995336 | tf_op jit(solution)/shard_map/ppermute | solution.py:559
  147.9 12.1 %collective-permute-start.23 = (bf16[4,24,640]{2,1,0:T(8,128)(2,1)S(1)}, bf16[4,24,640]{2,1,0:T(8,128)(2,1)S(1)}, u32[]{:S(2)}, u32[]{:S(2)}) collective-permute-start(bf16[4,24,640]{2,1,0:T(8,128)(2,1)S(1)} %get-tuple-element.229), channel_id=1, source_target_pairs={{0,2},{1,3},{2,0},{3,1},{4,6},{5,7},{6,4},{7,5},{8,10},{9,11},{10,... | collective-permute-start | bytes 368648 | tf_op jit(solution)/shard_map/ppermute | solution.py:559
  154.2 7.1 %collective-permute-start.24 = (bf16[4,24,640]{2,1,0:T(8,128)(2,1)S(1)}, bf16[4,24,640]{2,1,0:T(8,128)(2,1)S(1)}, u32[]{:S(2)}, u32[]{:S(2)}) collective-permute-start(bf16[4,24,640]{2,1,0:T(8,128)(2,1)S(1)} %get-tuple-element.230), channel_id=1, source_target_pairs={{0,4},{1,5},{2,6},{3,7},{4,0},{5,1},{6,2},{7,3},{8,12},{9,13},{10,... | collective-permute-start | bytes 368648 | tf_op jit(solution)/shard_map/ppermute | solution.py:559
  156.1 10.0 %collective-permute-start.25 = (bf16[4,24,640]{2,1,0:T(8,128)(2,1)S(1)}, bf16[4,24,640]{2,1,0:T(8,128)(2,1)S(1)}, u32[]{:S(2)}, u32[]{:S(2)}) collective-permute-start(bf16[4,24,640]{2,1,0:T(8,128)(2,1)S(1)} %get-tuple-element.231), channel_id=1, source_target_pairs={{0,6},{1,7},{2,4},{3,5},{4,2},{5,3},{6,0},{7,1},{8,14},{9,15},{10,... | collective-permute-start | bytes 368648 | tf_op jit(solution)/shard_map/ppermute | solution.py:559
  158.4 9.8 %collective-permute-start.29 = (bf16[48,768]{1,0:T(8,128)(2,1)S(1)}, bf16[48,768]{1,0:T(8,128)(2,1)S(1)}, u32[]{:S(2)}, u32[]{:S(2)}) collective-permute-start(bf16[48,768]{1,0:T(8,128)(2,1)S(1)} %get-tuple-element.245), channel_id=1, source_target_pairs={{0,8},{8,0},{16,24},{24,16},{1,9},{9,1},{17,25},{25,17},{2,10},{10... | collective-permute-start | bytes 221192 | tf_op jit(solution)/shard_map/ppermute | solution.py:559
  166.2 1.9 %collective-permute-start.26 = (bf16[24,640]{1,0:T(8,128)(2,1)S(1)}, bf16[24,640]{1,0:T(8,128)(2,1)S(1)}, u32[]{:S(2)}, u32[]{:S(2)}) collective-permute-start(bf16[24,640]{1,0:T(8,128)(2,1)S(1)} %get-tuple-element.241), channel_id=1, source_target_pairs={{0,8},{8,0},{16,24},{24,16},{1,9},{9,1},{17,25},{25,17},{2,10},{10... | collective-permute-start | bytes 92168 | tf_op jit(solution)/shard_map/ppermute | solution.py:559
  166.3 4.0 %collective-permute-start.27 = (bf16[24,640]{1,0:T(8,128)(2,1)S(1)}, bf16[24,640]{1,0:T(8,128)(2,1)S(1)}, u32[]{:S(2)}, u32[]{:S(2)}) collective-permute-start(bf16[24,640]{1,0:T(8,128)(2,1)S(1)} %get-tuple-element.242), channel_id=1, source_target_pairs={{0,16},{8,24},{16,0},{24,8},{1,17},{9,25},{17,1},{25,9},{2,18},{10... | collective-permute-start | bytes 92168 | tf_op jit(solution)/shard_map/ppermute | solution.py:559
  167.6 3.3 %collective-permute-start.28 = (bf16[24,640]{1,0:T(8,128)(2,1)S(1)}, bf16[24,640]{1,0:T(8,128)(2,1)S(1)}, u32[]{:S(2)}, u32[]{:S(2)}) collective-permute-start(bf16[24,640]{1,0:T(8,128)(2,1)S(1)} %get-tuple-element.243), channel_id=1, source_target_pairs={{0,24},{8,16},{16,8},{24,0},{1,25},{9,17},{17,9},{25,1},{2,26},{10... | collective-permute-start | bytes 92168 | tf_op jit(solution)/shard_map/ppermute | solution.py:559

commit v4 on v3

--- a/solution.py
+++ b/solution.py
@@ -176,7 +176,7 @@
     if last:
         b2_in, gn_in, y_in, g2, y_send, g1_keep, gb, b2_keep, b2_send, gn_keep, gn_send, wide = refs
     else:
-        g2a, g2b, y_first, y_second, g1_keep, gb, b2, gn, wide = refs
+        g2a, g2m, g2b, y_first, y_second, g1_keep, gb, b2, gn, wide = refs
     tokens = normed2.shape[0]
     half = tokens // 2
     pre = dot(normed2[...], fc1[...]) + bias[...]
@@ -187,29 +187,28 @@
     grad1 = dot_lt(normed2[...], gh)
     if not fast:
         rows = grad1.shape[0] // 2
-        if last:
-            y_send[...] = grad1[:rows].astype(BF16)
-            g1_keep[...] = grad1[rows:].astype(BF16)
-        else:
-            y_first[...] = grad1[:rows].astype(BF16)
-            g1_keep[...] = grad1[rows:].astype(BF16)
+        (y_send if last else y_first)[...] = grad1[:rows].astype(BF16)
+        g1_keep[...] = grad1[rows:].astype(BF16)
     else:
-        x, y = sref[0] >> 1, bref[0] & 1
+        x, c = sref[0] >> 1, sref[0] & 1
+        y, z1, z2 = bref[0] & 1, (bref[0] >> 1) & 1, bref[0] >> 2
         wide[...] = grad1
         n, rows = g1_keep.shape[:2]
-        n = n // 2
         for m in range(2 * n):
-            base = 2 * rows * (((1 - x) if m < n else x) * n + m % n)
-            piece = wide[pl.ds(pl.multiple_of(base + (1 - y) * rows, 8), rows), :].astype(BF16)
-            if last:
-                y_send[n + m] = piece
-            elif m < n:
+            near = [(m >> k) & 1 for k in (4, 3, 2, 1, 0)]
+            yy, zz1, xx, zz2, cc = [own if r else 1 - own for own, r in zip((y, z1, x, z2, c), near)]
+            base = rows * (16 * xx + 8 * cc + 4 * zz2 + 2 * zz1 + yy)
+            piece = wide[pl.ds(pl.multiple_of(base, 8), rows), :].astype(BF16)
+            if m >= n:
+                g1_keep[m - n] = piece
+            elif last:
+                y_send[n // 2 + m] = piece
+            elif m < n // 2:
                 y_first[m] = piece
             else:
-                y_second[m - n] = piece
-            g1_keep[m] = wide[pl.ds(pl.multiple_of(base + y * rows, 8), rows), :].astype(BF16)
+                y_second[m - n // 2] = piece
         if last:
-            for m in range(n):
+            for m in range(n // 2):
                 y_send[m] = y_in[m]
     gb[...] = jnp.sum(gh.astype(F32), axis=0, keepdims=True)
     partn = dot_t(gh, fc1[...])
@@ -227,9 +226,18 @@
         b2[...] = part2
         gn[...] = partn
         grad2 = dot_lt(act, gb2[...]).astype(BF16)
-        rows = g2a.shape[0]
-        g2a[...] = grad2[:rows]
-        g2b[...] = grad2[rows:]
+        if not fast:
+            rows = g2a.shape[0]
+            g2a[...] = grad2[:rows]
+            g2m[...] = grad2[rows : 2 * rows]
+            g2b[...] = grad2[2 * rows :]
+        else:
+            n, rows = g2a.shape[:2]
+            for m in range(n):
+                base = 4 * rows * m
+                g2a[m] = grad2[base : base + rows]
+                g2m[m] = grad2[base + rows : base + 2 * rows]
+                g2b[m] = grad2[base + 2 * rows : base + 4 * rows]
 
 
 def split_rows(value, wide, bit, send, keep):
@@ -254,7 +262,11 @@
         outs = [SDS((hidden, width), BF16)]
         send = [SDS((3 * pairs // 2, per, hidden), BF16)]
     else:
-        outs = [SDS((hidden // 4, width), BF16), SDS((3 * hidden // 4, width), BF16)]
+        deep = hidden // 8
+        if fast:
+            outs = [SDS((8, deep // 4, width), BF16)] * 2 + [SDS((8, deep // 2, width), BF16)]
+        else:
+            outs = [SDS((hidden // 4, width), BF16)] * 2 + [SDS((hidden // 2, width), BF16)]
         send = [SDS((pairs // 2, per, hidden), BF16)] * 2
     keep = SDS((pairs, per, hidden), BF16)
     if not fast:
@@ -398,14 +410,14 @@
     )
 
 
-def norm1_kernel(g0, g12, w, keep, send):
+def norm1_kernel(g01, g2, w, keep, send):
     rows = keep.shape[0] // 2
-    cols = g0.shape[2]
+    cols = g2.shape[2]
     for i in range(4):
         at = pl.ds(i * rows, rows)
-        part = dot_t(g0[0, at, :], w[:, :cols])
-        part = part + dot_t(g12[0, at, :], w[:, cols : 2 * cols])
-        part = part + dot_t(g12[1, at, :], w[:, 2 * cols : 3 * cols])
+        part = dot_t(g01[0, at, :], w[:, :cols])
+        part = part + dot_t(g01[1, at, :], w[:, cols : 2 * cols])
+        part = part + dot_t(g2[0, at, :], w[:, 2 * cols : 3 * cols])
         to = pl.ds((i // 2) * rows, rows)
         if i % 2 == 0:
             keep[to, :] = part
@@ -413,13 +425,13 @@
             send[to, :] = part.astype(BF16)
 
 
-def qkv_grad_kernel(sref, bref, normed, g0, g12, s0, s12, w, early, send, keep, tile, wide):
-    width, cols = w.shape[0], g0.shape[2]
-    every = (g0[0], g12[0], g12[1])
+def qkv_grad_kernel(sref, bref, normed, g01, g2, s01, s2, w, early, send, keep, tile, wide):
+    width, cols = w.shape[0], g2.shape[2]
+    every = (g01[0], g01[1], g2[0])
     parts = [dot_lt(normed[...], g) for g in every]
     g = jnp.concatenate(parts, axis=1)
     w32 = w[:, : 3 * cols].astype(F32)
-    rows = jnp.concatenate([s0[0], s12[0], s12[1]], axis=1)
+    rows = jnp.concatenate([s01[0], s01[1], s2[0]], axis=1)
     both = jnp.sum(g * w32, axis=-1, keepdims=True)
     gshift = jnp.sum(w32 * rows, axis=-1, keepdims=True)
     ggain = (both - early[:, 1:2] * gshift) / early[:, 0:1]
@@ -428,7 +440,7 @@
     tail = jnp.where(lane == HEAD, ggain, tail)
     tail = jnp.where(lane == HEAD + 1, gshift, tail)
     tile[...] = jnp.where(lane >= HEAD + 4, early[...], tail)
-    ones = jnp.ones((g0.shape[1], LANES), BF16)
+    ones = jnp.ones((g2.shape[1], LANES), BF16)
     at = pl.multiple_of(sref[0] * cols, HEAD)
     for h, part in enumerate(every):
         col = dot_lt(part, ones)
@@ -445,37 +457,54 @@
 
 
 def stage1_kernel(
-    bref, keep_own, keep_oth, y1, y2, fc2, got2a, got2b, out, y3, msg_x, msg_a, part_b, part_o, part_a
+    bref, keep_own, keep_oth, y1, y2, fc2, g2a, g2m, g2b, out, y3,
+    msg_z, msg_y, msg_x, part_f, part_a, part_o,
 ):
-    y = bref[0] & 1
+    y, z1, z2 = bref[0] & 1, (bref[0] >> 1) & 1, bref[0] >> 2
     n = keep_own.shape[0] // 2
     for i in range(n):
-        msg_x[2 * i] = wide_sum(keep_own[i], y2[n + i]).astype(BF16)
-        msg_x[2 * i + 1] = wide_sum(keep_oth[i], y1[i]).astype(BF16)
-        part_b[2 * i] = wide_sum(keep_own[n + i], y2[2 * n + i])
-        part_b[2 * i + 1] = wide_sum(keep_oth[n + i], y2[i])
-    for j in range(4):
-        msg_x[2 * n + j] = wide_sum(out[1, j], y3[1, j]).astype(BF16)
-        part_o[j] = wide_sum(out[0, j], y3[0, j])
-        for bit, ref in ((1 - y, msg_a), (y, part_a)):
-            got = got2a[bit] if j == 0 else got2b[2 * j - 2 + bit]
-            ref[j] = wide_sum(fc2[2 * j + bit], got).astype(ref.dtype)
-
-
-def stage2_kernel(bref, part_b, part_o, part_a, got_x, got_a, z1, z2, z3, kept):
-    q = bref[0] >> 1
-    per = part_o.shape[1]
-    n = part_b.shape[0]
+        msg_z[i] = wide_sum(keep_own[i], y2[n + i]).astype(BF16)
+        msg_z[n + i] = wide_sum(keep_oth[i], y1[i]).astype(BF16)
+        part_f[i] = wide_sum(keep_own[n + i], y2[2 * n + i])
+        part_f[n + i] = wide_sum(keep_oth[n + i], y2[i])
+    rows = g2a.shape[1]
+    for i in range(4):
+        zz1 = z1 if i >> 1 else 1 - z1
+        zz2 = z2 if i & 1 else 1 - z2
+        m = 2 * zz2 + zz1
+        msg_x[i] = wide_sum(out[1, m], y3[1, m]).astype(BF16)
+        part_o[i] = wide_sum(out[0, m], y3[0, m])
+        for bit, ref in ((1 - y, msg_y), (y, part_a)):
+            b = 2 * m + bit
+            ref[i, :rows] = wide_sum(fc2[b, :rows], g2a[b]).astype(ref.dtype)
+            ref[i, rows : 2 * rows] = wide_sum(fc2[b, rows : 2 * rows], g2m[b]).astype(ref.dtype)
+            ref[i, 2 * rows :] = wide_sum(fc2[b, 2 * rows :], g2b[b]).astype(ref.dtype)
+
+
+def stage2_kernel(part_f, got_z, part_a, got_y, part_o, got_x, msg_x, msg_z, part_g, part_c):
+    for half in range(2):
+        for i in range(4):
+            k = 8 * half + i
+            msg_x[4 * half + i] = wide_sum(part_f[k], got_z[k]).astype(BF16)
+            part_g[4 * half + i] = wide_sum(part_f[k + 4], got_z[k + 4])
     deep = part_a.shape[1]
-    for k, ref in enumerate((kept, z1, z2, z3)):
-        j = q ^ k
-        for c in range(2):
-            i = 2 * (c * 4 + j)
-            for half in range(2):
-                at = pl.ds((2 * c + half) * per, per)
-                ref[at, :] = wide_sum(part_b[i + half], got_x[i + 1 - half]).astype(ref.dtype)
-        ref[pl.ds(4 * per, deep), :] = wide_sum(part_a[j], got_a[j]).astype(ref.dtype)
-        ref[pl.ds(4 * per + deep, per), :] = wide_sum(part_o[j], got_x[n + j]).astype(ref.dtype)
+    for i in range(2):
+        for k, ref in ((i, msg_z), (2 + i, part_c)):
+            ref[i, :deep] = wide_sum(part_a[k], got_y[k]).astype(ref.dtype)
+            ref[i, deep:] = wide_sum(part_o[k], got_x[k]).astype(ref.dtype)
+
+
+def stage3_kernel(part_g, got_x, part_c, got_z, msg, kept):
+    per = part_g.shape[1]
+    for half in range(2):
+        for i in range(2):
+            at = pl.ds((2 * half + i) * per, per)
+            k, other = 4 * half + i, 4 * (1 - half) + i
+            msg[at, :] = wide_sum(part_g[k], got_x[other]).astype(BF16)
+            kept[at, :] = wide_sum(part_g[k + 2], got_x[other + 2])
+    at = pl.ds(4 * per, part_c.shape[1])
+    msg[at, :] = wide_sum(part_c[0], got_z[0]).astype(BF16)
+    kept[at, :] = wide_sum(part_c[1], got_z[1])
 
 
 def shift_kernel(keep, got, send):
@@ -491,16 +520,16 @@
             ref[r] = wide_sum(keep[m], got[m]).astype(ref.dtype)
 
 
-def sums_kernel(sref, kept, z1, z2, z3, swap_send, swap_keep, fc2, out):
-    c = sref[0] & 1
-    rows = swap_send.shape[0]
+def sums_kernel(kept, got, swap_send, swap_keep, fc2, out):
+    per = out.shape[0]
+    for half in range(2):
+        for i, ref in ((0, swap_send), (1, swap_keep)):
+            at = pl.ds((2 * half + i) * per, per)
+            ref[pl.ds(half * per, per), :] = wide_sum(kept[at, :], got[at, :]).astype(ref.dtype)
     deep = fc2.shape[0]
-    for pos, ref in ((1 - c, swap_send), (c, swap_keep)):
-        at = pl.ds(pl.multiple_of(pos * rows, 8), rows)
-        ref[...] = wide_sum(kept[at, :], z1[at, :], z2[at, :], z3[at, :]).astype(ref.dtype)
-    for lo, ref in ((2 * rows, fc2), (2 * rows + deep, out)):
+    for lo, ref in ((4 * per, fc2), (4 * per + deep, out)):
         at = pl.ds(lo, ref.shape[0])
-        ref[...] = wide_sum(kept[at, :], z1[at, :], z2[at, :], z3[at, :])
+        ref[...] = wide_sum(kept[at, :], got[at, :])
 
 
 def owner_kernel(sref, kept, z1, z2, z3, s1, s2, s3, own):
@@ -508,6 +537,15 @@
     for k, ref in enumerate((own, s1, s2, s3)):
         m = s ^ k
         ref[...] = wide_sum(kept[m], z1[m], z2[m], z3[m]).astype(ref.dtype)
+
+
+def tail_kernel(
+    sref, bref, qa, ka, va, lse, ga, gx, normed, g01, s01, w, early, gn_keep, gn_send, send, keep,
+    g2, s2, goa, dq, dk, dv, tile, wide,
+):
+    attend_back_kernel(2, 1, qa, ka, va, lse, ga, gx, g2, s2, goa, dq, dk, dv)
+    norm1_kernel(g01, g2, w, gn_keep, gn_send)
+    qkv_grad_kernel(sref, bref, normed, g01, g2, s01, s2, w, early, send, keep, tile, wide)
 
 
 def final_kernel(k0, c0, x0, p0, gmid, gain, gpat, gspe):
@@ -701,26 +739,23 @@
     )
     per = width // (4 * nb)
     fast = nb == 8
-    fc2_a, fc2_b, y1, y_rest, keep_oth, fb_oth, b2, gn = feed(
+    fc2_a, fc2_m, fc2_b, y1, y_rest, keep_oth, fb_oth, b2, gn = feed(
         False, fast, per, sidx, bidx, normed2, gb2, w1[0], fb[0], w2[0]
     )
     got2a = swap_seq(fc2_a, 2)
-    if fast:
-        got_y1 = swap("batch", y1, 1)
-        ahead = (got2a, got_y1)
-    else:
+    if not fast:
         y1, keep_oth = by_batch_bit(jnp.concatenate([y1, keep_oth], axis=0), per)
-        got_y1 = swap("batch", y1, 1)
-        ahead = (got2a, got_y1)
+    got_y1 = swap("batch", y1, 1)
+    ahead = (got2a, got_y1)
     fc2_keep, y2, keep_own, fb_own, b2_keep, b2_send, gn_keep, gn_send = feed(
         True, fast, per, sidx, bidx, normed2, gb2, w1[1], fb[1], w2[1], (b2, gn, y_rest)
     )
     if not fast:
         y2, keep_own = by_batch_bit(jnp.concatenate([y2, keep_own], axis=0), per)
-    gn_send, b2_send, fc2_b, y2, (got2a, got_y1) = lax.optimization_barrier((gn_send, b2_send, fc2_b, y2, ahead))
+    gn_send, b2_send, fc2_m, y2, (got2a, got_y1) = lax.optimization_barrier((gn_send, b2_send, fc2_m, y2, ahead))
     gn_got = swap_seq(gn_send, 1)
     b2_got = swap_seq(b2_send, 1)
-    got2b = swap_seq(fc2_b, 2)
+    got2m = swap_seq(fc2_m, 2)
     got_y2 = swap("batch", y2, 1)
 
     gmid, gbr, gatt_send, line_sums = call(
@@ -749,42 +784,40 @@
         halves = [by_batch_bit(jnp.concatenate([go_send[j], go_keep[j]], axis=0), per) for j in range(2)]
         go_send, go_keep = [jnp.stack([halves[j][k] for j in range(2)]) for k in range(2)]
     got_o = swap("batch", go_send, 1)
-    got_y2, got2b = after((got_y2, got2b), gatt_send)
-    gatt_x = after(gatt_x, go_send)
+    gatt_x, fc2_b = lax.optimization_barrier((after(gatt_x, go_send), fc2_b))
+    got2b = swap_seq(fc2_b, 2)
     pairs = (keep_own, keep_oth, got_y1, got_y2)
 
-    def head_grads(first, heads, lse):
-        return attend_back(first, heads, qa, ka, va, lse, gatt, gatt_x)
-
-    def norm_part(g0, g12):
-        return call(
-            norm1_kernel,
-            [SDS((chip, width), F32), SDS((chip, width), BF16)],
-            (g0, g12, w_own),
-            flops=2 * whole * width * 5 * LANES,
-        )
-
-    def qkv_part(g0, s0, g12, s12, early):
+    def first_heads(lse):
+        return attend_back(0, 2, qa, ka, va, lse, gatt, gatt_x)
+
+    def tail_part(lse, g01, s01):
         wide = 5 * LANES
         if fast:
             outs = [SDS((width // (2 * per), per, wide), BF16)] * 2
         else:
             outs = [SDS((width // 2, wide), BF16)] * 2
         out = call(
-            qkv_grad_kernel,
-            outs,
-            (sidx, bidx, normed, g0, g12, s0, s12, w_own, early),
-            [pltpu.VMEM((width, LANES), F32), pltpu.VMEM((width, wide), F32)],
-            flops=2 * whole * width * wide,
+            tail_kernel,
+            [SDS((chip, width), F32), SDS((chip, width), BF16)] + outs,
+            (sidx, bidx, qa, ka, va, lse, gatt, gatt_x, normed, g01, s01, w_own, early),
+            [pltpu.VMEM((1, whole, cols), BF16), pltpu.VMEM((1, 1, cols), F32)]
+            + [pltpu.VMEM((1, whole, LANES), BF16)]
+            + [pltpu.VMEM((1, whole, LANES), F32)] * 3
+            + [pltpu.VMEM((width, LANES), F32), pltpu.VMEM((width, wide), F32)],
+            flops=10 * whole * whole * LANES + 4 * whole * width * wide,
             scalars=2,
+            room=28,
         )
-        return out if fast else by_batch_bit(jnp.concatenate(out, axis=0), per)
+        if fast:
+            return out
+        return list(out[:2]) + by_batch_bit(jnp.concatenate(out[2:], axis=0), per)
 
     rest = (sidx, bidx, per, block, chip, hidden, cols, count, extra, width)
     reduce_all = reduce_eight if fast else reduce_any
     out_fc2, out_out, out_fc1, out_qkv, vec, gpat, gspe = reduce_all(
-        rest, pairs, (fc2_keep, got2a, got2b), (go_keep, got_o), lse, gatt_x, early,
-        head_grads, norm_part, qkv_part, pay, gmid, gain1,
+        rest, pairs, (fc2_keep, got2a, got2m, got2b), (go_keep, got_o), lse, gatt_x,
+        first_heads, tail_part, pay, gmid, gain1,
     )
     grad_gains = jnp.stack([vec[:, 0], vec[:, 4]])
     grad_shifts = jnp.stack([vec[:, 1], vec[:, 5]])
@@ -806,64 +839,64 @@
 
 
 def reduce_eight(
-    rest, pairs, twos, outs, lse, gatt_x, early, head_grads, norm_part, qkv_part, pay, gmid, gain1
+    rest, pairs, twos, outs, lse, gatt_x, first_heads, tail_part, pay, gmid, gain1
 ):
     sidx, bidx, per, block, chip, hidden, cols, count, extra, width = rest
-    fc2_keep, got2a, got2b = twos
+    fc2_keep, got2a, got2m, got2b = twos
     go_keep, got_o = outs
     wide = 5 * LANES
     deep = hidden // 8
     fc2_keep = fc2_keep.reshape(8, deep, width)
-    got2a = got2a.reshape(2, deep, width)
-    got2b = got2b.reshape(6, deep, width)
-    g0, s0 = head_grads(0, 1, after(lse, gatt_x))
-    g0, got_y2, got2b, got_o = lax.optimization_barrier((g0, pairs[3], got2b, got_o))
+    g01, s01 = first_heads(after(lse, gatt_x))
+    g01, got_y2, got2m, got2b, got_o = lax.optimization_barrier((g01, pairs[3], got2m, got2b, got_o))
     keep_own, keep_oth, got_y1 = pairs[:3]
-    msg_x, msg_a, part_b, part_o, part_a = call(
+    msg_z, msg_y, msg_x, part_f, part_a, part_o = call(
         stage1_kernel,
-        [SDS((20, per, width), BF16), SDS((4, deep, width), BF16)]
-        + [SDS((16, per, width), F32), SDS((4, per, width), F32), SDS((4, deep, width), F32)],
-        (bidx, keep_own, keep_oth, got_y1, got_y2, fc2_keep, got2a, got2b, go_keep, got_o),
+        [SDS((16, per, width), BF16), SDS((4, deep, width), BF16), SDS((4, per, width), BF16)]
+        + [SDS((16, per, width), F32), SDS((4, deep, width), F32), SDS((4, per, width), F32)],
+        (bidx, keep_own, keep_oth, got_y1, got_y2, fc2_keep, got2a, got2m, got2b, go_keep, got_o),
         scalars=1,
     )
-    msg_x, msg_a, lse = lax.optimization_barrier((msg_x, msg_a, after(lse, g0)))
+    msg_z, msg_y, msg_x, lse = lax.optimization_barrier((msg_z, msg_y, msg_x, after(lse, g01)))
+    got_z = swap("batch", msg_z, 2)
+    got_y = swap("batch", msg_y, 1)
     got_x = swap_seq(msg_x, 2)
-    got_a = swap("batch", msg_a, 1)
-    g12, s12 = head_grads(1, 2, lse)
-    g12, got_x, got_a = lax.optimization_barrier((g12, got_x, got_a))
-
-    gn1_keep, gn1_send = norm_part(g0, g12)
+    gn1_keep, gn1_send, q_send, q_keep = tail_part(lse, g01, s01)
+    gn1_send, q_send, got_x, got_y, got_z = lax.optimization_barrier((gn1_send, q_send, got_x, got_y, got_z))
     gn1_c = swap_seq(gn1_send, 1)
-    q_send, q_keep = qkv_part(g0, s0, g12, s12, after(early, gn1_send))
-    q_send, gn1_c, got_x, got_a = lax.optimization_barrier((q_send, gn1_c, got_x, got_a))
     got_q = swap("batch", q_send, 1)
-    (xsend,) = call(shift_kernel, [SDS((block, width), BF16)], (gn1_keep, gn1_c))
+    msg_x, msg_z, part_g, part_c = call(
+        stage2_kernel,
+        [SDS((8, per, width), BF16), SDS((2, per + deep, width), BF16)]
+        + [SDS((8, per, width), F32), SDS((2, per + deep, width), F32)],
+        (part_f, got_z, part_a, got_y, part_o, got_x),
+    )
+    got_x = swap_seq(msg_x, 2)
+    got_z = swap("batch", msg_z, 2)
+    (xsend,) = call(shift_kernel, [SDS((block, width), BF16)], (after(gn1_keep, msg_x), gn1_c))
     gn1_x = swap_seq(xsend, 2)
-    quarter = SDS((5 * per + deep, width), BF16)
-    z1, z2, z3, kept = call(
-        stage2_kernel,
-        [quarter, quarter, quarter, SDS(quarter.shape, F32)],
-        (bidx, part_b, part_o, part_a, got_x, got_a),
-        scalars=1,
-    )
-    got_z = swap_four((z1, z2, z3), 1)
+    msg, kept = call(
+        stage3_kernel,
+        [SDS((5 * per + deep, width), BF16), SDS((5 * per + deep, width), F32)],
+        (part_g, after(got_x, xsend), part_c, got_z),
+    )
+    got_last = swap("batch", msg, 4)
+    got_q = after(got_q, msg)
+    quarter = SDS((4, per, wide), BF16)
+    q1, q2, q3, q_kept = call(
+        quarter_kernel, [quarter, quarter, quarter, SDS(quarter.shape, F32)], (bidx, q_keep, got_q), scalars=1
+    )
+    got_qz = swap_four((q1, q2, q3), 1)
     gpat, gspe = call(
         final_kernel,
         [SDS((count, width), F32), SDS((extra, width), F32)],
-        (gn1_keep, gn1_c, after(gn1_x, z1), pay, gmid, gain1),
-    )
-    got_q = after(got_q, gpat)
-    quarter = SDS((4, per, wide), BF16)
-    q1, q2, q3, q_kept = call(
-        quarter_kernel, [quarter, quarter, quarter, SDS(quarter.shape, F32)], (bidx, q_keep, got_q), scalars=1
-    )
-    (q1, q2, q3), got_z = lax.optimization_barrier(((q1, q2, q3), got_z))
-    got_qz = swap_four((q1, q2, q3), 1)
+        (gn1_keep, gn1_c, after(gn1_x, q1), pay, gmid, gain1),
+    )
+    got_last = after(got_last, gpat)
     swap_send, swap_keep, out_fc2, out_out = call(
         sums_kernel,
         [SDS((2 * per, width), BF16), SDS((2 * per, width), F32), SDS((deep, width), F32), SDS((per, width), F32)],
-        (sidx, kept, *got_z),
-        scalars=1,
+        (kept, got_last),
     )
     swap_got = swap_seq(swap_send, 1)
     row = SDS((per, wide), BF16)
@@ -882,20 +915,19 @@
 
 
 def reduce_any(
-    rest, pairs, twos, outs, lse, gatt_x, early, head_grads, norm_part, qkv_part, pay, gmid, gain1
+    rest, pairs, twos, outs, lse, gatt_x, first_heads, tail_part, pay, gmid, gain1
 ):
     sidx, bidx, per, block, chip, hidden, cols, count, extra, width = rest
     s = lax.axis_index("seq")
     nb = lax.axis_size("batch")
     nbits = bits_of("batch")
     low = nbits - 1
-    fc2_keep, got2a, got2b = twos
+    fc2_keep, got2a, got2m, got2b = twos
     go_keep, got_o = outs
     keep_own, keep_oth, got_oth, got_own = [
         split_bits(p.reshape(2, 2, nb // 2, per, hidden), 2, low) for p in pairs
     ]
-    g0, s0 = head_grads(0, 1, lse)
-    g12, s12 = head_grads(1, 2, lse)
+    g01, s01 = first_heads(lse)
     send_own, parts_own = to_send([keep_own, got_own], 0, 1, "seq")
     send_oth, parts_oth = to_send([keep_oth, got_oth], 0, 1, "seq")
     got_b = swap_seq(jnp.concatenate([send_own, send_oth], axis=-1), 2)
@@ -906,13 +938,13 @@
     got = swap_seq(other.astype(BF16), 1).astype(F32)
     rel = jnp.stack([pick(sum_own, own_c, 0), got[:, :hidden], pick(sum_oth, own_c, 0), got[:, hidden:]])
     out_fc1 = jnp.concatenate([pick(rel, s ^ a, 0) for a in range(4)], axis=1)
-    got2 = jnp.concatenate([got2a, got2b], axis=0)
+    got2 = jnp.concatenate([got2a, got2m, got2b], axis=0)
     parts = [split_bits(p.reshape(nb, -1, width), 0, nbits) for p in (fc2_keep, got2)]
     out_fc2 = sum_rest(parts, 0, 0)
     parts = [split_bits(p.reshape(2, nb // 2, per, width), 1, low) for p in (go_keep, got_o)]
     parts = [p[0] for p in parts] + [swap_seq(total([p[1] for p in parts]).astype(BF16), 2)]
     out_out = sum_rest(parts, 0, 1)
-    gn1_keep, gn1_send = norm_part(g0, g12)
+    gn1_keep, gn1_send, q_send, q_keep = tail_part(lse, g01, s01)
     gn1_c = swap_seq(gn1_send, 1)
     gn1_x = swap_seq((gn1_keep[block:] + gn1_c[block:].astype(F32)).astype(BF16), 2)
     gpat, gspe = call(
@@ -920,7 +952,6 @@
         [SDS((count, width), F32), SDS((extra, width), F32)],
         (gn1_keep, gn1_c, gn1_x, pay, gmid, gain1),
     )
-    q_send, q_keep = qkv_part(g0, s0, g12, s12, early)
     wide = 5 * LANES
     parts = [split_bits(p.reshape(4, nb // 2, per, wide), 1, low) for p in (q_keep, swap("batch", q_send, 1))]
     sum_q = sum_rest(parts, 1, 1)

time: 175 us -> 159 us (0.909)
  waiting for transfers between devices: 60.8 us -> 48.3 us
  local copies, waits for them, and re-layouts: 15.9 us -> 13.6 us
    ppermute x30 -> x32, waiting for transfers between devices: 60.8 us -> 48.3 us  [swap(): lax.ppermute(v, kind, [(i, i ^ mask) for i in range(lax.axis_size(kind))])]
    unnamed x50 -> x44, local copies, waits for them, and re-layouts: 3.69 us -> 1.33 us
    ppermute x30 -> x32, starting transfers between devices: 32.2 us -> 30.8 us  [swap(): lax.ppermute(v, kind, [(i, i ^ mask) for i in range(lax.axis_size(kind))])]
    pallas_call x19 -> x18, Pallas kernels: 60.1 us -> 60.4 us  [call(): pl.pallas_call(kernel, out_shape=outs, in_specs=[smem()] * scalars + [vme...]
  transfers between devices with their start and end apart: 30 -> 32, of which waited for: 19 -> 16; matrix products, arithmetic and copies ran while one was open for 6% -> 7% of each run, Pallas kernels for 28% -> 32%
where the time goes in v4:
time: 159 us
  Pallas kernels  60.4 us (38%)
  waiting for transfers between devices  48.3 us (30%)
  starting transfers between devices  30.8 us (19%)
  local copies, waits for them, and re-layouts  13.6 us (9%)
  other arithmetic  4.37 us (3%)
    pallas_call x18, Pallas kernels, call(): pl.pallas_call(kernel, out_shape=outs, in_specs=[smem()] * scalars + [vme...  60.4 us
    ppermute x32, waiting for transfers between devices, swap(): lax.ppermute(v, kind, [(i, i ^ mask) for i in range(lax.axis_size(kind))])  48.3 us
    ppermute x32, starting transfers between devices, swap(): lax.ppermute(v, kind, [(i, i ^ mask) for i in range(lax.axis_size(kind))])  30.8 us
    dynamic_slice x1, local copies, waits for them, and re-layouts, body(): lax.dynamic_slice(w_fc2, ((s ^ j) * hidden, 0), (hidden, width))  4.96 us
  transfers between devices with their start and end apart: 32, of which 16 were waited for; matrix products, arithmetic and copies ran while one was open for 7% of the time, Pallas kernels for 32%

profile of v4, /device:TPU:0, one launch (start us, length us, event | category | flops | bytes accessed | tf_op | source)
XLA Modules:
  0.0 158.5 jit_solution(12539025742954714616)
XLA Ops:
  0.7 0.7 and_select_fusion
  1.4 0.8 pad_add_fusion
  2.2 1.1 pad_maximum_fusion.p0
  3.3 3.0 %collective-permute-start.1 = (bf16[288,896]{1,0:T(8,128)(2,1)S(1)}, bf16[288,896]{1,0:T(8,128)(2,1)}, u32[]{:S(2)}, u32[]{:S(2)}) collective-permute-start(bf16[288,896]{1,0:T(8,128)(2,1)S(1)} %pad_maximum_fusion.p0), channel_id=1, source_target_pairs={{0,16},{8,24},{16,0},{24,8},{1,17},{9,25},{17,1},{25,9},{2,18},{10... | collective-permute-start | bytes 1548296 | tf_op jit(solution)/shard_map/ppermute | solution.py:597
  6.8 2.9 %constant_dynamic-slice_fusion.10 = (bf16[768,64]{1,0:T(8,128)(2,1)S(1)}, bf16[768,64]{1,0:T(8,128)(2,1)S(1)}, bf16[768,64]{1,0:T(8,128)(2,1)S(1)}, bf16[768,64]...) fusion(bf16[768,2304]{1,0:T(8,128)(2,1)} %param.22, ...), kind=kLoop, calls=%fused_computation.21 | loop fusion | bytes 1769508 | tf_op jit(solution)/shard_map/dynamic_slice | solution.py:696
  9.7 0.7 broadcast_in_dim.31
  10.4 2.3 %concatenate.21.w = bf16[768,640]{1,0:T(8,128)(2,1)S(1)} concatenate(bf16[768,64]{1,0:T(8,128)(2,1)} %get-tuple-element.265, bf16[768,64]{1,0:T(8,128)(2,1)S(1)} %get-tuple-element.264, bf16[768,64]{1,0:T(8,128)(2,1)S(1)} %get-tuple-element.263, bf16[768,64]{1,0:T(8,128)(2,1)S(1)} %get-tuple-element.262, bf16[768,64]{1,0:T(8,128)(2,1)S(1)} %get-tuple-element.261, ...), dimensions={1} | concatenate | bytes 1966080 | tf_op jit(solution)/shard_map/concatenate | solution.py:697
  12.7 5.0 %constant_dynamic-slice_fusion = (bf16[768,768]{1,0:T(8,128)(2,1)}, bf16[768,768]{1,0:T(8,128)(2,1)}, bf16[768,768]{1,0:T(8,128)(2,1)}, bf16[768,768]{1,0:T(8,128)(2,1)}) fusion(bf16[3072,768]{1,0:T(8,128)(2,1)} %param.27, s32[]{:T(128)S(6)} %select_n.68, s32[]{:T(128)S(6)} %select_n.67, bf16[768,3072]{1,0:T(8,128)(2,1)} %param.25), kind=kLoop, calls=%fused_computation.11 | loop fusion | bytes 9437192 | tf_op jit(solution)/shard_map/dynamic_slice | solution.py:702
  17.7 0.5 collective-permute-done.1.p2
  18.2 0.6 collective-permute-start.6
  18.8 1.5 collective-permute-done.2.p3
  20.3 11.3 %shard_map.238 = (bf16[3,1152,128]{2,1,0:T(8,128)(2,1)S(1)}, bf16[3,1152,128]{2,1,0:T(8,128)(2,1)S(1)}, bf16[3,1152,128]{2,1,0:T(8,128)(2,1)S(1)}, f32[3,3,8,384...) custom-call(bf16[288,896]{1,0:T(8,128)(2,1)S(1)} %pad_maximum_fusion, ...), custom_call_target="tpu_custom_call" | custom-call | flops 2548039680 | bytes 7885312 | tf_op jit(solution)/shard_map/pallas_call | solution.py:76
  31.6 1.2 copy-done.13
  32.9 1.7 %collective-permute-start.4 = (bf16[576,192]{1,0:T(8,128)(2,1)S(1)}, bf16[576,192]{1,0:T(8,128)(2,1)S(1)}, u32[]{:S(2)}, u32[]{:S(2)}) collective-permute-start(bf16[576,192]{1,0:T(8,128)(2,1)S(1)} %get-tuple-element.138), channel_id=1, source_target_pairs={{0,16},{8,24},{16,0},{24,8},{1,17},{9,25},{17,1},{25,9},{2,18},{10... | collective-permute-start | bytes 663560 | tf_op jit(solution)/shard_map/ppermute | solution.py:597
  34.6 4.8 %shard_map.239 = (bf16[576,192]{1,0:T(8,128)(2,1)}, f32[3,3,8,384]{3,2,1,0:T(8,128)S(1)}) custom-call(bf16[3,1152,128]{2,1,0:T(8,128)(2,1)S(1)} %get-tuple-element.132.qa, bf16[3,1152,128]{2,1,0:T(8,128)(2,1)S(1)} %get-tuple-element.133.ka, bf16[3,1152,128]{2,1,0:T(8,128)(2,1)S(1)} %get-tuple-element.134.va, f32[3,3,8,384]{3,2,1,0:T(8,128)S(1)} %get-tuple-element.135.lse_in, ...), custom_call_target="tpu_custom_call" | custom-call | flops 509607936 | bytes 3170304 | tf_op jit(solution)/shard_map/pallas_call | solution.py:76
  39.5 2.4 %collective-permute-done.4.a2 = bf16[576,192]{1,0:T(8,128)(2,1)S(1)} collective-permute-done((bf16[576,192]{1,0:T(8,128)(2,1)S(1)}, bf16[576,192]{1,0:T(8,128)(2,1)S(1)}, u32[]{:S(2)}, u32[]{:S(2)}) %collective-permute-start.4) | collective-permute-done | bytes 221216 | tf_op jit(solution)/shard_map/ppermute | solution.py:597
  41.9 1.7 %collective-permute-done.5.a3 = bf16[576,192]{1,0:T(8,128)(2,1)} collective-permute-done((bf16[576,192]{1,0:T(8,128)(2,1)S(1)}, bf16[576,192]{1,0:T(8,128)(2,1)}, u32[]{:S(2)}, u32[]{:S(2)}) %collective-permute-start.5) | collective-permute-done | bytes 221216 | tf_op jit(solution)/shard_map/ppermute | solution.py:597
  43.7 3.1 %shard_map.240 = (f32[576,768]{1,0:T(8,128)S(1)}, bf16[576,768]{1,0:T(8,128)(2,1)S(1)}, bf16[576,768]{1,0:T(8,128)(2,1)S(1)}) custom-call(s32[1]{0:T(128)} %bitcast.sref, bf16[576,192]{1,0:T(8,128)(2,1)} %get-tuple-element.137.a0, bf16[576,192]{1,0:T(8,128)(2,1)} %collective-permute-done.3.a1, bf16[576,192]{1,0:T(8,128)(2,1)S(1)} %collective-permute-done.4.a2, ...), custom_call_target="tpu_custom_call" | custom-call | flops 679477248 | bytes 7533572 | tf_op jit(solution)/shard_map/pallas_call | solution.py:76
  46.9 5.1 %shard_map.241 = (bf16[8,24,768]{2,1,0:T(8,128)(2,1)S(1)}, bf16[8,24,768]{2,1,0:T(8,128)(2,1)S(1)}, bf16[8,48,768]{2,1,0:T(8,128)(2,1)S(1)}, bf16[8,24,768]{2,1,...) custom-call(s32[1]{0:T(128)} %bitcast.sref, ...), custom_call_target="tpu_custom_call" | custom-call | flops 4076863488 | bytes 10033160 | tf_op jit(solution)/shard_map/pallas_call | solution.py:76
  52.0 1.8 %collective-permute-start.7 = (bf16[8,24,768]{2,1,0:T(8,128)(2,1)S(1)}, bf16[8,24,768]{2,1,0:T(8,128)(2,1)S(1)}, u32[]{:S(2)}, u32[]{:S(2)}) collective-permute-start(bf16[8,24,768]{2,1,0:T(8,128)(2,1)S(1)} %get-tuple-element.156), channel_id=1, source_target_pairs={{0,16},{8,24},{16,0},{24,8},{1,17},{9,25},{17,1},{25,9},{2,18},{10... | collective-permute-start | bytes 884744 | tf_op jit(solution)/shard_map/ppermute | solution.py:597
  53.8 1.5 collective-permute-start.8
  55.3 5.2 %shard_map.242 = (bf16[768,768]{1,0:T(8,128)(2,1)S(1)}, bf16[24,24,768]{2,1,0:T(8,128)(2,1)S(1)}, bf16[16,24,768]{2,1,0:T(8,128)(2,1)S(1)}, f32[1,768]{1,0:T(1,1...) custom-call(s32[1]{0:T(128)} %bitcast.sref, ...), custom_call_target="tpu_custom_call" | custom-call | flops 4076863488 | bytes 14604296 | tf_op jit(solution)/shard_map/pallas_call | solution.py:76
  60.5 0.6 collective-permute-done.7.g2a
  61.1 1.5 collective-permute-done.8.y1
  62.6 0.5 collective-permute-start.10
  63.1 1.5 collective-permute-start.12
  64.6 0.4 collective-permute-done.9.gn_got
  65.0 2.0 %shard_map.243 = (f32[288,768]{1,0:T(8,128)S(1)}, bf16[576,768]{1,0:T(8,128)(2,1)S(1)}, bf16[576,192]{1,0:T(8,128)(2,1)S(1)}, f32[8,768]{1,0:T(8,128)S(1)}) custom-call(s32[1]{0:T(128)} %bitcast.sref, f32[576,768]{1,0:T(8,128)S(1)} %get-tuple-element.151.gn_keep, bf16[576,768]{1,0:T(8,128)(2,1)S(1)} %collective-permute-done.9.gn_got, ...), custom_call_target="tpu_custom_call" | custom-call | flops 169869312 | bytes 10427396 | tf_op jit(solution)/shard_map/pallas_call | solution.py:76
  67.0 0.4 collective-permute-start.11
  67.5 2.8 %shard_map.244 = (bf16[576,192]{1,0:T(8,128)(2,1)S(1)}, bf16[2,4,24,768]{3,2,1,0:T(8,128)(2,1)S(1)}, bf16[2,4,24,768]{3,2,1,0:T(8,128)(2,1)S(1)}, f32[768,128]{1...) custom-call(s32[1]{0:T(128)} %bitcast.sref, s32[1]{0:T(128)} %bitcast.1.bref, ...), custom_call_target="tpu_custom_call" | custom-call | flops 509607936 | bytes 7767048 | tf_op jit(solution)/shard_map/pallas_call | solution.py:76
  70.2 5.9 %collective-permute-done.11.gx = bf16[576,192]{1,0:T(8,128)(2,1)S(1)} collective-permute-done((bf16[576,192]{1,0:T(8,128)(2,1)S(1)}, bf16[576,192]{1,0:T(8,128)(2,1)S(1)}, u32[]{:S(2)}, u32[]{:S(2)}) %collective-permute-start.11) | collective-permute-done | bytes 221216 | tf_op jit(solution)/shard_map/ppermute | solution.py:597
  76.1 0.4 collective-permute-start.14
  76.5 1.7 %collective-permute-start.13 = (bf16[8,24,768]{2,1,0:T(8,128)(2,1)S(1)}, bf16[8,24,768]{2,1,0:T(8,128)(2,1)S(1)}, u32[]{:S(2)}, u32[]{:S(2)}) collective-permute-start(bf16[8,24,768]{2,1,0:T(8,128)(2,1)S(1)} %get-tuple-element.181), channel_id=1, source_target_pairs={{0,16},{8,24},{16,0},{24,8},{1,17},{9,25},{17,1},{25,9},{2,18},{10... | collective-permute-start | bytes 884744 | tf_op jit(solution)/shard_map/ppermute | solution.py:597
  78.2 1.5 collective-permute-start.15
  79.7 11.1 %shard_map.245 = (bf16[2,1152,192]{2,1,0:T(8,128)(2,1)S(1)}, f32[2,1,192]{2,1,0:T(1,128)S(1)}) custom-call(bf16[3,1152,128]{2,1,0:T(8,128)(2,1)S(1)} %copy-done.8, bf16[3,1152,128]{2,1,0:T(8,128)(2,1)S(1)} %copy-done.10, bf16[3,1152,128]{2,1,0:T(8,128)(2,1)S(1)} %copy-done.12, f32[3,3,8,384]{3,2,1,0:T(8,128)S(1)} %get-tuple-element.195.lse, ...), custom_call_target="tpu_custom_call" | custom-call | flops 3397386240 | bytes 4093440 | tf_op jit(solution)/shard_map/pallas_call | solution.py:76
  90.8 6.2 %collective-permute-done.13.g2m = bf16[8,24,768]{2,1,0:T(8,128)(2,1)S(1)} collective-permute-done((bf16[8,24,768]{2,1,0:T(8,128)(2,1)S(1)}, bf16[8,24,768]{2,1,0:T(8,128)(2,1)S(1)}, u32[]{:S(2)}, u32[]{:S(2)}) %collective-permute-start.13) | collective-permute-done | bytes 294944 | tf_op jit(solution)/shard_map/ppermute | solution.py:597
  97.0 0.6 shard_map.246
  97.6 1.6 collective-permute-start.17
  99.2 1.6 collective-permute-start.18
  100.8 0.5 collective-permute-start.16
  101.3 10.5 %shard_map.247 = (f32[576,768]{1,0:T(8,128)S(1)}, bf16[576,768]{1,0:T(8,128)(2,1)S(1)}, bf16[16,24,640]{2,1,0:T(8,128)(2,1)S(1)}, bf16[16,24,640]{2,1,0:T(8,128)(2,1)S(1)}) custom-call(s32[1]{0:T(128)} %bitcast.sref, s32[1]{0:T(128)} %bitcast.1.bref, bf16[3,1152,128]{2,1,0:T(8,128)(2,1)S(1)} %copy-done.8, bf16[3,1152,128]{2,1,0:T(8,128)(2,1)S(1)} %copy-done.10, ...), custom_call_target="tpu_custom_call" | custom-call | flops 3963617280 | bytes 10876424 | tf_op jit(solution)/shard_map/pallas_call | solution.py:76
  111.9 0.7 collective-permute-done.18.got_z
  112.8 1.6 %collective-permute-start.23 = (bf16[2,120,768]{2,1,0:T(8,128)(2,1)S(1)}, bf16[2,120,768]{2,1,0:T(8,128)(2,1)S(1)}, u32[]{:S(2)}, u32[]{:S(2)}) collective-permute-start(bf16[2,120,768]{2,1,0:T(8,128)(2,1)S(1)} %get-tuple-element.219), channel_id=1, source_target_pairs={{0,2},{1,3},{2,0},{3,1},{4,6},{5,7},{6,4},{7,5},{8,10},{9,11},{10,... | collective-permute-start | bytes 1105928 | tf_op jit(solution)/shard_map/ppermute | solution.py:597
  114.4 0.5 collective-permute-start.22
  114.9 0.5 collective-permute-start.21
  115.5 1.6 collective-permute-start.20
  117.1 7.2 %collective-permute-done.22.got_x = bf16[8,24,768]{2,1,0:T(8,128)(2,1)S(1)} collective-permute-done((bf16[8,24,768]{2,1,0:T(8,128)(2,1)S(1)}, bf16[8,24,768]{2,1,0:T(8,128)(2,1)S(1)}, u32[]{:S(2)}, u32[]{:S(2)}) %collective-permute-start.22) | collective-permute-done | bytes 294944 | tf_op jit(solution)/shard_map/ppermute | solution.py:597
  124.4 2.6 %collective-permute-start.27 = (bf16[216,768]{1,0:T(8,128)(2,1)S(1)}, bf16[216,768]{1,0:T(8,128)(2,1)S(1)}, u32[]{:S(2)}, u32[]{:S(2)}) collective-permute-start(bf16[216,768]{1,0:T(8,128)(2,1)S(1)} %get-tuple-element.220), channel_id=1, source_target_pairs={{0,4},{1,5},{2,6},{3,7},{4,0},{5,1},{6,2},{7,3},{8,12},{9,13},{10,... | collective-permute-start | bytes 995336 | tf_op jit(solution)/shard_map/ppermute | solution.py:597
  127.0 1.0 collective-permute-done.21.got
  128.1 2.6 %collective-permute-start.25 = (bf16[4,24,640]{2,1,0:T(8,128)(2,1)S(1)}, bf16[4,24,640]{2,1,0:T(8,128)(2,1)S(1)}, u32[]{:S(2)}, u32[]{:S(2)}) collective-permute-start(bf16[4,24,640]{2,1,0:T(8,128)(2,1)S(1)} %get-tuple-element.228), channel_id=1, source_target_pairs={{0,4},{1,5},{2,6},{3,7},{4,0},{5,1},{6,2},{7,3},{8,12},{9,13},{10,... | collective-permute-start | bytes 368648 | tf_op jit(solution)/shard_map/ppermute | solution.py:597
  130.8 0.6 collective-permute-start.26
  131.7 1.3 collective-permute-done.20.x0
  133.0 1.5 shard_map.252
  134.6 13.3 %collective-permute-done.27.got = bf16[216,768]{1,0:T(8,128)(2,1)S(1)} collective-permute-done((bf16[216,768]{1,0:T(8,128)(2,1)S(1)}, bf16[216,768]{1,0:T(8,128)(2,1)S(1)}, u32[]{:S(2)}, u32[]{:S(2)}) %collective-permute-start.27) | collective-permute-done | bytes 331808 | tf_op jit(solution)/shard_map/ppermute | solution.py:597
  147.9 0.8 shard_map.253
  148.7 1.8 %collective-permute-done.25.z2 = bf16[4,24,640]{2,1,0:T(8,128)(2,1)S(1)} collective-permute-done((bf16[4,24,640]{2,1,0:T(8,128)(2,1)S(1)}, bf16[4,24,640]{2,1,0:T(8,128)(2,1)S(1)}, u32[]{:S(2)}, u32[]{:S(2)}) %collective-permute-start.25) | collective-permute-done | bytes 122912 | tf_op jit(solution)/shard_map/ppermute | solution.py:597
  150.7 0.6 collective-permute-start.29
  151.3 1.3 collective-permute-start.30
  152.6 2.3 %collective-permute-done.29.g2 = bf16[24,640]{1,0:T(8,128)(2,1)S(1)} collective-permute-done((bf16[24,640]{1,0:T(8,128)(2,1)S(1)}, bf16[24,640]{1,0:T(8,128)(2,1)S(1)}, u32[]{:S(2)}, u32[]{:S(2)}) %collective-permute-start.29) | collective-permute-done | bytes 30752 | tf_op jit(solution)/shard_map/ppermute | solution.py:597
  154.9 0.9 shard_map.255
  156.2 0.6 reshape.58
  156.8 0.6 pad_maximum_fusion.4
  157.3 0.6 pad_maximum_fusion.3
  157.9 0.6 pad_maximum_fusion.2
  (93 shorter events, 2.2 us)
Async XLA Ops:
  0.6 5.7 %copy-start.16 = (f32[4,768]{1,0:T(4,128)S(1)}, f32[4,768]{1,0:T(4,128)}, u32[]{:S(2)}) copy-start(f32[4,768]{1,0:T(4,128)} %param.23) | copy-start | bytes 36868
  0.7 5.7 %copy-start.20 = (f32[3072]{0:T(1024)S(1)}, f32[3072]{0:T(1024)}, u32[]{:S(2)}) copy-start(f32[3072]{0:T(1024)} %param.26) | copy-start | bytes 36868
  0.7 5.8 %copy-start.21 = (s32[1,16]{1,0:T(1,128)S(1)}, s32[1,16]{1,0:T(1,128)}, u32[]{:S(2)}) copy-start(s32[1,16]{1,0:T(1,128)} %param.19) | copy-start | bytes 196
  3.3 14.9 %collective-permute-start.1 = (bf16[288,896]{1,0:T(8,128)(2,1)S(1)}, bf16[288,896]{1,0:T(8,128)(2,1)}, u32[]{:S(2)}, u32[]{:S(2)}) collective-permute-start(bf16[288,896]{1,0:T(8,128)(2,1)S(1)} %pad_maximum_fusion.p0), channel_id=1, source_target_pairs={{0,16},{8,24},{16,0},{24,8},{1,17},{9,25},{17,1},{25,9},{2,18},{10... | collective-permute-start | bytes 1548296 | tf_op jit(solution)/shard_map/ppermute | solution.py:597
  6.3 12.5 %collective-permute-start = (bf16[288,896]{1,0:T(8,128)(2,1)S(1)}, bf16[288,896]{1,0:T(8,128)(2,1)S(1)}, u32[]{:S(2)}, u32[]{:S(2)}) collective-permute-start(bf16[288,896]{1,0:T(8,128)(2,1)S(1)} %pad_maximum_fusion.p0), channel_id=1, source_target_pairs={{0,8},{8,0},{16,24},{24,16},{1,9},{9,1},{17,25},{25,17},{2,10},{10... | collective-permute-start | bytes 1548296 | tf_op jit(solution)/shard_map/ppermute | solution.py:597
  12.7 7.6 %copy-start.5 = (bf16[768,640]{1,0:T(8,128)(2,1)}, bf16[768,640]{1,0:T(8,128)(2,1)S(1)}, u32[]{:S(2)}) copy-start(bf16[768,640]{1,0:T(8,128)(2,1)S(1)} %concatenate.21.w) | copy-start | bytes 2949124
  12.7 5.5 %copy-start.15 = (bf16[1,256,768]{2,1,0:T(8,128)(2,1)S(1)}, bf16[1,256,768]{2,1,0:T(8,128)(2,1)}, u32[]{:S(2)}) copy-start(bf16[1,256,768]{2,1,0:T(8,128)(2,1)} %param.28) | copy-start | bytes 1179652
  12.7 5.5 %copy-start.17 = (bf16[1,4,768]{2,1,0:T(4,128)(2,1)S(1)}, bf16[1,4,768]{2,1,0:T(4,128)(2,1)}, u32[]{:S(2)}) copy-start(bf16[1,4,768]{2,1,0:T(4,128)(2,1)} %param.29) | copy-start | bytes 18436
  12.7 6.1 %copy-start.18 = (f32[2,768]{1,0:T(2,128)S(1)}, f32[2,768]{1,0:T(2,128)}, u32[]{:S(2)}) copy-start(f32[2,768]{1,0:T(2,128)} %param.21) | copy-start | bytes 18436
  12.7 6.1 %copy-start.19 = (f32[2,768]{1,0:T(2,128)S(1)}, f32[2,768]{1,0:T(2,128)}, u32[]{:S(2)}) copy-start(f32[2,768]{1,0:T(2,128)} %param.20) | copy-start | bytes 18436
  18.2 2.1 %collective-permute-start.2 = (bf16[288,896]{1,0:T(8,128)(2,1)}, bf16[288,896]{1,0:T(8,128)(2,1)S(1)}, u32[]{:S(2)}, u32[]{:S(2)}) collective-permute-start(bf16[288,896]{1,0:T(8,128)(2,1)} %collective-permute-done.1.p2), channel_id=1, source_target_pairs={{0,8},{8,0},{16,24},{24,16},{1,9},{9,1},{17,25},{25,17},{2,10},{10... | collective-permute-start | bytes 1548296 | tf_op jit(solution)/shard_map/ppermute | solution.py:597
  18.2 23.7 %collective-permute-start.6 = (bf16[288,768]{1,0:T(8,128)(2,1)S(1)}, bf16[288,768]{1,0:T(8,128)(2,1)S(1)}, u32[]{:S(2)}, u32[]{:S(2)}) collective-permute-start(bf16[288,768]{1,0:T(8,128)(2,1)S(1)} %pad_maximum_fusion.1.c0), channel_id=1, source_target_pairs={{0,8},{8,0},{16,24},{24,16},{1,9},{9,1},{17,25},{25,17},{2,10},{10... | collective-permute-start | bytes 1327112 | tf_op jit(solution)/shard_map/ppermute | solution.py:597
  31.6 1.3 copy-start.13
  32.9 6.6 %copy-start.7 = (bf16[3,1152,128]{2,1,0:T(8,128)(2,1)}, bf16[3,1152,128]{2,1,0:T(8,128)(2,1)S(1)}, u32[]{:S(2)}) copy-start(bf16[3,1152,128]{2,1,0:T(8,128)(2,1)S(1)} %get-tuple-element.132.qa) | copy-start | bytes 2654212
  32.9 6.6 %copy-start.9 = (bf16[3,1152,128]{2,1,0:T(8,128)(2,1)}, bf16[3,1152,128]{2,1,0:T(8,128)(2,1)S(1)}, u32[]{:S(2)}) copy-start(bf16[3,1152,128]{2,1,0:T(8,128)(2,1)S(1)} %get-tuple-element.133.ka) | copy-start | bytes 2654212
  32.9 6.6 %copy-start.11 = (bf16[3,1152,128]{2,1,0:T(8,128)(2,1)}, bf16[3,1152,128]{2,1,0:T(8,128)(2,1)S(1)}, u32[]{:S(2)}) copy-start(bf16[3,1152,128]{2,1,0:T(8,128)(2,1)S(1)} %get-tuple-element.134.va) | copy-start | bytes 2654212
  32.9 9.1 %collective-permute-start.4 = (bf16[576,192]{1,0:T(8,128)(2,1)S(1)}, bf16[576,192]{1,0:T(8,128)(2,1)S(1)}, u32[]{:S(2)}, u32[]{:S(2)}) collective-permute-start(bf16[576,192]{1,0:T(8,128)(2,1)S(1)} %get-tuple-element.138), channel_id=1, source_target_pairs={{0,16},{8,24},{16,0},{24,8},{1,17},{9,25},{17,1},{25,9},{2,18},{10... | collective-permute-start | bytes 663560 | tf_op jit(solution)/shard_map/ppermute | solution.py:597
  34.6 9.0 %copy-start = (bf16[768,768]{1,0:T(8,128)(2,1)S(1)}, bf16[768,768]{1,0:T(8,128)(2,1)}, u32[]{:S(2)}) copy-start(bf16[768,768]{1,0:T(8,128)(2,1)} %w_out.5) | copy-start | bytes 3538948
  39.4 2.5 %collective-permute-start.3 = (bf16[576,192]{1,0:T(8,128)(2,1)}, bf16[576,192]{1,0:T(8,128)(2,1)}, u32[]{:S(2)}, u32[]{:S(2)}) collective-permute-start(bf16[576,192]{1,0:T(8,128)(2,1)} %get-tuple-element.137.a0), channel_id=1, source_target_pairs={{0,8},{8,0},{16,24},{24,16},{1,9},{9,1},{17,25},{25,17},{2,10},{10... | collective-permute-start | bytes 663560 | tf_op jit(solution)/shard_map/ppermute | solution.py:597
  41.9 1.7 %collective-permute-start.5 = (bf16[576,192]{1,0:T(8,128)(2,1)S(1)}, bf16[576,192]{1,0:T(8,128)(2,1)}, u32[]{:S(2)}, u32[]{:S(2)}) collective-permute-start(bf16[576,192]{1,0:T(8,128)(2,1)S(1)} %collective-permute-done.4.a2), channel_id=1, source_target_pairs={{0,8},{8,0},{16,24},{24,16},{1,9},{9,1},{17,25},{25,17},{2,10},{10... | collective-permute-start | bytes 663560 | tf_op jit(solution)/shard_map/ppermute | solution.py:597
  43.7 3.2 %copy-start.3 = (bf16[768,768]{1,0:T(8,128)(2,1)S(1)}, bf16[768,768]{1,0:T(8,128)(2,1)}, u32[]{:S(2)}) copy-start(bf16[768,768]{1,0:T(8,128)(2,1)} %get-tuple-element.147.fc2) | copy-start | bytes 3538948
  43.7 3.2 %copy-start.4 = (bf16[768,768]{1,0:T(8,128)(2,1)S(1)}, bf16[768,768]{1,0:T(8,128)(2,1)}, u32[]{:S(2)}) copy-start(bf16[768,768]{1,0:T(8,128)(2,1)} %get-tuple-element.145.fc1) | copy-start | bytes 3538948
  46.8 8.5 %copy-start.1 = (bf16[768,768]{1,0:T(8,128)(2,1)S(1)}, bf16[768,768]{1,0:T(8,128)(2,1)}, u32[]{:S(2)}) copy-start(bf16[768,768]{1,0:T(8,128)(2,1)} %get-tuple-element.144.fc2) | copy-start | bytes 3538948
  46.8 8.5 %copy-start.2 = (bf16[768,768]{1,0:T(8,128)(2,1)S(1)}, bf16[768,768]{1,0:T(8,128)(2,1)}, u32[]{:S(2)}) copy-start(bf16[768,768]{1,0:T(8,128)(2,1)} %get-tuple-element.142.fc1) | copy-start | bytes 3538948
  52.0 9.1 %collective-permute-start.7 = (bf16[8,24,768]{2,1,0:T(8,128)(2,1)S(1)}, bf16[8,24,768]{2,1,0:T(8,128)(2,1)S(1)}, u32[]{:S(2)}, u32[]{:S(2)}) collective-permute-start(bf16[8,24,768]{2,1,0:T(8,128)(2,1)S(1)} %get-tuple-element.156), channel_id=1, source_target_pairs={{0,16},{8,24},{16,0},{24,8},{1,17},{9,25},{17,1},{25,9},{2,18},{10... | collective-permute-start | bytes 884744 | tf_op jit(solution)/shard_map/ppermute | solution.py:597
  53.8 8.8 %collective-permute-start.8 = (bf16[8,24,768]{2,1,0:T(8,128)(2,1)S(1)}, bf16[8,24,768]{2,1,0:T(8,128)(2,1)S(1)}, u32[]{:S(2)}, u32[]{:S(2)}) collective-permute-start(bf16[8,24,768]{2,1,0:T(8,128)(2,1)S(1)} %get-tuple-element.157), channel_id=1, source_target_pairs={{0,1},{1,0},{2,3},{3,2},{4,5},{5,4},{6,7},{7,6},{8,9},{9,8},{10,11... | collective-permute-start | bytes 884744 | tf_op jit(solution)/shard_map/ppermute | solution.py:597
  62.6 2.4 %collective-permute-start.9 = (bf16[576,768]{1,0:T(8,128)(2,1)S(1)}, bf16[576,768]{1,0:T(8,128)(2,1)S(1)}, u32[]{:S(2)}, u32[]{:S(2)}) collective-permute-start(bf16[576,768]{1,0:T(8,128)(2,1)S(1)} %get-tuple-element.158), channel_id=1, source_target_pairs={{0,8},{8,0},{16,24},{24,16},{1,9},{9,1},{17,25},{25,17},{2,10},{10... | collective-permute-start | bytes 2654216 | tf_op jit(solution)/shard_map/ppermute | solution.py:597
  62.6 4.9 %collective-permute-start.10 = (bf16[288,768]{1,0:T(8,128)(2,1)S(1)}, bf16[288,768]{1,0:T(8,128)(2,1)S(1)}, u32[]{:S(2)}, u32[]{:S(2)}) collective-permute-start(bf16[288,768]{1,0:T(8,128)(2,1)S(1)} %get-tuple-element.162), channel_id=1, source_target_pairs={{0,8},{8,0},{16,24},{24,16},{1,9},{9,1},{17,25},{25,17},{2,10},{10... | collective-permute-start | bytes 1327112 | tf_op jit(solution)/shard_map/ppermute | solution.py:597
  63.1 33.9 %collective-permute-start.12 = (bf16[24,24,768]{2,1,0:T(8,128)(2,1)S(1)}, bf16[24,24,768]{2,1,0:T(8,128)(2,1)S(1)}, u32[]{:S(2)}, u32[]{:S(2)}) collective-permute-start(bf16[24,24,768]{2,1,0:T(8,128)(2,1)S(1)} %get-tuple-element.180), channel_id=1, source_target_pairs={{0,1},{1,0},{2,3},{3,2},{4,5},{5,4},{6,7},{7,6},{8,9},{9,8},{10,11... | collective-permute-start | bytes 2654216 | tf_op jit(solution)/shard_map/ppermute | solution.py:597
  67.0 9.1 %collective-permute-start.11 = (bf16[576,192]{1,0:T(8,128)(2,1)S(1)}, bf16[576,192]{1,0:T(8,128)(2,1)S(1)}, u32[]{:S(2)}, u32[]{:S(2)}) collective-permute-start(bf16[576,192]{1,0:T(8,128)(2,1)S(1)} %get-tuple-element.172), channel_id=1, source_target_pairs={{0,16},{8,24},{16,0},{24,8},{1,17},{9,25},{17,1},{25,9},{2,18},{10... | collective-permute-start | bytes 663560 | tf_op jit(solution)/shard_map/ppermute | solution.py:597
  67.4 12.2 %copy-start.8 = (bf16[3,1152,128]{2,1,0:T(8,128)(2,1)S(1)}, bf16[3,1152,128]{2,1,0:T(8,128)(2,1)}, u32[]{:S(2)}) copy-start(bf16[3,1152,128]{2,1,0:T(8,128)(2,1)} %copy-done.7) | copy-start | bytes 2654212
  67.4 12.2 %copy-start.10 = (bf16[3,1152,128]{2,1,0:T(8,128)(2,1)S(1)}, bf16[3,1152,128]{2,1,0:T(8,128)(2,1)}, u32[]{:S(2)}) copy-start(bf16[3,1152,128]{2,1,0:T(8,128)(2,1)} %copy-done.9) | copy-start | bytes 2654212
  67.5 12.2 %copy-start.12 = (bf16[3,1152,128]{2,1,0:T(8,128)(2,1)S(1)}, bf16[3,1152,128]{2,1,0:T(8,128)(2,1)}, u32[]{:S(2)}) copy-start(bf16[3,1152,128]{2,1,0:T(8,128)(2,1)} %copy-done.11) | copy-start | bytes 2654212
  76.1 20.9 %collective-permute-start.14 = (bf16[8,48,768]{2,1,0:T(8,128)(2,1)S(1)}, bf16[8,48,768]{2,1,0:T(8,128)(2,1)S(1)}, u32[]{:S(2)}, u32[]{:S(2)}) collective-permute-start(bf16[8,48,768]{2,1,0:T(8,128)(2,1)S(1)} %get-tuple-element.182), channel_id=1, source_target_pairs={{0,16},{8,24},{16,0},{24,8},{1,17},{9,25},{17,1},{25,9},{2,18},{10... | collective-permute-start | bytes 1769480 | tf_op jit(solution)/shard_map/ppermute | solution.py:597
  76.5 20.5 %collective-permute-start.13 = (bf16[8,24,768]{2,1,0:T(8,128)(2,1)S(1)}, bf16[8,24,768]{2,1,0:T(8,128)(2,1)S(1)}, u32[]{:S(2)}, u32[]{:S(2)}) collective-permute-start(bf16[8,24,768]{2,1,0:T(8,128)(2,1)S(1)} %get-tuple-element.181), channel_id=1, source_target_pairs={{0,16},{8,24},{16,0},{24,8},{1,17},{9,25},{17,1},{25,9},{2,18},{10... | collective-permute-start | bytes 884744 | tf_op jit(solution)/shard_map/ppermute | solution.py:597
  78.2 18.8 %collective-permute-start.15 = (bf16[2,4,24,768]{3,2,1,0:T(8,128)(2,1)S(1)}, bf16[2,4,24,768]{3,2,1,0:T(8,128)(2,1)S(1)}, u32[]{:S(2)}, u32[]{:S(2)}) collective-permute-start(bf16[2,4,24,768]{3,2,1,0:T(8,128)(2,1)S(1)} %get-tuple-element.173), channel_id=1, source_target_pairs={{0,1},{1,0},{2,3},{3,2},{4,5},{5,4},{6,7},{7,6},{8,9},{9,8},{10,11... | collective-permute-start | bytes 884744 | tf_op jit(solution)/shard_map/ppermute | solution.py:597
  97.0 4.3 %copy-start.6 = (bf16[768,640]{1,0:T(8,128)(2,1)S(1)}, bf16[768,640]{1,0:T(8,128)(2,1)}, u32[]{:S(2)}) copy-start(bf16[768,640]{1,0:T(8,128)(2,1)} %copy-done.5) | copy-start | bytes 2949124
  97.0 4.3 %copy-start.14 = (bf16[1152,768]{1,0:T(8,128)(2,1)S(1)}, bf16[1152,768]{1,0:T(8,128)(2,1)}, u32[]{:S(2)}) copy-start(bf16[1152,768]{1,0:T(8,128)(2,1)} %copy-done.13) | copy-start | bytes 5308420
  97.6 14.2 %collective-permute-start.17 = (bf16[4,96,768]{2,1,0:T(8,128)(2,1)S(1)}, bf16[4,96,768]{2,1,0:T(8,128)(2,1)S(1)}, u32[]{:S(2)}, u32[]{:S(2)}) collective-permute-start(bf16[4,96,768]{2,1,0:T(8,128)(2,1)S(1)} %get-tuple-element.203), channel_id=1, source_target_pairs={{0,1},{1,0},{2,3},{3,2},{4,5},{5,4},{6,7},{7,6},{8,9},{9,8},{10,11... | collective-permute-start | bytes 1769480 | tf_op jit(solution)/shard_map/ppermute | solution.py:597
  99.2 13.3 %collective-permute-start.18 = (bf16[16,24,768]{2,1,0:T(8,128)(2,1)S(1)}, bf16[16,24,768]{2,1,0:T(8,128)(2,1)S(1)}, u32[]{:S(2)}, u32[]{:S(2)}) collective-permute-start(bf16[16,24,768]{2,1,0:T(8,128)(2,1)S(1)} %get-tuple-element.204), channel_id=1, source_target_pairs={{0,2},{1,3},{2,0},{3,1},{4,6},{5,7},{6,4},{7,5},{8,10},{9,11},{10,... | collective-permute-start | bytes 1769480 | tf_op jit(solution)/shard_map/ppermute | solution.py:597
  100.8 11.1 %collective-permute-start.16 = (bf16[4,24,768]{2,1,0:T(8,128)(2,1)S(1)}, bf16[4,24,768]{2,1,0:T(8,128)(2,1)S(1)}, u32[]{:S(2)}, u32[]{:S(2)}) collective-permute-start(bf16[4,24,768]{2,1,0:T(8,128)(2,1)S(1)} %get-tuple-element.202), channel_id=1, source_target_pairs={{0,16},{8,24},{16,0},{24,8},{1,17},{9,25},{17,1},{25,9},{2,18},{10... | collective-permute-start | bytes 442376 | tf_op jit(solution)/shard_map/ppermute | solution.py:597
  112.6 2.9 %collective-permute-start.19 = (bf16[576,768]{1,0:T(8,128)(2,1)S(1)}, bf16[576,768]{1,0:T(8,128)(2,1)S(1)}, u32[]{:S(2)}, u32[]{:S(2)}) collective-permute-start(bf16[576,768]{1,0:T(8,128)(2,1)S(1)} %get-tuple-element.205), channel_id=1, source_target_pairs={{0,8},{8,0},{16,24},{24,16},{1,9},{9,1},{17,25},{25,17},{2,10},{10... | collective-permute-start | bytes 2654216 | tf_op jit(solution)/shard_map/ppermute | solution.py:597
  112.8 11.5 %collective-permute-start.23 = (bf16[2,120,768]{2,1,0:T(8,128)(2,1)S(1)}, bf16[2,120,768]{2,1,0:T(8,128)(2,1)S(1)}, u32[]{:S(2)}, u32[]{:S(2)}) collective-permute-start(bf16[2,120,768]{2,1,0:T(8,128)(2,1)S(1)} %get-tuple-element.219), channel_id=1, source_target_pairs={{0,2},{1,3},{2,0},{3,1},{4,6},{5,7},{6,4},{7,5},{8,10},{9,11},{10,... | collective-permute-start | bytes 1105928 | tf_op jit(solution)/shard_map/ppermute | solution.py:597
  114.4 9.8 %collective-permute-start.22 = (bf16[8,24,768]{2,1,0:T(8,128)(2,1)S(1)}, bf16[8,24,768]{2,1,0:T(8,128)(2,1)S(1)}, u32[]{:S(2)}, u32[]{:S(2)}) collective-permute-start(bf16[8,24,768]{2,1,0:T(8,128)(2,1)S(1)} %get-tuple-element.212), channel_id=1, source_target_pairs={{0,16},{8,24},{16,0},{24,8},{1,17},{9,25},{17,1},{25,9},{2,18},{10... | collective-permute-start | bytes 884744 | tf_op jit(solution)/shard_map/ppermute | solution.py:597
  114.9 13.1 %collective-permute-start.21 = (bf16[16,24,640]{2,1,0:T(8,128)(2,1)S(1)}, bf16[16,24,640]{2,1,0:T(8,128)(2,1)S(1)}, u32[]{:S(2)}, u32[]{:S(2)}) collective-permute-start(bf16[16,24,640]{2,1,0:T(8,128)(2,1)S(1)} %get-tuple-element.215), channel_id=1, source_target_pairs={{0,1},{1,0},{2,3},{3,2},{4,5},{5,4},{6,7},{7,6},{8,9},{9,8},{10,11... | collective-permute-start | bytes 1474568 | tf_op jit(solution)/shard_map/ppermute | solution.py:597
  115.5 17.5 %collective-permute-start.20 = (bf16[288,768]{1,0:T(8,128)(2,1)S(1)}, bf16[288,768]{1,0:T(8,128)(2,1)S(1)}, u32[]{:S(2)}, u32[]{:S(2)}) collective-permute-start(bf16[288,768]{1,0:T(8,128)(2,1)S(1)} %shard_map.249), channel_id=1, source_target_pairs={{0,16},{8,24},{16,0},{24,8},{1,17},{9,25},{17,1},{25,9},{2,18},{10... | collective-permute-start | bytes 1327112 | tf_op jit(solution)/shard_map/ppermute | solution.py:597
  124.4 23.5 %collective-permute-start.27 = (bf16[216,768]{1,0:T(8,128)(2,1)S(1)}, bf16[216,768]{1,0:T(8,128)(2,1)S(1)}, u32[]{:S(2)}, u32[]{:S(2)}) collective-permute-start(bf16[216,768]{1,0:T(8,128)(2,1)S(1)} %get-tuple-element.220), channel_id=1, source_target_pairs={{0,4},{1,5},{2,6},{3,7},{4,0},{5,1},{6,2},{7,3},{8,12},{9,13},{10,... | collective-permute-start | bytes 995336 | tf_op jit(solution)/shard_map/ppermute | solution.py:597
  128.1 22.4 %collective-permute-start.25 = (bf16[4,24,640]{2,1,0:T(8,128)(2,1)S(1)}, bf16[4,24,640]{2,1,0:T(8,128)(2,1)S(1)}, u32[]{:S(2)}, u32[]{:S(2)}) collective-permute-start(bf16[4,24,640]{2,1,0:T(8,128)(2,1)S(1)} %get-tuple-element.228), channel_id=1, source_target_pairs={{0,4},{1,5},{2,6},{3,7},{4,0},{5,1},{6,2},{7,3},{8,12},{9,13},{10,... | collective-permute-start | bytes 368648 | tf_op jit(solution)/shard_map/ppermute | solution.py:597
  130.8 19.8 %collective-permute-start.26 = (bf16[4,24,640]{2,1,0:T(8,128)(2,1)S(1)}, bf16[4,24,640]{2,1,0:T(8,128)(2,1)S(1)}, u32[]{:S(2)}, u32[]{:S(2)}) collective-permute-start(bf16[4,24,640]{2,1,0:T(8,128)(2,1)S(1)} %get-tuple-element.229), channel_id=1, source_target_pairs={{0,6},{1,7},{2,4},{3,5},{4,2},{5,3},{6,0},{7,1},{8,14},{9,15},{10,... | collective-permute-start | bytes 368648 | tf_op jit(solution)/shard_map/ppermute | solution.py:597
  131.4 19.2 %collective-permute-start.24 = (bf16[4,24,640]{2,1,0:T(8,128)(2,1)S(1)}, bf16[4,24,640]{2,1,0:T(8,128)(2,1)S(1)}, u32[]{:S(2)}, u32[]{:S(2)}) collective-permute-start(bf16[4,24,640]{2,1,0:T(8,128)(2,1)S(1)} %get-tuple-element.222), channel_id=1, source_target_pairs={{0,2},{1,3},{2,0},{3,1},{4,6},{5,7},{6,4},{7,5},{8,10},{9,11},{10,... | collective-permute-start | bytes 368648 | tf_op jit(solution)/shard_map/ppermute | solution.py:597
  148.7 6.2 %collective-permute-start.31 = (bf16[48,768]{1,0:T(8,128)(2,1)S(1)}, bf16[48,768]{1,0:T(8,128)(2,1)S(1)}, u32[]{:S(2)}, u32[]{:S(2)}) collective-permute-start(bf16[48,768]{1,0:T(8,128)(2,1)S(1)} %get-tuple-element.241), channel_id=1, source_target_pairs={{0,8},{8,0},{16,24},{24,16},{1,9},{9,1},{17,25},{25,17},{2,10},{10... | collective-permute-start | bytes 221192 | tf_op jit(solution)/shard_map/ppermute | solution.py:597
  150.6 1.9 %collective-permute-start.28 = (bf16[24,640]{1,0:T(8,128)(2,1)S(1)}, bf16[24,640]{1,0:T(8,128)(2,1)S(1)}, u32[]{:S(2)}, u32[]{:S(2)}) collective-permute-start(bf16[24,640]{1,0:T(8,128)(2,1)S(1)} %get-tuple-element.237), channel_id=1, source_target_pairs={{0,8},{8,0},{16,24},{24,16},{1,9},{9,1},{17,25},{25,17},{2,10},{10... | collective-permute-start | bytes 92168 | tf_op jit(solution)/shard_map/ppermute | solution.py:597
  150.7 4.2 %collective-permute-start.29 = (bf16[24,640]{1,0:T(8,128)(2,1)S(1)}, bf16[24,640]{1,0:T(8,128)(2,1)S(1)}, u32[]{:S(2)}, u32[]{:S(2)}) collective-permute-start(bf16[24,640]{1,0:T(8,128)(2,1)S(1)} %get-tuple-element.238), channel_id=1, source_target_pairs={{0,16},{8,24},{16,0},{24,8},{1,17},{9,25},{17,1},{25,9},{2,18},{10... | collective-permute-start | bytes 92168 | tf_op jit(solution)/shard_map/ppermute | solution.py:597
  151.3 3.6 %collective-permute-start.30 = (bf16[24,640]{1,0:T(8,128)(2,1)S(1)}, bf16[24,640]{1,0:T(8,128)(2,1)S(1)}, u32[]{:S(2)}, u32[]{:S(2)}) collective-permute-start(bf16[24,640]{1,0:T(8,128)(2,1)S(1)} %get-tuple-element.239), channel_id=1, source_target_pairs={{0,24},{8,16},{16,8},{24,0},{1,25},{9,17},{17,9},{25,1},{2,26},{10... | collective-permute-start | bytes 92168 | tf_op jit(solution)/shard_map/ppermute | solution.py:597

commit v5 on v4

v5 whole, which is shorter than its diff:
```python
import functools

import jax
import jax.numpy as jnp
from jax import lax
from jax.experimental import pallas as pl
from jax.experimental.pallas import tpu as pltpu
from jax.sharding import PartitionSpec as P

HEADS = 12
HEAD = 64
PAD = 32
LANES = 128
OWN = 3
FAR = -(2.0**100)
F32 = jnp.float32
BF16 = jnp.bfloat16
SDS = jax.ShapeDtypeStruct


def dot(a, b):
    return jnp.dot(a, b, preferred_element_type=F32)


def dot_t(a, b):
    return lax.dot_general(a, b, (((1,), (1,)), ((), ())), preferred_element_type=F32)


def dot_lt(a, b):
    return lax.dot_general(a, b, (((0,), (0,)), ((), ())), preferred_element_type=F32)


def normalize(v):
    center = v - jnp.mean(v, axis=-1, keepdims=True)
    spread = jnp.mean(center * center, axis=-1, keepdims=True)
    scale = lax.rsqrt(spread + 1e-06)
    return center * scale, scale


def normalize_back(grad_hat, hat, scale):
    mean_g = jnp.mean(grad_hat, axis=-1, keepdims=True)
    mean_gh = jnp.mean(grad_hat * hat, axis=-1, keepdims=True)
    return scale * (grad_hat - mean_g - hat * mean_gh)


def gelu_pair(v):
    half = 0.5 * (1.0 + lax.erf(v * 0.5**0.5))
    slope = half + v * jnp.exp(-0.5 * v * v) * 0.3989422804014327
    return v * half, slope


def lane_of(rows):
    return lax.broadcasted_iota(jnp.int32, (rows, LANES), 1)


def unpack_head(tiles, e):
    tile = tiles[:, (e // 2) * LANES : (e // 2 + 1) * LANES]
    return tile if e % 2 == 0 else pltpu.roll(tile, HEAD, 1)


def pack_pair(low, high):
    return jnp.where(lane_of(low.shape[0]) < HEAD, low, pltpu.roll(high, HEAD, 1))


def vmem():
    return pl.BlockSpec(memory_space=pltpu.VMEM)


def smem():
    return pl.BlockSpec(memory_space=pltpu.SMEM)


def call(kernel, outs, args, scratch=(), flops=0, scalars=0, room=16, far=()):
    args = [pltpu.with_memory_space_constraint(a, pltpu.HBM) if i in far else a for i, a in enumerate(args)]
    nbytes = sum(a.size * a.dtype.itemsize for a in args)
    nbytes += sum(o.size * o.dtype.itemsize for o in outs)
    return pl.pallas_call(
        kernel,
        out_shape=outs,
        in_specs=[
            smem() if i < scalars else pl.BlockSpec(memory_space=pltpu.HBM) if i in far else vmem()
            for i in range(len(args))
        ],
        out_specs=[vmem()] * len(outs),
        scratch_shapes=list(scratch),
        compiler_params=pltpu.CompilerParams(vmem_limit_bytes=room << 20),
        cost_estimate=pl.CostEstimate(flops=flops, bytes_accessed=nbytes, transcendentals=0),
    )(*args)


def prep_kernel(sref, w, biases, w_own, bias_own):
    width = w.shape[0]
    per = width // HEAD
    line = lax.broadcasted_iota(jnp.int32, (1, LANES), 1)
    for t in range((3 * OWN + 1) // 2):
        out, bias = jnp.zeros((width, LANES), F32), jnp.zeros((1, LANES), F32)
        for dest in range(2):
            e = 2 * t + dest
            if e == 3 * OWN:
                continue
            h, j = e // 3, e % 3
            u = per * j + OWN * sref[0] + h
            side = (lane_of(width) >= HEAD) == (dest == 1)
            moved = jnp.broadcast_to((u & 1) != dest, (1, LANES))
            tile = w[:, pl.ds(pl.multiple_of((u >> 1) * LANES, LANES), LANES)].astype(F32)
            tile = jnp.where(moved, pltpu.roll(tile, HEAD, 1), tile)
            out = jnp.where(side, tile, out)
            if j != 1:
                v = per * 0 + OWN * sref[0] + h
                tile = biases[j // 2 : j // 2 + 1, pl.ds(pl.multiple_of((v >> 1) * LANES, LANES), LANES)]
                tile = jnp.broadcast_to(tile, (8, LANES))
                away = jnp.broadcast_to((v & 1) != dest, (8, LANES))
                tile = jnp.where(away, pltpu.roll(tile, HEAD, 1), tile)[:1]
                bias = jnp.where((line >= HEAD) == (dest == 1), tile, bias)
        w_own[:, t * LANES : (t + 1) * LANES] = out.astype(BF16)
        bias_own[:, t * LANES : (t + 1) * LANES] = bias


def tokens_of(patches, small):
    parts = [patches[...].astype(F32), small[:16, :].astype(F32)]
    return jnp.concatenate(parts + [jnp.zeros((PAD - 16, patches.shape[1]), F32)], axis=0)


def cots_of(patches, small):
    parts = [patches[...].astype(F32), small[16:, :].astype(F32)]
    return jnp.concatenate(parts + [jnp.zeros((PAD - 16, patches.shape[1]), F32)], axis=0)


def images_of(small, rows):
    size = -(-rows // LANES) * LANES
    line = small[:16, :size].astype(F32)[4:5]
    return jnp.broadcast_to(line, (LANES, size)).T[:rows]


def project(patches, small, gain, shift, w, bias, at, qa, ka, va, normed):
    tok = tokens_of(patches, small)
    rows = tok.shape[0]
    lane = lane_of(rows)
    hat, _ = normalize(tok)
    nrm = (hat * gain[...] + shift[...]).astype(BF16)
    normed[at, :] = nrm
    qkv = dot(nrm, w[...]) + bias[...]
    image = images_of(small, rows)
    hot = jnp.where((lane >= HEAD) & (image == (lane - HEAD).astype(F32)), 1.0, 0.0)
    far = jnp.where((lane >= HEAD) & (lane < HEAD + 8) & (hot == 0.0), FAR, 0.0)
    one = jnp.where(lane == HEAD, 1.0, 0.0)
    for h in range(OWN):
        q = unpack_head(qkv, 3 * h) * HEAD**-0.5
        qa[h, at, :] = jnp.where(lane < HEAD, q, hot).astype(BF16)
        ka[h, at, :] = jnp.where(lane < HEAD, unpack_head(qkv, 3 * h + 1), far).astype(BF16)
        va[h, at, :] = jnp.where(lane < HEAD, unpack_head(qkv, 3 * h + 2), one).astype(BF16)
    return tok, image


def project_kernel(flags, p0, s0, p1, s1, gain, shift, w, bias, qa, ka, va, normed, toks, keeps):
    rows = normed.shape[0] // 2
    lane = lane_of(rows)
    for i, (p, small) in enumerate(((p0, s0), (p1, s1))):
        at = pl.ds(i * rows, rows)
        tok, image = project(p, small, gain, shift, w, bias, at, qa, ka, va, normed)
        toks[at, :] = tok.astype(BF16)
        keep = jnp.zeros((rows, LANES), F32)
        half = flags.shape[1] // 2
        for j in range(half):
            first = flags[0, j].astype(F32) / 0.75
            second = flags[0, half + j].astype(F32) / 0.75
            keep = jnp.where(image == float(j), jnp.where(lane == 0, first, second), keep)
        keeps[at, :] = keep


def attend_block(h, at, keys, values, queries, oacc):
    sc = dot_t(queries[h, at, :], keys[h])
    top = jnp.max(sc, axis=-1, keepdims=True)
    e = jnp.exp(sc - top).astype(BF16)
    o = dot(e, values[h])
    tot = o[:, HEAD : HEAD + 1]
    mark = jnp.where(lane_of(o.shape[0]) == HEAD + 1, top + jnp.log(tot), o * (1.0 / tot))
    return mark


def attend_first_kernel(
    q0, k0, v0, n0, p2, s2, p3, s3, gain, shift, w, bias, qa, ka, va, send, oacc, normed
):
    half = n0.shape[0]
    rows = half // 2
    own = pl.ds(0, half)
    for h in range(OWN):
        qa[h, own, :] = q0[h]
        ka[h, own, :] = k0[h]
        va[h, own, :] = v0[h]
    normed[own, :] = n0[...]
    for i, (p, small) in enumerate(((p2, s2), (p3, s3))):
        project(p, small, gain, shift, w, bias, pl.ds(half + i * rows, rows), qa, ka, va, normed)

    def block(i, carry):
        h, b = i // 2, i % 2
        at = pl.ds(pl.multiple_of(half + b * rows, 16), rows)
        oacc[h, pl.ds(pl.multiple_of(b * rows, 16), rows), :] = attend_block(h, at, ka, va, qa, oacc)
        return carry

    lax.fori_loop(0, 2 * OWN, block, 0)
    gather_heads(oacc, send)


def gather_heads(oacc, out):
    out[:, :LANES] = pack_pair(oacc[0], oacc[1]).astype(BF16)
    out[:, LANES:] = oacc[2, :, :HEAD].astype(BF16)


def attend_second_kernel(qa, ka, va, other, keep, lse, oacc):
    half = oacc.shape[1]
    rows = half // 2

    def block(i, carry):
        h, b = i // 2, i % 2
        at = pl.ds(pl.multiple_of(b * rows, 16), rows)
        oacc[h, at, :] = attend_block(h, at, ka, va, qa, oacc)
        return carry

    lax.fori_loop(0, 2 * OWN, block, 0)
    gather_heads(oacc, keep)
    step = 2 * half // 3
    for h in range(OWN):
        parts = [
            oacc[h, :step, :],
            jnp.concatenate([oacc[h, step:, :], other[h, : step - (half - step), :]], axis=0),
            other[h, half - step :, :],
        ]
        for b in range(3):
            lse[h, b] = jnp.broadcast_to(parts[b].T[HEAD + 1 : HEAD + 2], (8, step))


def middle_kernel(
    sref, a0, a1, a2, a3, toks, keeps, cp0, cp1, c0, c1, w_out, bias, gain, shift, w_fc1, w_fc2,
    middle, normed2, gb2, w1, w2, sems,
):
    s = sref[0]
    copies = fetch(s ^ 2, w_fc1, w_fc2, w1, w2, sems)
    chip, width = toks.shape
    rows = chip // 2
    cols = a0.shape[1]
    acc = jnp.zeros((chip, width), F32) + bias[...]
    for j, a in ((0, a0), (2, a2)):
        w = w_out[pl.ds(pl.multiple_of((s ^ j) * cols, HEAD), cols), :]
        acc = acc + dot(a[...], w)
    for j, a in ((1, a1), (3, a3)):
        w = w_out[pl.ds(pl.multiple_of((s ^ j) * cols, HEAD), cols), :]
        part = dot(a[...], w)
        acc = acc + jnp.concatenate([part[rows:], part[:rows]], axis=0)
    mid = toks[...].astype(F32) + keeps[:, 0:1] * acc
    middle[...] = mid
    hat, _ = normalize(mid)
    normed2[...] = (hat * gain[...] + shift[...]).astype(BF16)
    gout = jnp.concatenate([cots_of(cp0, c0), cots_of(cp1, c1)], axis=0)
    gb2[...] = (keeps[:, 1:2] * gout).astype(BF16)
    for copy in copies:
        copy.wait()


def fetch(block, w_fc1, w_fc2, w1, w2, sems):
    size = w1.shape[1]
    at = pl.ds(pl.multiple_of(block * size, LANES), size)
    copies = [
        pltpu.make_async_copy(w_fc1.at[:, at], w1, sems.at[0]),
        pltpu.make_async_copy(w_fc2.at[at, :], w2, sems.at[1]),
    ]
    for copy in copies:
        copy.start()
    return copies


def feed_kernel(last, fast, sref, bref, normed2, gb2, fc1, bias, fc2, *refs):
    copies = []
    if last:
        b2_in, gn_in, y_in, g2, zb_send, zb_keep, y_send, g1_keep, gb, b2_keep, b2_send, gn_keep, gn_send, wide, wide2 = refs
    else:
        w_fc1, w_fc2, g2a, g2m, zb_send, zb_keep, y_first, y_second, g1_keep, gb, b2, gn = refs[:12]
        w1, w2, wide, wide2, sems = refs[12:]
        copies = fetch(sref[0], w_fc1, w_fc2, w1, w2, sems)
    tokens = normed2.shape[0]
    half = tokens // 2
    pre = dot(normed2[...], fc1[...]) + bias[...]
    gact = dot_t(gb2[...], fc2[...])
    act, slope = gelu_pair(pre)
    act = act.astype(BF16)
    gh = (gact * slope).astype(BF16)
    grad1 = dot_lt(normed2[...], gh)
    if not fast:
        rows = grad1.shape[0] // 2
        (y_send if last else y_first)[...] = grad1[:rows].astype(BF16)
        g1_keep[...] = grad1[rows:].astype(BF16)
    else:
        x, c = sref[0] >> 1, sref[0] & 1
        y, z1, z2 = bref[0] & 1, (bref[0] >> 1) & 1, bref[0] >> 2
        wide[...] = grad1
        n, rows = g1_keep.shape[:2]
        for m in range(2 * n):
            near = [(m >> k) & 1 for k in (4, 3, 2, 1, 0)]
            yy, zz1, xx, zz2, cc = [own if r else 1 - own for own, r in zip((y, z1, x, z2, c), near)]
            base = rows * (16 * xx + 8 * cc + 4 * zz2 + 2 * zz1 + yy)
            piece = wide[pl.ds(pl.multiple_of(base, 8), rows), :].astype(BF16)
            if m >= n:
                g1_keep[m - n] = piece
            elif last:
                y_send[n // 2 + m] = piece
            elif m < n // 2:
                y_first[m] = piece
            else:
                y_second[m - n // 2] = piece
        if last:
            for m in range(n // 2):
                y_send[m] = y_in[m]
    gb[...] = jnp.sum(gh.astype(F32), axis=0, keepdims=True)
    partn = dot_t(gh, fc1[...])
    part2 = dot(act, fc2[...])
    if last:
        partn = partn + gn_in[...]
        part2 = part2 + b2_in[...]
        b2_keep[...] = part2[:half]
        b2_send[...] = part2[half:].astype(BF16)
        gn_keep[...] = partn
        gn_send[:half] = partn[half:].astype(BF16)
        gn_send[half:] = partn[:half].astype(BF16)
    else:
        b2[...] = part2
        gn[...] = partn
    grad2 = dot_lt(act, gb2[...])
    if not fast:
        rows = zb_send.shape[0]
        if last:
            g2[...] = grad2[: 2 * rows].astype(BF16)
        else:
            g2a[...] = grad2[:rows].astype(BF16)
            g2m[...] = grad2[rows : 2 * rows].astype(BF16)
        zb_send[...] = grad2[2 * rows : 3 * rows].astype(BF16)
        zb_keep[...] = grad2[3 * rows :].astype(BF16)
    else:
        deep = grad2.shape[0] // 8
        half = deep // 2
        for m in range(8):
            if last:
                g2[m] = grad2[m * deep : m * deep + half].astype(BF16)
            else:
                mid = m * deep + half // 2
                g2a[m] = grad2[m * deep : mid].astype(BF16)
                g2m[m] = grad2[mid : mid + half // 2].astype(BF16)
            wide2[pl.ds(m * half, half), :] = grad2[m * deep + half : (m + 1) * deep]
        for m in range(8):
            near = [(m >> k) & 1 for k in (2, 1, 0)]
            zz1, zz2, yy = [own if r else 1 - own for own, r in zip((z1, z2, y), near)]
            base = half * (4 * zz2 + 2 * zz1 + yy)
            piece = wide2[pl.ds(pl.multiple_of(base, 8), half), :].astype(BF16)
            (zb_keep if m >= 4 else zb_send)[m % 4] = piece
    for copy in copies:
        copy.wait()


def split_rows(value, wide, bit, send, keep):
    if len(send.shape) == 2:
        rows = value.shape[0] // 2
        send[...] = value[:rows].astype(BF16)
        keep[...] = value[rows:].astype(BF16)
        return
    wide[...] = value
    rows = send.shape[1]
    for m in range(send.shape[0]):
        base = 2 * m * rows
        send[m] = wide[pl.ds(pl.multiple_of(base + (1 - bit) * rows, 8), rows), :].astype(BF16)
        keep[m] = wide[pl.ds(pl.multiple_of(base + bit * rows, 8), rows), :].astype(BF16)


def feed(last, fast, per, sidx, bidx, normed2, gb2, fc1, bias, fc2, prev=()):
    tokens, width = normed2.shape
    hidden = fc1.shape[1]
    pairs = width // (2 * per)
    deep = hidden // 8
    if fast:
        outs = [SDS((8, deep // 2, width), BF16)] if last else [SDS((8, deep // 4, width), BF16)] * 2
        outs += [SDS((4, deep // 2, width), BF16)] * 2
    else:
        outs = [SDS((hidden // 2, width), BF16)] if last else [SDS((hidden // 4, width), BF16)] * 2
        outs += [SDS((hidden // 4, width), BF16)] * 2
    send = [SDS((3 * pairs // 2, per, hidden), BF16)] if last else [SDS((pairs // 2, per, hidden), BF16)] * 2
    keep = SDS((pairs, per, hidden), BF16)
    if not fast:
        keep = SDS((width // 2, hidden), BF16)
        send = [keep] if last else [keep, SDS((8, LANES), BF16)]
    outs += send + [keep, SDS((1, hidden), F32)]
    if last:
        outs += [SDS((tokens // 2, width), F32), SDS((tokens // 2, width), BF16)]
        outs += [SDS((tokens, width), F32), SDS((tokens, width), BF16)]
    else:
        outs += [SDS((tokens, width), F32)] * 2 + [SDS((width, hidden), BF16), SDS((hidden, width), BF16)]
    return call(
        functools.partial(feed_kernel, last, fast),
        outs,
        (sidx, bidx, normed2, gb2, fc1, bias, fc2) + tuple(prev),
        [pltpu.VMEM((width, hidden), F32), pltpu.VMEM((hidden // 2, width), F32)]
        + ([] if last else [pltpu.SemaphoreType.DMA((2,))]),
        flops=12 * tokens * width * hidden,
        scalars=2,
        far=() if last else (7, 8),
    )


def by_batch_bit(arr, per):
    arr = arr.reshape(-1, 2, per, arr.shape[-1])
    own = lax.axis_index("batch") & 1
    return [pick(arr, 1 - own, 1), pick(arr, own, 1)]


def middle_back_kernel(
    sref, gn_keep, gn_got, middle, keeps, cp0, cp1, c0, c1, w_out, gain, gb2, gmid_own, gbr_out, gatt_send, sums
):
    s = sref[0]
    rows, width = gmid_own.shape
    cols = gatt_send.shape[1]
    hat, scale = normalize(middle[...])
    g = gn_keep[...] + gn_got[...].astype(F32)
    gout = jnp.concatenate([cots_of(cp0, c0), cots_of(cp1, c1)], axis=0)
    gmid = gout + normalize_back(g * gain[...], hat, scale)
    gbr = (keeps[:, 0:1] * gmid).astype(BF16)
    gbr_out[...] = gbr
    w_oth = w_out[pl.ds(pl.multiple_of((s ^ 2) * cols, HEAD), cols), :]
    gatt_send[...] = dot_t(gbr, w_oth).astype(BF16)
    gmid_own[...] = gmid[:rows]
    own = slice(0, rows)
    lines = [
        jnp.sum(g[own] * hat[own], axis=0, keepdims=True),
        jnp.sum(g[own], axis=0, keepdims=True),
        jnp.sum(gb2[own, :].astype(F32), axis=0, keepdims=True),
        jnp.sum(gbr[own].astype(F32), axis=0, keepdims=True),
        jnp.zeros((4, width), F32),
    ]
    sums[...] = jnp.concatenate(lines, axis=0)


def branch_back_kernel(
    sref, bref, gbr, w_out, a0, a2, middle, keeps, b2_keep, b2_got, bias, gain1, shift1, sums, fb_own, fb_oth,
    gatt, go_send, go_keep, early, opat, ospe, fcol, wide,
):
    s = sref[0]
    cols = a0.shape[1]
    rows, width = b2_keep.shape
    w_own = w_out[pl.ds(pl.multiple_of(s * cols, HEAD), cols), :]
    gatt[...] = dot_t(gbr[...], w_own).astype(BF16)
    for j, a in enumerate((a0, a2)):
        split_rows(dot_lt(a[...], gbr[...]), wide, bref[0] & 1, go_send.at[j], go_keep.at[j])
    res = middle[:rows, :] + keeps[:rows, 1:2] * (b2_keep[...] + b2_got[...].astype(F32) + bias[...])
    res = res.astype(BF16)
    opat[...] = res[: opat.shape[0]]
    ospe[...] = res[opat.shape[0] : opat.shape[0] + ospe.shape[0]]
    blank = functools.partial(jnp.zeros, dtype=F32)
    lines = [gain1[...], shift1[...], blank((HEAD + 2, width)), sums[:4, :], blank((LANES - HEAD - 8, width))]
    early[...] = jnp.concatenate(lines, axis=0).T
    lane = lane_of(cols)
    for j, ref in ((0, fb_own), (2, fb_oth)):
        fcol[...] = jnp.broadcast_to(ref[...], (LANES, ref.shape[1])).T
        at = pl.ds(pl.multiple_of((s ^ j) * cols, HEAD), cols)
        val = early[at, :]
        for k in range(4):
            val = jnp.where(lane == HEAD + 8 + k, fcol[pl.ds(k, cols, stride=4), :], val)
        early[at, :] = val


def attend_back_kernel(first, heads, qa, ka, va, lse, ga, gx, out, sums, goa, dq, dk, dv):
    whole = qa.shape[1]
    half = ga.shape[0]
    lane = lane_of(half)
    for i in range(heads):
        h = first + i
        for ref, start in ((ga, 0), (gx, half)):
            if h < 2:
                t = ref[:, :LANES].astype(F32)
                t = jnp.where(lane < HEAD, t if h == 0 else pltpu.roll(t, HEAD, 1), 0.0)
            else:
                t = ref[:, LANES:].astype(F32)
                t = jnp.concatenate([t, jnp.zeros_like(t)], axis=1)
            goa[i, pl.ds(start, half), :] = t.astype(BF16)
    step = whole // 3

    def block(n, carry):
        i, b = n // 3, n % 3
        h = first + i
        at = pl.ds(pl.multiple_of(b * step, step), step)
        q, go = qa[h, at, :], goa[i, at, :]
        prob = jnp.exp(dot_t(ka[h], q) - lse[h, b][0:1, :])
        gp = dot_t(va[h], go)
        inner = jnp.sum(gp * prob, axis=0, keepdims=True)
        gs = (prob * (gp - inner)).astype(BF16)
        pv = dot(prob.astype(BF16), go)
        pk = dot(gs, q)
        dq[i, at, :] = dot_lt(gs, ka[h])

        @pl.when(b == 0)
        def _():
            dv[i] = pv
            dk[i] = pk

        @pl.when(b > 0)
        def _():
            dv[i] += pv
            dk[i] += pk

        return carry

    lax.fori_loop(0, 3 * heads, block, 0)
    for i in range(heads):
        out[i, :, :LANES] = pack_pair(dq[i] * HEAD**-0.5, dk[i]).astype(BF16)
        out[i, :, LANES:] = dv[i, :, :HEAD].astype(BF16)
        sums[i] = jnp.sum(out[i].astype(F32), axis=0, keepdims=True)


def attend_back(first, heads, qa, ka, va, lse, ga, gx):
    whole = qa.shape[1]
    return call(
        functools.partial(attend_back_kernel, first, heads),
        [SDS((heads, whole, 3 * HEAD), BF16), SDS((heads, 1, 3 * HEAD), F32)],
        (qa, ka, va, lse, ga, gx),
        [pltpu.VMEM((heads, whole, LANES), BF16)] + [pltpu.VMEM((heads, whole, LANES), F32)] * 3,
        flops=10 * heads * whole * whole * LANES,
    )


def norm1_kernel(g01, g2, w, keep, send):
    rows = keep.shape[0] // 2
    cols = g2.shape[2]
    for i in range(4):
        at = pl.ds(i * rows, rows)
        part = dot_t(g01[0, at, :], w[:, :cols])
        part = part + dot_t(g01[1, at, :], w[:, cols : 2 * cols])
        part = part + dot_t(g2[0, at, :], w[:, 2 * cols : 3 * cols])
        to = pl.ds((i // 2) * rows, rows)
        if i % 2 == 0:
            keep[to, :] = part
        else:
            send[to, :] = part.astype(BF16)


def qkv_grad(sref, normed, grads, sums, w, first, tile, bound):
    width, cols = w.shape[0], grads[0].shape[1]
    g = jnp.concatenate([dot_lt(normed[...], v) for v in grads], axis=1)
    w32 = w[:, first * cols : (first + len(grads)) * cols].astype(F32)
    rows = jnp.concatenate(sums, axis=1)
    both = jnp.sum(g * w32, axis=-1, keepdims=True)
    gshift = jnp.sum(w32 * rows, axis=-1, keepdims=True)
    lane = lane_of(width)
    old = bound[...]
    tile[...] = jnp.where(lane == HEAD, old + both, jnp.where(lane == HEAD + 1, old + gshift, old))
    ones = jnp.ones((grads[0].shape[0], LANES), BF16)
    at = pl.multiple_of(sref[0] * cols, HEAD)
    lanes = lane_of(HEAD)
    for i, v in enumerate(grads):
        col = dot_lt(v, ones)
        here = pl.ds(at + (first + i) * HEAD, HEAD)
        row = tile[here, :]
        row = jnp.where(lanes == HEAD + 2, col[:HEAD], row)
        tile[here, :] = jnp.where(lanes == HEAD + 3, col[2 * HEAD :], row)
    return g


def heads_kernel(
    fast, sref, bref, qa, ka, va, lse, ga, gx, normed, w, early, g01, send, keep, tile,
    s01, goa, dq, dk, dv, wide,
):
    attend_back_kernel(0, 2, qa, ka, va, lse, ga, gx, g01, s01, goa, dq, dk, dv)
    g = qkv_grad(sref, normed, (g01[0], g01[1]), (s01[0], s01[1]), w, 0, tile, early)
    if not fast:
        rows = g.shape[0] // 2
        send[...] = g[:rows].astype(BF16)
        keep[...] = g[rows:].astype(BF16)
        return
    wide[...] = g
    y, z1, z2 = bref[0] & 1, (bref[0] >> 1) & 1, bref[0] >> 2
    per, cols = send.shape[1], g.shape[1]
    for m in range(8):
        zz1 = z1 if m & 4 else 1 - z1
        zz2 = z2 if m & 2 else 1 - z2
        for j in range(2):
            base = per * ((2 * (m & 1) + j) * 8 + 4 * zz2 + 2 * zz1)
            to = slice(j * cols, (j + 1) * cols)
            send[m, :, to] = wide[pl.ds(pl.multiple_of(base + (1 - y) * per, 8), per), :].astype(BF16)
            keep[m, :, to] = wide[pl.ds(pl.multiple_of(base + y * per, 8), per), :].astype(BF16)


def tail_kernel(
    sref, bref, qa, ka, va, lse, ga, gx, normed, g01, w, early, gn_keep, gn_send, send, keep,
    g2, s2, goa, dq, dk, dv, tile, wide,
):
    attend_back_kernel(2, 1, qa, ka, va, lse, ga, gx, g2, s2, goa, dq, dk, dv)
    norm1_kernel(g01, g2, w, gn_keep, gn_send)
    g = qkv_grad(sref, normed, (g2[0],), (s2[0],), w, 2, tile, early)
    width = g.shape[0]
    lane = lane_of(width)
    val = tile[...]
    gshift = val[:, HEAD + 1 : HEAD + 2]
    ggain = (val[:, HEAD : HEAD + 1] - val[:, 1:2] * gshift) / val[:, 0:1]
    val = jnp.where(lane == HEAD, ggain, val)
    last = jnp.concatenate([g[:, LANES:], jnp.zeros((width, LANES - HEAD), F32)], axis=1)
    out = jnp.concatenate([g[:, :LANES], jnp.where(lane < HEAD, last, val)], axis=1)
    split_rows(out, wide, bref[0] & 1, send, keep)


def wide_sum(*parts):
    return sum(p.astype(F32) for p in parts[1:]) + parts[0].astype(F32)


def stage0_kernel(own_keep, own_got, oth_keep, oth_got, msg, part):
    for i in range(2):
        msg[i] = wide_sum(own_keep[i], own_got[i]).astype(BF16)
        msg[2 + i] = wide_sum(oth_keep[i], oth_got[i]).astype(BF16)
        part[i] = wide_sum(own_keep[2 + i], own_got[2 + i])
        part[2 + i] = wide_sum(oth_keep[2 + i], oth_got[2 + i])


def stage1_kernel(
    bref, keep_own, keep_oth, y1, y2, fc2, g2a, g2m, out, y3, part_0, got_0, q_send,
    msg_z, msg_y, msg_x, part_f, part_a, part_o, part_p,
):
    y, z1, z2 = bref[0] & 1, (bref[0] >> 1) & 1, bref[0] >> 2
    n = keep_own.shape[0] // 2
    for i in range(n):
        msg_z[i] = wide_sum(keep_own[i], y2[n + i]).astype(BF16)
        msg_z[n + i] = wide_sum(keep_oth[i], y1[i]).astype(BF16)
        part_f[i] = wide_sum(keep_own[n + i], y2[2 * n + i])
        part_f[n + i] = wide_sum(keep_oth[n + i], y2[i])
        msg_y[8 + i] = q_send[i]
    rows = g2a.shape[1]
    for i in range(4):
        zz1 = z1 if i >> 1 else 1 - z1
        zz2 = z2 if i & 1 else 1 - z2
        m = 2 * zz2 + zz1
        msg_x[i] = wide_sum(out[1, m], y3[1, m]).astype(BF16)
        part_o[i] = wide_sum(out[0, m], y3[0, m])
        for k, got in enumerate((g2a, g2m)):
            at = slice(k * rows, (k + 1) * rows)
            b = 2 * m + 1 - y
            msg_y[2 * i + k] = wide_sum(fc2[b, at], got[b]).astype(BF16)
            b = 2 * m + y
            part_a[2 * i + k] = wide_sum(fc2[b, at], got[b])
    for i in range(2):
        for k in range(2):
            at = slice(k * rows, (k + 1) * rows)
            msg_x[4 + 2 * i + k] = wide_sum(part_0[2 + i, at], got_0[2 + i, at]).astype(BF16)
            part_p[2 * i + k] = wide_sum(part_0[i, at], got_0[i, at])


def stage2_kernel(
    part_f, got_z, part_a, got_y, part_o, got_x, part_p, q_keep, msg_x, msg_z, msg_y, part_g, part_c, part_q
):
    for half in range(2):
        for i in range(4):
            k = 8 * half + i
            msg_x[4 * half + i] = wide_sum(part_f[k], got_z[k]).astype(BF16)
            part_g[4 * half + i] = wide_sum(part_f[k + 4], got_z[k + 4])
    for i in range(4):
        msg_z[i] = wide_sum(part_a[i], got_y[i]).astype(BF16)
        part_c[i] = wide_sum(part_a[4 + i], got_y[4 + i])
        msg_z[6 + i] = wide_sum(q_keep[i], got_y[8 + i]).astype(BF16)
        part_c[6 + i] = wide_sum(q_keep[4 + i], got_y[12 + i])
    for i in range(2):
        msg_z[4 + i] = wide_sum(part_o[i], got_x[i]).astype(BF16)
        part_c[4 + i] = wide_sum(part_o[2 + i], got_x[2 + i])
        msg_y[i] = wide_sum(part_p[i], got_x[4 + i]).astype(BF16)
        part_q[i] = wide_sum(part_p[2 + i], got_x[6 + i])


def stage3_kernel(part_g, got_x, part_c, got_z, msg, kept):
    for half in range(2):
        for i in range(2):
            k, other = 4 * half + i, 4 * (1 - half) + i
            msg[2 * half + i] = wide_sum(part_g[k], got_x[other]).astype(BF16)
            kept[2 * half + i] = wide_sum(part_g[k + 2], got_x[other + 2])
    for to, a, b in ((4, 0, 2), (5, 1, 3), (6, 4, 5), (7, 6, 8), (8, 7, 9)):
        msg[to] = wide_sum(part_c[a], got_z[a]).astype(BF16)
        kept[to] = wide_sum(part_c[b], got_z[b])


def shift_kernel(keep, got, send):
    rows = send.shape[0]
    send[...] = wide_sum(keep[rows:, :], got[rows:, :]).astype(BF16)


def quarter_kernel(bref, keep, got, z1, z2, z3, kept):
    q = bref[0] >> 1
    for r in range(4):
        for k, ref in enumerate((kept, z1, z2, z3)):
            m = r * 4 + (q ^ k)
            ref[r] = wide_sum(keep[m], got[m]).astype(ref.dtype)


def sums_kernel(kept, got, part_q, got_q, swap_send, swap_keep, fc2, out):
    per = out.shape[0]
    for half in range(2):
        at = pl.ds(half * per, per)
        swap_send[at, :] = wide_sum(kept[2 * half], got[2 * half]).astype(BF16)
        swap_keep[at, :] = wide_sum(kept[2 * half + 1], got[2 * half + 1])
        fc2[at, :] = wide_sum(kept[4 + half], got[4 + half])
        fc2[pl.ds((2 + half) * per, per), :] = wide_sum(part_q[half], got_q[half])
    out[...] = wide_sum(kept[6], got[6])


def owner_kernel(sref, most, got, kept, z1, z2, z3, s1, s2, s3, own, every):
    s = sref[0]
    cols = most.shape[2] // 2
    for m in range(4):
        at = slice((m % 2) * cols, (m % 2 + 1) * cols)
        every[m, :, :cols] = wide_sum(most[7 + m // 2, :, at], got[7 + m // 2, :, at])
        every[m, :, cols:] = wide_sum(kept[m], z1[m], z2[m], z3[m])
    for k, ref in enumerate((own, s1, s2, s3)):
        ref[...] = every[s ^ k].astype(ref.dtype)


def final_kernel(k0, c0, x0, p0, s0, gmid, gain, gpat, gspe):
    rows, width = x0.shape
    count = gpat.shape[0]
    hat, scale = normalize(tokens_of(p0, s0))
    g = wide_sum(k0[:rows], c0[:rows], x0[...])
    res = gmid[...] + normalize_back(g * gain[...], hat, scale)
    gpat[...] = res[:count]
    gspe[...] = res[count : count + gspe.shape[0]]


def collect_kernel(sref, own, g1, g2, g3, swap_keep, swap_got, out, vec, fc1, every):
    s = sref[0]
    per, hidden = swap_keep.shape[0] // 2, swap_keep.shape[1]
    for j, value in ((0, swap_keep[:per]), (2, swap_keep[per:]), (1, swap_got[:per]), (3, swap_got[per:])):
        fc1[:, pl.ds(pl.multiple_of((s ^ j) * hidden, LANES), hidden)] = value.astype(F32)
    for k, ref in enumerate((own, g1, g2, g3)):
        every[k] = ref[...].astype(F32)
    pieces = [every[s ^ a] for a in range(4)]

    def part(u):
        j, a, h = u // 12, (u // 3) % 4, u % 3
        e = 3 * h + j
        return pieces[a][:, (e // 2) * LANES : (e // 2 + 1) * LANES], e % 2

    lane = lane_of(out.shape[0])
    for t in range(out.shape[1] // LANES):
        (low, lo), (high, hi) = part(2 * t), part(2 * t + 1)
        low = pltpu.roll(low, HEAD, 1) if lo else low
        high = high if hi else pltpu.roll(high, HEAD, 1)
        out[:, t * LANES : (t + 1) * LANES] = jnp.where(lane < HEAD, low, high)
    tail = 4 * LANES
    vec[...] = wide_sum(*[every[k, :, tail:] for k in range(4)])


def pick(arr, index, axis):
    return lax.dynamic_index_in_dim(arr, index, axis, keepdims=False)


def total(parts):
    out = parts[0].astype(F32)
    for part in parts[1:]:
        out = out + part.astype(F32)
    return out


def swap(kind, v, mask):
    return lax.ppermute(v, kind, [(i, i ^ mask) for i in range(lax.axis_size(kind))])


def swap_seq(v, mask):
    return swap("seq", v, mask)


def after(value, *first):
    return lax.optimization_barrier((value, first))[0]


def bits_of(kind):
    return lax.axis_size(kind).bit_length() - 1


def split_bits(arr, axis, count):
    shape = arr.shape
    return arr.reshape(shape[:axis] + (2,) * count + shape[axis + 1 :])


def to_send(parts, axis, bit, kind):
    own = (lax.axis_index(kind) >> bit) & 1
    send = total([pick(p, 1 - own, axis) for p in parts]).astype(BF16)
    return send, [pick(p, own, axis) for p in parts]


def send_four(parts, axis, low):
    own = (lax.axis_index("batch") >> low) & 3

    def quarter(p, k):
        return pick(pick(p, k >> 1, axis), k & 1, axis)

    sends = [total([quarter(p, own ^ k) for p in parts]).astype(BF16) for k in (1, 2, 3)]
    return sends, [quarter(p, own) for p in parts]


def swap_four(sends, low):
    return [swap("batch", v, k << low) for k, v in zip((1, 2, 3), sends)]


def sum_rest(parts, axis, low):
    top = bits_of("batch")
    while low < top:
        if low + 1 < top:
            sends, kept = send_four(parts, axis + top - low - 2, low)
            parts, low = kept + swap_four(sends, low), low + 2
        else:
            send, kept = to_send(parts, axis, low, "batch")
            parts, low = kept + [swap("batch", send, 1 << low)], low + 1
    return total(parts)


def body(
    patches,
    specials,
    segment_ids,
    special_order,
    keep_mask,
    norm_gains,
    norm_shifts,
    w_qkv,
    biases,
    w_out,
    w_fc1,
    fc1_bias,
    w_fc2,
    cot_patches,
    cot_specials,
):
    count, width = patches.shape[1:]
    extra = specials.shape[1]
    images = keep_mask.shape[1] // 2
    block = count + PAD
    chip = 2 * block
    whole = 4 * block
    cols = OWN * HEAD
    hidden = w_fc1.shape[1] // 4
    s = lax.axis_index("seq")
    sidx = s.astype(jnp.int32).reshape(1)
    bidx = lax.axis_index("batch").astype(jnp.int32).reshape(1)
    nb = lax.axis_size("batch")
    nbits = bits_of("batch")

    own_p, own_cot = patches[0], cot_patches[0]
    got_px = swap_seq(own_p, 2)
    got_pc = swap_seq(own_p, 1)
    ids = jnp.concatenate([segment_ids[0], special_order[0] // 2])
    line = jnp.full((width,), -1, jnp.int32).at[: count + extra].set(ids).astype(BF16)
    blank = jnp.zeros((16, width), BF16)
    small = jnp.concatenate(
        [specials[0], line[None], blank[: 15 - extra], cot_specials[0], blank[: 16 - extra]], axis=0
    )
    got_sx = swap_seq(small, 2)
    got_sc = swap_seq(small, 1)
    cot_c = swap_seq(own_cot, 1)
    gain1, gain2 = norm_gains[0:1], norm_gains[1:2]
    shift1, shift2 = norm_shifts[0:1], norm_shifts[1:2]
    fb = [lax.dynamic_slice(fc1_bias, ((s ^ j) * hidden,), (hidden,))[None] for j in (2, 0)]
    sidx, bidx, fb, small = lax.optimization_barrier((sidx, bidx, fb, small))
    w_own, bias_own = call(
        prep_kernel,
        [SDS((width, 5 * LANES), BF16), SDS((1, 5 * LANES), F32)],
        (sidx, w_qkv, biases),
        scalars=1,
    )
    headed = SDS((OWN, chip, LANES), BF16)
    q0, k0, v0, n0, toks, keeps = call(
        project_kernel,
        [headed] * 3 + [SDS((chip, width), BF16), SDS((chip, width), BF16), SDS((chip, LANES), F32)],
        (keep_mask, own_p, small, got_pc, got_sc, gain1, shift1, w_own, bias_own),
        flops=2 * chip * width * 3 * cols,
        scalars=1,
    )
    got_px, got_sx, n0 = lax.optimization_barrier((got_px, got_sx, n0))
    got_pd = swap_seq(got_px, 1)
    got_sd = swap_seq(got_sx, 1)

    headed = SDS((OWN, whole, LANES), BF16)
    heads32 = SDS((OWN, chip, LANES), F32)
    qa, ka, va, att_send, other, normed = call(
        attend_first_kernel,
        [headed] * 3 + [SDS((chip, cols), BF16), heads32, SDS((whole, width), BF16)],
        (q0, k0, v0, n0, got_px, got_sx, got_pd, got_sd, gain1, shift1, w_own, bias_own),
        flops=2 * chip * width * 3 * cols + 2 * OWN * whole * whole * LANES,
    )
    a2 = swap_seq(att_send, 2)
    a0, lse = call(
        attend_second_kernel,
        [SDS((chip, cols), BF16), SDS((OWN, 3, 8, whole // 3), F32)],
        (qa, ka, va, other),
        [pltpu.VMEM((OWN, chip, LANES), F32)],
        flops=2 * OWN * whole * whole * LANES,
    )
    a1 = swap_seq(a0, 1)
    a3 = swap_seq(a2, 1)

    middle, normed2, gb2, w1, w2 = call(
        middle_kernel,
        [SDS((chip, width), F32), SDS((chip, width), BF16), SDS((chip, width), BF16)]
        + [SDS((width, hidden), BF16), SDS((hidden, width), BF16)],
        (sidx, a0, a1, a2, a3, toks, keeps, own_cot, cot_c, small, got_sc, w_out, biases[2:3], gain2, shift2)
        + (w_fc1, w_fc2),
        [pltpu.SemaphoreType.DMA((2,))],
        flops=2 * chip * width * width,
        scalars=1,
        far=(15, 16),
    )
    per = width // (4 * nb)
    fast = nb == 8
    fc2_a, fc2_m, zo_send, zo_keep, y1, y_rest, keep_oth, fb_oth, b2, gn, w1, w2 = feed(
        False, fast, per, sidx, bidx, normed2, gb2, w1, fb[0], w2, (w_fc1, w_fc2)
    )
    got2a = swap_seq(fc2_a, 2)
    if not fast:
        y1, keep_oth = by_batch_bit(jnp.concatenate([y1, keep_oth], axis=0), per)
    got_y1 = swap("batch", y1, 1)
    got_zo = swap("batch", zo_send, 2) if fast else zo_send
    ahead = (got2a, got_y1, got_zo)
    fc2_keep, zn_send, zn_keep, y2, keep_own, fb_own, b2_keep, b2_send, gn_keep, gn_send = feed(
        True, fast, per, sidx, bidx, normed2, gb2, w1, fb[1], w2, (b2, gn, y_rest)
    )
    if not fast:
        y2, keep_own = by_batch_bit(jnp.concatenate([y2, keep_own], axis=0), per)
    gn_send, b2_send, zn_send, y2, (got2a, got_y1, got_zo) = lax.optimization_barrier(
        (gn_send, b2_send, zn_send, y2, ahead)
    )
    gn_got = swap_seq(gn_send, 1)
    b2_got = swap_seq(b2_send, 1)
    got_zn = swap("batch", zn_send, 2) if fast else zn_send
    got_y2 = swap("batch", y2, 1)

    gmid, gbr, gatt_send, line_sums = call(
        middle_back_kernel,
        [SDS((block, width), F32), SDS((chip, width), BF16), SDS((chip, cols), BF16), SDS((8, width), F32)],
        (sidx, gn_keep, gn_got, middle, keeps, own_cot, cot_c, small, got_sc, w_out, gain2, gb2),
        flops=2 * chip * width * cols,
        scalars=1,
    )
    gatt_x = swap_seq(gatt_send, 2)
    if fast:
        split = SDS((2, cols // (2 * per), per, width), BF16)
    else:
        split = SDS((2, cols // 2, width), BF16)
    gatt, go_send, go_keep, early, opat, ospe = call(
        branch_back_kernel,
        [SDS((chip, cols), BF16), split, split, SDS((width, LANES), F32)]
        + [SDS((count, width), BF16), SDS((extra, width), BF16)],
        (sidx, bidx, gbr, w_out, a0, a2, middle, keeps, b2_keep, b2_got, biases[3:4], gain1, shift1)
        + (line_sums, fb_own, fb_oth),
        [pltpu.VMEM((hidden, LANES), F32), pltpu.VMEM((cols, width), F32)],
        flops=6 * chip * width * cols,
        scalars=2,
    )
    if not fast:
        halves = [by_batch_bit(jnp.concatenate([go_send[j], go_keep[j]], axis=0), per) for j in range(2)]
        go_send, go_keep = [jnp.stack([halves[j][k] for j in range(2)]) for k in range(2)]
    got_o = swap("batch", go_send, 1)
    msg_0, part_0 = None, None
    if fast:
        msg_0, part_0 = call(
            stage0_kernel,
            [SDS(zn_keep.shape, BF16), SDS(zn_keep.shape, F32)],
            (zn_keep, after(got_zn, go_send), zo_keep, got_zo),
        )
        gatt_x = after(gatt_x, msg_0)
    gatt_x, fc2_m = lax.optimization_barrier((after(gatt_x, go_send), fc2_m))
    got2m = swap_seq(fc2_m, 2)
    pairs = (keep_own, keep_oth, got_y1, got_y2)

    def heads_scratch(heads):
        return [pltpu.VMEM((heads, whole, LANES), BF16)] + [pltpu.VMEM((heads, whole, LANES), F32)] * 3

    def first_heads(lse):
        if fast:
            split = [SDS((8, per, 4 * cols), BF16)] * 2
        else:
            split = [SDS((width // 2, 2 * cols), BF16)] * 2
        return call(
            functools.partial(heads_kernel, fast),
            [SDS((2, whole, cols), BF16)] + split + [SDS((width, LANES), F32)],
            (sidx, bidx, qa, ka, va, lse, gatt, gatt_x, normed, w_own, early),
            [pltpu.VMEM((2, 1, cols), F32)] + heads_scratch(2) + [pltpu.VMEM((width, 2 * cols), F32)],
            flops=20 * whole * whole * LANES,
            scalars=2,
            room=20,
        )

    def tail_part(lse, g01, tile):
        wide = cols + HEAD
        if fast:
            outs = [SDS((width // (2 * per), per, wide), BF16)] * 2
        else:
            outs = [SDS((width // 2, wide), BF16)] * 2
        return call(
            tail_kernel,
            [SDS((chip, width), F32), SDS((chip, width), BF16)] + outs,
            (sidx, bidx, qa, ka, va, lse, gatt, gatt_x, normed, g01, w_own, tile),
            [pltpu.VMEM((1, whole, cols), BF16), pltpu.VMEM((1, 1, cols), F32)]
            + heads_scratch(1)
            + [pltpu.VMEM((width, LANES), F32), pltpu.VMEM((width, wide), F32)],
            flops=10 * whole * whole * LANES,
            scalars=2,
            room=20,
        )

    rest = (sidx, bidx, per, block, chip, hidden, cols, count, extra, width)
    zs = (zn_send, zn_keep, zo_send, zo_keep, msg_0, part_0)
    reduce_all = reduce_eight if fast else reduce_any
    out_fc2, out_out, out_fc1, out_qkv, vec, gpat, gspe = reduce_all(
        rest, pairs, (fc2_keep, got2a, got2m, zs), (go_keep, got_o), lse, gatt_x,
        first_heads, tail_part, (own_p, small), gmid, gain1,
    )
    grad_gains = jnp.stack([vec[:, 0], vec[:, 4]])
    grad_shifts = jnp.stack([vec[:, 1], vec[:, 5]])
    grad_biases = jnp.stack([vec[:, 2], vec[:, 3], vec[:, 7], vec[:, 6]])
    return (
        opat[None],
        ospe[None],
        gpat[None],
        gspe[None],
        grad_gains,
        grad_shifts,
        out_qkv,
        grad_biases,
        out_out,
        out_fc1,
        vec[:, 8:12].reshape(-1),
        out_fc2,
    )


def reduce_eight(
    rest, pairs, twos, outs, lse, gatt_x, first_heads, tail_part, pay, gmid, gain1
):
    sidx, bidx, per, block, chip, hidden, cols, count, extra, width = rest
    fc2_keep, got2a, got2m, zs = twos
    go_keep, got_o = outs
    deep = hidden // 8
    got_0 = swap("batch", zs[4], 4)
    part_0 = zs[5]
    g01, q01_send, q01_keep, tile = first_heads(after(lse, gatt_x))
    g01, got_y2, got2m, got_o, got_0 = lax.optimization_barrier((g01, pairs[3], got2m, got_o, got_0))
    keep_own, keep_oth, got_y1 = pairs[:3]

    def blocks(n, dtype=BF16):
        return SDS((n, per, width), dtype)

    msg_z, msg_y, msg_x, part_f, part_a, part_o, part_p = call(
        stage1_kernel,
        [blocks(16), blocks(16), blocks(8), blocks(16, F32), blocks(8, F32), blocks(4, F32), blocks(4, F32)],
        (bidx, keep_own, keep_oth, got_y1, got_y2, fc2_keep, got2a, got2m, go_keep, got_o, part_0, got_0)
        + (q01_send,),
        scalars=1,
    )
    msg_z, msg_y, msg_x, lse = lax.optimization_barrier((msg_z, msg_y, msg_x, after(lse, g01)))
    got_z = swap("batch", msg_z, 2)
    got_y = swap("batch", msg_y, 1)
    got_x = swap_seq(msg_x, 2)
    gn1_keep, gn1_send, q_send, q_keep = tail_part(lse, g01, tile)
    gn1_send, q_send, got_x, got_y, got_z = lax.optimization_barrier((gn1_send, q_send, got_x, got_y, got_z))
    gn1_c = swap_seq(gn1_send, 1)
    got_q = swap("batch", q_send, 1)
    msg_x, msg_z, msg_y, part_g, part_c, part_q = call(
        stage2_kernel,
        [blocks(8), blocks(10), blocks(2), blocks(8, F32), blocks(10, F32), blocks(2, F32)],
        (part_f, got_z, part_a, got_y, part_o, got_x, part_p, q01_keep),
    )
    got_x = swap_seq(msg_x, 2)
    got_z = swap("batch", msg_z, 2)
    (xsend,) = call(shift_kernel, [SDS((block, width), BF16)], (after(gn1_keep, msg_x), gn1_c))
    gn1_x = swap_seq(xsend, 2)
    msg, kept = call(
        stage3_kernel, [blocks(9), blocks(9, F32)], (part_g, after(got_x, xsend, got_q), part_c, got_z)
    )
    got_last = swap("batch", msg, 4)
    got_q = after(got_q, msg)
    quarter = SDS((4, per, cols + HEAD), BF16)
    q1, q2, q3, q_kept = call(
        quarter_kernel, [quarter, quarter, quarter, SDS(quarter.shape, F32)], (bidx, q_keep, got_q), scalars=1
    )
    got_qz = swap_four((q1, q2, q3), 1)
    got_yb = swap("batch", after(msg_y, q1), 1)
    gpat, gspe = call(
        final_kernel,
        [SDS((count, width), F32), SDS((extra, width), F32)],
        (gn1_keep, gn1_c, after(gn1_x, q1), *pay, gmid, gain1),
    )
    got_last = after(got_last, gpat)
    swap_send, swap_keep, out_fc2, out_out = call(
        sums_kernel,
        [SDS((2 * per, width), BF16), SDS((2 * per, width), F32), SDS((deep, width), F32), SDS((per, width), F32)],
        (kept, got_last, part_q, got_yb),
    )
    swap_got = swap_seq(swap_send, 1)
    row = SDS((per, 5 * LANES), BF16)
    s1, s2, s3, own = call(
        owner_kernel,
        [row, row, row, SDS(row.shape, F32)],
        (sidx, kept, got_last, q_kept, *after(got_qz, out_out)),
        [pltpu.VMEM((4, per, 5 * LANES), F32)],
        scalars=1,
    )
    gots = [swap_seq(v, k) for k, v in ((1, s1), (2, s2), (3, s3))]
    out_qkv, vec, out_fc1 = call(
        collect_kernel,
        [SDS((per, 3 * width), F32), SDS((per, LANES), F32), SDS((per, 4 * hidden), F32)],
        (sidx, own, *gots, swap_keep, swap_got),
        [pltpu.VMEM((4, per, 5 * LANES), F32)],
        scalars=1,
    )
    return out_fc2, out_out, out_fc1, out_qkv, vec[:, HEAD:], gpat, gspe


def reduce_any(
    rest, pairs, twos, outs, lse, gatt_x, first_heads, tail_part, pay, gmid, gain1
):
    sidx, bidx, per, block, chip, hidden, cols, count, extra, width = rest
    s = lax.axis_index("seq")
    nb = lax.axis_size("batch")
    nbits = bits_of("batch")
    low = nbits - 1
    fc2_keep, got2a, got2m, zs = twos
    go_keep, got_o = outs
    keep_own, keep_oth, got_oth, got_own = [
        split_bits(p.reshape(2, 2, nb // 2, per, hidden), 2, low) for p in pairs
    ]
    g01, q01_top, q01_low, tile = first_heads(lse)
    send_own, parts_own = to_send([keep_own, got_own], 0, 1, "seq")
    send_oth, parts_oth = to_send([keep_oth, got_oth], 0, 1, "seq")
    got_b = swap_seq(jnp.concatenate([send_own, send_oth], axis=-1), 2)
    sum_own = sum_rest(parts_own + [got_b[..., hidden:]], 1, 1)
    sum_oth = sum_rest(parts_oth + [got_b[..., :hidden]], 1, 1)
    own_c = s & 1
    other = jnp.concatenate([pick(sum_own, 1 - own_c, 0), pick(sum_oth, 1 - own_c, 0)], axis=-1)
    got = swap_seq(other.astype(BF16), 1).astype(F32)
    rel = jnp.stack([pick(sum_own, own_c, 0), got[:, :hidden], pick(sum_oth, own_c, 0), got[:, hidden:]])
    out_fc1 = jnp.concatenate([pick(rel, s ^ a, 0) for a in range(4)], axis=1)
    zn_send, zn_keep, zo_send, zo_keep = zs[:4]
    got2 = jnp.concatenate([got2a, got2m, swap_seq(jnp.concatenate([zo_send, zo_keep], axis=0), 2)], axis=0)
    fc2_keep = jnp.concatenate([fc2_keep, zn_send, zn_keep], axis=0)
    parts = [split_bits(p.reshape(nb, -1, width), 0, nbits) for p in (fc2_keep, got2)]
    out_fc2 = sum_rest(parts, 0, 0)
    parts = [split_bits(p.reshape(2, nb // 2, per, width), 1, low) for p in (go_keep, got_o)]
    parts = [p[0] for p in parts] + [swap_seq(total([p[1] for p in parts]).astype(BF16), 2)]
    out_out = sum_rest(parts, 0, 1)
    gn1_keep, gn1_send, q2_top, q2_low = tail_part(lse, g01, tile)
    q_all = [jnp.concatenate(v, axis=1) for v in ((q01_top, q2_top), (q01_low, q2_low))]
    q_send, q_keep = by_batch_bit(jnp.concatenate(q_all, axis=0), per)
    gn1_c = swap_seq(gn1_send, 1)
    gn1_x = swap_seq((gn1_keep[block:] + gn1_c[block:].astype(F32)).astype(BF16), 2)
    gpat, gspe = call(
        final_kernel,
        [SDS((count, width), F32), SDS((extra, width), F32)],
        (gn1_keep, gn1_c, gn1_x, *pay, gmid, gain1),
    )
    wide = 5 * LANES
    parts = [split_bits(p.reshape(4, nb // 2, per, wide), 1, low) for p in (q_keep, swap("batch", q_send, 1))]
    sum_q = sum_rest(parts, 1, 1)
    pieces = [pick(sum_q, s, 0)] + [
        swap_seq(pick(sum_q, s ^ j, 0).astype(BF16), j).astype(F32) for j in (1, 2, 3)
    ]
    rel = jnp.stack([p[:, : 3 * cols] for p in pieces])
    absolute = jnp.stack([pick(rel, s ^ a, 0) for a in range(4)], axis=1)
    out_qkv = absolute.reshape(-1, 4, OWN, 3, HEAD).transpose(0, 3, 1, 2, 4).reshape(-1, 3 * width)
    vec = total([p[:, 3 * cols :] for p in pieces])
    return out_fc2, out_out, out_fc1, out_qkv, vec, gpat, gspe


def solution(mesh):
    tok = P("batch", "seq", None)
    ids = P("batch", "seq")
    split = P(None, ("seq", "batch"))
    rows = P(("seq", "batch"), None)
    return jax.shard_map(
        body,
        mesh=mesh,
        in_specs=(tok, tok, ids, ids, P("batch", None)) + (P(),) * 8 + (tok, tok),
        out_specs=(tok, tok, tok, tok, split, split, rows, split, rows, rows, P(("seq", "batch")), rows),
        check_vma=False,
    )
```

time: 159 us -> 143 us (0.90)
  waiting for transfers between devices: 48.3 us -> 32.8 us
  starting transfers between devices: 30.8 us -> 37.6 us
  local copies, waits for them, and re-layouts: 13.6 us -> 7.2 us
    ppermute x32 -> x38, waiting for transfers between devices: 48.3 us -> 32.8 us  [swap(): lax.ppermute(v, kind, [(i, i ^ mask) for i in range(lax.axis_size(kind))])]
    dynamic_slice x3 -> x0, local copies, waits for them, and re-layouts: 7.89 us -> none  [the longest x1 4.96 us: body(): lax.dynamic_slice(w_fc2, ((s ^ j) * hidden, 0), (hidden, width))]
    ppermute x32 -> x38, starting transfers between devices: 30.8 us -> 37.6 us  [swap(): lax.ppermute(v, kind, [(i, i ^ mask) for i in range(lax.axis_size(kind))])]
    concatenate x3 -> x1, other arithmetic: 1.85 us -> 0.01 us  [body(): ids = jnp.concatenate([segment_ids[0], special_order[0] // 2])]
    pallas_call x18 -> x21, Pallas kernels: 60.4 us -> 60.8 us  [call(): pl.pallas_call(kernel, out_shape=outs, in_specs=[smem() if i < scalars el...]
  transfers between devices with their start and end apart: 32 -> 38, of which waited for: 16 -> 17; matrix products, arithmetic and copies ran while one was open for 7% -> 3% of each run, Pallas kernels for 32% -> 29%
where the time goes in v5:
time: 143 us; the launch traced here: 142 us
  Pallas kernels  60.8 us (43%)
  starting transfers between devices  37.6 us (26%)
  waiting for transfers between devices  32.8 us (23%)
  local copies, waits for them, and re-layouts  7.2 us (5%)
  other arithmetic  3.1 us (2%)
    pallas_call x21, Pallas kernels, call(): pl.pallas_call(kernel, out_shape=outs, in_specs=[smem() if i < scalars el...  60.8 us
    ppermute x38, starting transfers between devices, swap(): lax.ppermute(v, kind, [(i, i ^ mask) for i in range(lax.axis_size(kind))])  37.6 us
    ppermute x38, waiting for transfers between devices, swap(): lax.ppermute(v, kind, [(i, i ^ mask) for i in range(lax.axis_size(kind))])  32.8 us
    unnamed x14, local copies, waits for them, and re-layouts  2.86 us
  transfers between devices with their start and end apart: 38, of which 17 were waited for; matrix products, arithmetic and copies ran while one was open for 3% of the time, Pallas kernels for 29%

profile of v5, /device:TPU:0, one launch (start us, length us, event | category | flops | bytes accessed | tf_op | source)
XLA Modules:
  0.0 142.4 jit_solution(13776595848289717513)
XLA Ops:
  0.6 3.0 %collective-permute-start.2 = (bf16[256,768]{1,0:T(8,128)(2,1)}, bf16[256,768]{1,0:T(8,128)(2,1)S(1)}, u32[]{:S(2)}, u32[]{:S(2)}) collective-permute-start(bf16[256,768]{1,0:T(8,128)(2,1)} %bitcast.31), channel_id=1, source_target_pairs={{0,16},{8,24},{16,0},{24,8},{1,17},{9,25},{17,1},{25,9},{2,18},{10... | collective-permute-start | bytes 1179656 | tf_op jit(solution)/shard_map/ppermute | solution.py:760
  3.6 0.7 convert_reduce_fusion
  4.3 0.7 fusion.3
  5.1 1.7 %concatenate.10.s0.c0 = bf16[32,768]{1,0:T(8,128)(2,1)S(1)} concatenate(bf16[4,768]{1,0:T(4,128)(2,1)} %bitcast.35, bf16[1,768]{1,0:T(2,128)(2,1)S(1)} %broadcast_in_dim.24, bf16[11,768]{1,0:T(8,128)(2,1)S(1)} %slice.72, bf16[4,768]{1,0:T(4,128)(2,1)} %bitcast.36, bf16[12,768]{1,0:T(8,128)(2,1)S(1)} %slice.73), dimensions={0} | concatenate | bytes 98304 | tf_op jit(solution)/shard_map/concatenate | solution.py:849
  7.4 0.8 fusion.6
  8.2 0.9 fusion.5
  9.1 2.0 %copy-done.1 = bf16[768,2304]{1,0:T(8,128)(2,1)S(1)} copy-done((bf16[768,2304]{1,0:T(8,128)(2,1)S(1)}, bf16[768,2304]{1,0:T(8,128)(2,1)}, u32[]{:S(2)}) %copy-start.1) | copy-done | bytes 3538968
  11.1 0.7 copy-done.4
  11.8 0.8 shard_map.238
  12.8 1.9 %shard_map.239 = (bf16[3,576,128]{2,1,0:T(8,128)(2,1)S(1)}, bf16[3,576,128]{2,1,0:T(8,128)(2,1)S(1)}, bf16[3,576,128]{2,1,0:T(8,128)(2,1)S(1)}, bf16[576,768]{1,...) custom-call(s32[1,16]{1,0:T(1,128)S(1)} %copy-done.6, bf16[256,768]{1,0:T(8,128)(2,1)S(1)} %bitcast.33, ...), custom_call_target="tpu_custom_call" | custom-call | flops 509607936 | bytes 5268032 | tf_op jit(solution)/shard_map/pallas_call | solution.py:77
  15.3 1.3 collective-permute-done.5.s3
  16.6 7.9 %shard_map.240 = (bf16[3,1152,128]{2,1,0:T(8,128)(2,1)S(1)}, bf16[3,1152,128]{2,1,0:T(8,128)(2,1)S(1)}, bf16[3,1152,128]{2,1,0:T(8,128)(2,1)S(1)}, bf16[576,192]...) custom-call(bf16[3,576,128]{2,1,0:T(8,128)(2,1)S(1)} %get-tuple-element.169.q0, ...), custom_call_target="tpu_custom_call" | custom-call | flops 1528823808 | bytes 9617920 | tf_op jit(solution)/shard_map/pallas_call | solution.py:77
  24.5 1.7 %collective-permute-start.7 = (bf16[576,192]{1,0:T(8,128)(2,1)S(1)}, bf16[576,192]{1,0:T(8,128)(2,1)S(1)}, u32[]{:S(2)}, u32[]{:S(2)}) collective-permute-start(bf16[576,192]{1,0:T(8,128)(2,1)S(1)} %get-tuple-element.181), channel_id=1, source_target_pairs={{0,16},{8,24},{16,0},{24,8},{1,17},{9,25},{17,1},{25,9},{2,18},{10... | collective-permute-start | bytes 663560 | tf_op jit(solution)/shard_map/ppermute | solution.py:760
  26.3 7.0 %shard_map.241 = (bf16[576,192]{1,0:T(8,128)(2,1)S(1)}, f32[3,3,8,384]{3,2,1,0:T(8,128)S(1)}) custom-call(bf16[3,1152,128]{2,1,0:T(8,128)(2,1)S(1)} %get-tuple-element.176.qa, bf16[3,1152,128]{2,1,0:T(8,128)(2,1)S(1)} %get-tuple-element.177.ka, bf16[3,1152,128]{2,1,0:T(8,128)(2,1)S(1)} %get-tuple-element.178.va, f32[3,576,128]{2,1,0:T(8,128)S(1)} %get-tuple-element.179.other), custom_call_target="tpu_custom_call" | custom-call | flops 1019215872 | bytes 3870720 | tf_op jit(solution)/shard_map/pallas_call | solution.py:77
  33.3 0.6 collective-permute-start.6
  34.0 1.1 collective-permute-done.6.a1
  35.5 3.2 %shard_map.242 = (f32[576,768]{1,0:T(8,128)S(1)}, bf16[576,768]{1,0:T(8,128)(2,1)S(1)}, bf16[576,768]{1,0:T(8,128)(2,1)S(1)}, bf16[768,768]{1,0:T(8,128)(2,1)S(1)}, bf16[768,768]{1,0:T(8,128)(2,1)S(1)}) custom-call(s32[1]{0:T(128)} %bitcast.sref, bf16[576,192]{1,0:T(8,128)(2,1)S(1)} %get-tuple-element.180.a0, ...), custom_call_target="tpu_custom_call" | custom-call | flops 679477248 | bytes 19473412 | tf_op jit(solution)/shard_map/pallas_call | solution.py:77
  38.7 6.4 %shard_map.243 = (bf16[8,24,768]{2,1,0:T(8,128)(2,1)S(1)}, bf16[8,24,768]{2,1,0:T(8,128)(2,1)S(1)}, bf16[4,48,768]{2,1,0:T(8,128)(2,1)S(1)}, bf16[4,48,768]{2,1,...) custom-call(s32[1]{0:T(128)} %bitcast.sref, ...), custom_call_target="tpu_custom_call" | custom-call | flops 4076863488 | bytes 21829640 | tf_op jit(solution)/shard_map/pallas_call | solution.py:77
  45.1 1.6 %collective-permute-start.10 = (bf16[8,24,768]{2,1,0:T(8,128)(2,1)S(1)}, bf16[8,24,768]{2,1,0:T(8,128)(2,1)S(1)}, u32[]{:S(2)}, u32[]{:S(2)}) collective-permute-start(bf16[8,24,768]{2,1,0:T(8,128)(2,1)S(1)} %get-tuple-element.200), channel_id=1, source_target_pairs={{0,16},{8,24},{16,0},{24,8},{1,17},{9,25},{17,1},{25,9},{2,18},{10... | collective-permute-start | bytes 884744 | tf_op jit(solution)/shard_map/ppermute | solution.py:760
  46.7 1.5 %collective-permute-start.11 = (bf16[8,24,768]{2,1,0:T(8,128)(2,1)S(1)}, bf16[8,24,768]{2,1,0:T(8,128)(2,1)S(1)}, u32[]{:S(2)}, u32[]{:S(2)}) collective-permute-start(bf16[8,24,768]{2,1,0:T(8,128)(2,1)S(1)} %get-tuple-element.201), channel_id=1, source_target_pairs={{0,1},{1,0},{2,3},{3,2},{4,5},{5,4},{6,7},{7,6},{8,9},{9,8},{10,11... | collective-permute-start | bytes 884744 | tf_op jit(solution)/shard_map/ppermute | solution.py:760
  48.2 1.6 %collective-permute-start.12 = (bf16[4,48,768]{2,1,0:T(8,128)(2,1)S(1)}, bf16[4,48,768]{2,1,0:T(8,128)(2,1)S(1)}, u32[]{:S(2)}, u32[]{:S(2)}) collective-permute-start(bf16[4,48,768]{2,1,0:T(8,128)(2,1)S(1)} %get-tuple-element.202), channel_id=1, source_target_pairs={{0,2},{1,3},{2,0},{3,1},{4,6},{5,7},{6,4},{7,5},{8,10},{9,11},{10,... | collective-permute-start | bytes 884744 | tf_op jit(solution)/shard_map/ppermute | solution.py:760
  49.8 5.1 %shard_map.244 = (bf16[8,48,768]{2,1,0:T(8,128)(2,1)S(1)}, bf16[4,48,768]{2,1,0:T(8,128)(2,1)S(1)}, bf16[4,48,768]{2,1,0:T(8,128)(2,1)S(1)}, bf16[24,24,768]{2,1...) custom-call(s32[1]{0:T(128)} %bitcast.sref, ...), custom_call_target="tpu_custom_call" | custom-call | flops 4076863488 | bytes 14604296 | tf_op jit(solution)/shard_map/pallas_call | solution.py:77
  54.9 0.5 collective-permute-done.11.y1
  55.4 1.2 collective-permute-done.12.oth_got
  56.7 0.5 collective-permute-start.17
  57.4 1.6 %collective-permute-start.16 = (bf16[4,48,768]{2,1,0:T(8,128)(2,1)S(1)}, bf16[4,48,768]{2,1,0:T(8,128)(2,1)S(1)}, u32[]{:S(2)}, u32[]{:S(2)}) collective-permute-start(bf16[4,48,768]{2,1,0:T(8,128)(2,1)S(1)} %get-tuple-element.219), channel_id=1, source_target_pairs={{0,2},{1,3},{2,0},{3,1},{4,6},{5,7},{6,4},{7,5},{8,10},{9,11},{10,... | collective-permute-start | bytes 884744 | tf_op jit(solution)/shard_map/ppermute | solution.py:760
  59.1 2.0 %shard_map.245 = (f32[288,768]{1,0:T(8,128)S(1)}, bf16[576,768]{1,0:T(8,128)(2,1)S(1)}, bf16[576,192]{1,0:T(8,128)(2,1)S(1)}, f32[8,768]{1,0:T(8,128)S(1)}) custom-call(s32[1]{0:T(128)} %bitcast.sref, f32[576,768]{1,0:T(8,128)S(1)} %get-tuple-element.195.gn_keep, bf16[576,768]{1,0:T(8,128)(2,1)S(1)} %collective-permute-done.13.gn_got, ...), custom_call_target="tpu_custom_call" | custom-call | flops 169869312 | bytes 9686020 | tf_op jit(solution)/shard_map/pallas_call | solution.py:77
  61.1 0.8 collective-permute-start.15
  61.9 1.7 %shard_map.246 = (bf16[576,192]{1,0:T(8,128)(2,1)S(1)}, bf16[2,4,24,768]{3,2,1,0:T(8,128)(2,1)S(1)}, bf16[2,4,24,768]{3,2,1,0:T(8,128)(2,1)S(1)}, f32[768,128]{1...) custom-call(s32[1]{0:T(128)} %bitcast.sref, s32[1]{0:T(128)} %bitcast.1.bref, ...), custom_call_target="tpu_custom_call" | custom-call | flops 509607936 | bytes 7541768 | tf_op jit(solution)/shard_map/pallas_call | solution.py:77
  63.6 1.4 collective-permute-start.19
  65.0 1.6 %collective-permute-done.16.own_got = bf16[4,48,768]{2,1,0:T(8,128)(2,1)S(1)} collective-permute-done((bf16[4,48,768]{2,1,0:T(8,128)(2,1)S(1)}, bf16[4,48,768]{2,1,0:T(8,128)(2,1)S(1)}, u32[]{:S(2)}, u32[]{:S(2)}) %collective-permute-start.16) | collective-permute-done | bytes 294944 | tf_op jit(solution)/shard_map/ppermute | solution.py:760
  66.8 2.6 %collective-permute-start.20 = (bf16[4,48,768]{2,1,0:T(8,128)(2,1)S(1)}, bf16[4,48,768]{2,1,0:T(8,128)(2,1)S(1)}, u32[]{:S(2)}, u32[]{:S(2)}) collective-permute-start(bf16[4,48,768]{2,1,0:T(8,128)(2,1)S(1)} %get-tuple-element.224), channel_id=1, source_target_pairs={{0,4},{1,5},{2,6},{3,7},{4,0},{5,1},{6,2},{7,3},{8,12},{9,13},{10,... | collective-permute-start | bytes 884744 | tf_op jit(solution)/shard_map/ppermute | solution.py:760
  69.4 0.8 collective-permute-done.15.gx
  70.2 0.8 collective-permute-start.18
  70.9 12.1 %shard_map.248 = (bf16[2,1152,192]{2,1,0:T(8,128)(2,1)S(1)}, bf16[8,24,768]{2,1,0:T(8,128)(2,1)S(1)}, bf16[8,24,768]{2,1,0:T(8,128)(2,1)S(1)}, f32[768,128]{1,0:T(8,128)S(1)}) custom-call(s32[1]{0:T(128)} %bitcast.sref, s32[1]{0:T(128)} %bitcast.1.bref, bf16[3,1152,128]{2,1,0:T(8,128)(2,1)S(1)} %get-tuple-element.176.qa, ...), custom_call_target="tpu_custom_call" | custom-call | flops 3397386240 | bytes 8220680 | tf_op jit(solution)/shard_map/pallas_call | solution.py:77
  83.1 2.0 %collective-permute-done.19.y3 = bf16[2,4,24,768]{3,2,1,0:T(8,128)(2,1)S(1)} collective-permute-done((bf16[2,4,24,768]{3,2,1,0:T(8,128)(2,1)S(1)}, bf16[2,4,24,768]{3,2,1,0:T(8,128)(2,1)S(1)}, u32[]{:S(2)}, u32[]{:S(2)}) %collective-permute-start.19) | collective-permute-done | bytes 294944 | tf_op jit(solution)/shard_map/ppermute | solution.py:760
  85.0 0.5 shard_map.249
  85.6 0.6 collective-permute-start.22
  86.1 1.6 %collective-permute-start.23 = (bf16[16,24,768]{2,1,0:T(8,128)(2,1)S(1)}, bf16[16,24,768]{2,1,0:T(8,128)(2,1)S(1)}, u32[]{:S(2)}, u32[]{:S(2)}) collective-permute-start(bf16[16,24,768]{2,1,0:T(8,128)(2,1)S(1)} %get-tuple-element.257), channel_id=1, source_target_pairs={{0,2},{1,3},{2,0},{3,1},{4,6},{5,7},{6,4},{7,5},{8,10},{9,11},{10,... | collective-permute-start | bytes 1769480 | tf_op jit(solution)/shard_map/ppermute | solution.py:760
  87.7 0.8 collective-permute-start.21
  88.5 8.2 %shard_map.250 = (f32[576,768]{1,0:T(8,128)S(1)}, bf16[576,768]{1,0:T(8,128)(2,1)S(1)}, bf16[16,24,256]{2,1,0:T(8,128)(2,1)S(1)}, bf16[16,24,256]{2,1,0:T(8,128)(2,1)S(1)}) custom-call(s32[1]{0:T(128)} %bitcast.sref, s32[1]{0:T(128)} %bitcast.1.bref, bf16[3,1152,128]{2,1,0:T(8,128)(2,1)S(1)} %get-tuple-element.176.qa, ...), custom_call_target="tpu_custom_call" | custom-call | flops 1698693120 | bytes 10285064 | tf_op jit(solution)/shard_map/pallas_call | solution.py:77
  96.8 3.8 %collective-permute-done.22.got_y = bf16[16,24,768]{2,1,0:T(8,128)(2,1)S(1)} collective-permute-done((bf16[16,24,768]{2,1,0:T(8,128)(2,1)S(1)}, bf16[16,24,768]{2,1,0:T(8,128)(2,1)S(1)}, u32[]{:S(2)}, u32[]{:S(2)}) %collective-permute-start.22) | collective-permute-done | bytes 589856 | tf_op jit(solution)/shard_map/ppermute | solution.py:760
  101.1 1.6 %collective-permute-start.28 = (bf16[10,24,768]{2,1,0:T(8,128)(2,1)S(1)}, bf16[10,24,768]{2,1,0:T(8,128)(2,1)S(1)}, u32[]{:S(2)}, u32[]{:S(2)}) collective-permute-start(bf16[10,24,768]{2,1,0:T(8,128)(2,1)S(1)} %get-tuple-element.274), channel_id=1, source_target_pairs={{0,2},{1,3},{2,0},{3,1},{4,6},{5,7},{6,4},{7,5},{8,10},{9,11},{10,... | collective-permute-start | bytes 1105928 | tf_op jit(solution)/shard_map/ppermute | solution.py:760
  102.8 0.8 collective-permute-start.27
  103.5 1.5 %collective-permute-start.26 = (bf16[16,24,256]{2,1,0:T(8,128)(2,1)S(1)}, bf16[16,24,256]{2,1,0:T(8,128)(2,1)S(1)}, u32[]{:S(2)}, u32[]{:S(2)}) collective-permute-start(bf16[16,24,256]{2,1,0:T(8,128)(2,1)S(1)} %get-tuple-element.270), channel_id=1, source_target_pairs={{0,1},{1,0},{2,3},{3,2},{4,5},{5,4},{6,7},{7,6},{8,9},{9,8},{10,11... | collective-permute-start | bytes 589832 | tf_op jit(solution)/shard_map/ppermute | solution.py:760
  105.1 1.3 collective-permute-start.25
  106.5 3.8 %collective-permute-done.26.got = bf16[16,24,256]{2,1,0:T(8,128)(2,1)S(1)} collective-permute-done((bf16[16,24,256]{2,1,0:T(8,128)(2,1)S(1)}, bf16[16,24,256]{2,1,0:T(8,128)(2,1)S(1)}, u32[]{:S(2)}, u32[]{:S(2)}) %collective-permute-start.26) | collective-permute-done | bytes 196640 | tf_op jit(solution)/shard_map/ppermute | solution.py:760
  110.3 2.3 %collective-permute-done.27.got_x = bf16[8,24,768]{2,1,0:T(8,128)(2,1)S(1)} collective-permute-done((bf16[8,24,768]{2,1,0:T(8,128)(2,1)S(1)}, bf16[8,24,768]{2,1,0:T(8,128)(2,1)S(1)}, u32[]{:S(2)}, u32[]{:S(2)}) %collective-permute-start.27) | collective-permute-done | bytes 294944 | tf_op jit(solution)/shard_map/ppermute | solution.py:760
  112.7 2.7 %collective-permute-start.29 = (bf16[9,24,768]{2,1,0:T(8,128)(2,1)S(1)}, bf16[9,24,768]{2,1,0:T(8,128)(2,1)S(1)}, u32[]{:S(2)}, u32[]{:S(2)}) collective-permute-start(bf16[9,24,768]{2,1,0:T(8,128)(2,1)S(1)} %get-tuple-element.275), channel_id=1, source_target_pairs={{0,4},{1,5},{2,6},{3,7},{4,0},{5,1},{6,2},{7,3},{8,12},{9,13},{10,... | collective-permute-start | bytes 995336 | tf_op jit(solution)/shard_map/ppermute | solution.py:760
  115.4 1.6 %collective-permute-start.33 = (bf16[2,24,768]{2,1,0:T(8,128)(2,1)S(1)}, bf16[2,24,768]{2,1,0:T(8,128)(2,1)S(1)}, u32[]{:S(2)}, u32[]{:S(2)}) collective-permute-start(bf16[2,24,768]{2,1,0:T(8,128)(2,1)S(1)} %get-tuple-element.289), channel_id=1, source_target_pairs={{0,1},{1,0},{2,3},{3,2},{4,5},{5,4},{6,7},{7,6},{8,9},{9,8},{10,11... | collective-permute-start | bytes 221192 | tf_op jit(solution)/shard_map/ppermute | solution.py:760
  117.3 3.2 %collective-permute-start.32 = (bf16[4,24,256]{2,1,0:T(8,128)(2,1)S(1)}, bf16[4,24,256]{2,1,0:T(8,128)(2,1)S(1)}, u32[]{:S(2)}, u32[]{:S(2)}) collective-permute-start(bf16[4,24,256]{2,1,0:T(8,128)(2,1)S(1)} %get-tuple-element.286), channel_id=1, source_target_pairs={{0,6},{1,7},{2,4},{3,5},{4,2},{5,3},{6,0},{7,1},{8,14},{9,15},{10,... | collective-permute-start | bytes 147464 | tf_op jit(solution)/shard_map/ppermute | solution.py:760
  120.5 0.9 collective-permute-done.25.x0
  121.8 1.5 %shard_map.255 = (f32[256,768]{1,0:T(8,128)}, f32[4,768]{1,0:T(4,128)}) custom-call(f32[576,768]{1,0:T(8,128)S(1)} %get-tuple-element.268.keep.k0, bf16[576,768]{1,0:T(8,128)(2,1)S(1)} %collective-permute-done.24.got.c0, bf16[288,768]{1,0:T(8,128)(2,1)S(1)} %collective-permute-done.25.x0, bf16[256,768]{1,0:T(8,128)(2,1)S(1)} %bitcast.34, ...), custom_call_target="tpu_custom_call" | custom-call | bytes 5225472 | tf_op jit(solution)/shard_map/pallas_call | solution.py:77
  123.3 9.7 %collective-permute-done.29.got = bf16[9,24,768]{2,1,0:T(8,128)(2,1)S(1)} collective-permute-done((bf16[9,24,768]{2,1,0:T(8,128)(2,1)S(1)}, bf16[9,24,768]{2,1,0:T(8,128)(2,1)S(1)}, u32[]{:S(2)}, u32[]{:S(2)}) %collective-permute-start.29) | collective-permute-done | bytes 331808 | tf_op jit(solution)/shard_map/ppermute | solution.py:760
  133.0 0.8 shard_map.256
  133.9 0.6 collective-permute-start.34
  134.4 0.8 collective-permute-start.35
  135.2 0.7 collective-permute-start.36
  135.9 2.6 %collective-permute-done.35.g2 = bf16[24,640]{1,0:T(8,128)(2,1)S(1)} collective-permute-done((bf16[24,640]{1,0:T(8,128)(2,1)S(1)}, bf16[24,640]{1,0:T(8,128)(2,1)S(1)}, u32[]{:S(2)}, u32[]{:S(2)}) %collective-permute-start.35) | collective-permute-done | bytes 30752 | tf_op jit(solution)/shard_map/ppermute | solution.py:760
  138.8 0.9 shard_map.258
  140.1 0.6 reshape.57
  140.7 0.6 pad_maximum_fusion.2
  141.3 0.6 pad_maximum_fusion.1
  141.8 0.6 pad_maximum_fusion
  (65 shorter events, 4.8 us)
Async XLA Ops:
  0.6 14.1 %collective-permute-start.2 = (bf16[256,768]{1,0:T(8,128)(2,1)}, bf16[256,768]{1,0:T(8,128)(2,1)S(1)}, u32[]{:S(2)}, u32[]{:S(2)}) collective-permute-start(bf16[256,768]{1,0:T(8,128)(2,1)} %bitcast.31), channel_id=1, source_target_pairs={{0,16},{8,24},{16,0},{24,8},{1,17},{9,25},{17,1},{25,9},{2,18},{10... | collective-permute-start | bytes 1179656 | tf_op jit(solution)/shard_map/ppermute | solution.py:760
  3.6 9.0 %collective-permute-start = (bf16[256,768]{1,0:T(8,128)(2,1)}, bf16[256,768]{1,0:T(8,128)(2,1)S(1)}, u32[]{:S(2)}, u32[]{:S(2)}) collective-permute-start(bf16[256,768]{1,0:T(8,128)(2,1)} %bitcast.32), channel_id=1, source_target_pairs={{0,8},{8,0},{16,24},{24,16},{1,9},{9,1},{17,25},{25,17},{2,10},{10... | collective-permute-start | bytes 1179656 | tf_op jit(solution)/shard_map/ppermute | solution.py:760
  6.7 8.0 %collective-permute-start.3 = (bf16[32,768]{1,0:T(8,128)(2,1)S(1)}, bf16[32,768]{1,0:T(8,128)(2,1)S(1)}, u32[]{:S(2)}, u32[]{:S(2)}) collective-permute-start(bf16[32,768]{1,0:T(8,128)(2,1)S(1)} %concatenate.10.s0.c0), channel_id=1, source_target_pairs={{0,16},{8,24},{16,0},{24,8},{1,17},{9,25},{17,1},{25,9},{2,18},{10... | collective-permute-start | bytes 147464 | tf_op jit(solution)/shard_map/ppermute | solution.py:760
  6.9 5.7 %collective-permute-start.1 = (bf16[32,768]{1,0:T(8,128)(2,1)S(1)}, bf16[32,768]{1,0:T(8,128)(2,1)S(1)}, u32[]{:S(2)}, u32[]{:S(2)}) collective-permute-start(bf16[32,768]{1,0:T(8,128)(2,1)S(1)} %concatenate.10.s0.c0), channel_id=1, source_target_pairs={{0,8},{8,0},{16,24},{24,16},{1,9},{9,1},{17,25},{25,17},{2,10},{10... | collective-permute-start | bytes 147464 | tf_op jit(solution)/shard_map/ppermute | solution.py:760
  9.1 2.0 %copy-start.1 = (bf16[768,2304]{1,0:T(8,128)(2,1)S(1)}, bf16[768,2304]{1,0:T(8,128)(2,1)}, u32[]{:S(2)}) copy-start(bf16[768,2304]{1,0:T(8,128)(2,1)} %w.1) | copy-start | bytes 10616836
  11.1 0.7 copy-start.4
  11.8 1.0 copy-start.3
  11.8 1.0 copy-start.6
  14.7 1.9 %collective-permute-start.4 = (bf16[256,768]{1,0:T(8,128)(2,1)S(1)}, bf16[256,768]{1,0:T(8,128)(2,1)S(1)}, u32[]{:S(2)}, u32[]{:S(2)}) collective-permute-start(bf16[256,768]{1,0:T(8,128)(2,1)S(1)} %collective-permute-done.2.p2), channel_id=1, source_target_pairs={{0,8},{8,0},{16,24},{24,16},{1,9},{9,1},{17,25},{25,17},{2,10},{10... | collective-permute-start | bytes 1179656 | tf_op jit(solution)/shard_map/ppermute | solution.py:760
  14.8 1.8 %collective-permute-start.5 = (bf16[32,768]{1,0:T(8,128)(2,1)S(1)}, bf16[32,768]{1,0:T(8,128)(2,1)S(1)}, u32[]{:S(2)}, u32[]{:S(2)}) collective-permute-start(bf16[32,768]{1,0:T(8,128)(2,1)S(1)} %collective-permute-done.3.s2), channel_id=1, source_target_pairs={{0,8},{8,0},{16,24},{24,16},{1,9},{9,1},{17,25},{25,17},{2,10},{10... | collective-permute-start | bytes 147464 | tf_op jit(solution)/shard_map/ppermute | solution.py:760
  16.6 9.7 %copy-start.2 = (bf16[1,256,768]{2,1,0:T(8,128)(2,1)S(1)}, bf16[1,256,768]{2,1,0:T(8,128)(2,1)}, u32[]{:S(2)}) copy-start(bf16[1,256,768]{2,1,0:T(8,128)(2,1)} %param.30) | copy-start | bytes 1179652
  24.5 9.3 %collective-permute-start.7 = (bf16[576,192]{1,0:T(8,128)(2,1)S(1)}, bf16[576,192]{1,0:T(8,128)(2,1)S(1)}, u32[]{:S(2)}, u32[]{:S(2)}) collective-permute-start(bf16[576,192]{1,0:T(8,128)(2,1)S(1)} %get-tuple-element.181), channel_id=1, source_target_pairs={{0,16},{8,24},{16,0},{24,8},{1,17},{9,25},{17,1},{25,9},{2,18},{10... | collective-permute-start | bytes 663560 | tf_op jit(solution)/shard_map/ppermute | solution.py:760
  26.3 7.7 %collective-permute-start.9 = (bf16[256,768]{1,0:T(8,128)(2,1)S(1)}, bf16[256,768]{1,0:T(8,128)(2,1)S(1)}, u32[]{:S(2)}, u32[]{:S(2)}) collective-permute-start(bf16[256,768]{1,0:T(8,128)(2,1)S(1)} %bitcast.28), channel_id=1, source_target_pairs={{0,8},{8,0},{16,24},{24,16},{1,9},{9,1},{17,25},{25,17},{2,10},{10... | collective-permute-start | bytes 1179656 | tf_op jit(solution)/shard_map/ppermute | solution.py:760
  26.3 7.7 %copy-start.5 = (f32[4,768]{1,0:T(4,128)S(1)}, f32[4,768]{1,0:T(4,128)}, u32[]{:S(2)}) copy-start(f32[4,768]{1,0:T(4,128)} %biases.1) | copy-start | bytes 36868
  26.3 9.2 %copy-start = (bf16[768,768]{1,0:T(8,128)(2,1)S(1)}, bf16[768,768]{1,0:T(8,128)(2,1)}, u32[]{:S(2)}) copy-start(bf16[768,768]{1,0:T(8,128)(2,1)} %w_out.5) | copy-start | bytes 3538948
  33.3 1.8 %collective-permute-start.6 = (bf16[576,192]{1,0:T(8,128)(2,1)S(1)}, bf16[576,192]{1,0:T(8,128)(2,1)S(1)}, u32[]{:S(2)}, u32[]{:S(2)}) collective-permute-start(bf16[576,192]{1,0:T(8,128)(2,1)S(1)} %get-tuple-element.180.a0), channel_id=1, source_target_pairs={{0,8},{8,0},{16,24},{24,16},{1,9},{9,1},{17,25},{25,17},{2,10},{10... | collective-permute-start | bytes 663560 | tf_op jit(solution)/shard_map/ppermute | solution.py:760
  33.9 1.6 %collective-permute-start.8 = (bf16[576,192]{1,0:T(8,128)(2,1)S(1)}, bf16[576,192]{1,0:T(8,128)(2,1)S(1)}, u32[]{:S(2)}, u32[]{:S(2)}) collective-permute-start(bf16[576,192]{1,0:T(8,128)(2,1)S(1)} %collective-permute-done.7.a2), channel_id=1, source_target_pairs={{0,8},{8,0},{16,24},{24,16},{1,9},{9,1},{17,25},{25,17},{2,10},{10... | collective-permute-start | bytes 663560 | tf_op jit(solution)/shard_map/ppermute | solution.py:760
  45.1 9.8 %collective-permute-start.10 = (bf16[8,24,768]{2,1,0:T(8,128)(2,1)S(1)}, bf16[8,24,768]{2,1,0:T(8,128)(2,1)S(1)}, u32[]{:S(2)}, u32[]{:S(2)}) collective-permute-start(bf16[8,24,768]{2,1,0:T(8,128)(2,1)S(1)} %get-tuple-element.200), channel_id=1, source_target_pairs={{0,16},{8,24},{16,0},{24,8},{1,17},{9,25},{17,1},{25,9},{2,18},{10... | collective-permute-start | bytes 884744 | tf_op jit(solution)/shard_map/ppermute | solution.py:760
  46.7 8.8 %collective-permute-start.11 = (bf16[8,24,768]{2,1,0:T(8,128)(2,1)S(1)}, bf16[8,24,768]{2,1,0:T(8,128)(2,1)S(1)}, u32[]{:S(2)}, u32[]{:S(2)}) collective-permute-start(bf16[8,24,768]{2,1,0:T(8,128)(2,1)S(1)} %get-tuple-element.201), channel_id=1, source_target_pairs={{0,1},{1,0},{2,3},{3,2},{4,5},{5,4},{6,7},{7,6},{8,9},{9,8},{10,11... | collective-permute-start | bytes 884744 | tf_op jit(solution)/shard_map/ppermute | solution.py:760
  48.2 8.5 %collective-permute-start.12 = (bf16[4,48,768]{2,1,0:T(8,128)(2,1)S(1)}, bf16[4,48,768]{2,1,0:T(8,128)(2,1)S(1)}, u32[]{:S(2)}, u32[]{:S(2)}) collective-permute-start(bf16[4,48,768]{2,1,0:T(8,128)(2,1)S(1)} %get-tuple-element.202), channel_id=1, source_target_pairs={{0,2},{1,3},{2,0},{3,1},{4,6},{5,7},{6,4},{7,5},{8,10},{9,11},{10,... | collective-permute-start | bytes 884744 | tf_op jit(solution)/shard_map/ppermute | solution.py:760
  56.7 2.4 %collective-permute-start.13 = (bf16[576,768]{1,0:T(8,128)(2,1)S(1)}, bf16[576,768]{1,0:T(8,128)(2,1)S(1)}, u32[]{:S(2)}, u32[]{:S(2)}) collective-permute-start(bf16[576,768]{1,0:T(8,128)(2,1)S(1)} %get-tuple-element.203), channel_id=1, source_target_pairs={{0,8},{8,0},{16,24},{24,16},{1,9},{9,1},{17,25},{25,17},{2,10},{10... | collective-permute-start | bytes 2654216 | tf_op jit(solution)/shard_map/ppermute | solution.py:760
  56.7 26.4 %collective-permute-start.17 = (bf16[24,24,768]{2,1,0:T(8,128)(2,1)S(1)}, bf16[24,24,768]{2,1,0:T(8,128)(2,1)S(1)}, u32[]{:S(2)}, u32[]{:S(2)}) collective-permute-start(bf16[24,24,768]{2,1,0:T(8,128)(2,1)S(1)} %get-tuple-element.234), channel_id=1, source_target_pairs={{0,1},{1,0},{2,3},{3,2},{4,5},{5,4},{6,7},{7,6},{8,9},{9,8},{10,11... | collective-permute-start | bytes 2654216 | tf_op jit(solution)/shard_map/ppermute | solution.py:760
  57.2 4.7 %collective-permute-start.14 = (bf16[288,768]{1,0:T(8,128)(2,1)S(1)}, bf16[288,768]{1,0:T(8,128)(2,1)S(1)}, u32[]{:S(2)}, u32[]{:S(2)}) collective-permute-start(bf16[288,768]{1,0:T(8,128)(2,1)S(1)} %get-tuple-element.207), channel_id=1, source_target_pairs={{0,8},{8,0},{16,24},{24,16},{1,9},{9,1},{17,25},{25,17},{2,10},{10... | collective-permute-start | bytes 1327112 | tf_op jit(solution)/shard_map/ppermute | solution.py:760
  57.4 9.2 %collective-permute-start.16 = (bf16[4,48,768]{2,1,0:T(8,128)(2,1)S(1)}, bf16[4,48,768]{2,1,0:T(8,128)(2,1)S(1)}, u32[]{:S(2)}, u32[]{:S(2)}) collective-permute-start(bf16[4,48,768]{2,1,0:T(8,128)(2,1)S(1)} %get-tuple-element.219), channel_id=1, source_target_pairs={{0,2},{1,3},{2,0},{3,1},{4,6},{5,7},{6,4},{7,5},{8,10},{9,11},{10,... | collective-permute-start | bytes 884744 | tf_op jit(solution)/shard_map/ppermute | solution.py:760
  61.1 9.1 %collective-permute-start.15 = (bf16[576,192]{1,0:T(8,128)(2,1)S(1)}, bf16[576,192]{1,0:T(8,128)(2,1)S(1)}, u32[]{:S(2)}, u32[]{:S(2)}) collective-permute-start(bf16[576,192]{1,0:T(8,128)(2,1)S(1)} %get-tuple-element.217), channel_id=1, source_target_pairs={{0,16},{8,24},{16,0},{24,8},{1,17},{9,25},{17,1},{25,9},{2,18},{10... | collective-permute-start | bytes 663560 | tf_op jit(solution)/shard_map/ppermute | solution.py:760
  63.6 21.5 %collective-permute-start.19 = (bf16[2,4,24,768]{3,2,1,0:T(8,128)(2,1)S(1)}, bf16[2,4,24,768]{3,2,1,0:T(8,128)(2,1)S(1)}, u32[]{:S(2)}, u32[]{:S(2)}) collective-permute-start(bf16[2,4,24,768]{3,2,1,0:T(8,128)(2,1)S(1)} %get-tuple-element.220), channel_id=1, source_target_pairs={{0,1},{1,0},{2,3},{3,2},{4,5},{5,4},{6,7},{7,6},{8,9},{9,8},{10,11... | collective-permute-start | bytes 884744 | tf_op jit(solution)/shard_map/ppermute | solution.py:760
  66.8 16.3 %collective-permute-start.20 = (bf16[4,48,768]{2,1,0:T(8,128)(2,1)S(1)}, bf16[4,48,768]{2,1,0:T(8,128)(2,1)S(1)}, u32[]{:S(2)}, u32[]{:S(2)}) collective-permute-start(bf16[4,48,768]{2,1,0:T(8,128)(2,1)S(1)} %get-tuple-element.224), channel_id=1, source_target_pairs={{0,4},{1,5},{2,6},{3,7},{4,0},{5,1},{6,2},{7,3},{8,12},{9,13},{10,... | collective-permute-start | bytes 884744 | tf_op jit(solution)/shard_map/ppermute | solution.py:760
  70.2 14.9 %collective-permute-start.18 = (bf16[8,24,768]{2,1,0:T(8,128)(2,1)S(1)}, bf16[8,24,768]{2,1,0:T(8,128)(2,1)S(1)}, u32[]{:S(2)}, u32[]{:S(2)}) collective-permute-start(bf16[8,24,768]{2,1,0:T(8,128)(2,1)S(1)} %get-tuple-element.235), channel_id=1, source_target_pairs={{0,16},{8,24},{16,0},{24,8},{1,17},{9,25},{17,1},{25,9},{2,18},{10... | collective-permute-start | bytes 884744 | tf_op jit(solution)/shard_map/ppermute | solution.py:760
  85.6 15.0 %collective-permute-start.22 = (bf16[16,24,768]{2,1,0:T(8,128)(2,1)S(1)}, bf16[16,24,768]{2,1,0:T(8,128)(2,1)S(1)}, u32[]{:S(2)}, u32[]{:S(2)}) collective-permute-start(bf16[16,24,768]{2,1,0:T(8,128)(2,1)S(1)} %get-tuple-element.256), channel_id=1, source_target_pairs={{0,1},{1,0},{2,3},{3,2},{4,5},{5,4},{6,7},{7,6},{8,9},{9,8},{10,11... | collective-permute-start | bytes 1769480 | tf_op jit(solution)/shard_map/ppermute | solution.py:760
  86.1 14.7 %collective-permute-start.23 = (bf16[16,24,768]{2,1,0:T(8,128)(2,1)S(1)}, bf16[16,24,768]{2,1,0:T(8,128)(2,1)S(1)}, u32[]{:S(2)}, u32[]{:S(2)}) collective-permute-start(bf16[16,24,768]{2,1,0:T(8,128)(2,1)S(1)} %get-tuple-element.257), channel_id=1, source_target_pairs={{0,2},{1,3},{2,0},{3,1},{4,6},{5,7},{6,4},{7,5},{8,10},{9,11},{10,... | collective-permute-start | bytes 1769480 | tf_op jit(solution)/shard_map/ppermute | solution.py:760
  87.7 9.0 %collective-permute-start.21 = (bf16[8,24,768]{2,1,0:T(8,128)(2,1)S(1)}, bf16[8,24,768]{2,1,0:T(8,128)(2,1)S(1)}, u32[]{:S(2)}, u32[]{:S(2)}) collective-permute-start(bf16[8,24,768]{2,1,0:T(8,128)(2,1)S(1)} %get-tuple-element.255), channel_id=1, source_target_pairs={{0,16},{8,24},{16,0},{24,8},{1,17},{9,25},{17,1},{25,9},{2,18},{10... | collective-permute-start | bytes 884744 | tf_op jit(solution)/shard_map/ppermute | solution.py:760
  100.8 4.2 %collective-permute-start.24 = (bf16[576,768]{1,0:T(8,128)(2,1)S(1)}, bf16[576,768]{1,0:T(8,128)(2,1)S(1)}, u32[]{:S(2)}, u32[]{:S(2)}) collective-permute-start(bf16[576,768]{1,0:T(8,128)(2,1)S(1)} %get-tuple-element.258), channel_id=1, source_target_pairs={{0,8},{8,0},{16,24},{24,16},{1,9},{9,1},{17,25},{25,17},{2,10},{10... | collective-permute-start | bytes 2654216 | tf_op jit(solution)/shard_map/ppermute | solution.py:760
  101.1 11.5 %collective-permute-start.28 = (bf16[10,24,768]{2,1,0:T(8,128)(2,1)S(1)}, bf16[10,24,768]{2,1,0:T(8,128)(2,1)S(1)}, u32[]{:S(2)}, u32[]{:S(2)}) collective-permute-start(bf16[10,24,768]{2,1,0:T(8,128)(2,1)S(1)} %get-tuple-element.274), channel_id=1, source_target_pairs={{0,2},{1,3},{2,0},{3,1},{4,6},{5,7},{6,4},{7,5},{8,10},{9,11},{10,... | collective-permute-start | bytes 1105928 | tf_op jit(solution)/shard_map/ppermute | solution.py:760
  102.8 9.8 %collective-permute-start.27 = (bf16[8,24,768]{2,1,0:T(8,128)(2,1)S(1)}, bf16[8,24,768]{2,1,0:T(8,128)(2,1)S(1)}, u32[]{:S(2)}, u32[]{:S(2)}) collective-permute-start(bf16[8,24,768]{2,1,0:T(8,128)(2,1)S(1)} %get-tuple-element.267), channel_id=1, source_target_pairs={{0,16},{8,24},{16,0},{24,8},{1,17},{9,25},{17,1},{25,9},{2,18},{10... | collective-permute-start | bytes 884744 | tf_op jit(solution)/shard_map/ppermute | solution.py:760
  103.5 6.8 %collective-permute-start.26 = (bf16[16,24,256]{2,1,0:T(8,128)(2,1)S(1)}, bf16[16,24,256]{2,1,0:T(8,128)(2,1)S(1)}, u32[]{:S(2)}, u32[]{:S(2)}) collective-permute-start(bf16[16,24,256]{2,1,0:T(8,128)(2,1)S(1)} %get-tuple-element.270), channel_id=1, source_target_pairs={{0,1},{1,0},{2,3},{3,2},{4,5},{5,4},{6,7},{7,6},{8,9},{9,8},{10,11... | collective-permute-start | bytes 589832 | tf_op jit(solution)/shard_map/ppermute | solution.py:760
  105.1 16.2 %collective-permute-start.25 = (bf16[288,768]{1,0:T(8,128)(2,1)S(1)}, bf16[288,768]{1,0:T(8,128)(2,1)S(1)}, u32[]{:S(2)}, u32[]{:S(2)}) collective-permute-start(bf16[288,768]{1,0:T(8,128)(2,1)S(1)} %shard_map.252), channel_id=1, source_target_pairs={{0,16},{8,24},{16,0},{24,8},{1,17},{9,25},{17,1},{25,9},{2,18},{10... | collective-permute-start | bytes 1327112 | tf_op jit(solution)/shard_map/ppermute | solution.py:760
  112.7 20.3 %collective-permute-start.29 = (bf16[9,24,768]{2,1,0:T(8,128)(2,1)S(1)}, bf16[9,24,768]{2,1,0:T(8,128)(2,1)S(1)}, u32[]{:S(2)}, u32[]{:S(2)}) collective-permute-start(bf16[9,24,768]{2,1,0:T(8,128)(2,1)S(1)} %get-tuple-element.275), channel_id=1, source_target_pairs={{0,4},{1,5},{2,6},{3,7},{4,0},{5,1},{6,2},{7,3},{8,12},{9,13},{10,... | collective-permute-start | bytes 995336 | tf_op jit(solution)/shard_map/ppermute | solution.py:760
  115.4 17.6 %collective-permute-start.33 = (bf16[2,24,768]{2,1,0:T(8,128)(2,1)S(1)}, bf16[2,24,768]{2,1,0:T(8,128)(2,1)S(1)}, u32[]{:S(2)}, u32[]{:S(2)}) collective-permute-start(bf16[2,24,768]{2,1,0:T(8,128)(2,1)S(1)} %get-tuple-element.289), channel_id=1, source_target_pairs={{0,1},{1,0},{2,3},{3,2},{4,5},{5,4},{6,7},{7,6},{8,9},{9,8},{10,11... | collective-permute-start | bytes 221192 | tf_op jit(solution)/shard_map/ppermute | solution.py:760
  117.0 16.8 %collective-permute-start.31 = (bf16[4,24,256]{2,1,0:T(8,128)(2,1)S(1)}, bf16[4,24,256]{2,1,0:T(8,128)(2,1)S(1)}, u32[]{:S(2)}, u32[]{:S(2)}) collective-permute-start(bf16[4,24,256]{2,1,0:T(8,128)(2,1)S(1)} %get-tuple-element.285), channel_id=1, source_target_pairs={{0,4},{1,5},{2,6},{3,7},{4,0},{5,1},{6,2},{7,3},{8,12},{9,13},{10,... | collective-permute-start | bytes 147464 | tf_op jit(solution)/shard_map/ppermute | solution.py:760
  117.3 16.5 %collective-permute-start.32 = (bf16[4,24,256]{2,1,0:T(8,128)(2,1)S(1)}, bf16[4,24,256]{2,1,0:T(8,128)(2,1)S(1)}, u32[]{:S(2)}, u32[]{:S(2)}) collective-permute-start(bf16[4,24,256]{2,1,0:T(8,128)(2,1)S(1)} %get-tuple-element.286), channel_id=1, source_target_pairs={{0,6},{1,7},{2,4},{3,5},{4,2},{5,3},{6,0},{7,1},{8,14},{9,15},{10,... | collective-permute-start | bytes 147464 | tf_op jit(solution)/shard_map/ppermute | solution.py:760
  121.4 12.4 %collective-permute-start.30 = (bf16[4,24,256]{2,1,0:T(8,128)(2,1)S(1)}, bf16[4,24,256]{2,1,0:T(8,128)(2,1)S(1)}, u32[]{:S(2)}, u32[]{:S(2)}) collective-permute-start(bf16[4,24,256]{2,1,0:T(8,128)(2,1)S(1)} %get-tuple-element.277), channel_id=1, source_target_pairs={{0,2},{1,3},{2,0},{3,1},{4,6},{5,7},{6,4},{7,5},{8,10},{9,11},{10,... | collective-permute-start | bytes 147464 | tf_op jit(solution)/shard_map/ppermute | solution.py:760
  133.8 5.1 %collective-permute-start.37 = (bf16[48,768]{1,0:T(8,128)(2,1)S(1)}, bf16[48,768]{1,0:T(8,128)(2,1)S(1)}, u32[]{:S(2)}, u32[]{:S(2)}) collective-permute-start(bf16[48,768]{1,0:T(8,128)(2,1)S(1)} %get-tuple-element.299), channel_id=1, source_target_pairs={{0,8},{8,0},{16,24},{24,16},{1,9},{9,1},{17,25},{25,17},{2,10},{10... | collective-permute-start | bytes 221192 | tf_op jit(solution)/shard_map/ppermute | solution.py:760
  133.9 2.0 %collective-permute-start.34 = (bf16[24,640]{1,0:T(8,128)(2,1)S(1)}, bf16[24,640]{1,0:T(8,128)(2,1)S(1)}, u32[]{:S(2)}, u32[]{:S(2)}) collective-permute-start(bf16[24,640]{1,0:T(8,128)(2,1)S(1)} %get-tuple-element.295), channel_id=1, source_target_pairs={{0,8},{8,0},{16,24},{24,16},{1,9},{9,1},{17,25},{25,17},{2,10},{10... | collective-permute-start | bytes 92168 | tf_op jit(solution)/shard_map/ppermute | solution.py:760
  134.4 4.0 %collective-permute-start.35 = (bf16[24,640]{1,0:T(8,128)(2,1)S(1)}, bf16[24,640]{1,0:T(8,128)(2,1)S(1)}, u32[]{:S(2)}, u32[]{:S(2)}) collective-permute-start(bf16[24,640]{1,0:T(8,128)(2,1)S(1)} %get-tuple-element.296), channel_id=1, source_target_pairs={{0,16},{8,24},{16,0},{24,8},{1,17},{9,25},{17,1},{25,9},{2,18},{10... | collective-permute-start | bytes 92168 | tf_op jit(solution)/shard_map/ppermute | solution.py:760
  135.2 3.6 %collective-permute-start.36 = (bf16[24,640]{1,0:T(8,128)(2,1)S(1)}, bf16[24,640]{1,0:T(8,128)(2,1)S(1)}, u32[]{:S(2)}, u32[]{:S(2)}) collective-permute-start(bf16[24,640]{1,0:T(8,128)(2,1)S(1)} %get-tuple-element.297), channel_id=1, source_target_pairs={{0,24},{8,16},{16,8},{24,0},{1,25},{9,17},{17,9},{25,1},{2,26},{10... | collective-permute-start | bytes 92168 | tf_op jit(solution)/shard_map/ppermute | solution.py:760

commit v6 on v5

--- a/solution.py
+++ b/solution.py
@@ -10,6 +10,7 @@
 HEADS = 12
 HEAD = 64
 PAD = 32
+SPECIAL = 4
 LANES = 128
 OWN = 3
 FAR = -(2.0**100)
@@ -88,9 +89,17 @@
     )(*args)
 
 
-def prep_kernel(sref, w, biases, w_own, bias_own):
+def prep_kernel(sref, w, biases, w_own, bias_own, tiles, lines, sems):
     width = w.shape[0]
     per = width // HEAD
+    spots = [per * (e % 3) + OWN * sref[0] + e // 3 for e in range(3 * OWN)]
+    copies = [pltpu.make_async_copy(biases, lines, sems.at[3 * OWN])]
+    for e, u in enumerate(spots):
+        tile = w.at[:, pl.ds(pl.multiple_of((u >> 1) * LANES, LANES), LANES)]
+        copies.append(pltpu.make_async_copy(tile, tiles.at[e], sems.at[e]))
+    for copy in copies:
+        copy.start()
+    copies[0].wait()
     line = lax.broadcasted_iota(jnp.int32, (1, LANES), 1)
     for t in range((3 * OWN + 1) // 2):
         out, bias = jnp.zeros((width, LANES), F32), jnp.zeros((1, LANES), F32)
@@ -98,16 +107,16 @@
             e = 2 * t + dest
             if e == 3 * OWN:
                 continue
-            h, j = e // 3, e % 3
-            u = per * j + OWN * sref[0] + h
+            copies[1 + e].wait()
+            u, j = spots[e], e % 3
             side = (lane_of(width) >= HEAD) == (dest == 1)
             moved = jnp.broadcast_to((u & 1) != dest, (1, LANES))
-            tile = w[:, pl.ds(pl.multiple_of((u >> 1) * LANES, LANES), LANES)].astype(F32)
+            tile = tiles[e].astype(F32)
             tile = jnp.where(moved, pltpu.roll(tile, HEAD, 1), tile)
             out = jnp.where(side, tile, out)
             if j != 1:
-                v = per * 0 + OWN * sref[0] + h
-                tile = biases[j // 2 : j // 2 + 1, pl.ds(pl.multiple_of((v >> 1) * LANES, LANES), LANES)]
+                v = OWN * sref[0] + e // 3
+                tile = lines[j // 2 : j // 2 + 1, pl.ds(pl.multiple_of((v >> 1) * LANES, LANES), LANES)]
                 tile = jnp.broadcast_to(tile, (8, LANES))
                 away = jnp.broadcast_to((v & 1) != dest, (8, LANES))
                 tile = jnp.where(away, pltpu.roll(tile, HEAD, 1), tile)[:1]
@@ -116,6 +125,24 @@
         bias_own[:, t * LANES : (t + 1) * LANES] = bias
 
 
+def small_kernel(specials_in, segments_in, order_in, cots_in, small, specials, segments, order, cots, wide, sems):
+    pairs = ((specials_in, specials), (segments_in, segments), (order_in, order), (cots_in, cots))
+    copies = [pltpu.make_async_copy(src, dst, sems.at[i]) for i, (src, dst) in enumerate(pairs)]
+    for copy in copies:
+        copy.start()
+    extra, width = specials.shape
+    count = segments.shape[1]
+    wide[...] = jnp.zeros_like(wide)
+    wide[extra : extra + 1, :] = jnp.full((1, width), -1.0, F32)
+    for copy in copies:
+        copy.wait()
+    wide[:extra, :] = specials[...].astype(F32)
+    wide[16 : 16 + extra, :] = cots[...].astype(F32)
+    wide[extra : extra + 1, :count] = segments[...].astype(F32)
+    wide[extra : extra + 1, count : count + extra] = (order[...] >> 1).astype(F32)
+    small[...] = wide[...].astype(BF16)
+
+
 def tokens_of(patches, small):
     parts = [patches[...].astype(F32), small[:16, :].astype(F32)]
     return jnp.concatenate(parts + [jnp.zeros((PAD - 16, patches.shape[1]), F32)], axis=0)
@@ -128,7 +155,7 @@
 
 def images_of(small, rows):
     size = -(-rows // LANES) * LANES
-    line = small[:16, :size].astype(F32)[4:5]
+    line = small[:16, :size].astype(F32)[SPECIAL : SPECIAL + 1]
     return jnp.broadcast_to(line, (LANES, size)).T[:rows]
 
 
@@ -137,7 +164,7 @@
     rows = tok.shape[0]
     lane = lane_of(rows)
     hat, _ = normalize(tok)
-    nrm = (hat * gain[...] + shift[...]).astype(BF16)
+    nrm = (hat * gain[0:1, :] + shift[0:1, :]).astype(BF16)
     normed[at, :] = nrm
     qkv = dot(nrm, w[...]) + bias[...]
     image = images_of(small, rows)
@@ -198,7 +225,7 @@
         oacc[h, pl.ds(pl.multiple_of(b * rows, 16), rows), :] = attend_block(h, at, ka, va, qa, oacc)
         return carry
 
-    lax.fori_loop(0, 2 * OWN, block, 0)
+    lax.fori_loop(0, 2 * OWN, block, 0, unroll=3)
     gather_heads(oacc, send)
 
 
@@ -217,7 +244,7 @@
         oacc[h, at, :] = attend_block(h, at, ka, va, qa, oacc)
         return carry
 
-    lax.fori_loop(0, 2 * OWN, block, 0)
+    lax.fori_loop(0, 2 * OWN, block, 0, unroll=3)
     gather_heads(oacc, keep)
     step = 2 * half // 3
     for h in range(OWN):
@@ -239,7 +266,7 @@
     chip, width = toks.shape
     rows = chip // 2
     cols = a0.shape[1]
-    acc = jnp.zeros((chip, width), F32) + bias[...]
+    acc = jnp.zeros((chip, width), F32) + bias[2:3, :]
     for j, a in ((0, a0), (2, a2)):
         w = w_out[pl.ds(pl.multiple_of((s ^ j) * cols, HEAD), cols), :]
         acc = acc + dot(a[...], w)
@@ -250,7 +277,7 @@
     mid = toks[...].astype(F32) + keeps[:, 0:1] * acc
     middle[...] = mid
     hat, _ = normalize(mid)
-    normed2[...] = (hat * gain[...] + shift[...]).astype(BF16)
+    normed2[...] = (hat * gain[1:2, :] + shift[1:2, :]).astype(BF16)
     gout = jnp.concatenate([cots_of(cp0, c0), cots_of(cp1, c1)], axis=0)
     gb2[...] = (keeps[:, 1:2] * gout).astype(BF16)
     for copy in copies:
@@ -279,7 +306,8 @@
         copies = fetch(sref[0], w_fc1, w_fc2, w1, w2, sems)
     tokens = normed2.shape[0]
     half = tokens // 2
-    pre = dot(normed2[...], fc1[...]) + bias[...]
+    block = sref[0] if last else sref[0] ^ 2
+    pre = dot(normed2[...], fc1[...]) + bias[:, pl.ds(pl.multiple_of(block * fc1.shape[1], LANES), fc1.shape[1])]
     gact = dot_t(gb2[...], fc2[...])
     act, slope = gelu_pair(pre)
     act = act.astype(BF16)
@@ -302,13 +330,13 @@
             if m >= n:
                 g1_keep[m - n] = piece
             elif last:
-                y_send[n // 2 + m] = piece
-            elif m < n // 2:
+                y_send[n // 4 + m] = piece
+            elif m < 3 * n // 4:
                 y_first[m] = piece
             else:
-                y_second[m - n // 2] = piece
+                y_second[m - 3 * n // 4] = piece
         if last:
-            for m in range(n // 2):
+            for m in range(n // 4):
                 y_send[m] = y_in[m]
     gb[...] = jnp.sum(gh.astype(F32), axis=0, keepdims=True)
     partn = dot_t(gh, fc1[...])
@@ -380,7 +408,10 @@
     else:
         outs = [SDS((hidden // 2, width), BF16)] if last else [SDS((hidden // 4, width), BF16)] * 2
         outs += [SDS((hidden // 4, width), BF16)] * 2
-    send = [SDS((3 * pairs // 2, per, hidden), BF16)] if last else [SDS((pairs // 2, per, hidden), BF16)] * 2
+    if last:
+        send = [SDS((5 * pairs // 4, per, hidden), BF16)]
+    else:
+        send = [SDS((n, per, hidden), BF16) for n in (3 * pairs // 4, pairs // 4)]
     keep = SDS((pairs, per, hidden), BF16)
     if not fast:
         keep = SDS((width // 2, hidden), BF16)
@@ -418,7 +449,7 @@
     hat, scale = normalize(middle[...])
     g = gn_keep[...] + gn_got[...].astype(F32)
     gout = jnp.concatenate([cots_of(cp0, c0), cots_of(cp1, c1)], axis=0)
-    gmid = gout + normalize_back(g * gain[...], hat, scale)
+    gmid = gout + normalize_back(g * gain[1:2, :], hat, scale)
     gbr = (keeps[:, 0:1] * gmid).astype(BF16)
     gbr_out[...] = gbr
     w_oth = w_out[pl.ds(pl.multiple_of((s ^ 2) * cols, HEAD), cols), :]
@@ -436,7 +467,7 @@
 
 
 def branch_back_kernel(
-    sref, bref, gbr, w_out, a0, a2, middle, keeps, b2_keep, b2_got, bias, gain1, shift1, sums, fb_own, fb_oth,
+    per, sref, bref, gbr, w_out, a0, a2, middle, keeps, b2_keep, b2_got, bias, gain1, shift1, sums, fb_own, fb_oth,
     gatt, go_send, go_keep, early, opat, ospe, fcol, wide,
 ):
     s = sref[0]
@@ -446,12 +477,12 @@
     gatt[...] = dot_t(gbr[...], w_own).astype(BF16)
     for j, a in enumerate((a0, a2)):
         split_rows(dot_lt(a[...], gbr[...]), wide, bref[0] & 1, go_send.at[j], go_keep.at[j])
-    res = middle[:rows, :] + keeps[:rows, 1:2] * (b2_keep[...] + b2_got[...].astype(F32) + bias[...])
+    res = middle[:rows, :] + keeps[:rows, 1:2] * (b2_keep[...] + b2_got[...].astype(F32) + bias[3:4, :])
     res = res.astype(BF16)
     opat[...] = res[: opat.shape[0]]
     ospe[...] = res[opat.shape[0] : opat.shape[0] + ospe.shape[0]]
     blank = functools.partial(jnp.zeros, dtype=F32)
-    lines = [gain1[...], shift1[...], blank((HEAD + 2, width)), sums[:4, :], blank((LANES - HEAD - 8, width))]
+    lines = [gain1[0:1, :], shift1[0:1, :], blank((HEAD + 2, width)), sums[:4, :], blank((LANES - HEAD - 8, width))]
     early[...] = jnp.concatenate(lines, axis=0).T
     lane = lane_of(cols)
     for j, ref in ((0, fb_own), (2, fb_oth)):
@@ -459,11 +490,12 @@
         at = pl.ds(pl.multiple_of((s ^ j) * cols, HEAD), cols)
         val = early[at, :]
         for k in range(4):
-            val = jnp.where(lane == HEAD + 8 + k, fcol[pl.ds(k, cols, stride=4), :], val)
+            lines = [fcol[(4 * b + k) * per : (4 * b + k + 1) * per, :] for b in range(cols // per)]
+            val = jnp.where(lane == HEAD + 8 + k, jnp.concatenate(lines, axis=0), val)
         early[at, :] = val
 
 
-def attend_back_kernel(first, heads, qa, ka, va, lse, ga, gx, out, sums, goa, dq, dk, dv):
+def attend_back_kernel(first, heads, unroll, qa, ka, va, lse, ga, gx, out, sums, goa, dq, dk, dv):
     whole = qa.shape[1]
     half = ga.shape[0]
     lane = lane_of(half)
@@ -492,19 +524,11 @@
         pk = dot(gs, q)
         dq[i, at, :] = dot_lt(gs, ka[h])
 
-        @pl.when(b == 0)
-        def _():
-            dv[i] = pv
-            dk[i] = pk
-
-        @pl.when(b > 0)
-        def _():
-            dv[i] += pv
-            dk[i] += pk
-
+        dv[i] = jnp.where(b == 0, pv, dv[i] + pv)
+        dk[i] = jnp.where(b == 0, pk, dk[i] + pk)
         return carry
 
-    lax.fori_loop(0, 3 * heads, block, 0)
+    lax.fori_loop(0, 3 * heads, block, 0, unroll=unroll)
     for i in range(heads):
         out[i, :, :LANES] = pack_pair(dq[i] * HEAD**-0.5, dk[i]).astype(BF16)
         out[i, :, LANES:] = dv[i, :, :HEAD].astype(BF16)
@@ -563,7 +587,7 @@
     fast, sref, bref, qa, ka, va, lse, ga, gx, normed, w, early, g01, send, keep, tile,
     s01, goa, dq, dk, dv, wide,
 ):
-    attend_back_kernel(0, 2, qa, ka, va, lse, ga, gx, g01, s01, goa, dq, dk, dv)
+    attend_back_kernel(0, 2, 2, qa, ka, va, lse, ga, gx, g01, s01, goa, dq, dk, dv)
     g = qkv_grad(sref, normed, (g01[0], g01[1]), (s01[0], s01[1]), w, 0, tile, early)
     if not fast:
         rows = g.shape[0] // 2
@@ -587,7 +611,7 @@
     sref, bref, qa, ka, va, lse, ga, gx, normed, g01, w, early, gn_keep, gn_send, send, keep,
     g2, s2, goa, dq, dk, dv, tile, wide,
 ):
-    attend_back_kernel(2, 1, qa, ka, va, lse, ga, gx, g2, s2, goa, dq, dk, dv)
+    attend_back_kernel(2, 1, 1, qa, ka, va, lse, ga, gx, g2, s2, goa, dq, dk, dv)
     norm1_kernel(g01, g2, w, gn_keep, gn_send)
     g = qkv_grad(sref, normed, (g2[0],), (s2[0],), w, 2, tile, early)
     width = g.shape[0]
@@ -620,10 +644,11 @@
     y, z1, z2 = bref[0] & 1, (bref[0] >> 1) & 1, bref[0] >> 2
     n = keep_own.shape[0] // 2
     for i in range(n):
-        msg_z[i] = wide_sum(keep_own[i], y2[n + i]).astype(BF16)
+        more = n // 2
+        msg_z[i] = wide_sum(keep_own[i], y2[more + i]).astype(BF16)
         msg_z[n + i] = wide_sum(keep_oth[i], y1[i]).astype(BF16)
-        part_f[i] = wide_sum(keep_own[n + i], y2[2 * n + i])
-        part_f[n + i] = wide_sum(keep_oth[n + i], y2[i])
+        part_f[i] = wide_sum(keep_own[n + i], y2[more + n + i])
+        part_f[n + i] = wide_sum(keep_oth[n + i], y1[n + i] if i < more else y2[i - more])
         msg_y[8 + i] = q_send[i]
     rows = g2a.shape[1]
     for i in range(4):
@@ -646,8 +671,11 @@
 
 
 def stage2_kernel(
-    part_f, got_z, part_a, got_y, part_o, got_x, part_p, q_keep, msg_x, msg_z, msg_y, part_g, part_c, part_q
+    part_f, got_z, part_a, got_y, part_o, got_x, part_p, q_keep, q2_send, msg_x, msg_z, msg_y, part_g, part_c, part_q
 ):
+    n, _, cols = q2_send.shape
+    for i in range(n):
+        msg_y[i] = q2_send[i]
     for half in range(2):
         for i in range(4):
             k = 8 * half + i
@@ -661,11 +689,13 @@
     for i in range(2):
         msg_z[4 + i] = wide_sum(part_o[i], got_x[i]).astype(BF16)
         part_c[4 + i] = wide_sum(part_o[2 + i], got_x[2 + i])
-        msg_y[i] = wide_sum(part_p[i], got_x[4 + i]).astype(BF16)
+        rest = wide_sum(part_p[i], got_x[4 + i]).astype(BF16)
+        for k in range(3):
+            msg_y[n + 3 * i + k] = rest[:, k * cols : (k + 1) * cols]
         part_q[i] = wide_sum(part_p[2 + i], got_x[6 + i])
 
 
-def stage3_kernel(part_g, got_x, part_c, got_z, msg, kept):
+def stage3_kernel(bref, part_g, got_x, part_c, got_z, q_keep, got_y, msg, kept, z1, z2, z3, q_kept):
     for half in range(2):
         for i in range(2):
             k, other = 4 * half + i, 4 * (1 - half) + i
@@ -674,19 +704,16 @@
     for to, a, b in ((4, 0, 2), (5, 1, 3), (6, 4, 5), (7, 6, 8), (8, 7, 9)):
         msg[to] = wide_sum(part_c[a], got_z[a]).astype(BF16)
         kept[to] = wide_sum(part_c[b], got_z[b])
+    q = bref[0] >> 1
+    for r in range(4):
+        for k, ref in enumerate((q_kept, z1, z2, z3)):
+            m = r * 4 + (q ^ k)
+            ref[r] = wide_sum(q_keep[m], got_y[m]).astype(ref.dtype)
 
 
 def shift_kernel(keep, got, send):
     rows = send.shape[0]
     send[...] = wide_sum(keep[rows:, :], got[rows:, :]).astype(BF16)
-
-
-def quarter_kernel(bref, keep, got, z1, z2, z3, kept):
-    q = bref[0] >> 1
-    for r in range(4):
-        for k, ref in enumerate((kept, z1, z2, z3)):
-            m = r * 4 + (q ^ k)
-            ref[r] = wide_sum(keep[m], got[m]).astype(ref.dtype)
 
 
 def sums_kernel(kept, got, part_q, got_q, swap_send, swap_keep, fc2, out):
@@ -696,7 +723,10 @@
         swap_send[at, :] = wide_sum(kept[2 * half], got[2 * half]).astype(BF16)
         swap_keep[at, :] = wide_sum(kept[2 * half + 1], got[2 * half + 1])
         fc2[at, :] = wide_sum(kept[4 + half], got[4 + half])
-        fc2[pl.ds((2 + half) * per, per), :] = wide_sum(part_q[half], got_q[half])
+        cols = got_q.shape[2]
+        for k in range(3):
+            at3 = slice(k * cols, (k + 1) * cols)
+            fc2[pl.ds((2 + half) * per, per), at3] = wide_sum(part_q[half, :, at3], got_q[16 + 3 * half + k])
     out[...] = wide_sum(kept[6], got[6])
 
 
@@ -716,12 +746,14 @@
     count = gpat.shape[0]
     hat, scale = normalize(tokens_of(p0, s0))
     g = wide_sum(k0[:rows], c0[:rows], x0[...])
-    res = gmid[...] + normalize_back(g * gain[...], hat, scale)
+    res = gmid[...] + normalize_back(g * gain[0:1, :], hat, scale)
     gpat[...] = res[:count]
     gspe[...] = res[count : count + gspe.shape[0]]
 
 
-def collect_kernel(sref, own, g1, g2, g3, swap_keep, swap_got, out, vec, fc1, every):
+def collect_kernel(
+    sref, own, g1, g2, g3, swap_keep, swap_got, out, gains, shifts, biases, fc1_bias, fc1, every
+):
     s = sref[0]
     per, hidden = swap_keep.shape[0] // 2, swap_keep.shape[1]
     for j, value in ((0, swap_keep[:per]), (2, swap_keep[per:]), (1, swap_got[:per]), (3, swap_got[per:])):
@@ -742,7 +774,11 @@
         high = high if hi else pltpu.roll(high, HEAD, 1)
         out[:, t * LANES : (t + 1) * LANES] = jnp.where(lane < HEAD, low, high)
     tail = 4 * LANES
-    vec[...] = wide_sum(*[every[k, :, tail:] for k in range(4)])
+    vec = wide_sum(*[every[k, :, tail:] for k in range(4)])
+    vec = jnp.concatenate([vec, jnp.zeros((LANES - per, LANES), F32)], axis=0).T[:, :per]
+    for ref, lines in ((gains, (0, 4)), (shifts, (1, 5)), (biases, (2, 3, 7, 6)), (fc1_bias, (8, 9, 10, 11))):
+        for i, k in enumerate(lines):
+            ref[i : i + 1, :] = vec[HEAD + k : HEAD + k + 1]
 
 
 def pick(arr, index, axis):
@@ -843,30 +879,33 @@
     own_p, own_cot = patches[0], cot_patches[0]
     got_px = swap_seq(own_p, 2)
     got_pc = swap_seq(own_p, 1)
-    ids = jnp.concatenate([segment_ids[0], special_order[0] // 2])
-    line = jnp.full((width,), -1, jnp.int32).at[: count + extra].set(ids).astype(BF16)
-    blank = jnp.zeros((16, width), BF16)
-    small = jnp.concatenate(
-        [specials[0], line[None], blank[: 15 - extra], cot_specials[0], blank[: 16 - extra]], axis=0
+    (small,) = call(
+        small_kernel,
+        [SDS((32, width), BF16)],
+        (specials[0], segment_ids, special_order, cot_specials[0]),
+        [pltpu.VMEM((extra, width), BF16), pltpu.VMEM((1, count), jnp.int32), pltpu.VMEM((1, extra), jnp.int32)]
+        + [pltpu.VMEM((extra, width), BF16), pltpu.VMEM((32, width), F32), pltpu.SemaphoreType.DMA((4,))],
+        far=(0, 1, 2, 3),
     )
     got_sx = swap_seq(small, 2)
     got_sc = swap_seq(small, 1)
     cot_c = swap_seq(own_cot, 1)
-    gain1, gain2 = norm_gains[0:1], norm_gains[1:2]
-    shift1, shift2 = norm_shifts[0:1], norm_shifts[1:2]
-    fb = [lax.dynamic_slice(fc1_bias, ((s ^ j) * hidden,), (hidden,))[None] for j in (2, 0)]
-    sidx, bidx, fb, small = lax.optimization_barrier((sidx, bidx, fb, small))
+    fb = fc1_bias.reshape(1, -1)
+    sidx, bidx, small = lax.optimization_barrier((sidx, bidx, small))
     w_own, bias_own = call(
         prep_kernel,
         [SDS((width, 5 * LANES), BF16), SDS((1, 5 * LANES), F32)],
         (sidx, w_qkv, biases),
+        [pltpu.VMEM((3 * OWN, width, LANES), BF16), pltpu.VMEM(biases.shape, F32)]
+        + [pltpu.SemaphoreType.DMA((3 * OWN + 1,))],
         scalars=1,
+        far=(1, 2),
     )
     headed = SDS((OWN, chip, LANES), BF16)
     q0, k0, v0, n0, toks, keeps = call(
         project_kernel,
         [headed] * 3 + [SDS((chip, width), BF16), SDS((chip, width), BF16), SDS((chip, LANES), F32)],
-        (keep_mask, own_p, small, got_pc, got_sc, gain1, shift1, w_own, bias_own),
+        (keep_mask, own_p, small, got_pc, got_sc, norm_gains, norm_shifts, w_own, bias_own),
         flops=2 * chip * width * 3 * cols,
         scalars=1,
     )
@@ -879,7 +918,7 @@
     qa, ka, va, att_send, other, normed = call(
         attend_first_kernel,
         [headed] * 3 + [SDS((chip, cols), BF16), heads32, SDS((whole, width), BF16)],
-        (q0, k0, v0, n0, got_px, got_sx, got_pd, got_sd, gain1, shift1, w_own, bias_own),
+        (q0, k0, v0, n0, got_px, got_sx, got_pd, got_sd, norm_gains, norm_shifts, w_own, bias_own),
         flops=2 * chip * width * 3 * cols + 2 * OWN * whole * whole * LANES,
     )
     a2 = swap_seq(att_send, 2)
@@ -897,7 +936,7 @@
         middle_kernel,
         [SDS((chip, width), F32), SDS((chip, width), BF16), SDS((chip, width), BF16)]
         + [SDS((width, hidden), BF16), SDS((hidden, width), BF16)],
-        (sidx, a0, a1, a2, a3, toks, keeps, own_cot, cot_c, small, got_sc, w_out, biases[2:3], gain2, shift2)
+        (sidx, a0, a1, a2, a3, toks, keeps, own_cot, cot_c, small, got_sc, w_out, biases, norm_gains, norm_shifts)
         + (w_fc1, w_fc2),
         [pltpu.SemaphoreType.DMA((2,))],
         flops=2 * chip * width * width,
@@ -907,7 +946,7 @@
     per = width // (4 * nb)
     fast = nb == 8
     fc2_a, fc2_m, zo_send, zo_keep, y1, y_rest, keep_oth, fb_oth, b2, gn, w1, w2 = feed(
-        False, fast, per, sidx, bidx, normed2, gb2, w1, fb[0], w2, (w_fc1, w_fc2)
+        False, fast, per, sidx, bidx, normed2, gb2, w1, fb, w2, (w_fc1, w_fc2)
     )
     got2a = swap_seq(fc2_a, 2)
     if not fast:
@@ -916,7 +955,7 @@
     got_zo = swap("batch", zo_send, 2) if fast else zo_send
     ahead = (got2a, got_y1, got_zo)
     fc2_keep, zn_send, zn_keep, y2, keep_own, fb_own, b2_keep, b2_send, gn_keep, gn_send = feed(
-        True, fast, per, sidx, bidx, normed2, gb2, w1, fb[1], w2, (b2, gn, y_rest)
+        True, fast, per, sidx, bidx, normed2, gb2, w1, fb, w2, (b2, gn, y_rest)
     )
     if not fast:
         y2, keep_own = by_batch_bit(jnp.concatenate([y2, keep_own], axis=0), per)
@@ -931,7 +970,7 @@
     gmid, gbr, gatt_send, line_sums = call(
         middle_back_kernel,
         [SDS((block, width), F32), SDS((chip, width), BF16), SDS((chip, cols), BF16), SDS((8, width), F32)],
-        (sidx, gn_keep, gn_got, middle, keeps, own_cot, cot_c, small, got_sc, w_out, gain2, gb2),
+        (sidx, gn_keep, gn_got, middle, keeps, own_cot, cot_c, small, got_sc, w_out, norm_gains, gb2),
         flops=2 * chip * width * cols,
         scalars=1,
     )
@@ -941,10 +980,10 @@
     else:
         split = SDS((2, cols // 2, width), BF16)
     gatt, go_send, go_keep, early, opat, ospe = call(
-        branch_back_kernel,
+        functools.partial(branch_back_kernel, per),
         [SDS((chip, cols), BF16), split, split, SDS((width, LANES), F32)]
         + [SDS((count, width), BF16), SDS((extra, width), BF16)],
-        (sidx, bidx, gbr, w_out, a0, a2, middle, keeps, b2_keep, b2_got, biases[3:4], gain1, shift1)
+        (sidx, bidx, gbr, w_out, a0, a2, middle, keeps, b2_keep, b2_got, biases, norm_gains, norm_shifts)
         + (line_sums, fb_own, fb_oth),
         [pltpu.VMEM((hidden, LANES), F32), pltpu.VMEM((cols, width), F32)],
         flops=6 * chip * width * cols,
@@ -1005,13 +1044,11 @@
     rest = (sidx, bidx, per, block, chip, hidden, cols, count, extra, width)
     zs = (zn_send, zn_keep, zo_send, zo_keep, msg_0, part_0)
     reduce_all = reduce_eight if fast else reduce_any
-    out_fc2, out_out, out_fc1, out_qkv, vec, gpat, gspe = reduce_all(
+    out_fc2, out_out, out_fc1, out_qkv, smalls, gpat, gspe = reduce_all(
         rest, pairs, (fc2_keep, got2a, got2m, zs), (go_keep, got_o), lse, gatt_x,
-        first_heads, tail_part, (own_p, small), gmid, gain1,
-    )
-    grad_gains = jnp.stack([vec[:, 0], vec[:, 4]])
-    grad_shifts = jnp.stack([vec[:, 1], vec[:, 5]])
-    grad_biases = jnp.stack([vec[:, 2], vec[:, 3], vec[:, 7], vec[:, 6]])
+        first_heads, tail_part, (own_p, small), gmid, norm_gains,
+    )
+    grad_gains, grad_shifts, grad_biases, grad_fc1_bias = smalls
     return (
         opat[None],
         ospe[None],
@@ -1023,13 +1060,13 @@
         grad_biases,
         out_out,
         out_fc1,
-        vec[:, 8:12].reshape(-1),
+        grad_fc1_bias.reshape(-1),
         out_fc2,
     )
 
 
 def reduce_eight(
-    rest, pairs, twos, outs, lse, gatt_x, first_heads, tail_part, pay, gmid, gain1
+    rest, pairs, twos, outs, lse, gatt_x, first_heads, tail_part, pay, gmid, gains
 ):
     sidx, bidx, per, block, chip, hidden, cols, count, extra, width = rest
     fc2_keep, got2a, got2m, zs = twos
@@ -1056,62 +1093,62 @@
     got_y = swap("batch", msg_y, 1)
     got_x = swap_seq(msg_x, 2)
     gn1_keep, gn1_send, q_send, q_keep = tail_part(lse, g01, tile)
-    gn1_send, q_send, got_x, got_y, got_z = lax.optimization_barrier((gn1_send, q_send, got_x, got_y, got_z))
+    gn1_send, got_x, got_y, got_z = lax.optimization_barrier((gn1_send, got_x, got_y, got_z))
     gn1_c = swap_seq(gn1_send, 1)
-    got_q = swap("batch", q_send, 1)
+    part = SDS((22, per, cols + HEAD), BF16)
     msg_x, msg_z, msg_y, part_g, part_c, part_q = call(
         stage2_kernel,
-        [blocks(8), blocks(10), blocks(2), blocks(8, F32), blocks(10, F32), blocks(2, F32)],
-        (part_f, got_z, part_a, got_y, part_o, got_x, part_p, q01_keep),
+        [blocks(8), blocks(10), part, blocks(8, F32), blocks(10, F32), blocks(2, F32)],
+        (part_f, got_z, part_a, got_y, part_o, got_x, part_p, q01_keep, q_send),
     )
     got_x = swap_seq(msg_x, 2)
     got_z = swap("batch", msg_z, 2)
+    got_y = swap("batch", msg_y, 1)
     (xsend,) = call(shift_kernel, [SDS((block, width), BF16)], (after(gn1_keep, msg_x), gn1_c))
     gn1_x = swap_seq(xsend, 2)
-    msg, kept = call(
-        stage3_kernel, [blocks(9), blocks(9, F32)], (part_g, after(got_x, xsend, got_q), part_c, got_z)
+    quarter = SDS((4, per, cols + HEAD), BF16)
+    msg, kept, q1, q2, q3, q_kept = call(
+        stage3_kernel,
+        [blocks(9), blocks(9, F32), quarter, quarter, quarter, SDS(quarter.shape, F32)],
+        (bidx, part_g, after(got_x, xsend), part_c, got_z, q_keep, got_y),
+        scalars=1,
     )
     got_last = swap("batch", msg, 4)
-    got_q = after(got_q, msg)
-    quarter = SDS((4, per, cols + HEAD), BF16)
-    q1, q2, q3, q_kept = call(
-        quarter_kernel, [quarter, quarter, quarter, SDS(quarter.shape, F32)], (bidx, q_keep, got_q), scalars=1
-    )
     got_qz = swap_four((q1, q2, q3), 1)
-    got_yb = swap("batch", after(msg_y, q1), 1)
     gpat, gspe = call(
         final_kernel,
         [SDS((count, width), F32), SDS((extra, width), F32)],
-        (gn1_keep, gn1_c, after(gn1_x, q1), *pay, gmid, gain1),
+        (gn1_keep, gn1_c, after(gn1_x, q1), *pay, gmid, gains),
     )
     got_last = after(got_last, gpat)
-    swap_send, swap_keep, out_fc2, out_out = call(
-        sums_kernel,
-        [SDS((2 * per, width), BF16), SDS((2 * per, width), F32), SDS((deep, width), F32), SDS((per, width), F32)],
-        (kept, got_last, part_q, got_yb),
-    )
-    swap_got = swap_seq(swap_send, 1)
     row = SDS((per, 5 * LANES), BF16)
     s1, s2, s3, own = call(
         owner_kernel,
         [row, row, row, SDS(row.shape, F32)],
-        (sidx, kept, got_last, q_kept, *after(got_qz, out_out)),
+        (sidx, kept, got_last, q_kept, *got_qz),
         [pltpu.VMEM((4, per, 5 * LANES), F32)],
         scalars=1,
     )
+    swap_send, swap_keep, out_fc2, out_out = call(
+        sums_kernel,
+        [SDS((2 * per, width), BF16), SDS((2 * per, width), F32), SDS((deep, width), F32), SDS((per, width), F32)],
+        (kept, after(got_last, s1), part_q, got_y),
+    )
+    swap_got = swap_seq(swap_send, 1)
     gots = [swap_seq(v, k) for k, v in ((1, s1), (2, s2), (3, s3))]
-    out_qkv, vec, out_fc1 = call(
+    lines = [SDS((n, per), F32) for n in (2, 2, 4, 4)]
+    out_qkv, *smalls, out_fc1 = call(
         collect_kernel,
-        [SDS((per, 3 * width), F32), SDS((per, LANES), F32), SDS((per, 4 * hidden), F32)],
+        [SDS((per, 3 * width), F32), *lines, SDS((per, 4 * hidden), F32)],
         (sidx, own, *gots, swap_keep, swap_got),
         [pltpu.VMEM((4, per, 5 * LANES), F32)],
         scalars=1,
     )
-    return out_fc2, out_out, out_fc1, out_qkv, vec[:, HEAD:], gpat, gspe
+    return out_fc2, out_out, out_fc1, out_qkv, smalls, gpat, gspe
 
 
 def reduce_any(
-    rest, pairs, twos, outs, lse, gatt_x, first_heads, tail_part, pay, gmid, gain1
+    rest, pairs, twos, outs, lse, gatt_x, first_heads, tail_part, pay, gmid, gains
 ):
     sidx, bidx, per, block, chip, hidden, cols, count, extra, width = rest
     s = lax.axis_index("seq")
@@ -1150,7 +1187,7 @@
     gpat, gspe = call(
         final_kernel,
         [SDS((count, width), F32), SDS((extra, width), F32)],
-        (gn1_keep, gn1_c, gn1_x, *pay, gmid, gain1),
+        (gn1_keep, gn1_c, gn1_x, *pay, gmid, gains),
     )
     wide = 5 * LANES
     parts = [split_bits(p.reshape(4, nb // 2, per, wide), 1, low) for p in (q_keep, swap("batch", q_send, 1))]
@@ -1161,8 +1198,9 @@
     rel = jnp.stack([p[:, : 3 * cols] for p in pieces])
     absolute = jnp.stack([pick(rel, s ^ a, 0) for a in range(4)], axis=1)
     out_qkv = absolute.reshape(-1, 4, OWN, 3, HEAD).transpose(0, 3, 1, 2, 4).reshape(-1, 3 * width)
-    vec = total([p[:, 3 * cols :] for p in pieces])
-    return out_fc2, out_out, out_fc1, out_qkv, vec, gpat, gspe
+    vec = total([p[:, 3 * cols :] for p in pieces]).T
+    smalls = [vec[jnp.array(k)] for k in ((0, 4), (1, 5), (2, 3, 7, 6), (8, 9, 10, 11))]
+    return out_fc2, out_out, out_fc1, out_qkv, smalls, gpat, gspe
 
 
 def solution(mesh):

time: 143 us -> 138 us (0.965)
  waiting for transfers between devices: 32.8 us -> 39.8 us
  local copies, waits for them, and re-layouts: 7.2 us -> 0.62 us
  other arithmetic: 3.1 us -> 0 us
  Pallas kernels: 60.8 us -> 58.9 us
    ppermute x38 -> x37, waiting for transfers between devices: 32.8 us -> 39.8 us  [swap(): lax.ppermute(v, kind, [(i, i ^ mask) for i in range(lax.axis_size(kind))])]
    another operation x5 -> x0, other arithmetic: 3.09 us -> none
    unnamed x14 -> x16, local copies, waits for them, and re-layouts: 2.86 us -> 0.03 us
    pallas_call x21, Pallas kernels: 60.8 us -> 58.9 us  [call(): pl.pallas_call(kernel, out_shape=outs, in_specs=[smem() if i < scalars el...]
    concatenate x1 -> x0, local copies, waits for them, and re-layouts: 1.68 us -> none  [body(): jnp.concatenate([specials[0], line[None], blank[:15 - extra], cot_special...]
    ppermute x38 -> x37, starting transfers between devices: 37.6 us -> 37.3 us  [swap(): lax.ppermute(v, kind, [(i, i ^ mask) for i in range(lax.axis_size(kind))])]
  transfers between devices with their start and end apart: 38 -> 37, of which waited for: 17 -> 17; matrix products, arithmetic and copies ran while one was open for 3% -> 0% of each run, Pallas kernels for 29% -> 30%
where the time goes in v6:
time: 138 us; the launch traced here: 137 us
  Pallas kernels  58.9 us (43%)
  waiting for transfers between devices  39.8 us (29%)
  starting transfers between devices  37.3 us (27%)
    pallas_call x21, Pallas kernels, call(): pl.pallas_call(kernel, out_shape=outs, in_specs=[smem() if i < scalars el...  58.9 us
    ppermute x37, waiting for transfers between devices, swap(): lax.ppermute(v, kind, [(i, i ^ mask) for i in range(lax.axis_size(kind))])  39.8 us
    ppermute x37, starting transfers between devices, swap(): lax.ppermute(v, kind, [(i, i ^ mask) for i in range(lax.axis_size(kind))])  37.3 us
  transfers between devices with their start and end apart: 37, of which 17 were waited for; matrix products, arithmetic and copies ran while one was open for 0% of the time, Pallas kernels for 30%

profile of v6, /device:TPU:0, one launch (start us, length us, event | category | flops | bytes accessed | tf_op | source)
XLA Modules:
  0.0 137.5 jit_solution(15295060830445488734)
XLA Ops:
  0.6 0.5 collective-permute-start
  1.2 2.6 %collective-permute-start.2 = (bf16[256,768]{1,0:T(8,128)(2,1)}, bf16[256,768]{1,0:T(8,128)(2,1)S(1)}, u32[]{:S(2)}, u32[]{:S(2)}) collective-permute-start(bf16[256,768]{1,0:T(8,128)(2,1)} %bitcast.15), channel_id=1, source_target_pairs={{0,16},{8,24},{16,0},{24,8},{1,17},{9,25},{17,1},{25,9},{2,18},{10... | collective-permute-start | bytes 1179656 | tf_op jit(solution)/shard_map/ppermute | solution.py:796
  3.7 0.8 shard_map.238.s0.c0
  4.5 0.2 collective-permute-start.1
  4.8 0.3 collective-permute-start.3
  5.0 2.2 %shard_map.239 = (bf16[768,640]{1,0:T(8,128)(2,1)S(1)}, f32[1,640]{1,0:T(1,128)S(1)}) custom-call(s32[1]{0:T(128)} %bitcast.sref, bf16[768,2304]{1,0:T(8,128)(2,1)} %w.1, f32[4,768]{1,0:T(4,128)} %bias.3), custom_call_target="tpu_custom_call" | custom-call | bytes 4536836 | tf_op jit(solution)/shard_map/pallas_call | solution.py:78
  7.3 2.0 %shard_map.240 = (bf16[3,576,128]{2,1,0:T(8,128)(2,1)S(1)}, bf16[3,576,128]{2,1,0:T(8,128)(2,1)S(1)}, bf16[3,576,128]{2,1,0:T(8,128)(2,1)S(1)}, bf16[576,768]{1,...) custom-call(s32[1,16]{1,0:T(1,128)S(1)} %copy-done.7, bf16[256,768]{1,0:T(8,128)(2,1)S(1)} %bitcast.16, ...), custom_call_target="tpu_custom_call" | custom-call | flops 509607936 | bytes 5274176 | tf_op jit(solution)/shard_map/pallas_call | solution.py:78
  9.3 5.4 %collective-permute-done.3.s2 = bf16[32,768]{1,0:T(8,128)(2,1)S(1)} collective-permute-done((bf16[32,768]{1,0:T(8,128)(2,1)S(1)}, bf16[32,768]{1,0:T(8,128)(2,1)S(1)}, u32[]{:S(2)}, u32[]{:S(2)}) %collective-permute-start.3) | collective-permute-done | bytes 49184 | tf_op jit(solution)/shard_map/ppermute | solution.py:796
  14.7 0.5 collective-permute-start.5
  15.2 1.3 collective-permute-done.5.s3
  16.5 6.0 %shard_map.241 = (bf16[3,1152,128]{2,1,0:T(8,128)(2,1)S(1)}, bf16[3,1152,128]{2,1,0:T(8,128)(2,1)S(1)}, bf16[3,1152,128]{2,1,0:T(8,128)(2,1)S(1)}, bf16[576,192]...) custom-call(bf16[3,576,128]{2,1,0:T(8,128)(2,1)S(1)} %get-tuple-element.153.q0, ...), custom_call_target="tpu_custom_call" | custom-call | flops 1528823808 | bytes 9624064 | tf_op jit(solution)/shard_map/pallas_call | solution.py:78
  22.5 1.8 %collective-permute-start.7 = (bf16[576,192]{1,0:T(8,128)(2,1)S(1)}, bf16[576,192]{1,0:T(8,128)(2,1)S(1)}, u32[]{:S(2)}, u32[]{:S(2)}) collective-permute-start(bf16[576,192]{1,0:T(8,128)(2,1)S(1)} %get-tuple-element.165), channel_id=1, source_target_pairs={{0,16},{8,24},{16,0},{24,8},{1,17},{9,25},{17,1},{25,9},{2,18},{10... | collective-permute-start | bytes 663560 | tf_op jit(solution)/shard_map/ppermute | solution.py:796
  24.3 5.1 %shard_map.242 = (bf16[576,192]{1,0:T(8,128)(2,1)S(1)}, f32[3,3,8,384]{3,2,1,0:T(8,128)S(1)}) custom-call(bf16[3,1152,128]{2,1,0:T(8,128)(2,1)S(1)} %get-tuple-element.160.qa, bf16[3,1152,128]{2,1,0:T(8,128)(2,1)S(1)} %get-tuple-element.161.ka, bf16[3,1152,128]{2,1,0:T(8,128)(2,1)S(1)} %get-tuple-element.162.va, f32[3,576,128]{2,1,0:T(8,128)S(1)} %get-tuple-element.163.other), custom_call_target="tpu_custom_call" | custom-call | flops 1019215872 | bytes 3870720 | tf_op jit(solution)/shard_map/pallas_call | solution.py:78
  29.4 0.6 collective-permute-start.6
  30.0 1.7 %collective-permute-done.7.a2 = bf16[576,192]{1,0:T(8,128)(2,1)S(1)} collective-permute-done((bf16[576,192]{1,0:T(8,128)(2,1)S(1)}, bf16[576,192]{1,0:T(8,128)(2,1)S(1)}, u32[]{:S(2)}, u32[]{:S(2)}) %collective-permute-start.7) | collective-permute-done | bytes 221216 | tf_op jit(solution)/shard_map/ppermute | solution.py:796
  31.6 1.6 %collective-permute-done.8.a3 = bf16[576,192]{1,0:T(8,128)(2,1)S(1)} collective-permute-done((bf16[576,192]{1,0:T(8,128)(2,1)S(1)}, bf16[576,192]{1,0:T(8,128)(2,1)S(1)}, u32[]{:S(2)}, u32[]{:S(2)}) %collective-permute-start.8) | collective-permute-done | bytes 221216 | tf_op jit(solution)/shard_map/ppermute | solution.py:796
  33.2 3.3 %shard_map.243 = (f32[576,768]{1,0:T(8,128)S(1)}, bf16[576,768]{1,0:T(8,128)(2,1)S(1)}, bf16[576,768]{1,0:T(8,128)(2,1)S(1)}, bf16[768,768]{1,0:T(8,128)(2,1)S(1)}, bf16[768,768]{1,0:T(8,128)(2,1)S(1)}) custom-call(s32[1]{0:T(128)} %bitcast.sref, bf16[576,192]{1,0:T(8,128)(2,1)S(1)} %get-tuple-element.164.a0, ...), custom_call_target="tpu_custom_call" | custom-call | flops 679477248 | bytes 19488772 | tf_op jit(solution)/shard_map/pallas_call | solution.py:78
  36.5 6.5 %shard_map.244 = (bf16[8,24,768]{2,1,0:T(8,128)(2,1)S(1)}, bf16[8,24,768]{2,1,0:T(8,128)(2,1)S(1)}, bf16[4,48,768]{2,1,0:T(8,128)(2,1)S(1)}, bf16[4,48,768]{2,1,...) custom-call(s32[1]{0:T(128)} %bitcast.sref, ...), custom_call_target="tpu_custom_call" | custom-call | flops 4076863488 | bytes 21838856 | tf_op jit(solution)/shard_map/pallas_call | solution.py:78
  43.1 1.8 %collective-permute-start.11 = (bf16[12,24,768]{2,1,0:T(8,128)(2,1)S(1)}, bf16[12,24,768]{2,1,0:T(8,128)(2,1)S(1)}, u32[]{:S(2)}, u32[]{:S(2)}) collective-permute-start(bf16[12,24,768]{2,1,0:T(8,128)(2,1)S(1)} %get-tuple-element.183), channel_id=1, source_target_pairs={{0,1},{1,0},{2,3},{3,2},{4,5},{5,4},{6,7},{7,6},{8,9},{9,8},{10,11... | collective-permute-start | bytes 1327112 | tf_op jit(solution)/shard_map/ppermute | solution.py:796
  44.9 1.5 %collective-permute-start.10 = (bf16[8,24,768]{2,1,0:T(8,128)(2,1)S(1)}, bf16[8,24,768]{2,1,0:T(8,128)(2,1)S(1)}, u32[]{:S(2)}, u32[]{:S(2)}) collective-permute-start(bf16[8,24,768]{2,1,0:T(8,128)(2,1)S(1)} %get-tuple-element.182), channel_id=1, source_target_pairs={{0,16},{8,24},{16,0},{24,8},{1,17},{9,25},{17,1},{25,9},{2,18},{10... | collective-permute-start | bytes 884744 | tf_op jit(solution)/shard_map/ppermute | solution.py:796
  46.4 1.6 %collective-permute-start.12 = (bf16[4,48,768]{2,1,0:T(8,128)(2,1)S(1)}, bf16[4,48,768]{2,1,0:T(8,128)(2,1)S(1)}, u32[]{:S(2)}, u32[]{:S(2)}) collective-permute-start(bf16[4,48,768]{2,1,0:T(8,128)(2,1)S(1)} %get-tuple-element.184), channel_id=1, source_target_pairs={{0,2},{1,3},{2,0},{3,1},{4,6},{5,7},{6,4},{7,5},{8,10},{9,11},{10,... | collective-permute-start | bytes 884744 | tf_op jit(solution)/shard_map/ppermute | solution.py:796
  48.0 5.2 %shard_map.245 = (bf16[8,48,768]{2,1,0:T(8,128)(2,1)S(1)}, bf16[4,48,768]{2,1,0:T(8,128)(2,1)S(1)}, bf16[4,48,768]{2,1,0:T(8,128)(2,1)S(1)}, bf16[20,24,768]{2,1...) custom-call(s32[1]{0:T(128)} %bitcast.sref, ...), custom_call_target="tpu_custom_call" | custom-call | flops 4076863488 | bytes 14318600 | tf_op jit(solution)/shard_map/pallas_call | solution.py:78
  53.2 0.4 collective-permute-done.10.g2a
  53.7 1.2 collective-permute-done.12.oth_got
  54.9 0.5 collective-permute-done.11.y1
  55.4 0.5 collective-permute-start.14
  55.9 1.7 %collective-permute-start.17 = (bf16[20,24,768]{2,1,0:T(8,128)(2,1)S(1)}, bf16[20,24,768]{2,1,0:T(8,128)(2,1)S(1)}, u32[]{:S(2)}, u32[]{:S(2)}) collective-permute-start(bf16[20,24,768]{2,1,0:T(8,128)(2,1)S(1)} %get-tuple-element.216), channel_id=1, source_target_pairs={{0,1},{1,0},{2,3},{3,2},{4,5},{5,4},{6,7},{7,6},{8,9},{9,8},{10,11... | collective-permute-start | bytes 2211848 | tf_op jit(solution)/shard_map/ppermute | solution.py:796
  57.6 1.6 %collective-permute-start.16 = (bf16[4,48,768]{2,1,0:T(8,128)(2,1)S(1)}, bf16[4,48,768]{2,1,0:T(8,128)(2,1)S(1)}, u32[]{:S(2)}, u32[]{:S(2)}) collective-permute-start(bf16[4,48,768]{2,1,0:T(8,128)(2,1)S(1)} %get-tuple-element.201), channel_id=1, source_target_pairs={{0,2},{1,3},{2,0},{3,1},{4,6},{5,7},{6,4},{7,5},{8,10},{9,11},{10,... | collective-permute-start | bytes 884744 | tf_op jit(solution)/shard_map/ppermute | solution.py:796
  59.2 2.0 %shard_map.246 = (f32[288,768]{1,0:T(8,128)S(1)}, bf16[576,768]{1,0:T(8,128)(2,1)S(1)}, bf16[576,192]{1,0:T(8,128)(2,1)S(1)}, f32[8,768]{1,0:T(8,128)S(1)}) custom-call(s32[1]{0:T(128)} %bitcast.sref, f32[576,768]{1,0:T(8,128)S(1)} %get-tuple-element.177.gn_keep, bf16[576,768]{1,0:T(8,128)(2,1)S(1)} %collective-permute-done.13.gn_got, ...), custom_call_target="tpu_custom_call" | custom-call | flops 169869312 | bytes 9689092 | tf_op jit(solution)/shard_map/pallas_call | solution.py:78
  61.2 1.6 %collective-permute-start.15 = (bf16[576,192]{1,0:T(8,128)(2,1)S(1)}, bf16[576,192]{1,0:T(8,128)(2,1)S(1)}, u32[]{:S(2)}, u32[]{:S(2)}) collective-permute-start(bf16[576,192]{1,0:T(8,128)(2,1)S(1)} %get-tuple-element.199), channel_id=1, source_target_pairs={{0,16},{8,24},{16,0},{24,8},{1,17},{9,25},{17,1},{25,9},{2,18},{10... | collective-permute-start | bytes 663560 | tf_op jit(solution)/shard_map/ppermute | solution.py:796
  62.8 1.6 %shard_map.247 = (bf16[576,192]{1,0:T(8,128)(2,1)S(1)}, bf16[2,4,24,768]{3,2,1,0:T(8,128)(2,1)S(1)}, bf16[2,4,24,768]{3,2,1,0:T(8,128)(2,1)S(1)}, f32[768,128]{1...) custom-call(s32[1]{0:T(128)} %bitcast.sref, s32[1]{0:T(128)} %bitcast.1.bref, ...), custom_call_target="tpu_custom_call" | custom-call | flops 509607936 | bytes 7557128 | tf_op jit(solution)/shard_map/pallas_call | solution.py:78
  64.4 0.5 collective-permute-start.19
  64.9 1.3 collective-permute-done.16.own_got
  66.4 2.7 %collective-permute-start.20 = (bf16[4,48,768]{2,1,0:T(8,128)(2,1)S(1)}, bf16[4,48,768]{2,1,0:T(8,128)(2,1)S(1)}, u32[]{:S(2)}, u32[]{:S(2)}) collective-permute-start(bf16[4,48,768]{2,1,0:T(8,128)(2,1)S(1)} %get-tuple-element.206), channel_id=1, source_target_pairs={{0,4},{1,5},{2,6},{3,7},{4,0},{5,1},{6,2},{7,3},{8,12},{9,13},{10,... | collective-permute-start | bytes 884744 | tf_op jit(solution)/shard_map/ppermute | solution.py:796
  69.0 0.6 collective-permute-done.15.gx
  69.7 1.5 %collective-permute-start.18 = (bf16[8,24,768]{2,1,0:T(8,128)(2,1)S(1)}, bf16[8,24,768]{2,1,0:T(8,128)(2,1)S(1)}, u32[]{:S(2)}, u32[]{:S(2)}) collective-permute-start(bf16[8,24,768]{2,1,0:T(8,128)(2,1)S(1)} %get-tuple-element.217), channel_id=1, source_target_pairs={{0,16},{8,24},{16,0},{24,8},{1,17},{9,25},{17,1},{25,9},{2,18},{10... | collective-permute-start | bytes 884744 | tf_op jit(solution)/shard_map/ppermute | solution.py:796
  71.2 11.3 %shard_map.249 = (bf16[2,1152,192]{2,1,0:T(8,128)(2,1)S(1)}, bf16[8,24,768]{2,1,0:T(8,128)(2,1)S(1)}, bf16[8,24,768]{2,1,0:T(8,128)(2,1)S(1)}, f32[768,128]{1,0:T(8,128)S(1)}) custom-call(s32[1]{0:T(128)} %bitcast.sref, s32[1]{0:T(128)} %bitcast.1.bref, bf16[3,1152,128]{2,1,0:T(8,128)(2,1)S(1)} %get-tuple-element.160.qa, ...), custom_call_target="tpu_custom_call" | custom-call | flops 3397386240 | bytes 8220680 | tf_op jit(solution)/shard_map/pallas_call | solution.py:78
  82.5 0.5 shard_map.250
  83.1 1.1 collective-permute-start.22
  84.1 1.6 %collective-permute-start.23 = (bf16[16,24,768]{2,1,0:T(8,128)(2,1)S(1)}, bf16[16,24,768]{2,1,0:T(8,128)(2,1)S(1)}, u32[]{:S(2)}, u32[]{:S(2)}) collective-permute-start(bf16[16,24,768]{2,1,0:T(8,128)(2,1)S(1)} %get-tuple-element.238), channel_id=1, source_target_pairs={{0,2},{1,3},{2,0},{3,1},{4,6},{5,7},{6,4},{7,5},{8,10},{9,11},{10,... | collective-permute-start | bytes 1769480 | tf_op jit(solution)/shard_map/ppermute | solution.py:796
  85.7 0.5 collective-permute-start.21
  86.3 8.2 %shard_map.251 = (f32[576,768]{1,0:T(8,128)S(1)}, bf16[576,768]{1,0:T(8,128)(2,1)S(1)}, bf16[16,24,256]{2,1,0:T(8,128)(2,1)S(1)}, bf16[16,24,256]{2,1,0:T(8,128)(2,1)S(1)}) custom-call(s32[1]{0:T(128)} %bitcast.sref, s32[1]{0:T(128)} %bitcast.1.bref, bf16[3,1152,128]{2,1,0:T(8,128)(2,1)S(1)} %get-tuple-element.160.qa, ...), custom_call_target="tpu_custom_call" | custom-call | flops 1698693120 | bytes 10285064 | tf_op jit(solution)/shard_map/pallas_call | solution.py:78
  94.5 2.1 %collective-permute-done.22.got_y = bf16[16,24,768]{2,1,0:T(8,128)(2,1)S(1)} collective-permute-done((bf16[16,24,768]{2,1,0:T(8,128)(2,1)S(1)}, bf16[16,24,768]{2,1,0:T(8,128)(2,1)S(1)}, u32[]{:S(2)}, u32[]{:S(2)}) %collective-permute-start.22) | collective-permute-done | bytes 589856 | tf_op jit(solution)/shard_map/ppermute | solution.py:796
  96.6 1.4 collective-permute-done.23.got_z
  98.0 0.3 shard_map.252
  98.3 1.8 %collective-permute-start.27 = (bf16[10,24,768]{2,1,0:T(8,128)(2,1)S(1)}, bf16[10,24,768]{2,1,0:T(8,128)(2,1)S(1)}, u32[]{:S(2)}, u32[]{:S(2)}) collective-permute-start(bf16[10,24,768]{2,1,0:T(8,128)(2,1)S(1)} %get-tuple-element.254), channel_id=1, source_target_pairs={{0,2},{1,3},{2,0},{3,1},{4,6},{5,7},{6,4},{7,5},{8,10},{9,11},{10,... | collective-permute-start | bytes 1105928 | tf_op jit(solution)/shard_map/ppermute | solution.py:796
  100.1 0.5 collective-permute-start.26
  100.6 0.9 collective-permute-start.28
  101.6 1.1 collective-permute-start.25
  102.7 7.2 %collective-permute-done.26.got_x = bf16[8,24,768]{2,1,0:T(8,128)(2,1)S(1)} collective-permute-done((bf16[8,24,768]{2,1,0:T(8,128)(2,1)S(1)}, bf16[8,24,768]{2,1,0:T(8,128)(2,1)S(1)}, u32[]{:S(2)}, u32[]{:S(2)}) %collective-permute-start.26) | collective-permute-done | bytes 294944 | tf_op jit(solution)/shard_map/ppermute | solution.py:796
  110.1 2.7 %collective-permute-start.29 = (bf16[9,24,768]{2,1,0:T(8,128)(2,1)S(1)}, bf16[9,24,768]{2,1,0:T(8,128)(2,1)S(1)}, u32[]{:S(2)}, u32[]{:S(2)}) collective-permute-start(bf16[9,24,768]{2,1,0:T(8,128)(2,1)S(1)} %get-tuple-element.263), channel_id=1, source_target_pairs={{0,4},{1,5},{2,6},{3,7},{4,0},{5,1},{6,2},{7,3},{8,12},{9,13},{10,... | collective-permute-start | bytes 995336 | tf_op jit(solution)/shard_map/ppermute | solution.py:796
  112.8 0.3 collective-permute-start.31
  113.1 3.2 %collective-permute-start.32 = (bf16[4,24,256]{2,1,0:T(8,128)(2,1)S(1)}, bf16[4,24,256]{2,1,0:T(8,128)(2,1)S(1)}, u32[]{:S(2)}, u32[]{:S(2)}) collective-permute-start(bf16[4,24,256]{2,1,0:T(8,128)(2,1)S(1)} %get-tuple-element.267), channel_id=1, source_target_pairs={{0,6},{1,7},{2,4},{3,5},{4,2},{5,3},{6,0},{7,1},{8,14},{9,15},{10,... | collective-permute-start | bytes 147464 | tf_op jit(solution)/shard_map/ppermute | solution.py:796
  116.3 2.4 %collective-permute-done.25.x0 = bf16[288,768]{1,0:T(8,128)(2,1)S(1)} collective-permute-done((bf16[288,768]{1,0:T(8,128)(2,1)S(1)}, bf16[288,768]{1,0:T(8,128)(2,1)S(1)}, u32[]{:S(2)}, u32[]{:S(2)}) %collective-permute-start.25) | collective-permute-done | bytes 442400 | tf_op jit(solution)/shard_map/ppermute | solution.py:796
  118.7 1.5 %shard_map.255 = (f32[256,768]{1,0:T(8,128)}, f32[4,768]{1,0:T(4,128)}) custom-call(f32[576,768]{1,0:T(8,128)S(1)} %get-tuple-element.250.keep.k0, bf16[576,768]{1,0:T(8,128)(2,1)S(1)} %collective-permute-done.24.got.c0, bf16[288,768]{1,0:T(8,128)(2,1)S(1)} %collective-permute-done.25.x0, bf16[256,768]{1,0:T(8,128)(2,1)S(1)} %bitcast.17, ...), custom_call_target="tpu_custom_call" | custom-call | bytes 5228544 | tf_op jit(solution)/shard_map/pallas_call | solution.py:78
  120.2 10.0 %collective-permute-done.29.got = bf16[9,24,768]{2,1,0:T(8,128)(2,1)S(1)} collective-permute-done((bf16[9,24,768]{2,1,0:T(8,128)(2,1)S(1)}, bf16[9,24,768]{2,1,0:T(8,128)(2,1)S(1)}, u32[]{:S(2)}, u32[]{:S(2)}) %collective-permute-start.29) | collective-permute-done | bytes 331808 | tf_op jit(solution)/shard_map/ppermute | solution.py:796
  130.2 0.5 collective-permute-done.31.z2
  130.8 0.8 shard_map.257
  131.6 0.7 collective-permute-start.34
  132.3 1.2 collective-permute-start.35
  133.5 0.3 collective-permute-start.33
  133.7 2.0 %collective-permute-done.34.g2 = bf16[24,640]{1,0:T(8,128)(2,1)S(1)} collective-permute-done((bf16[24,640]{1,0:T(8,128)(2,1)S(1)}, bf16[24,640]{1,0:T(8,128)(2,1)S(1)}, u32[]{:S(2)}, u32[]{:S(2)}) %collective-permute-start.34) | collective-permute-done | bytes 30752 | tf_op jit(solution)/shard_map/ppermute | solution.py:796
  135.9 0.9 shard_map.258
  136.9 0.6 reshape.39
  (48 shorter events, 0.8 us)
Async XLA Ops:
  0.6 6.7 %collective-permute-start = (bf16[256,768]{1,0:T(8,128)(2,1)}, bf16[256,768]{1,0:T(8,128)(2,1)S(1)}, u32[]{:S(2)}, u32[]{:S(2)}) collective-permute-start(bf16[256,768]{1,0:T(8,128)(2,1)} %bitcast.14), channel_id=1, source_target_pairs={{0,8},{8,0},{16,24},{24,16},{1,9},{9,1},{17,25},{25,17},{2,10},{10... | collective-permute-start | bytes 1179656 | tf_op jit(solution)/shard_map/ppermute | solution.py:796
  1.2 13.5 %collective-permute-start.2 = (bf16[256,768]{1,0:T(8,128)(2,1)}, bf16[256,768]{1,0:T(8,128)(2,1)S(1)}, u32[]{:S(2)}, u32[]{:S(2)}) collective-permute-start(bf16[256,768]{1,0:T(8,128)(2,1)} %bitcast.15), channel_id=1, source_target_pairs={{0,16},{8,24},{16,0},{24,8},{1,17},{9,25},{17,1},{25,9},{2,18},{10... | collective-permute-start | bytes 1179656 | tf_op jit(solution)/shard_map/ppermute | solution.py:796
  4.5 2.8 %collective-permute-start.1 = (bf16[32,768]{1,0:T(8,128)(2,1)S(1)}, bf16[32,768]{1,0:T(8,128)(2,1)S(1)}, u32[]{:S(2)}, u32[]{:S(2)}) collective-permute-start(bf16[32,768]{1,0:T(8,128)(2,1)S(1)} %shard_map.238.s0.c0), channel_id=1, source_target_pairs={{0,8},{8,0},{16,24},{24,16},{1,9},{9,1},{17,25},{25,17},{2,10},{10... | collective-permute-start | bytes 147464 | tf_op jit(solution)/shard_map/ppermute | solution.py:796
  4.8 9.9 %collective-permute-start.3 = (bf16[32,768]{1,0:T(8,128)(2,1)S(1)}, bf16[32,768]{1,0:T(8,128)(2,1)S(1)}, u32[]{:S(2)}, u32[]{:S(2)}) collective-permute-start(bf16[32,768]{1,0:T(8,128)(2,1)S(1)} %shard_map.238.s0.c0), channel_id=1, source_target_pairs={{0,16},{8,24},{16,0},{24,8},{1,17},{9,25},{17,1},{25,9},{2,18},{10... | collective-permute-start | bytes 147464 | tf_op jit(solution)/shard_map/ppermute | solution.py:796
  5.0 2.3 %copy-start.2 = (bf16[1,256,768]{2,1,0:T(8,128)(2,1)S(1)}, bf16[1,256,768]{2,1,0:T(8,128)(2,1)}, u32[]{:S(2)}) copy-start(bf16[1,256,768]{2,1,0:T(8,128)(2,1)} %param.15) | copy-start | bytes 1179652
  5.0 2.3 %copy-start.4 = (f32[2,768]{1,0:T(2,128)S(1)}, f32[2,768]{1,0:T(2,128)}, u32[]{:S(2)}) copy-start(f32[2,768]{1,0:T(2,128)} %gain.9) | copy-start | bytes 18436
  5.0 2.3 %copy-start.5 = (f32[2,768]{1,0:T(2,128)S(1)}, f32[2,768]{1,0:T(2,128)}, u32[]{:S(2)}) copy-start(f32[2,768]{1,0:T(2,128)} %shift1.1) | copy-start | bytes 18436
  5.0 2.3 %copy-start.7 = (s32[1,16]{1,0:T(1,128)S(1)}, s32[1,16]{1,0:T(1,128)}, u32[]{:S(2)}) copy-start(s32[1,16]{1,0:T(1,128)} %flags.1) | copy-start | bytes 196
  14.7 1.8 %collective-permute-start.4 = (bf16[256,768]{1,0:T(8,128)(2,1)S(1)}, bf16[256,768]{1,0:T(8,128)(2,1)S(1)}, u32[]{:S(2)}, u32[]{:S(2)}) collective-permute-start(bf16[256,768]{1,0:T(8,128)(2,1)S(1)} %collective-permute-done.2.p2), channel_id=1, source_target_pairs={{0,8},{8,0},{16,24},{24,16},{1,9},{9,1},{17,25},{25,17},{2,10},{10... | collective-permute-start | bytes 1179656 | tf_op jit(solution)/shard_map/ppermute | solution.py:796
  14.7 1.8 %collective-permute-start.5 = (bf16[32,768]{1,0:T(8,128)(2,1)S(1)}, bf16[32,768]{1,0:T(8,128)(2,1)S(1)}, u32[]{:S(2)}, u32[]{:S(2)}) collective-permute-start(bf16[32,768]{1,0:T(8,128)(2,1)S(1)} %collective-permute-done.3.s2), channel_id=1, source_target_pairs={{0,8},{8,0},{16,24},{24,16},{1,9},{9,1},{17,25},{25,17},{2,10},{10... | collective-permute-start | bytes 147464 | tf_op jit(solution)/shard_map/ppermute | solution.py:796
  16.5 7.8 %copy-start.1 = (bf16[1,256,768]{2,1,0:T(8,128)(2,1)S(1)}, bf16[1,256,768]{2,1,0:T(8,128)(2,1)}, u32[]{:S(2)}) copy-start(bf16[1,256,768]{2,1,0:T(8,128)(2,1)} %param.28) | copy-start | bytes 1179652
  22.5 9.1 %collective-permute-start.7 = (bf16[576,192]{1,0:T(8,128)(2,1)S(1)}, bf16[576,192]{1,0:T(8,128)(2,1)S(1)}, u32[]{:S(2)}, u32[]{:S(2)}) collective-permute-start(bf16[576,192]{1,0:T(8,128)(2,1)S(1)} %get-tuple-element.165), channel_id=1, source_target_pairs={{0,16},{8,24},{16,0},{24,8},{1,17},{9,25},{17,1},{25,9},{2,18},{10... | collective-permute-start | bytes 663560 | tf_op jit(solution)/shard_map/ppermute | solution.py:796
  24.3 7.3 %collective-permute-start.9 = (bf16[256,768]{1,0:T(8,128)(2,1)S(1)}, bf16[256,768]{1,0:T(8,128)(2,1)S(1)}, u32[]{:S(2)}, u32[]{:S(2)}) collective-permute-start(bf16[256,768]{1,0:T(8,128)(2,1)S(1)} %bitcast.11), channel_id=1, source_target_pairs={{0,8},{8,0},{16,24},{24,16},{1,9},{9,1},{17,25},{25,17},{2,10},{10... | collective-permute-start | bytes 1179656 | tf_op jit(solution)/shard_map/ppermute | solution.py:796
  24.3 8.9 %copy-start = (bf16[768,768]{1,0:T(8,128)(2,1)S(1)}, bf16[768,768]{1,0:T(8,128)(2,1)}, u32[]{:S(2)}) copy-start(bf16[768,768]{1,0:T(8,128)(2,1)} %w_out.5) | copy-start | bytes 3538948
  24.3 8.9 %copy-start.3 = (f32[4,768]{1,0:T(4,128)S(1)}, f32[4,768]{1,0:T(4,128)}, u32[]{:S(2)}) copy-start(f32[4,768]{1,0:T(4,128)} %bias.3) | copy-start | bytes 36868
  29.4 2.2 %collective-permute-start.6 = (bf16[576,192]{1,0:T(8,128)(2,1)S(1)}, bf16[576,192]{1,0:T(8,128)(2,1)S(1)}, u32[]{:S(2)}, u32[]{:S(2)}) collective-permute-start(bf16[576,192]{1,0:T(8,128)(2,1)S(1)} %get-tuple-element.164.a0), channel_id=1, source_target_pairs={{0,8},{8,0},{16,24},{24,16},{1,9},{9,1},{17,25},{25,17},{2,10},{10... | collective-permute-start | bytes 663560 | tf_op jit(solution)/shard_map/ppermute | solution.py:796
  31.6 1.6 %collective-permute-start.8 = (bf16[576,192]{1,0:T(8,128)(2,1)S(1)}, bf16[576,192]{1,0:T(8,128)(2,1)S(1)}, u32[]{:S(2)}, u32[]{:S(2)}) collective-permute-start(bf16[576,192]{1,0:T(8,128)(2,1)S(1)} %collective-permute-done.7.a2), channel_id=1, source_target_pairs={{0,8},{8,0},{16,24},{24,16},{1,9},{9,1},{17,25},{25,17},{2,10},{10... | collective-permute-start | bytes 663560 | tf_op jit(solution)/shard_map/ppermute | solution.py:796
  33.2 3.3 %copy-start.6 = (f32[3072]{0:T(1024)S(1)}, f32[3072]{0:T(1024)}, u32[]{:S(2)}) copy-start(f32[3072]{0:T(1024)} %param.26) | copy-start | bytes 36868
  43.1 12.3 %collective-permute-start.11 = (bf16[12,24,768]{2,1,0:T(8,128)(2,1)S(1)}, bf16[12,24,768]{2,1,0:T(8,128)(2,1)S(1)}, u32[]{:S(2)}, u32[]{:S(2)}) collective-permute-start(bf16[12,24,768]{2,1,0:T(8,128)(2,1)S(1)} %get-tuple-element.183), channel_id=1, source_target_pairs={{0,1},{1,0},{2,3},{3,2},{4,5},{5,4},{6,7},{7,6},{8,9},{9,8},{10,11... | collective-permute-start | bytes 1327112 | tf_op jit(solution)/shard_map/ppermute | solution.py:796
  44.9 8.8 %collective-permute-start.10 = (bf16[8,24,768]{2,1,0:T(8,128)(2,1)S(1)}, bf16[8,24,768]{2,1,0:T(8,128)(2,1)S(1)}, u32[]{:S(2)}, u32[]{:S(2)}) collective-permute-start(bf16[8,24,768]{2,1,0:T(8,128)(2,1)S(1)} %get-tuple-element.182), channel_id=1, source_target_pairs={{0,16},{8,24},{16,0},{24,8},{1,17},{9,25},{17,1},{25,9},{2,18},{10... | collective-permute-start | bytes 884744 | tf_op jit(solution)/shard_map/ppermute | solution.py:796
  46.4 8.5 %collective-permute-start.12 = (bf16[4,48,768]{2,1,0:T(8,128)(2,1)S(1)}, bf16[4,48,768]{2,1,0:T(8,128)(2,1)S(1)}, u32[]{:S(2)}, u32[]{:S(2)}) collective-permute-start(bf16[4,48,768]{2,1,0:T(8,128)(2,1)S(1)} %get-tuple-element.184), channel_id=1, source_target_pairs={{0,2},{1,3},{2,0},{3,1},{4,6},{5,7},{6,4},{7,5},{8,10},{9,11},{10,... | collective-permute-start | bytes 884744 | tf_op jit(solution)/shard_map/ppermute | solution.py:796
  55.4 3.8 %collective-permute-start.13 = (bf16[576,768]{1,0:T(8,128)(2,1)S(1)}, bf16[576,768]{1,0:T(8,128)(2,1)S(1)}, u32[]{:S(2)}, u32[]{:S(2)}) collective-permute-start(bf16[576,768]{1,0:T(8,128)(2,1)S(1)} %get-tuple-element.185), channel_id=1, source_target_pairs={{0,8},{8,0},{16,24},{24,16},{1,9},{9,1},{17,25},{25,17},{2,10},{10... | collective-permute-start | bytes 2654216 | tf_op jit(solution)/shard_map/ppermute | solution.py:796
  55.4 7.4 %collective-permute-start.14 = (bf16[288,768]{1,0:T(8,128)(2,1)S(1)}, bf16[288,768]{1,0:T(8,128)(2,1)S(1)}, u32[]{:S(2)}, u32[]{:S(2)}) collective-permute-start(bf16[288,768]{1,0:T(8,128)(2,1)S(1)} %get-tuple-element.189), channel_id=1, source_target_pairs={{0,8},{8,0},{16,24},{24,16},{1,9},{9,1},{17,25},{25,17},{2,10},{10... | collective-permute-start | bytes 1327112 | tf_op jit(solution)/shard_map/ppermute | solution.py:796
  55.9 26.6 %collective-permute-start.17 = (bf16[20,24,768]{2,1,0:T(8,128)(2,1)S(1)}, bf16[20,24,768]{2,1,0:T(8,128)(2,1)S(1)}, u32[]{:S(2)}, u32[]{:S(2)}) collective-permute-start(bf16[20,24,768]{2,1,0:T(8,128)(2,1)S(1)} %get-tuple-element.216), channel_id=1, source_target_pairs={{0,1},{1,0},{2,3},{3,2},{4,5},{5,4},{6,7},{7,6},{8,9},{9,8},{10,11... | collective-permute-start | bytes 2211848 | tf_op jit(solution)/shard_map/ppermute | solution.py:796
  57.6 8.6 %collective-permute-start.16 = (bf16[4,48,768]{2,1,0:T(8,128)(2,1)S(1)}, bf16[4,48,768]{2,1,0:T(8,128)(2,1)S(1)}, u32[]{:S(2)}, u32[]{:S(2)}) collective-permute-start(bf16[4,48,768]{2,1,0:T(8,128)(2,1)S(1)} %get-tuple-element.201), channel_id=1, source_target_pairs={{0,2},{1,3},{2,0},{3,1},{4,6},{5,7},{6,4},{7,5},{8,10},{9,11},{10,... | collective-permute-start | bytes 884744 | tf_op jit(solution)/shard_map/ppermute | solution.py:796
  61.2 8.4 %collective-permute-start.15 = (bf16[576,192]{1,0:T(8,128)(2,1)S(1)}, bf16[576,192]{1,0:T(8,128)(2,1)S(1)}, u32[]{:S(2)}, u32[]{:S(2)}) collective-permute-start(bf16[576,192]{1,0:T(8,128)(2,1)S(1)} %get-tuple-element.199), channel_id=1, source_target_pairs={{0,16},{8,24},{16,0},{24,8},{1,17},{9,25},{17,1},{25,9},{2,18},{10... | collective-permute-start | bytes 663560 | tf_op jit(solution)/shard_map/ppermute | solution.py:796
  64.4 18.1 %collective-permute-start.19 = (bf16[2,4,24,768]{3,2,1,0:T(8,128)(2,1)S(1)}, bf16[2,4,24,768]{3,2,1,0:T(8,128)(2,1)S(1)}, u32[]{:S(2)}, u32[]{:S(2)}) collective-permute-start(bf16[2,4,24,768]{3,2,1,0:T(8,128)(2,1)S(1)} %get-tuple-element.202), channel_id=1, source_target_pairs={{0,1},{1,0},{2,3},{3,2},{4,5},{5,4},{6,7},{7,6},{8,9},{9,8},{10,11... | collective-permute-start | bytes 884744 | tf_op jit(solution)/shard_map/ppermute | solution.py:796
  66.4 16.1 %collective-permute-start.20 = (bf16[4,48,768]{2,1,0:T(8,128)(2,1)S(1)}, bf16[4,48,768]{2,1,0:T(8,128)(2,1)S(1)}, u32[]{:S(2)}, u32[]{:S(2)}) collective-permute-start(bf16[4,48,768]{2,1,0:T(8,128)(2,1)S(1)} %get-tuple-element.206), channel_id=1, source_target_pairs={{0,4},{1,5},{2,6},{3,7},{4,0},{5,1},{6,2},{7,3},{8,12},{9,13},{10,... | collective-permute-start | bytes 884744 | tf_op jit(solution)/shard_map/ppermute | solution.py:796
  69.7 12.9 %collective-permute-start.18 = (bf16[8,24,768]{2,1,0:T(8,128)(2,1)S(1)}, bf16[8,24,768]{2,1,0:T(8,128)(2,1)S(1)}, u32[]{:S(2)}, u32[]{:S(2)}) collective-permute-start(bf16[8,24,768]{2,1,0:T(8,128)(2,1)S(1)} %get-tuple-element.217), channel_id=1, source_target_pairs={{0,16},{8,24},{16,0},{24,8},{1,17},{9,25},{17,1},{25,9},{2,18},{10... | collective-permute-start | bytes 884744 | tf_op jit(solution)/shard_map/ppermute | solution.py:796
  83.1 13.5 %collective-permute-start.22 = (bf16[16,24,768]{2,1,0:T(8,128)(2,1)S(1)}, bf16[16,24,768]{2,1,0:T(8,128)(2,1)S(1)}, u32[]{:S(2)}, u32[]{:S(2)}) collective-permute-start(bf16[16,24,768]{2,1,0:T(8,128)(2,1)S(1)} %get-tuple-element.237), channel_id=1, source_target_pairs={{0,1},{1,0},{2,3},{3,2},{4,5},{5,4},{6,7},{7,6},{8,9},{9,8},{10,11... | collective-permute-start | bytes 1769480 | tf_op jit(solution)/shard_map/ppermute | solution.py:796
  84.1 13.8 %collective-permute-start.23 = (bf16[16,24,768]{2,1,0:T(8,128)(2,1)S(1)}, bf16[16,24,768]{2,1,0:T(8,128)(2,1)S(1)}, u32[]{:S(2)}, u32[]{:S(2)}) collective-permute-start(bf16[16,24,768]{2,1,0:T(8,128)(2,1)S(1)} %get-tuple-element.238), channel_id=1, source_target_pairs={{0,2},{1,3},{2,0},{3,1},{4,6},{5,7},{6,4},{7,5},{8,10},{9,11},{10,... | collective-permute-start | bytes 1769480 | tf_op jit(solution)/shard_map/ppermute | solution.py:796
  85.7 8.7 %collective-permute-start.21 = (bf16[8,24,768]{2,1,0:T(8,128)(2,1)S(1)}, bf16[8,24,768]{2,1,0:T(8,128)(2,1)S(1)}, u32[]{:S(2)}, u32[]{:S(2)}) collective-permute-start(bf16[8,24,768]{2,1,0:T(8,128)(2,1)S(1)} %get-tuple-element.236), channel_id=1, source_target_pairs={{0,16},{8,24},{16,0},{24,8},{1,17},{9,25},{17,1},{25,9},{2,18},{10... | collective-permute-start | bytes 884744 | tf_op jit(solution)/shard_map/ppermute | solution.py:796
  98.0 3.6 %collective-permute-start.24 = (bf16[576,768]{1,0:T(8,128)(2,1)S(1)}, bf16[576,768]{1,0:T(8,128)(2,1)S(1)}, u32[]{:S(2)}, u32[]{:S(2)}) collective-permute-start(bf16[576,768]{1,0:T(8,128)(2,1)S(1)} %get-tuple-element.239), channel_id=1, source_target_pairs={{0,8},{8,0},{16,24},{24,16},{1,9},{9,1},{17,25},{25,17},{2,10},{10... | collective-permute-start | bytes 2654216 | tf_op jit(solution)/shard_map/ppermute | solution.py:796
  98.3 11.7 %collective-permute-start.27 = (bf16[10,24,768]{2,1,0:T(8,128)(2,1)S(1)}, bf16[10,24,768]{2,1,0:T(8,128)(2,1)S(1)}, u32[]{:S(2)}, u32[]{:S(2)}) collective-permute-start(bf16[10,24,768]{2,1,0:T(8,128)(2,1)S(1)} %get-tuple-element.254), channel_id=1, source_target_pairs={{0,2},{1,3},{2,0},{3,1},{4,6},{5,7},{6,4},{7,5},{8,10},{9,11},{10,... | collective-permute-start | bytes 1105928 | tf_op jit(solution)/shard_map/ppermute | solution.py:796
  100.1 9.8 %collective-permute-start.26 = (bf16[8,24,768]{2,1,0:T(8,128)(2,1)S(1)}, bf16[8,24,768]{2,1,0:T(8,128)(2,1)S(1)}, u32[]{:S(2)}, u32[]{:S(2)}) collective-permute-start(bf16[8,24,768]{2,1,0:T(8,128)(2,1)S(1)} %get-tuple-element.249), channel_id=1, source_target_pairs={{0,16},{8,24},{16,0},{24,8},{1,17},{9,25},{17,1},{25,9},{2,18},{10... | collective-permute-start | bytes 884744 | tf_op jit(solution)/shard_map/ppermute | solution.py:796
  100.6 9.3 %collective-permute-start.28 = (bf16[22,24,256]{2,1,0:T(8,128)(2,1)S(1)}, bf16[22,24,256]{2,1,0:T(8,128)(2,1)S(1)}, u32[]{:S(2)}, u32[]{:S(2)}) collective-permute-start(bf16[22,24,256]{2,1,0:T(8,128)(2,1)S(1)} %get-tuple-element.256), channel_id=1, source_target_pairs={{0,1},{1,0},{2,3},{3,2},{4,5},{5,4},{6,7},{7,6},{8,9},{9,8},{10,11... | collective-permute-start | bytes 811016 | tf_op jit(solution)/shard_map/ppermute | solution.py:796
  101.6 17.1 %collective-permute-start.25 = (bf16[288,768]{1,0:T(8,128)(2,1)S(1)}, bf16[288,768]{1,0:T(8,128)(2,1)S(1)}, u32[]{:S(2)}, u32[]{:S(2)}) collective-permute-start(bf16[288,768]{1,0:T(8,128)(2,1)S(1)} %shard_map.253), channel_id=1, source_target_pairs={{0,16},{8,24},{16,0},{24,8},{1,17},{9,25},{17,1},{25,9},{2,18},{10... | collective-permute-start | bytes 1327112 | tf_op jit(solution)/shard_map/ppermute | solution.py:796
  110.1 20.1 %collective-permute-start.29 = (bf16[9,24,768]{2,1,0:T(8,128)(2,1)S(1)}, bf16[9,24,768]{2,1,0:T(8,128)(2,1)S(1)}, u32[]{:S(2)}, u32[]{:S(2)}) collective-permute-start(bf16[9,24,768]{2,1,0:T(8,128)(2,1)S(1)} %get-tuple-element.263), channel_id=1, source_target_pairs={{0,4},{1,5},{2,6},{3,7},{4,0},{5,1},{6,2},{7,3},{8,12},{9,13},{10,... | collective-permute-start | bytes 995336 | tf_op jit(solution)/shard_map/ppermute | solution.py:796
  112.8 17.9 %collective-permute-start.31 = (bf16[4,24,256]{2,1,0:T(8,128)(2,1)S(1)}, bf16[4,24,256]{2,1,0:T(8,128)(2,1)S(1)}, u32[]{:S(2)}, u32[]{:S(2)}) collective-permute-start(bf16[4,24,256]{2,1,0:T(8,128)(2,1)S(1)} %get-tuple-element.266), channel_id=1, source_target_pairs={{0,4},{1,5},{2,6},{3,7},{4,0},{5,1},{6,2},{7,3},{8,12},{9,13},{10,... | collective-permute-start | bytes 147464 | tf_op jit(solution)/shard_map/ppermute | solution.py:796
  113.1 17.6 %collective-permute-start.32 = (bf16[4,24,256]{2,1,0:T(8,128)(2,1)S(1)}, bf16[4,24,256]{2,1,0:T(8,128)(2,1)S(1)}, u32[]{:S(2)}, u32[]{:S(2)}) collective-permute-start(bf16[4,24,256]{2,1,0:T(8,128)(2,1)S(1)} %get-tuple-element.267), channel_id=1, source_target_pairs={{0,6},{1,7},{2,4},{3,5},{4,2},{5,3},{6,0},{7,1},{8,14},{9,15},{10,... | collective-permute-start | bytes 147464 | tf_op jit(solution)/shard_map/ppermute | solution.py:796
  116.3 14.4 %collective-permute-start.30 = (bf16[4,24,256]{2,1,0:T(8,128)(2,1)S(1)}, bf16[4,24,256]{2,1,0:T(8,128)(2,1)S(1)}, u32[]{:S(2)}, u32[]{:S(2)}) collective-permute-start(bf16[4,24,256]{2,1,0:T(8,128)(2,1)S(1)} %get-tuple-element.257), channel_id=1, source_target_pairs={{0,2},{1,3},{2,0},{3,1},{4,6},{5,7},{6,4},{7,5},{8,10},{9,11},{10,... | collective-permute-start | bytes 147464 | tf_op jit(solution)/shard_map/ppermute | solution.py:796
  131.6 4.3 %collective-permute-start.36 = (bf16[48,768]{1,0:T(8,128)(2,1)S(1)}, bf16[48,768]{1,0:T(8,128)(2,1)S(1)}, u32[]{:S(2)}, u32[]{:S(2)}) collective-permute-start(bf16[48,768]{1,0:T(8,128)(2,1)S(1)} %get-tuple-element.275), channel_id=1, source_target_pairs={{0,8},{8,0},{16,24},{24,16},{1,9},{9,1},{17,25},{25,17},{2,10},{10... | collective-permute-start | bytes 221192 | tf_op jit(solution)/shard_map/ppermute | solution.py:796
  131.6 4.1 %collective-permute-start.34 = (bf16[24,640]{1,0:T(8,128)(2,1)S(1)}, bf16[24,640]{1,0:T(8,128)(2,1)S(1)}, u32[]{:S(2)}, u32[]{:S(2)}) collective-permute-start(bf16[24,640]{1,0:T(8,128)(2,1)S(1)} %get-tuple-element.270), channel_id=1, source_target_pairs={{0,16},{8,24},{16,0},{24,8},{1,17},{9,25},{17,1},{25,9},{2,18},{10... | collective-permute-start | bytes 92168 | tf_op jit(solution)/shard_map/ppermute | solution.py:796
  132.3 3.6 %collective-permute-start.35 = (bf16[24,640]{1,0:T(8,128)(2,1)S(1)}, bf16[24,640]{1,0:T(8,128)(2,1)S(1)}, u32[]{:S(2)}, u32[]{:S(2)}) collective-permute-start(bf16[24,640]{1,0:T(8,128)(2,1)S(1)} %get-tuple-element.271), channel_id=1, source_target_pairs={{0,24},{8,16},{16,8},{24,0},{1,25},{9,17},{17,9},{25,1},{2,26},{10... | collective-permute-start | bytes 92168 | tf_op jit(solution)/shard_map/ppermute | solution.py:796
  133.5 2.5 %collective-permute-start.33 = (bf16[24,640]{1,0:T(8,128)(2,1)S(1)}, bf16[24,640]{1,0:T(8,128)(2,1)S(1)}, u32[]{:S(2)}, u32[]{:S(2)}) collective-permute-start(bf16[24,640]{1,0:T(8,128)(2,1)S(1)} %get-tuple-element.269), channel_id=1, source_target_pairs={{0,8},{8,0},{16,24},{24,16},{1,9},{9,1},{17,25},{25,17},{2,10},{10... | collective-permute-start | bytes 92168 | tf_op jit(solution)/shard_map/ppermute | solution.py:796

commit v7 on v6

--- a/solution.py
+++ b/solution.py
@@ -259,10 +259,10 @@
 
 def middle_kernel(
     sref, a0, a1, a2, a3, toks, keeps, cp0, cp1, c0, c1, w_out, bias, gain, shift, w_fc1, w_fc2,
-    middle, normed2, gb2, w1, w2, sems,
+    middle, normed2, gb2, w1, w2, w3, w4, sems,
 ):
     s = sref[0]
-    copies = fetch(s ^ 2, w_fc1, w_fc2, w1, w2, sems)
+    copies = fetch(s ^ 2, w_fc1, w_fc2, w1, w2, sems.at[0]) + fetch(s, w_fc1, w_fc2, w3, w4, sems.at[1])
     chip, width = toks.shape
     rows = chip // 2
     cols = a0.shape[1]
@@ -297,13 +297,10 @@
 
 
 def feed_kernel(last, fast, sref, bref, normed2, gb2, fc1, bias, fc2, *refs):
-    copies = []
     if last:
         b2_in, gn_in, y_in, g2, zb_send, zb_keep, y_send, g1_keep, gb, b2_keep, b2_send, gn_keep, gn_send, wide, wide2 = refs
     else:
-        w_fc1, w_fc2, g2a, g2m, zb_send, zb_keep, y_first, y_second, g1_keep, gb, b2, gn = refs[:12]
-        w1, w2, wide, wide2, sems = refs[12:]
-        copies = fetch(sref[0], w_fc1, w_fc2, w1, w2, sems)
+        g2a, g2m, zb_send, zb_keep, y_first, y_second, g1_keep, gb, b2, gn, wide, wide2 = refs
     tokens = normed2.shape[0]
     half = tokens // 2
     block = sref[0] if last else sref[0] ^ 2
@@ -379,8 +376,6 @@
             base = half * (4 * zz2 + 2 * zz1 + yy)
             piece = wide2[pl.ds(pl.multiple_of(base, 8), half), :].astype(BF16)
             (zb_keep if m >= 4 else zb_send)[m % 4] = piece
-    for copy in copies:
-        copy.wait()
 
 
 def split_rows(value, wide, bit, send, keep):
@@ -421,16 +416,14 @@
         outs += [SDS((tokens // 2, width), F32), SDS((tokens // 2, width), BF16)]
         outs += [SDS((tokens, width), F32), SDS((tokens, width), BF16)]
     else:
-        outs += [SDS((tokens, width), F32)] * 2 + [SDS((width, hidden), BF16), SDS((hidden, width), BF16)]
+        outs += [SDS((tokens, width), F32)] * 2
     return call(
         functools.partial(feed_kernel, last, fast),
         outs,
         (sidx, bidx, normed2, gb2, fc1, bias, fc2) + tuple(prev),
-        [pltpu.VMEM((width, hidden), F32), pltpu.VMEM((hidden // 2, width), F32)]
-        + ([] if last else [pltpu.SemaphoreType.DMA((2,))]),
+        [pltpu.VMEM((width, hidden), F32), pltpu.VMEM((hidden // 2, width), F32)],
         flops=12 * tokens * width * hidden,
         scalars=2,
-        far=() if last else (7, 8),
     )
 
 
@@ -775,10 +768,15 @@
         out[:, t * LANES : (t + 1) * LANES] = jnp.where(lane < HEAD, low, high)
     tail = 4 * LANES
     vec = wide_sum(*[every[k, :, tail:] for k in range(4)])
-    vec = jnp.concatenate([vec, jnp.zeros((LANES - per, LANES), F32)], axis=0).T[:, :per]
-    for ref, lines in ((gains, (0, 4)), (shifts, (1, 5)), (biases, (2, 3, 7, 6)), (fc1_bias, (8, 9, 10, 11))):
+    vec = jnp.concatenate([vec, jnp.zeros((LANES - per, LANES), F32)], axis=0).T
+    for ref, lines in ((gains, (0, 4)), (shifts, (1, 5)), (biases, (2, 3, 7, 6))):
         for i, k in enumerate(lines):
-            ref[i : i + 1, :] = vec[HEAD + k : HEAD + k + 1]
+            ref[i : i + 1, :] = vec[HEAD + k : HEAD + k + 1, :per]
+    flat = jnp.zeros((8, LANES), F32)
+    for k in range(4):
+        line = jnp.broadcast_to(vec[HEAD + 8 + k : HEAD + 9 + k], (8, LANES))
+        flat = flat + (pltpu.roll(line, k * per, 1) if k else line)
+    fc1_bias[...] = flat[:1, : 4 * per]
 
 
 def pick(arr, index, axis):
@@ -932,21 +930,21 @@
     a1 = swap_seq(a0, 1)
     a3 = swap_seq(a2, 1)
 
-    middle, normed2, gb2, w1, w2 = call(
+    middle, normed2, gb2, w1, w2, w3, w4 = call(
         middle_kernel,
         [SDS((chip, width), F32), SDS((chip, width), BF16), SDS((chip, width), BF16)]
-        + [SDS((width, hidden), BF16), SDS((hidden, width), BF16)],
+        + [SDS((width, hidden), BF16), SDS((hidden, width), BF16)] * 2,
         (sidx, a0, a1, a2, a3, toks, keeps, own_cot, cot_c, small, got_sc, w_out, biases, norm_gains, norm_shifts)
         + (w_fc1, w_fc2),
-        [pltpu.SemaphoreType.DMA((2,))],
+        [pltpu.SemaphoreType.DMA((2, 2))],
         flops=2 * chip * width * width,
         scalars=1,
         far=(15, 16),
     )
     per = width // (4 * nb)
     fast = nb == 8
-    fc2_a, fc2_m, zo_send, zo_keep, y1, y_rest, keep_oth, fb_oth, b2, gn, w1, w2 = feed(
-        False, fast, per, sidx, bidx, normed2, gb2, w1, fb, w2, (w_fc1, w_fc2)
+    fc2_a, fc2_m, zo_send, zo_keep, y1, y_rest, keep_oth, fb_oth, b2, gn = feed(
+        False, fast, per, sidx, bidx, normed2, gb2, w1, fb, w2
     )
     got2a = swap_seq(fc2_a, 2)
     if not fast:
@@ -955,7 +953,7 @@
     got_zo = swap("batch", zo_send, 2) if fast else zo_send
     ahead = (got2a, got_y1, got_zo)
     fc2_keep, zn_send, zn_keep, y2, keep_own, fb_own, b2_keep, b2_send, gn_keep, gn_send = feed(
-        True, fast, per, sidx, bidx, normed2, gb2, w1, fb, w2, (b2, gn, y_rest)
+        True, fast, per, sidx, bidx, normed2, gb2, w3, fb, w4, (b2, gn, y_rest)
     )
     if not fast:
         y2, keep_own = by_batch_bit(jnp.concatenate([y2, keep_own], axis=0), per)
@@ -1136,7 +1134,7 @@
     )
     swap_got = swap_seq(swap_send, 1)
     gots = [swap_seq(v, k) for k, v in ((1, s1), (2, s2), (3, s3))]
-    lines = [SDS((n, per), F32) for n in (2, 2, 4, 4)]
+    lines = [SDS((2, per), F32), SDS((2, per), F32), SDS((4, per), F32), SDS((1, 4 * per), F32)]
     out_qkv, *smalls, out_fc1 = call(
         collect_kernel,
         [SDS((per, 3 * width), F32), *lines, SDS((per, 4 * hidden), F32)],

time: 138 us -> 136 us (0.986)
  no operation moved by 1% of the time
where the time goes in v7:
time: 136 us
  Pallas kernels  58 us (43%)
  waiting for transfers between devices  39.8 us (29%)
  starting transfers between devices  37.3 us (27%)
    pallas_call x21, Pallas kernels, call(): pl.pallas_call(kernel, out_shape=outs, in_specs=[smem() if i < scalars el...  58 us
    ppermute x37, waiting for transfers between devices, swap(): lax.ppermute(v, kind, [(i, i ^ mask) for i in range(lax.axis_size(kind))])  39.8 us
    ppermute x37, starting transfers between devices, swap(): lax.ppermute(v, kind, [(i, i ^ mask) for i in range(lax.axis_size(kind))])  37.3 us
  transfers between devices with their start and end apart: 37, of which 17 were waited for; matrix products, arithmetic and copies ran while one was open for 0% of the time, Pallas kernels for 30%

profile of v7, /device:TPU:0, one launch (start us, length us, event | category | flops | bytes accessed | tf_op | source)
XLA Modules:
  0.0 136.0 jit_solution(8503010642664347424)
XLA Ops:
  0.6 0.5 collective-permute-start
  1.2 2.6 %collective-permute-start.2 = (bf16[256,768]{1,0:T(8,128)(2,1)}, bf16[256,768]{1,0:T(8,128)(2,1)S(1)}, u32[]{:S(2)}, u32[]{:S(2)}) collective-permute-start(bf16[256,768]{1,0:T(8,128)(2,1)} %bitcast.16), channel_id=1, source_target_pairs={{0,16},{8,24},{16,0},{24,8},{1,17},{9,25},{17,1},{25,9},{2,18},{10... | collective-permute-start | bytes 1179656 | tf_op jit(solution)/shard_map/ppermute | solution.py:794
  3.7 0.8 shard_map.238.s0.c0
  4.5 0.2 collective-permute-start.1
  4.8 0.3 collective-permute-start.3
  5.0 2.2 %shard_map.239 = (bf16[768,640]{1,0:T(8,128)(2,1)S(1)}, f32[1,640]{1,0:T(1,128)S(1)}) custom-call(s32[1]{0:T(128)} %bitcast.sref, bf16[768,2304]{1,0:T(8,128)(2,1)} %w.1, f32[4,768]{1,0:T(4,128)} %bias.3), custom_call_target="tpu_custom_call" | custom-call | bytes 4536836 | tf_op jit(solution)/shard_map/pallas_call | solution.py:78
  7.3 2.0 %shard_map.240 = (bf16[3,576,128]{2,1,0:T(8,128)(2,1)S(1)}, bf16[3,576,128]{2,1,0:T(8,128)(2,1)S(1)}, bf16[3,576,128]{2,1,0:T(8,128)(2,1)S(1)}, bf16[576,768]{1,...) custom-call(s32[1,16]{1,0:T(1,128)S(1)} %copy-done.7, bf16[256,768]{1,0:T(8,128)(2,1)S(1)} %bitcast.17, ...), custom_call_target="tpu_custom_call" | custom-call | flops 509607936 | bytes 5274176 | tf_op jit(solution)/shard_map/pallas_call | solution.py:78
  9.3 5.4 %collective-permute-done.3.s2 = bf16[32,768]{1,0:T(8,128)(2,1)S(1)} collective-permute-done((bf16[32,768]{1,0:T(8,128)(2,1)S(1)}, bf16[32,768]{1,0:T(8,128)(2,1)S(1)}, u32[]{:S(2)}, u32[]{:S(2)}) %collective-permute-start.3) | collective-permute-done | bytes 49184 | tf_op jit(solution)/shard_map/ppermute | solution.py:794
  14.7 0.5 collective-permute-start.5
  15.2 1.3 collective-permute-done.5.s3
  16.5 6.0 %shard_map.241 = (bf16[3,1152,128]{2,1,0:T(8,128)(2,1)S(1)}, bf16[3,1152,128]{2,1,0:T(8,128)(2,1)S(1)}, bf16[3,1152,128]{2,1,0:T(8,128)(2,1)S(1)}, bf16[576,192]...) custom-call(bf16[3,576,128]{2,1,0:T(8,128)(2,1)S(1)} %get-tuple-element.153.q0, ...), custom_call_target="tpu_custom_call" | custom-call | flops 1528823808 | bytes 9624064 | tf_op jit(solution)/shard_map/pallas_call | solution.py:78
  22.5 1.8 %collective-permute-start.7 = (bf16[576,192]{1,0:T(8,128)(2,1)S(1)}, bf16[576,192]{1,0:T(8,128)(2,1)S(1)}, u32[]{:S(2)}, u32[]{:S(2)}) collective-permute-start(bf16[576,192]{1,0:T(8,128)(2,1)S(1)} %get-tuple-element.165), channel_id=1, source_target_pairs={{0,16},{8,24},{16,0},{24,8},{1,17},{9,25},{17,1},{25,9},{2,18},{10... | collective-permute-start | bytes 663560 | tf_op jit(solution)/shard_map/ppermute | solution.py:794
  24.3 5.1 %shard_map.242 = (bf16[576,192]{1,0:T(8,128)(2,1)S(1)}, f32[3,3,8,384]{3,2,1,0:T(8,128)S(1)}) custom-call(bf16[3,1152,128]{2,1,0:T(8,128)(2,1)S(1)} %get-tuple-element.160.qa, bf16[3,1152,128]{2,1,0:T(8,128)(2,1)S(1)} %get-tuple-element.161.ka, bf16[3,1152,128]{2,1,0:T(8,128)(2,1)S(1)} %get-tuple-element.162.va, f32[3,576,128]{2,1,0:T(8,128)S(1)} %get-tuple-element.163.other), custom_call_target="tpu_custom_call" | custom-call | flops 1019215872 | bytes 3870720 | tf_op jit(solution)/shard_map/pallas_call | solution.py:78
  29.4 0.6 collective-permute-start.6
  30.0 1.7 %collective-permute-done.7.a2 = bf16[576,192]{1,0:T(8,128)(2,1)S(1)} collective-permute-done((bf16[576,192]{1,0:T(8,128)(2,1)S(1)}, bf16[576,192]{1,0:T(8,128)(2,1)S(1)}, u32[]{:S(2)}, u32[]{:S(2)}) %collective-permute-start.7) | collective-permute-done | bytes 221216 | tf_op jit(solution)/shard_map/ppermute | solution.py:794
  31.6 1.6 %collective-permute-done.8.a3 = bf16[576,192]{1,0:T(8,128)(2,1)S(1)} collective-permute-done((bf16[576,192]{1,0:T(8,128)(2,1)S(1)}, bf16[576,192]{1,0:T(8,128)(2,1)S(1)}, u32[]{:S(2)}, u32[]{:S(2)}) %collective-permute-start.8) | collective-permute-done | bytes 221216 | tf_op jit(solution)/shard_map/ppermute | solution.py:794
  33.2 3.9 %shard_map.243 = (f32[576,768]{1,0:T(8,128)S(1)}, bf16[576,768]{1,0:T(8,128)(2,1)S(1)}, bf16[576,768]{1,0:T(8,128)(2,1)S(1)}, bf16[768,768]{1,0:T(8,128)(2,1)S(1...) custom-call(s32[1]{0:T(128)} %bitcast.sref, ...), custom_call_target="tpu_custom_call" | custom-call | flops 679477248 | bytes 21848068 | tf_op jit(solution)/shard_map/pallas_call | solution.py:78
  37.1 5.2 %shard_map.244 = (bf16[8,24,768]{2,1,0:T(8,128)(2,1)S(1)}, bf16[8,24,768]{2,1,0:T(8,128)(2,1)S(1)}, bf16[4,48,768]{2,1,0:T(8,128)(2,1)S(1)}, bf16[4,48,768]{2,1,...) custom-call(s32[1]{0:T(128)} %bitcast.sref, ...), custom_call_target="tpu_custom_call" | custom-call | flops 4076863488 | bytes 10042376 | tf_op jit(solution)/shard_map/pallas_call | solution.py:78
  42.3 1.8 %collective-permute-start.11 = (bf16[12,24,768]{2,1,0:T(8,128)(2,1)S(1)}, bf16[12,24,768]{2,1,0:T(8,128)(2,1)S(1)}, u32[]{:S(2)}, u32[]{:S(2)}) collective-permute-start(bf16[12,24,768]{2,1,0:T(8,128)(2,1)S(1)} %get-tuple-element.183), channel_id=1, source_target_pairs={{0,1},{1,0},{2,3},{3,2},{4,5},{5,4},{6,7},{7,6},{8,9},{9,8},{10,11... | collective-permute-start | bytes 1327112 | tf_op jit(solution)/shard_map/ppermute | solution.py:794
  44.1 1.5 %collective-permute-start.10 = (bf16[8,24,768]{2,1,0:T(8,128)(2,1)S(1)}, bf16[8,24,768]{2,1,0:T(8,128)(2,1)S(1)}, u32[]{:S(2)}, u32[]{:S(2)}) collective-permute-start(bf16[8,24,768]{2,1,0:T(8,128)(2,1)S(1)} %get-tuple-element.182), channel_id=1, source_target_pairs={{0,16},{8,24},{16,0},{24,8},{1,17},{9,25},{17,1},{25,9},{2,18},{10... | collective-permute-start | bytes 884744 | tf_op jit(solution)/shard_map/ppermute | solution.py:794
  45.6 1.6 %collective-permute-start.12 = (bf16[4,48,768]{2,1,0:T(8,128)(2,1)S(1)}, bf16[4,48,768]{2,1,0:T(8,128)(2,1)S(1)}, u32[]{:S(2)}, u32[]{:S(2)}) collective-permute-start(bf16[4,48,768]{2,1,0:T(8,128)(2,1)S(1)} %get-tuple-element.184), channel_id=1, source_target_pairs={{0,2},{1,3},{2,0},{3,1},{4,6},{5,7},{6,4},{7,5},{8,10},{9,11},{10,... | collective-permute-start | bytes 884744 | tf_op jit(solution)/shard_map/ppermute | solution.py:794
  47.2 5.2 %shard_map.245 = (bf16[8,48,768]{2,1,0:T(8,128)(2,1)S(1)}, bf16[4,48,768]{2,1,0:T(8,128)(2,1)S(1)}, bf16[4,48,768]{2,1,0:T(8,128)(2,1)S(1)}, bf16[20,24,768]{2,1...) custom-call(s32[1]{0:T(128)} %bitcast.sref, ...), custom_call_target="tpu_custom_call" | custom-call | flops 4076863488 | bytes 14318600 | tf_op jit(solution)/shard_map/pallas_call | solution.py:78
  52.4 0.5 collective-permute-done.10.g2a
  52.9 1.2 collective-permute-done.12.oth_got
  54.1 0.5 collective-permute-done.11.y1
  54.6 0.5 collective-permute-start.14
  55.1 1.7 %collective-permute-start.17 = (bf16[20,24,768]{2,1,0:T(8,128)(2,1)S(1)}, bf16[20,24,768]{2,1,0:T(8,128)(2,1)S(1)}, u32[]{:S(2)}, u32[]{:S(2)}) collective-permute-start(bf16[20,24,768]{2,1,0:T(8,128)(2,1)S(1)} %get-tuple-element.216), channel_id=1, source_target_pairs={{0,1},{1,0},{2,3},{3,2},{4,5},{5,4},{6,7},{7,6},{8,9},{9,8},{10,11... | collective-permute-start | bytes 2211848 | tf_op jit(solution)/shard_map/ppermute | solution.py:794
  56.8 1.6 %collective-permute-start.16 = (bf16[4,48,768]{2,1,0:T(8,128)(2,1)S(1)}, bf16[4,48,768]{2,1,0:T(8,128)(2,1)S(1)}, u32[]{:S(2)}, u32[]{:S(2)}) collective-permute-start(bf16[4,48,768]{2,1,0:T(8,128)(2,1)S(1)} %get-tuple-element.201), channel_id=1, source_target_pairs={{0,2},{1,3},{2,0},{3,1},{4,6},{5,7},{6,4},{7,5},{8,10},{9,11},{10,... | collective-permute-start | bytes 884744 | tf_op jit(solution)/shard_map/ppermute | solution.py:794
  58.4 2.0 %shard_map.246 = (f32[288,768]{1,0:T(8,128)S(1)}, bf16[576,768]{1,0:T(8,128)(2,1)S(1)}, bf16[576,192]{1,0:T(8,128)(2,1)S(1)}, f32[8,768]{1,0:T(8,128)S(1)}) custom-call(s32[1]{0:T(128)} %bitcast.sref, f32[576,768]{1,0:T(8,128)S(1)} %get-tuple-element.177.gn_keep, bf16[576,768]{1,0:T(8,128)(2,1)S(1)} %collective-permute-done.13.gn_got, ...), custom_call_target="tpu_custom_call" | custom-call | flops 169869312 | bytes 9689092 | tf_op jit(solution)/shard_map/pallas_call | solution.py:78
  60.5 1.6 %collective-permute-start.15 = (bf16[576,192]{1,0:T(8,128)(2,1)S(1)}, bf16[576,192]{1,0:T(8,128)(2,1)S(1)}, u32[]{:S(2)}, u32[]{:S(2)}) collective-permute-start(bf16[576,192]{1,0:T(8,128)(2,1)S(1)} %get-tuple-element.199), channel_id=1, source_target_pairs={{0,16},{8,24},{16,0},{24,8},{1,17},{9,25},{17,1},{25,9},{2,18},{10... | collective-permute-start | bytes 663560 | tf_op jit(solution)/shard_map/ppermute | solution.py:794
  62.0 1.6 %shard_map.247 = (bf16[576,192]{1,0:T(8,128)(2,1)S(1)}, bf16[2,4,24,768]{3,2,1,0:T(8,128)(2,1)S(1)}, bf16[2,4,24,768]{3,2,1,0:T(8,128)(2,1)S(1)}, f32[768,128]{1...) custom-call(s32[1]{0:T(128)} %bitcast.sref, s32[1]{0:T(128)} %bitcast.1.bref, ...), custom_call_target="tpu_custom_call" | custom-call | flops 509607936 | bytes 7557128 | tf_op jit(solution)/shard_map/pallas_call | solution.py:78
  63.6 0.5 collective-permute-start.19
  64.2 1.3 collective-permute-done.16.own_got
  65.6 2.7 %collective-permute-start.20 = (bf16[4,48,768]{2,1,0:T(8,128)(2,1)S(1)}, bf16[4,48,768]{2,1,0:T(8,128)(2,1)S(1)}, u32[]{:S(2)}, u32[]{:S(2)}) collective-permute-start(bf16[4,48,768]{2,1,0:T(8,128)(2,1)S(1)} %get-tuple-element.206), channel_id=1, source_target_pairs={{0,4},{1,5},{2,6},{3,7},{4,0},{5,1},{6,2},{7,3},{8,12},{9,13},{10,... | collective-permute-start | bytes 884744 | tf_op jit(solution)/shard_map/ppermute | solution.py:794
  68.2 0.6 collective-permute-done.15.gx
  68.9 1.5 %collective-permute-start.18 = (bf16[8,24,768]{2,1,0:T(8,128)(2,1)S(1)}, bf16[8,24,768]{2,1,0:T(8,128)(2,1)S(1)}, u32[]{:S(2)}, u32[]{:S(2)}) collective-permute-start(bf16[8,24,768]{2,1,0:T(8,128)(2,1)S(1)} %get-tuple-element.217), channel_id=1, source_target_pairs={{0,16},{8,24},{16,0},{24,8},{1,17},{9,25},{17,1},{25,9},{2,18},{10... | collective-permute-start | bytes 884744 | tf_op jit(solution)/shard_map/ppermute | solution.py:794
  70.4 11.3 %shard_map.249 = (bf16[2,1152,192]{2,1,0:T(8,128)(2,1)S(1)}, bf16[8,24,768]{2,1,0:T(8,128)(2,1)S(1)}, bf16[8,24,768]{2,1,0:T(8,128)(2,1)S(1)}, f32[768,128]{1,0:T(8,128)S(1)}) custom-call(s32[1]{0:T(128)} %bitcast.sref, s32[1]{0:T(128)} %bitcast.1.bref, bf16[3,1152,128]{2,1,0:T(8,128)(2,1)S(1)} %get-tuple-element.160.qa, ...), custom_call_target="tpu_custom_call" | custom-call | flops 3397386240 | bytes 8220680 | tf_op jit(solution)/shard_map/pallas_call | solution.py:78
  81.8 0.5 shard_map.250
  82.3 1.1 collective-permute-start.22
  83.4 1.6 %collective-permute-start.23 = (bf16[16,24,768]{2,1,0:T(8,128)(2,1)S(1)}, bf16[16,24,768]{2,1,0:T(8,128)(2,1)S(1)}, u32[]{:S(2)}, u32[]{:S(2)}) collective-permute-start(bf16[16,24,768]{2,1,0:T(8,128)(2,1)S(1)} %get-tuple-element.238), channel_id=1, source_target_pairs={{0,2},{1,3},{2,0},{3,1},{4,6},{5,7},{6,4},{7,5},{8,10},{9,11},{10,... | collective-permute-start | bytes 1769480 | tf_op jit(solution)/shard_map/ppermute | solution.py:794
  84.9 0.5 collective-permute-start.21
  85.5 8.2 %shard_map.251 = (f32[576,768]{1,0:T(8,128)S(1)}, bf16[576,768]{1,0:T(8,128)(2,1)S(1)}, bf16[16,24,256]{2,1,0:T(8,128)(2,1)S(1)}, bf16[16,24,256]{2,1,0:T(8,128)(2,1)S(1)}) custom-call(s32[1]{0:T(128)} %bitcast.sref, s32[1]{0:T(128)} %bitcast.1.bref, bf16[3,1152,128]{2,1,0:T(8,128)(2,1)S(1)} %get-tuple-element.160.qa, ...), custom_call_target="tpu_custom_call" | custom-call | flops 1698693120 | bytes 10285064 | tf_op jit(solution)/shard_map/pallas_call | solution.py:78
  93.7 2.1 %collective-permute-done.22.got_y = bf16[16,24,768]{2,1,0:T(8,128)(2,1)S(1)} collective-permute-done((bf16[16,24,768]{2,1,0:T(8,128)(2,1)S(1)}, bf16[16,24,768]{2,1,0:T(8,128)(2,1)S(1)}, u32[]{:S(2)}, u32[]{:S(2)}) %collective-permute-start.22) | collective-permute-done | bytes 589856 | tf_op jit(solution)/shard_map/ppermute | solution.py:794
  95.8 1.4 %collective-permute-done.23.got_z = bf16[16,24,768]{2,1,0:T(8,128)(2,1)S(1)} collective-permute-done((bf16[16,24,768]{2,1,0:T(8,128)(2,1)S(1)}, bf16[16,24,768]{2,1,0:T(8,128)(2,1)S(1)}, u32[]{:S(2)}, u32[]{:S(2)}) %collective-permute-start.23) | collective-permute-done | bytes 589856 | tf_op jit(solution)/shard_map/ppermute | solution.py:794
  97.2 0.3 shard_map.252
  97.5 1.8 %collective-permute-start.27 = (bf16[10,24,768]{2,1,0:T(8,128)(2,1)S(1)}, bf16[10,24,768]{2,1,0:T(8,128)(2,1)S(1)}, u32[]{:S(2)}, u32[]{:S(2)}) collective-permute-start(bf16[10,24,768]{2,1,0:T(8,128)(2,1)S(1)} %get-tuple-element.254), channel_id=1, source_target_pairs={{0,2},{1,3},{2,0},{3,1},{4,6},{5,7},{6,4},{7,5},{8,10},{9,11},{10,... | collective-permute-start | bytes 1105928 | tf_op jit(solution)/shard_map/ppermute | solution.py:794
  99.3 0.5 collective-permute-start.26
  99.8 0.9 collective-permute-start.28
  100.8 1.1 collective-permute-start.25
  102.0 7.2 %collective-permute-done.26.got_x = bf16[8,24,768]{2,1,0:T(8,128)(2,1)S(1)} collective-permute-done((bf16[8,24,768]{2,1,0:T(8,128)(2,1)S(1)}, bf16[8,24,768]{2,1,0:T(8,128)(2,1)S(1)}, u32[]{:S(2)}, u32[]{:S(2)}) %collective-permute-start.26) | collective-permute-done | bytes 294944 | tf_op jit(solution)/shard_map/ppermute | solution.py:794
  109.3 2.7 %collective-permute-start.29 = (bf16[9,24,768]{2,1,0:T(8,128)(2,1)S(1)}, bf16[9,24,768]{2,1,0:T(8,128)(2,1)S(1)}, u32[]{:S(2)}, u32[]{:S(2)}) collective-permute-start(bf16[9,24,768]{2,1,0:T(8,128)(2,1)S(1)} %get-tuple-element.263), channel_id=1, source_target_pairs={{0,4},{1,5},{2,6},{3,7},{4,0},{5,1},{6,2},{7,3},{8,12},{9,13},{10,... | collective-permute-start | bytes 995336 | tf_op jit(solution)/shard_map/ppermute | solution.py:794
  112.0 0.3 collective-permute-start.31
  112.3 3.2 %collective-permute-start.32 = (bf16[4,24,256]{2,1,0:T(8,128)(2,1)S(1)}, bf16[4,24,256]{2,1,0:T(8,128)(2,1)S(1)}, u32[]{:S(2)}, u32[]{:S(2)}) collective-permute-start(bf16[4,24,256]{2,1,0:T(8,128)(2,1)S(1)} %get-tuple-element.267), channel_id=1, source_target_pairs={{0,6},{1,7},{2,4},{3,5},{4,2},{5,3},{6,0},{7,1},{8,14},{9,15},{10,... | collective-permute-start | bytes 147464 | tf_op jit(solution)/shard_map/ppermute | solution.py:794
  115.5 2.4 %collective-permute-done.25.x0 = bf16[288,768]{1,0:T(8,128)(2,1)S(1)} collective-permute-done((bf16[288,768]{1,0:T(8,128)(2,1)S(1)}, bf16[288,768]{1,0:T(8,128)(2,1)S(1)}, u32[]{:S(2)}, u32[]{:S(2)}) %collective-permute-start.25) | collective-permute-done | bytes 442400 | tf_op jit(solution)/shard_map/ppermute | solution.py:794
  117.9 1.5 %shard_map.255 = (f32[256,768]{1,0:T(8,128)}, f32[4,768]{1,0:T(4,128)}) custom-call(f32[576,768]{1,0:T(8,128)S(1)} %get-tuple-element.250.keep.k0, bf16[576,768]{1,0:T(8,128)(2,1)S(1)} %collective-permute-done.24.got.c0, bf16[288,768]{1,0:T(8,128)(2,1)S(1)} %collective-permute-done.25.x0, bf16[256,768]{1,0:T(8,128)(2,1)S(1)} %bitcast.18, ...), custom_call_target="tpu_custom_call" | custom-call | bytes 5228544 | tf_op jit(solution)/shard_map/pallas_call | solution.py:78
  119.5 10.0 %collective-permute-done.29.got = bf16[9,24,768]{2,1,0:T(8,128)(2,1)S(1)} collective-permute-done((bf16[9,24,768]{2,1,0:T(8,128)(2,1)S(1)}, bf16[9,24,768]{2,1,0:T(8,128)(2,1)S(1)}, u32[]{:S(2)}, u32[]{:S(2)}) %collective-permute-start.29) | collective-permute-done | bytes 331808 | tf_op jit(solution)/shard_map/ppermute | solution.py:794
  129.4 0.5 collective-permute-done.31.z2
  130.0 0.8 shard_map.257
  130.8 0.7 collective-permute-start.34
  131.5 1.2 collective-permute-start.35
  132.7 0.3 collective-permute-start.33
  133.0 2.0 %collective-permute-done.34.g2 = bf16[24,640]{1,0:T(8,128)(2,1)S(1)} collective-permute-done((bf16[24,640]{1,0:T(8,128)(2,1)S(1)}, bf16[24,640]{1,0:T(8,128)(2,1)S(1)}, u32[]{:S(2)}, u32[]{:S(2)}) %collective-permute-start.34) | collective-permute-done | bytes 30752 | tf_op jit(solution)/shard_map/ppermute | solution.py:794
  134.9 0.2 collective-permute-done.35.g3
  135.1 0.9 shard_map.258
  (47 shorter events, 0.6 us)
Async XLA Ops:
  0.6 6.7 %collective-permute-start = (bf16[256,768]{1,0:T(8,128)(2,1)}, bf16[256,768]{1,0:T(8,128)(2,1)S(1)}, u32[]{:S(2)}, u32[]{:S(2)}) collective-permute-start(bf16[256,768]{1,0:T(8,128)(2,1)} %bitcast.15), channel_id=1, source_target_pairs={{0,8},{8,0},{16,24},{24,16},{1,9},{9,1},{17,25},{25,17},{2,10},{10... | collective-permute-start | bytes 1179656 | tf_op jit(solution)/shard_map/ppermute | solution.py:794
  1.2 13.5 %collective-permute-start.2 = (bf16[256,768]{1,0:T(8,128)(2,1)}, bf16[256,768]{1,0:T(8,128)(2,1)S(1)}, u32[]{:S(2)}, u32[]{:S(2)}) collective-permute-start(bf16[256,768]{1,0:T(8,128)(2,1)} %bitcast.16), channel_id=1, source_target_pairs={{0,16},{8,24},{16,0},{24,8},{1,17},{9,25},{17,1},{25,9},{2,18},{10... | collective-permute-start | bytes 1179656 | tf_op jit(solution)/shard_map/ppermute | solution.py:794
  4.5 2.8 %collective-permute-start.1 = (bf16[32,768]{1,0:T(8,128)(2,1)S(1)}, bf16[32,768]{1,0:T(8,128)(2,1)S(1)}, u32[]{:S(2)}, u32[]{:S(2)}) collective-permute-start(bf16[32,768]{1,0:T(8,128)(2,1)S(1)} %shard_map.238.s0.c0), channel_id=1, source_target_pairs={{0,8},{8,0},{16,24},{24,16},{1,9},{9,1},{17,25},{25,17},{2,10},{10... | collective-permute-start | bytes 147464 | tf_op jit(solution)/shard_map/ppermute | solution.py:794
  4.8 9.9 %collective-permute-start.3 = (bf16[32,768]{1,0:T(8,128)(2,1)S(1)}, bf16[32,768]{1,0:T(8,128)(2,1)S(1)}, u32[]{:S(2)}, u32[]{:S(2)}) collective-permute-start(bf16[32,768]{1,0:T(8,128)(2,1)S(1)} %shard_map.238.s0.c0), channel_id=1, source_target_pairs={{0,16},{8,24},{16,0},{24,8},{1,17},{9,25},{17,1},{25,9},{2,18},{10... | collective-permute-start | bytes 147464 | tf_op jit(solution)/shard_map/ppermute | solution.py:794
  5.0 2.3 %copy-start.2 = (bf16[1,256,768]{2,1,0:T(8,128)(2,1)S(1)}, bf16[1,256,768]{2,1,0:T(8,128)(2,1)}, u32[]{:S(2)}) copy-start(bf16[1,256,768]{2,1,0:T(8,128)(2,1)} %param.15) | copy-start | bytes 1179652
  5.0 2.3 %copy-start.4 = (f32[2,768]{1,0:T(2,128)S(1)}, f32[2,768]{1,0:T(2,128)}, u32[]{:S(2)}) copy-start(f32[2,768]{1,0:T(2,128)} %gain.9) | copy-start | bytes 18436
  5.0 2.3 %copy-start.5 = (f32[2,768]{1,0:T(2,128)S(1)}, f32[2,768]{1,0:T(2,128)}, u32[]{:S(2)}) copy-start(f32[2,768]{1,0:T(2,128)} %shift1.1) | copy-start | bytes 18436
  5.0 2.3 %copy-start.7 = (s32[1,16]{1,0:T(1,128)S(1)}, s32[1,16]{1,0:T(1,128)}, u32[]{:S(2)}) copy-start(s32[1,16]{1,0:T(1,128)} %flags.1) | copy-start | bytes 196
  14.7 1.8 %collective-permute-start.4 = (bf16[256,768]{1,0:T(8,128)(2,1)S(1)}, bf16[256,768]{1,0:T(8,128)(2,1)S(1)}, u32[]{:S(2)}, u32[]{:S(2)}) collective-permute-start(bf16[256,768]{1,0:T(8,128)(2,1)S(1)} %collective-permute-done.2.p2), channel_id=1, source_target_pairs={{0,8},{8,0},{16,24},{24,16},{1,9},{9,1},{17,25},{25,17},{2,10},{10... | collective-permute-start | bytes 1179656 | tf_op jit(solution)/shard_map/ppermute | solution.py:794
  14.7 1.8 %collective-permute-start.5 = (bf16[32,768]{1,0:T(8,128)(2,1)S(1)}, bf16[32,768]{1,0:T(8,128)(2,1)S(1)}, u32[]{:S(2)}, u32[]{:S(2)}) collective-permute-start(bf16[32,768]{1,0:T(8,128)(2,1)S(1)} %collective-permute-done.3.s2), channel_id=1, source_target_pairs={{0,8},{8,0},{16,24},{24,16},{1,9},{9,1},{17,25},{25,17},{2,10},{10... | collective-permute-start | bytes 147464 | tf_op jit(solution)/shard_map/ppermute | solution.py:794
  16.5 7.8 %copy-start.1 = (bf16[1,256,768]{2,1,0:T(8,128)(2,1)S(1)}, bf16[1,256,768]{2,1,0:T(8,128)(2,1)}, u32[]{:S(2)}) copy-start(bf16[1,256,768]{2,1,0:T(8,128)(2,1)} %param.28) | copy-start | bytes 1179652
  22.5 9.1 %collective-permute-start.7 = (bf16[576,192]{1,0:T(8,128)(2,1)S(1)}, bf16[576,192]{1,0:T(8,128)(2,1)S(1)}, u32[]{:S(2)}, u32[]{:S(2)}) collective-permute-start(bf16[576,192]{1,0:T(8,128)(2,1)S(1)} %get-tuple-element.165), channel_id=1, source_target_pairs={{0,16},{8,24},{16,0},{24,8},{1,17},{9,25},{17,1},{25,9},{2,18},{10... | collective-permute-start | bytes 663560 | tf_op jit(solution)/shard_map/ppermute | solution.py:794
  24.3 7.3 %collective-permute-start.9 = (bf16[256,768]{1,0:T(8,128)(2,1)S(1)}, bf16[256,768]{1,0:T(8,128)(2,1)S(1)}, u32[]{:S(2)}, u32[]{:S(2)}) collective-permute-start(bf16[256,768]{1,0:T(8,128)(2,1)S(1)} %bitcast.12), channel_id=1, source_target_pairs={{0,8},{8,0},{16,24},{24,16},{1,9},{9,1},{17,25},{25,17},{2,10},{10... | collective-permute-start | bytes 1179656 | tf_op jit(solution)/shard_map/ppermute | solution.py:794
  24.3 8.9 %copy-start = (bf16[768,768]{1,0:T(8,128)(2,1)S(1)}, bf16[768,768]{1,0:T(8,128)(2,1)}, u32[]{:S(2)}) copy-start(bf16[768,768]{1,0:T(8,128)(2,1)} %w_out.5) | copy-start | bytes 3538948
  24.3 8.9 %copy-start.3 = (f32[4,768]{1,0:T(4,128)S(1)}, f32[4,768]{1,0:T(4,128)}, u32[]{:S(2)}) copy-start(f32[4,768]{1,0:T(4,128)} %bias.3) | copy-start | bytes 36868
  29.4 2.2 %collective-permute-start.6 = (bf16[576,192]{1,0:T(8,128)(2,1)S(1)}, bf16[576,192]{1,0:T(8,128)(2,1)S(1)}, u32[]{:S(2)}, u32[]{:S(2)}) collective-permute-start(bf16[576,192]{1,0:T(8,128)(2,1)S(1)} %get-tuple-element.164.a0), channel_id=1, source_target_pairs={{0,8},{8,0},{16,24},{24,16},{1,9},{9,1},{17,25},{25,17},{2,10},{10... | collective-permute-start | bytes 663560 | tf_op jit(solution)/shard_map/ppermute | solution.py:794
  31.6 1.6 %collective-permute-start.8 = (bf16[576,192]{1,0:T(8,128)(2,1)S(1)}, bf16[576,192]{1,0:T(8,128)(2,1)S(1)}, u32[]{:S(2)}, u32[]{:S(2)}) collective-permute-start(bf16[576,192]{1,0:T(8,128)(2,1)S(1)} %collective-permute-done.7.a2), channel_id=1, source_target_pairs={{0,8},{8,0},{16,24},{24,16},{1,9},{9,1},{17,25},{25,17},{2,10},{10... | collective-permute-start | bytes 663560 | tf_op jit(solution)/shard_map/ppermute | solution.py:794
  33.2 3.9 %copy-start.6 = (f32[3072]{0:T(1024)S(1)}, f32[3072]{0:T(1024)}, u32[]{:S(2)}) copy-start(f32[3072]{0:T(1024)} %param.26) | copy-start | bytes 36868
  42.3 12.3 %collective-permute-start.11 = (bf16[12,24,768]{2,1,0:T(8,128)(2,1)S(1)}, bf16[12,24,768]{2,1,0:T(8,128)(2,1)S(1)}, u32[]{:S(2)}, u32[]{:S(2)}) collective-permute-start(bf16[12,24,768]{2,1,0:T(8,128)(2,1)S(1)} %get-tuple-element.183), channel_id=1, source_target_pairs={{0,1},{1,0},{2,3},{3,2},{4,5},{5,4},{6,7},{7,6},{8,9},{9,8},{10,11... | collective-permute-start | bytes 1327112 | tf_op jit(solution)/shard_map/ppermute | solution.py:794
  44.1 8.8 %collective-permute-start.10 = (bf16[8,24,768]{2,1,0:T(8,128)(2,1)S(1)}, bf16[8,24,768]{2,1,0:T(8,128)(2,1)S(1)}, u32[]{:S(2)}, u32[]{:S(2)}) collective-permute-start(bf16[8,24,768]{2,1,0:T(8,128)(2,1)S(1)} %get-tuple-element.182), channel_id=1, source_target_pairs={{0,16},{8,24},{16,0},{24,8},{1,17},{9,25},{17,1},{25,9},{2,18},{10... | collective-permute-start | bytes 884744 | tf_op jit(solution)/shard_map/ppermute | solution.py:794
  45.6 8.5 %collective-permute-start.12 = (bf16[4,48,768]{2,1,0:T(8,128)(2,1)S(1)}, bf16[4,48,768]{2,1,0:T(8,128)(2,1)S(1)}, u32[]{:S(2)}, u32[]{:S(2)}) collective-permute-start(bf16[4,48,768]{2,1,0:T(8,128)(2,1)S(1)} %get-tuple-element.184), channel_id=1, source_target_pairs={{0,2},{1,3},{2,0},{3,1},{4,6},{5,7},{6,4},{7,5},{8,10},{9,11},{10,... | collective-permute-start | bytes 884744 | tf_op jit(solution)/shard_map/ppermute | solution.py:794
  54.6 3.8 %collective-permute-start.13 = (bf16[576,768]{1,0:T(8,128)(2,1)S(1)}, bf16[576,768]{1,0:T(8,128)(2,1)S(1)}, u32[]{:S(2)}, u32[]{:S(2)}) collective-permute-start(bf16[576,768]{1,0:T(8,128)(2,1)S(1)} %get-tuple-element.185), channel_id=1, source_target_pairs={{0,8},{8,0},{16,24},{24,16},{1,9},{9,1},{17,25},{25,17},{2,10},{10... | collective-permute-start | bytes 2654216 | tf_op jit(solution)/shard_map/ppermute | solution.py:794
  54.6 7.4 %collective-permute-start.14 = (bf16[288,768]{1,0:T(8,128)(2,1)S(1)}, bf16[288,768]{1,0:T(8,128)(2,1)S(1)}, u32[]{:S(2)}, u32[]{:S(2)}) collective-permute-start(bf16[288,768]{1,0:T(8,128)(2,1)S(1)} %get-tuple-element.189), channel_id=1, source_target_pairs={{0,8},{8,0},{16,24},{24,16},{1,9},{9,1},{17,25},{25,17},{2,10},{10... | collective-permute-start | bytes 1327112 | tf_op jit(solution)/shard_map/ppermute | solution.py:794
  55.1 26.6 %collective-permute-start.17 = (bf16[20,24,768]{2,1,0:T(8,128)(2,1)S(1)}, bf16[20,24,768]{2,1,0:T(8,128)(2,1)S(1)}, u32[]{:S(2)}, u32[]{:S(2)}) collective-permute-start(bf16[20,24,768]{2,1,0:T(8,128)(2,1)S(1)} %get-tuple-element.216), channel_id=1, source_target_pairs={{0,1},{1,0},{2,3},{3,2},{4,5},{5,4},{6,7},{7,6},{8,9},{9,8},{10,11... | collective-permute-start | bytes 2211848 | tf_op jit(solution)/shard_map/ppermute | solution.py:794
  56.8 8.6 %collective-permute-start.16 = (bf16[4,48,768]{2,1,0:T(8,128)(2,1)S(1)}, bf16[4,48,768]{2,1,0:T(8,128)(2,1)S(1)}, u32[]{:S(2)}, u32[]{:S(2)}) collective-permute-start(bf16[4,48,768]{2,1,0:T(8,128)(2,1)S(1)} %get-tuple-element.201), channel_id=1, source_target_pairs={{0,2},{1,3},{2,0},{3,1},{4,6},{5,7},{6,4},{7,5},{8,10},{9,11},{10,... | collective-permute-start | bytes 884744 | tf_op jit(solution)/shard_map/ppermute | solution.py:794
  60.5 8.4 %collective-permute-start.15 = (bf16[576,192]{1,0:T(8,128)(2,1)S(1)}, bf16[576,192]{1,0:T(8,128)(2,1)S(1)}, u32[]{:S(2)}, u32[]{:S(2)}) collective-permute-start(bf16[576,192]{1,0:T(8,128)(2,1)S(1)} %get-tuple-element.199), channel_id=1, source_target_pairs={{0,16},{8,24},{16,0},{24,8},{1,17},{9,25},{17,1},{25,9},{2,18},{10... | collective-permute-start | bytes 663560 | tf_op jit(solution)/shard_map/ppermute | solution.py:794
  63.6 18.1 %collective-permute-start.19 = (bf16[2,4,24,768]{3,2,1,0:T(8,128)(2,1)S(1)}, bf16[2,4,24,768]{3,2,1,0:T(8,128)(2,1)S(1)}, u32[]{:S(2)}, u32[]{:S(2)}) collective-permute-start(bf16[2,4,24,768]{3,2,1,0:T(8,128)(2,1)S(1)} %get-tuple-element.202), channel_id=1, source_target_pairs={{0,1},{1,0},{2,3},{3,2},{4,5},{5,4},{6,7},{7,6},{8,9},{9,8},{10,11... | collective-permute-start | bytes 884744 | tf_op jit(solution)/shard_map/ppermute | solution.py:794
  65.6 16.1 %collective-permute-start.20 = (bf16[4,48,768]{2,1,0:T(8,128)(2,1)S(1)}, bf16[4,48,768]{2,1,0:T(8,128)(2,1)S(1)}, u32[]{:S(2)}, u32[]{:S(2)}) collective-permute-start(bf16[4,48,768]{2,1,0:T(8,128)(2,1)S(1)} %get-tuple-element.206), channel_id=1, source_target_pairs={{0,4},{1,5},{2,6},{3,7},{4,0},{5,1},{6,2},{7,3},{8,12},{9,13},{10,... | collective-permute-start | bytes 884744 | tf_op jit(solution)/shard_map/ppermute | solution.py:794
  68.9 12.9 %collective-permute-start.18 = (bf16[8,24,768]{2,1,0:T(8,128)(2,1)S(1)}, bf16[8,24,768]{2,1,0:T(8,128)(2,1)S(1)}, u32[]{:S(2)}, u32[]{:S(2)}) collective-permute-start(bf16[8,24,768]{2,1,0:T(8,128)(2,1)S(1)} %get-tuple-element.217), channel_id=1, source_target_pairs={{0,16},{8,24},{16,0},{24,8},{1,17},{9,25},{17,1},{25,9},{2,18},{10... | collective-permute-start | bytes 884744 | tf_op jit(solution)/shard_map/ppermute | solution.py:794
  82.3 13.5 %collective-permute-start.22 = (bf16[16,24,768]{2,1,0:T(8,128)(2,1)S(1)}, bf16[16,24,768]{2,1,0:T(8,128)(2,1)S(1)}, u32[]{:S(2)}, u32[]{:S(2)}) collective-permute-start(bf16[16,24,768]{2,1,0:T(8,128)(2,1)S(1)} %get-tuple-element.237), channel_id=1, source_target_pairs={{0,1},{1,0},{2,3},{3,2},{4,5},{5,4},{6,7},{7,6},{8,9},{9,8},{10,11... | collective-permute-start | bytes 1769480 | tf_op jit(solution)/shard_map/ppermute | solution.py:794
  83.4 13.8 %collective-permute-start.23 = (bf16[16,24,768]{2,1,0:T(8,128)(2,1)S(1)}, bf16[16,24,768]{2,1,0:T(8,128)(2,1)S(1)}, u32[]{:S(2)}, u32[]{:S(2)}) collective-permute-start(bf16[16,24,768]{2,1,0:T(8,128)(2,1)S(1)} %get-tuple-element.238), channel_id=1, source_target_pairs={{0,2},{1,3},{2,0},{3,1},{4,6},{5,7},{6,4},{7,5},{8,10},{9,11},{10,... | collective-permute-start | bytes 1769480 | tf_op jit(solution)/shard_map/ppermute | solution.py:794
  84.9 8.7 %collective-permute-start.21 = (bf16[8,24,768]{2,1,0:T(8,128)(2,1)S(1)}, bf16[8,24,768]{2,1,0:T(8,128)(2,1)S(1)}, u32[]{:S(2)}, u32[]{:S(2)}) collective-permute-start(bf16[8,24,768]{2,1,0:T(8,128)(2,1)S(1)} %get-tuple-element.236), channel_id=1, source_target_pairs={{0,16},{8,24},{16,0},{24,8},{1,17},{9,25},{17,1},{25,9},{2,18},{10... | collective-permute-start | bytes 884744 | tf_op jit(solution)/shard_map/ppermute | solution.py:794
  97.2 3.6 %collective-permute-start.24 = (bf16[576,768]{1,0:T(8,128)(2,1)S(1)}, bf16[576,768]{1,0:T(8,128)(2,1)S(1)}, u32[]{:S(2)}, u32[]{:S(2)}) collective-permute-start(bf16[576,768]{1,0:T(8,128)(2,1)S(1)} %get-tuple-element.239), channel_id=1, source_target_pairs={{0,8},{8,0},{16,24},{24,16},{1,9},{9,1},{17,25},{25,17},{2,10},{10... | collective-permute-start | bytes 2654216 | tf_op jit(solution)/shard_map/ppermute | solution.py:794
  97.5 11.7 %collective-permute-start.27 = (bf16[10,24,768]{2,1,0:T(8,128)(2,1)S(1)}, bf16[10,24,768]{2,1,0:T(8,128)(2,1)S(1)}, u32[]{:S(2)}, u32[]{:S(2)}) collective-permute-start(bf16[10,24,768]{2,1,0:T(8,128)(2,1)S(1)} %get-tuple-element.254), channel_id=1, source_target_pairs={{0,2},{1,3},{2,0},{3,1},{4,6},{5,7},{6,4},{7,5},{8,10},{9,11},{10,... | collective-permute-start | bytes 1105928 | tf_op jit(solution)/shard_map/ppermute | solution.py:794
  99.3 9.8 %collective-permute-start.26 = (bf16[8,24,768]{2,1,0:T(8,128)(2,1)S(1)}, bf16[8,24,768]{2,1,0:T(8,128)(2,1)S(1)}, u32[]{:S(2)}, u32[]{:S(2)}) collective-permute-start(bf16[8,24,768]{2,1,0:T(8,128)(2,1)S(1)} %get-tuple-element.249), channel_id=1, source_target_pairs={{0,16},{8,24},{16,0},{24,8},{1,17},{9,25},{17,1},{25,9},{2,18},{10... | collective-permute-start | bytes 884744 | tf_op jit(solution)/shard_map/ppermute | solution.py:794
  99.8 9.3 %collective-permute-start.28 = (bf16[22,24,256]{2,1,0:T(8,128)(2,1)S(1)}, bf16[22,24,256]{2,1,0:T(8,128)(2,1)S(1)}, u32[]{:S(2)}, u32[]{:S(2)}) collective-permute-start(bf16[22,24,256]{2,1,0:T(8,128)(2,1)S(1)} %get-tuple-element.256), channel_id=1, source_target_pairs={{0,1},{1,0},{2,3},{3,2},{4,5},{5,4},{6,7},{7,6},{8,9},{9,8},{10,11... | collective-permute-start | bytes 811016 | tf_op jit(solution)/shard_map/ppermute | solution.py:794
  100.8 17.1 %collective-permute-start.25 = (bf16[288,768]{1,0:T(8,128)(2,1)S(1)}, bf16[288,768]{1,0:T(8,128)(2,1)S(1)}, u32[]{:S(2)}, u32[]{:S(2)}) collective-permute-start(bf16[288,768]{1,0:T(8,128)(2,1)S(1)} %shard_map.253), channel_id=1, source_target_pairs={{0,16},{8,24},{16,0},{24,8},{1,17},{9,25},{17,1},{25,9},{2,18},{10... | collective-permute-start | bytes 1327112 | tf_op jit(solution)/shard_map/ppermute | solution.py:794
  109.3 20.1 %collective-permute-start.29 = (bf16[9,24,768]{2,1,0:T(8,128)(2,1)S(1)}, bf16[9,24,768]{2,1,0:T(8,128)(2,1)S(1)}, u32[]{:S(2)}, u32[]{:S(2)}) collective-permute-start(bf16[9,24,768]{2,1,0:T(8,128)(2,1)S(1)} %get-tuple-element.263), channel_id=1, source_target_pairs={{0,4},{1,5},{2,6},{3,7},{4,0},{5,1},{6,2},{7,3},{8,12},{9,13},{10,... | collective-permute-start | bytes 995336 | tf_op jit(solution)/shard_map/ppermute | solution.py:794
  112.0 17.9 %collective-permute-start.31 = (bf16[4,24,256]{2,1,0:T(8,128)(2,1)S(1)}, bf16[4,24,256]{2,1,0:T(8,128)(2,1)S(1)}, u32[]{:S(2)}, u32[]{:S(2)}) collective-permute-start(bf16[4,24,256]{2,1,0:T(8,128)(2,1)S(1)} %get-tuple-element.266), channel_id=1, source_target_pairs={{0,4},{1,5},{2,6},{3,7},{4,0},{5,1},{6,2},{7,3},{8,12},{9,13},{10,... | collective-permute-start | bytes 147464 | tf_op jit(solution)/shard_map/ppermute | solution.py:794
  112.3 17.6 %collective-permute-start.32 = (bf16[4,24,256]{2,1,0:T(8,128)(2,1)S(1)}, bf16[4,24,256]{2,1,0:T(8,128)(2,1)S(1)}, u32[]{:S(2)}, u32[]{:S(2)}) collective-permute-start(bf16[4,24,256]{2,1,0:T(8,128)(2,1)S(1)} %get-tuple-element.267), channel_id=1, source_target_pairs={{0,6},{1,7},{2,4},{3,5},{4,2},{5,3},{6,0},{7,1},{8,14},{9,15},{10,... | collective-permute-start | bytes 147464 | tf_op jit(solution)/shard_map/ppermute | solution.py:794
  115.5 14.4 %collective-permute-start.30 = (bf16[4,24,256]{2,1,0:T(8,128)(2,1)S(1)}, bf16[4,24,256]{2,1,0:T(8,128)(2,1)S(1)}, u32[]{:S(2)}, u32[]{:S(2)}) collective-permute-start(bf16[4,24,256]{2,1,0:T(8,128)(2,1)S(1)} %get-tuple-element.257), channel_id=1, source_target_pairs={{0,2},{1,3},{2,0},{3,1},{4,6},{5,7},{6,4},{7,5},{8,10},{9,11},{10,... | collective-permute-start | bytes 147464 | tf_op jit(solution)/shard_map/ppermute | solution.py:794
  130.8 4.3 %collective-permute-start.36 = (bf16[48,768]{1,0:T(8,128)(2,1)S(1)}, bf16[48,768]{1,0:T(8,128)(2,1)S(1)}, u32[]{:S(2)}, u32[]{:S(2)}) collective-permute-start(bf16[48,768]{1,0:T(8,128)(2,1)S(1)} %get-tuple-element.275), channel_id=1, source_target_pairs={{0,8},{8,0},{16,24},{24,16},{1,9},{9,1},{17,25},{25,17},{2,10},{10... | collective-permute-start | bytes 221192 | tf_op jit(solution)/shard_map/ppermute | solution.py:794
  130.8 4.1 %collective-permute-start.34 = (bf16[24,640]{1,0:T(8,128)(2,1)S(1)}, bf16[24,640]{1,0:T(8,128)(2,1)S(1)}, u32[]{:S(2)}, u32[]{:S(2)}) collective-permute-start(bf16[24,640]{1,0:T(8,128)(2,1)S(1)} %get-tuple-element.270), channel_id=1, source_target_pairs={{0,16},{8,24},{16,0},{24,8},{1,17},{9,25},{17,1},{25,9},{2,18},{10... | collective-permute-start | bytes 92168 | tf_op jit(solution)/shard_map/ppermute | solution.py:794
  131.5 3.6 %collective-permute-start.35 = (bf16[24,640]{1,0:T(8,128)(2,1)S(1)}, bf16[24,640]{1,0:T(8,128)(2,1)S(1)}, u32[]{:S(2)}, u32[]{:S(2)}) collective-permute-start(bf16[24,640]{1,0:T(8,128)(2,1)S(1)} %get-tuple-element.271), channel_id=1, source_target_pairs={{0,24},{8,16},{16,8},{24,0},{1,25},{9,17},{17,9},{25,1},{2,26},{10... | collective-permute-start | bytes 92168 | tf_op jit(solution)/shard_map/ppermute | solution.py:794
  132.7 2.5 %collective-permute-start.33 = (bf16[24,640]{1,0:T(8,128)(2,1)S(1)}, bf16[24,640]{1,0:T(8,128)(2,1)S(1)}, u32[]{:S(2)}, u32[]{:S(2)}) collective-permute-start(bf16[24,640]{1,0:T(8,128)(2,1)S(1)} %get-tuple-element.269), channel_id=1, source_target_pairs={{0,8},{8,0},{16,24},{24,16},{1,9},{9,1},{17,25},{25,17},{2,10},{10... | collective-permute-start | bytes 92168 | tf_op jit(solution)/shard_map/ppermute | solution.py:794

commit v8 on v7

--- a/solution.py
+++ b/solution.py
@@ -234,7 +234,11 @@
     out[:, LANES:] = oacc[2, :, :HEAD].astype(BF16)
 
 
-def attend_second_kernel(qa, ka, va, other, keep, lse, oacc):
+def attend_second_kernel(
+    sref, qa, ka, va, other, w_fc1, w_fc2, keep, lse, w1, w2, w3, w4, oacc, sems
+):
+    s = sref[0]
+    copies = fetch(s ^ 2, w_fc1, w_fc2, w1, w2, sems.at[0]) + fetch(s, w_fc1, w_fc2, w3, w4, sems.at[1])
     half = oacc.shape[1]
     rows = half // 2
 
@@ -255,14 +259,15 @@
         ]
         for b in range(3):
             lse[h, b] = jnp.broadcast_to(parts[b].T[HEAD + 1 : HEAD + 2], (8, step))
+    for copy in copies:
+        copy.wait()
 
 
 def middle_kernel(
-    sref, a0, a1, a2, a3, toks, keeps, cp0, cp1, c0, c1, w_out, bias, gain, shift, w_fc1, w_fc2,
-    middle, normed2, gb2, w1, w2, w3, w4, sems,
+    sref, a0, a1, a2, a3, toks, keeps, cp0, cp1, c0, c1, w_out, bias, gain, shift,
+    middle, normed2, gb2,
 ):
     s = sref[0]
-    copies = fetch(s ^ 2, w_fc1, w_fc2, w1, w2, sems.at[0]) + fetch(s, w_fc1, w_fc2, w3, w4, sems.at[1])
     chip, width = toks.shape
     rows = chip // 2
     cols = a0.shape[1]
@@ -280,8 +285,6 @@
     normed2[...] = (hat * gain[1:2, :] + shift[1:2, :]).astype(BF16)
     gout = jnp.concatenate([cots_of(cp0, c0), cots_of(cp1, c1)], axis=0)
     gb2[...] = (keeps[:, 1:2] * gout).astype(BF16)
-    for copy in copies:
-        copy.wait()
 
 
 def fetch(block, w_fc1, w_fc2, w1, w2, sems):
@@ -920,26 +923,25 @@
         flops=2 * chip * width * 3 * cols + 2 * OWN * whole * whole * LANES,
     )
     a2 = swap_seq(att_send, 2)
-    a0, lse = call(
+    a0, lse, w1, w2, w3, w4 = call(
         attend_second_kernel,
-        [SDS((chip, cols), BF16), SDS((OWN, 3, 8, whole // 3), F32)],
-        (qa, ka, va, other),
-        [pltpu.VMEM((OWN, chip, LANES), F32)],
+        [SDS((chip, cols), BF16), SDS((OWN, 3, 8, whole // 3), F32)]
+        + [SDS((width, hidden), BF16), SDS((hidden, width), BF16)] * 2,
+        (sidx, qa, ka, va, other, w_fc1, w_fc2),
+        [pltpu.VMEM((OWN, chip, LANES), F32), pltpu.SemaphoreType.DMA((2, 2))],
         flops=2 * OWN * whole * whole * LANES,
+        scalars=1,
+        far=(5, 6),
     )
     a1 = swap_seq(a0, 1)
     a3 = swap_seq(a2, 1)
 
-    middle, normed2, gb2, w1, w2, w3, w4 = call(
+    middle, normed2, gb2 = call(
         middle_kernel,
-        [SDS((chip, width), F32), SDS((chip, width), BF16), SDS((chip, width), BF16)]
-        + [SDS((width, hidden), BF16), SDS((hidden, width), BF16)] * 2,
-        (sidx, a0, a1, a2, a3, toks, keeps, own_cot, cot_c, small, got_sc, w_out, biases, norm_gains, norm_shifts)
-        + (w_fc1, w_fc2),
-        [pltpu.SemaphoreType.DMA((2, 2))],
+        [SDS((chip, width), F32), SDS((chip, width), BF16), SDS((chip, width), BF16)],
+        (sidx, a0, a1, a2, a3, toks, keeps, own_cot, cot_c, small, got_sc, w_out, biases, norm_gains, norm_shifts),
         flops=2 * chip * width * width,
         scalars=1,
-        far=(15, 16),
     )
     per = width // (4 * nb)
     fast = nb == 8

time: 136 us -> 134 us (0.985)
  Pallas kernels: 58 us -> 56 us
    pallas_call x21, Pallas kernels: 58 us -> 56 us  [call(): pl.pallas_call(kernel, out_shape=outs, in_specs=[smem() if i < scalars el...]
where the time goes in v8:
time: 134 us
  Pallas kernels  56 us (42%)
  waiting for transfers between devices  39.7 us (30%)
  starting transfers between devices  37.3 us (28%)
    pallas_call x21, Pallas kernels, call(): pl.pallas_call(kernel, out_shape=outs, in_specs=[smem() if i < scalars el...  56 us
    ppermute x37, waiting for transfers between devices, swap(): lax.ppermute(v, kind, [(i, i ^ mask) for i in range(lax.axis_size(kind))])  39.7 us
    ppermute x37, starting transfers between devices, swap(): lax.ppermute(v, kind, [(i, i ^ mask) for i in range(lax.axis_size(kind))])  37.3 us
  transfers between devices with their start and end apart: 37, of which 17 were waited for; matrix products, arithmetic and copies ran while one was open for 0% of the time, Pallas kernels for 30%

profile of v8, /device:TPU:0, one launch (start us, length us, event | category | flops | bytes accessed | tf_op | source)
XLA Modules:
  0.0 134.0 jit_solution(197307853820146695)
XLA Ops:
  0.6 0.5 collective-permute-start
  1.2 2.6 %collective-permute-start.2 = (bf16[256,768]{1,0:T(8,128)(2,1)}, bf16[256,768]{1,0:T(8,128)(2,1)S(1)}, u32[]{:S(2)}, u32[]{:S(2)}) collective-permute-start(bf16[256,768]{1,0:T(8,128)(2,1)} %bitcast.16), channel_id=1, source_target_pairs={{0,16},{8,24},{16,0},{24,8},{1,17},{9,25},{17,1},{25,9},{2,18},{10... | collective-permute-start | bytes 1179656 | tf_op jit(solution)/shard_map/ppermute | solution.py:797
  3.7 0.8 shard_map.238.s0.c0
  4.5 0.2 collective-permute-start.1
  4.8 0.3 collective-permute-start.3
  5.0 2.2 %shard_map.239 = (bf16[768,640]{1,0:T(8,128)(2,1)S(1)}, f32[1,640]{1,0:T(1,128)S(1)}) custom-call(s32[1]{0:T(128)} %bitcast.sref, bf16[768,2304]{1,0:T(8,128)(2,1)} %w.1, f32[4,768]{1,0:T(4,128)} %bias.3), custom_call_target="tpu_custom_call" | custom-call | bytes 4536836 | tf_op jit(solution)/shard_map/pallas_call | solution.py:78
  7.3 2.0 %shard_map.240 = (bf16[3,576,128]{2,1,0:T(8,128)(2,1)S(1)}, bf16[3,576,128]{2,1,0:T(8,128)(2,1)S(1)}, bf16[3,576,128]{2,1,0:T(8,128)(2,1)S(1)}, bf16[576,768]{1,...) custom-call(s32[1,16]{1,0:T(1,128)S(1)} %copy-done.7, bf16[256,768]{1,0:T(8,128)(2,1)S(1)} %bitcast.17, ...), custom_call_target="tpu_custom_call" | custom-call | flops 509607936 | bytes 5274176 | tf_op jit(solution)/shard_map/pallas_call | solution.py:78
  9.3 5.4 %collective-permute-done.3.s2 = bf16[32,768]{1,0:T(8,128)(2,1)S(1)} collective-permute-done((bf16[32,768]{1,0:T(8,128)(2,1)S(1)}, bf16[32,768]{1,0:T(8,128)(2,1)S(1)}, u32[]{:S(2)}, u32[]{:S(2)}) %collective-permute-start.3) | collective-permute-done | bytes 49184 | tf_op jit(solution)/shard_map/ppermute | solution.py:797
  14.7 0.5 collective-permute-start.5
  15.2 1.3 collective-permute-done.5.s3
  16.5 6.0 %shard_map.241 = (bf16[3,1152,128]{2,1,0:T(8,128)(2,1)S(1)}, bf16[3,1152,128]{2,1,0:T(8,128)(2,1)S(1)}, bf16[3,1152,128]{2,1,0:T(8,128)(2,1)S(1)}, bf16[576,192]...) custom-call(bf16[3,576,128]{2,1,0:T(8,128)(2,1)S(1)} %get-tuple-element.153.q0, ...), custom_call_target="tpu_custom_call" | custom-call | flops 1528823808 | bytes 9624064 | tf_op jit(solution)/shard_map/pallas_call | solution.py:78
  22.5 1.8 %collective-permute-start.7 = (bf16[576,192]{1,0:T(8,128)(2,1)S(1)}, bf16[576,192]{1,0:T(8,128)(2,1)S(1)}, u32[]{:S(2)}, u32[]{:S(2)}) collective-permute-start(bf16[576,192]{1,0:T(8,128)(2,1)S(1)} %get-tuple-element.165), channel_id=1, source_target_pairs={{0,16},{8,24},{16,0},{24,8},{1,17},{9,25},{17,1},{25,9},{2,18},{10... | collective-permute-start | bytes 663560 | tf_op jit(solution)/shard_map/ppermute | solution.py:797
  24.3 5.1 %shard_map.242 = (bf16[576,192]{1,0:T(8,128)(2,1)S(1)}, f32[3,3,8,384]{3,2,1,0:T(8,128)S(1)}, bf16[768,768]{1,0:T(8,128)(2,1)S(1)}, bf16[768,768]{1,0:T(8,128)(2...) custom-call(s32[1]{0:T(128)} %bitcast.sref, bf16[3,1152,128]{2,1,0:T(8,128)(2,1)S(1)} %get-tuple-element.160.qa, ...), custom_call_target="tpu_custom_call" | custom-call | flops 1019215872 | bytes 18026500 | tf_op jit(solution)/shard_map/pallas_call | solution.py:78
  29.5 0.5 collective-permute-start.6
  30.1 1.6 %collective-permute-done.7.a2 = bf16[576,192]{1,0:T(8,128)(2,1)S(1)} collective-permute-done((bf16[576,192]{1,0:T(8,128)(2,1)S(1)}, bf16[576,192]{1,0:T(8,128)(2,1)S(1)}, u32[]{:S(2)}, u32[]{:S(2)}) %collective-permute-start.7) | collective-permute-done | bytes 221216 | tf_op jit(solution)/shard_map/ppermute | solution.py:797
  31.6 1.6 %collective-permute-done.8.a3 = bf16[576,192]{1,0:T(8,128)(2,1)S(1)} collective-permute-done((bf16[576,192]{1,0:T(8,128)(2,1)S(1)}, bf16[576,192]{1,0:T(8,128)(2,1)S(1)}, u32[]{:S(2)}, u32[]{:S(2)}) %collective-permute-start.8) | collective-permute-done | bytes 221216 | tf_op jit(solution)/shard_map/ppermute | solution.py:797
  33.2 1.8 %shard_map.243 = (f32[576,768]{1,0:T(8,128)S(1)}, bf16[576,768]{1,0:T(8,128)(2,1)S(1)}, bf16[576,768]{1,0:T(8,128)(2,1)S(1)}) custom-call(s32[1]{0:T(128)} %bitcast.sref, bf16[576,192]{1,0:T(8,128)(2,1)S(1)} %get-tuple-element.164.a0, bf16[576,192]{1,0:T(8,128)(2,1)S(1)} %collective-permute-done.6.a1, bf16[576,192]{1,0:T(8,128)(2,1)S(1)} %collective-permute-done.7.a2, ...), custom_call_target="tpu_custom_call" | custom-call | flops 679477248 | bytes 7692292 | tf_op jit(solution)/shard_map/pallas_call | solution.py:78
  35.0 5.2 %shard_map.244 = (bf16[8,24,768]{2,1,0:T(8,128)(2,1)S(1)}, bf16[8,24,768]{2,1,0:T(8,128)(2,1)S(1)}, bf16[4,48,768]{2,1,0:T(8,128)(2,1)S(1)}, bf16[4,48,768]{2,1,...) custom-call(s32[1]{0:T(128)} %bitcast.sref, ...), custom_call_target="tpu_custom_call" | custom-call | flops 4076863488 | bytes 10042376 | tf_op jit(solution)/shard_map/pallas_call | solution.py:78
  40.2 1.8 %collective-permute-start.11 = (bf16[12,24,768]{2,1,0:T(8,128)(2,1)S(1)}, bf16[12,24,768]{2,1,0:T(8,128)(2,1)S(1)}, u32[]{:S(2)}, u32[]{:S(2)}) collective-permute-start(bf16[12,24,768]{2,1,0:T(8,128)(2,1)S(1)} %get-tuple-element.183), channel_id=1, source_target_pairs={{0,1},{1,0},{2,3},{3,2},{4,5},{5,4},{6,7},{7,6},{8,9},{9,8},{10,11... | collective-permute-start | bytes 1327112 | tf_op jit(solution)/shard_map/ppermute | solution.py:797
  42.1 1.5 %collective-permute-start.10 = (bf16[8,24,768]{2,1,0:T(8,128)(2,1)S(1)}, bf16[8,24,768]{2,1,0:T(8,128)(2,1)S(1)}, u32[]{:S(2)}, u32[]{:S(2)}) collective-permute-start(bf16[8,24,768]{2,1,0:T(8,128)(2,1)S(1)} %get-tuple-element.182), channel_id=1, source_target_pairs={{0,16},{8,24},{16,0},{24,8},{1,17},{9,25},{17,1},{25,9},{2,18},{10... | collective-permute-start | bytes 884744 | tf_op jit(solution)/shard_map/ppermute | solution.py:797
  43.5 1.6 %collective-permute-start.12 = (bf16[4,48,768]{2,1,0:T(8,128)(2,1)S(1)}, bf16[4,48,768]{2,1,0:T(8,128)(2,1)S(1)}, u32[]{:S(2)}, u32[]{:S(2)}) collective-permute-start(bf16[4,48,768]{2,1,0:T(8,128)(2,1)S(1)} %get-tuple-element.184), channel_id=1, source_target_pairs={{0,2},{1,3},{2,0},{3,1},{4,6},{5,7},{6,4},{7,5},{8,10},{9,11},{10,... | collective-permute-start | bytes 884744 | tf_op jit(solution)/shard_map/ppermute | solution.py:797
  45.1 5.3 %shard_map.245 = (bf16[8,48,768]{2,1,0:T(8,128)(2,1)S(1)}, bf16[4,48,768]{2,1,0:T(8,128)(2,1)S(1)}, bf16[4,48,768]{2,1,0:T(8,128)(2,1)S(1)}, bf16[20,24,768]{2,1...) custom-call(s32[1]{0:T(128)} %bitcast.sref, ...), custom_call_target="tpu_custom_call" | custom-call | flops 4076863488 | bytes 14318600 | tf_op jit(solution)/shard_map/pallas_call | solution.py:78
  50.4 0.4 collective-permute-done.10.g2a
  50.8 1.2 collective-permute-done.12.oth_got
  52.0 0.5 collective-permute-done.11.y1
  52.5 0.5 collective-permute-start.14
  53.0 1.7 %collective-permute-start.17 = (bf16[20,24,768]{2,1,0:T(8,128)(2,1)S(1)}, bf16[20,24,768]{2,1,0:T(8,128)(2,1)S(1)}, u32[]{:S(2)}, u32[]{:S(2)}) collective-permute-start(bf16[20,24,768]{2,1,0:T(8,128)(2,1)S(1)} %get-tuple-element.216), channel_id=1, source_target_pairs={{0,1},{1,0},{2,3},{3,2},{4,5},{5,4},{6,7},{7,6},{8,9},{9,8},{10,11... | collective-permute-start | bytes 2211848 | tf_op jit(solution)/shard_map/ppermute | solution.py:797
  54.8 1.6 %collective-permute-start.16 = (bf16[4,48,768]{2,1,0:T(8,128)(2,1)S(1)}, bf16[4,48,768]{2,1,0:T(8,128)(2,1)S(1)}, u32[]{:S(2)}, u32[]{:S(2)}) collective-permute-start(bf16[4,48,768]{2,1,0:T(8,128)(2,1)S(1)} %get-tuple-element.201), channel_id=1, source_target_pairs={{0,2},{1,3},{2,0},{3,1},{4,6},{5,7},{6,4},{7,5},{8,10},{9,11},{10,... | collective-permute-start | bytes 884744 | tf_op jit(solution)/shard_map/ppermute | solution.py:797
  56.4 2.0 %shard_map.246 = (f32[288,768]{1,0:T(8,128)S(1)}, bf16[576,768]{1,0:T(8,128)(2,1)S(1)}, bf16[576,192]{1,0:T(8,128)(2,1)S(1)}, f32[8,768]{1,0:T(8,128)S(1)}) custom-call(s32[1]{0:T(128)} %bitcast.sref, f32[576,768]{1,0:T(8,128)S(1)} %get-tuple-element.177.gn_keep, bf16[576,768]{1,0:T(8,128)(2,1)S(1)} %collective-permute-done.13.gn_got, ...), custom_call_target="tpu_custom_call" | custom-call | flops 169869312 | bytes 9689092 | tf_op jit(solution)/shard_map/pallas_call | solution.py:78
  58.4 1.6 %collective-permute-start.15 = (bf16[576,192]{1,0:T(8,128)(2,1)S(1)}, bf16[576,192]{1,0:T(8,128)(2,1)S(1)}, u32[]{:S(2)}, u32[]{:S(2)}) collective-permute-start(bf16[576,192]{1,0:T(8,128)(2,1)S(1)} %get-tuple-element.199), channel_id=1, source_target_pairs={{0,16},{8,24},{16,0},{24,8},{1,17},{9,25},{17,1},{25,9},{2,18},{10... | collective-permute-start | bytes 663560 | tf_op jit(solution)/shard_map/ppermute | solution.py:797
  60.0 1.6 %shard_map.247 = (bf16[576,192]{1,0:T(8,128)(2,1)S(1)}, bf16[2,4,24,768]{3,2,1,0:T(8,128)(2,1)S(1)}, bf16[2,4,24,768]{3,2,1,0:T(8,128)(2,1)S(1)}, f32[768,128]{1...) custom-call(s32[1]{0:T(128)} %bitcast.sref, s32[1]{0:T(128)} %bitcast.1.bref, ...), custom_call_target="tpu_custom_call" | custom-call | flops 509607936 | bytes 7557128 | tf_op jit(solution)/shard_map/pallas_call | solution.py:78
  61.6 0.5 collective-permute-start.19
  62.1 1.3 collective-permute-done.16.own_got
  63.5 2.7 %collective-permute-start.20 = (bf16[4,48,768]{2,1,0:T(8,128)(2,1)S(1)}, bf16[4,48,768]{2,1,0:T(8,128)(2,1)S(1)}, u32[]{:S(2)}, u32[]{:S(2)}) collective-permute-start(bf16[4,48,768]{2,1,0:T(8,128)(2,1)S(1)} %get-tuple-element.206), channel_id=1, source_target_pairs={{0,4},{1,5},{2,6},{3,7},{4,0},{5,1},{6,2},{7,3},{8,12},{9,13},{10,... | collective-permute-start | bytes 884744 | tf_op jit(solution)/shard_map/ppermute | solution.py:797
  66.2 0.6 collective-permute-done.15.gx
  66.8 1.5 %collective-permute-start.18 = (bf16[8,24,768]{2,1,0:T(8,128)(2,1)S(1)}, bf16[8,24,768]{2,1,0:T(8,128)(2,1)S(1)}, u32[]{:S(2)}, u32[]{:S(2)}) collective-permute-start(bf16[8,24,768]{2,1,0:T(8,128)(2,1)S(1)} %get-tuple-element.217), channel_id=1, source_target_pairs={{0,16},{8,24},{16,0},{24,8},{1,17},{9,25},{17,1},{25,9},{2,18},{10... | collective-permute-start | bytes 884744 | tf_op jit(solution)/shard_map/ppermute | solution.py:797
  68.3 11.3 %shard_map.249 = (bf16[2,1152,192]{2,1,0:T(8,128)(2,1)S(1)}, bf16[8,24,768]{2,1,0:T(8,128)(2,1)S(1)}, bf16[8,24,768]{2,1,0:T(8,128)(2,1)S(1)}, f32[768,128]{1,0:T(8,128)S(1)}) custom-call(s32[1]{0:T(128)} %bitcast.sref, s32[1]{0:T(128)} %bitcast.1.bref, bf16[3,1152,128]{2,1,0:T(8,128)(2,1)S(1)} %get-tuple-element.160.qa, ...), custom_call_target="tpu_custom_call" | custom-call | flops 3397386240 | bytes 8220680 | tf_op jit(solution)/shard_map/pallas_call | solution.py:78
  79.7 0.5 shard_map.250
  80.2 1.1 collective-permute-start.22
  81.3 1.6 %collective-permute-start.23 = (bf16[16,24,768]{2,1,0:T(8,128)(2,1)S(1)}, bf16[16,24,768]{2,1,0:T(8,128)(2,1)S(1)}, u32[]{:S(2)}, u32[]{:S(2)}) collective-permute-start(bf16[16,24,768]{2,1,0:T(8,128)(2,1)S(1)} %get-tuple-element.238), channel_id=1, source_target_pairs={{0,2},{1,3},{2,0},{3,1},{4,6},{5,7},{6,4},{7,5},{8,10},{9,11},{10,... | collective-permute-start | bytes 1769480 | tf_op jit(solution)/shard_map/ppermute | solution.py:797
  82.9 0.5 collective-permute-start.21
  83.4 8.2 %shard_map.251 = (f32[576,768]{1,0:T(8,128)S(1)}, bf16[576,768]{1,0:T(8,128)(2,1)S(1)}, bf16[16,24,256]{2,1,0:T(8,128)(2,1)S(1)}, bf16[16,24,256]{2,1,0:T(8,128)(2,1)S(1)}) custom-call(s32[1]{0:T(128)} %bitcast.sref, s32[1]{0:T(128)} %bitcast.1.bref, bf16[3,1152,128]{2,1,0:T(8,128)(2,1)S(1)} %get-tuple-element.160.qa, ...), custom_call_target="tpu_custom_call" | custom-call | flops 1698693120 | bytes 10285064 | tf_op jit(solution)/shard_map/pallas_call | solution.py:78
  91.6 2.1 %collective-permute-done.22.got_y = bf16[16,24,768]{2,1,0:T(8,128)(2,1)S(1)} collective-permute-done((bf16[16,24,768]{2,1,0:T(8,128)(2,1)S(1)}, bf16[16,24,768]{2,1,0:T(8,128)(2,1)S(1)}, u32[]{:S(2)}, u32[]{:S(2)}) %collective-permute-start.22) | collective-permute-done | bytes 589856 | tf_op jit(solution)/shard_map/ppermute | solution.py:797
  93.8 1.4 %collective-permute-done.23.got_z = bf16[16,24,768]{2,1,0:T(8,128)(2,1)S(1)} collective-permute-done((bf16[16,24,768]{2,1,0:T(8,128)(2,1)S(1)}, bf16[16,24,768]{2,1,0:T(8,128)(2,1)S(1)}, u32[]{:S(2)}, u32[]{:S(2)}) %collective-permute-start.23) | collective-permute-done | bytes 589856 | tf_op jit(solution)/shard_map/ppermute | solution.py:797
  95.1 0.3 shard_map.252
  95.4 1.8 %collective-permute-start.27 = (bf16[10,24,768]{2,1,0:T(8,128)(2,1)S(1)}, bf16[10,24,768]{2,1,0:T(8,128)(2,1)S(1)}, u32[]{:S(2)}, u32[]{:S(2)}) collective-permute-start(bf16[10,24,768]{2,1,0:T(8,128)(2,1)S(1)} %get-tuple-element.254), channel_id=1, source_target_pairs={{0,2},{1,3},{2,0},{3,1},{4,6},{5,7},{6,4},{7,5},{8,10},{9,11},{10,... | collective-permute-start | bytes 1105928 | tf_op jit(solution)/shard_map/ppermute | solution.py:797
  97.2 0.5 collective-permute-start.26
  97.8 0.9 collective-permute-start.28
  98.8 1.1 collective-permute-start.25
  99.9 7.2 %collective-permute-done.26.got_x = bf16[8,24,768]{2,1,0:T(8,128)(2,1)S(1)} collective-permute-done((bf16[8,24,768]{2,1,0:T(8,128)(2,1)S(1)}, bf16[8,24,768]{2,1,0:T(8,128)(2,1)S(1)}, u32[]{:S(2)}, u32[]{:S(2)}) %collective-permute-start.26) | collective-permute-done | bytes 294944 | tf_op jit(solution)/shard_map/ppermute | solution.py:797
  107.3 2.7 %collective-permute-start.29 = (bf16[9,24,768]{2,1,0:T(8,128)(2,1)S(1)}, bf16[9,24,768]{2,1,0:T(8,128)(2,1)S(1)}, u32[]{:S(2)}, u32[]{:S(2)}) collective-permute-start(bf16[9,24,768]{2,1,0:T(8,128)(2,1)S(1)} %get-tuple-element.263), channel_id=1, source_target_pairs={{0,4},{1,5},{2,6},{3,7},{4,0},{5,1},{6,2},{7,3},{8,12},{9,13},{10,... | collective-permute-start | bytes 995336 | tf_op jit(solution)/shard_map/ppermute | solution.py:797
  109.9 0.3 collective-permute-start.31
  110.3 3.2 %collective-permute-start.32 = (bf16[4,24,256]{2,1,0:T(8,128)(2,1)S(1)}, bf16[4,24,256]{2,1,0:T(8,128)(2,1)S(1)}, u32[]{:S(2)}, u32[]{:S(2)}) collective-permute-start(bf16[4,24,256]{2,1,0:T(8,128)(2,1)S(1)} %get-tuple-element.267), channel_id=1, source_target_pairs={{0,6},{1,7},{2,4},{3,5},{4,2},{5,3},{6,0},{7,1},{8,14},{9,15},{10,... | collective-permute-start | bytes 147464 | tf_op jit(solution)/shard_map/ppermute | solution.py:797
  113.4 2.4 %collective-permute-done.25.x0 = bf16[288,768]{1,0:T(8,128)(2,1)S(1)} collective-permute-done((bf16[288,768]{1,0:T(8,128)(2,1)S(1)}, bf16[288,768]{1,0:T(8,128)(2,1)S(1)}, u32[]{:S(2)}, u32[]{:S(2)}) %collective-permute-start.25) | collective-permute-done | bytes 442400 | tf_op jit(solution)/shard_map/ppermute | solution.py:797
  115.8 1.5 %shard_map.255 = (f32[256,768]{1,0:T(8,128)}, f32[4,768]{1,0:T(4,128)}) custom-call(f32[576,768]{1,0:T(8,128)S(1)} %get-tuple-element.250.keep.k0, bf16[576,768]{1,0:T(8,128)(2,1)S(1)} %collective-permute-done.24.got.c0, bf16[288,768]{1,0:T(8,128)(2,1)S(1)} %collective-permute-done.25.x0, bf16[256,768]{1,0:T(8,128)(2,1)S(1)} %bitcast.18, ...), custom_call_target="tpu_custom_call" | custom-call | bytes 5228544 | tf_op jit(solution)/shard_map/pallas_call | solution.py:78
  117.4 10.0 %collective-permute-done.29.got = bf16[9,24,768]{2,1,0:T(8,128)(2,1)S(1)} collective-permute-done((bf16[9,24,768]{2,1,0:T(8,128)(2,1)S(1)}, bf16[9,24,768]{2,1,0:T(8,128)(2,1)S(1)}, u32[]{:S(2)}, u32[]{:S(2)}) %collective-permute-start.29) | collective-permute-done | bytes 331808 | tf_op jit(solution)/shard_map/ppermute | solution.py:797
  127.3 0.5 collective-permute-done.31.z2
  127.9 0.8 shard_map.257
  128.7 0.7 collective-permute-start.34
  129.4 1.2 collective-permute-start.35
  130.6 0.3 collective-permute-start.33
  130.9 2.0 %collective-permute-done.34.g2 = bf16[24,640]{1,0:T(8,128)(2,1)S(1)} collective-permute-done((bf16[24,640]{1,0:T(8,128)(2,1)S(1)}, bf16[24,640]{1,0:T(8,128)(2,1)S(1)}, u32[]{:S(2)}, u32[]{:S(2)}) %collective-permute-start.34) | collective-permute-done | bytes 30752 | tf_op jit(solution)/shard_map/ppermute | solution.py:797
  132.9 0.2 collective-permute-done.35.g3
  133.1 0.9 shard_map.258
  (47 shorter events, 0.6 us)
Async XLA Ops:
  0.6 6.7 %collective-permute-start = (bf16[256,768]{1,0:T(8,128)(2,1)}, bf16[256,768]{1,0:T(8,128)(2,1)S(1)}, u32[]{:S(2)}, u32[]{:S(2)}) collective-permute-start(bf16[256,768]{1,0:T(8,128)(2,1)} %bitcast.15), channel_id=1, source_target_pairs={{0,8},{8,0},{16,24},{24,16},{1,9},{9,1},{17,25},{25,17},{2,10},{10... | collective-permute-start | bytes 1179656 | tf_op jit(solution)/shard_map/ppermute | solution.py:797
  1.2 13.5 %collective-permute-start.2 = (bf16[256,768]{1,0:T(8,128)(2,1)}, bf16[256,768]{1,0:T(8,128)(2,1)S(1)}, u32[]{:S(2)}, u32[]{:S(2)}) collective-permute-start(bf16[256,768]{1,0:T(8,128)(2,1)} %bitcast.16), channel_id=1, source_target_pairs={{0,16},{8,24},{16,0},{24,8},{1,17},{9,25},{17,1},{25,9},{2,18},{10... | collective-permute-start | bytes 1179656 | tf_op jit(solution)/shard_map/ppermute | solution.py:797
  4.5 2.8 %collective-permute-start.1 = (bf16[32,768]{1,0:T(8,128)(2,1)S(1)}, bf16[32,768]{1,0:T(8,128)(2,1)S(1)}, u32[]{:S(2)}, u32[]{:S(2)}) collective-permute-start(bf16[32,768]{1,0:T(8,128)(2,1)S(1)} %shard_map.238.s0.c0), channel_id=1, source_target_pairs={{0,8},{8,0},{16,24},{24,16},{1,9},{9,1},{17,25},{25,17},{2,10},{10... | collective-permute-start | bytes 147464 | tf_op jit(solution)/shard_map/ppermute | solution.py:797
  4.8 9.9 %collective-permute-start.3 = (bf16[32,768]{1,0:T(8,128)(2,1)S(1)}, bf16[32,768]{1,0:T(8,128)(2,1)S(1)}, u32[]{:S(2)}, u32[]{:S(2)}) collective-permute-start(bf16[32,768]{1,0:T(8,128)(2,1)S(1)} %shard_map.238.s0.c0), channel_id=1, source_target_pairs={{0,16},{8,24},{16,0},{24,8},{1,17},{9,25},{17,1},{25,9},{2,18},{10... | collective-permute-start | bytes 147464 | tf_op jit(solution)/shard_map/ppermute | solution.py:797
  5.0 2.3 %copy-start.2 = (bf16[1,256,768]{2,1,0:T(8,128)(2,1)S(1)}, bf16[1,256,768]{2,1,0:T(8,128)(2,1)}, u32[]{:S(2)}) copy-start(bf16[1,256,768]{2,1,0:T(8,128)(2,1)} %param.15) | copy-start | bytes 1179652
  5.0 2.3 %copy-start.4 = (f32[2,768]{1,0:T(2,128)S(1)}, f32[2,768]{1,0:T(2,128)}, u32[]{:S(2)}) copy-start(f32[2,768]{1,0:T(2,128)} %gain.9) | copy-start | bytes 18436
  5.0 2.3 %copy-start.5 = (f32[2,768]{1,0:T(2,128)S(1)}, f32[2,768]{1,0:T(2,128)}, u32[]{:S(2)}) copy-start(f32[2,768]{1,0:T(2,128)} %shift1.1) | copy-start | bytes 18436
  5.0 2.3 %copy-start.7 = (s32[1,16]{1,0:T(1,128)S(1)}, s32[1,16]{1,0:T(1,128)}, u32[]{:S(2)}) copy-start(s32[1,16]{1,0:T(1,128)} %flags.1) | copy-start | bytes 196
  14.7 1.8 %collective-permute-start.4 = (bf16[256,768]{1,0:T(8,128)(2,1)S(1)}, bf16[256,768]{1,0:T(8,128)(2,1)S(1)}, u32[]{:S(2)}, u32[]{:S(2)}) collective-permute-start(bf16[256,768]{1,0:T(8,128)(2,1)S(1)} %collective-permute-done.2.p2), channel_id=1, source_target_pairs={{0,8},{8,0},{16,24},{24,16},{1,9},{9,1},{17,25},{25,17},{2,10},{10... | collective-permute-start | bytes 1179656 | tf_op jit(solution)/shard_map/ppermute | solution.py:797
  14.7 1.8 %collective-permute-start.5 = (bf16[32,768]{1,0:T(8,128)(2,1)S(1)}, bf16[32,768]{1,0:T(8,128)(2,1)S(1)}, u32[]{:S(2)}, u32[]{:S(2)}) collective-permute-start(bf16[32,768]{1,0:T(8,128)(2,1)S(1)} %collective-permute-done.3.s2), channel_id=1, source_target_pairs={{0,8},{8,0},{16,24},{24,16},{1,9},{9,1},{17,25},{25,17},{2,10},{10... | collective-permute-start | bytes 147464 | tf_op jit(solution)/shard_map/ppermute | solution.py:797
  16.5 7.8 %copy-start.1 = (bf16[1,256,768]{2,1,0:T(8,128)(2,1)S(1)}, bf16[1,256,768]{2,1,0:T(8,128)(2,1)}, u32[]{:S(2)}) copy-start(bf16[1,256,768]{2,1,0:T(8,128)(2,1)} %param.28) | copy-start | bytes 1179652
  22.5 9.1 %collective-permute-start.7 = (bf16[576,192]{1,0:T(8,128)(2,1)S(1)}, bf16[576,192]{1,0:T(8,128)(2,1)S(1)}, u32[]{:S(2)}, u32[]{:S(2)}) collective-permute-start(bf16[576,192]{1,0:T(8,128)(2,1)S(1)} %get-tuple-element.165), channel_id=1, source_target_pairs={{0,16},{8,24},{16,0},{24,8},{1,17},{9,25},{17,1},{25,9},{2,18},{10... | collective-permute-start | bytes 663560 | tf_op jit(solution)/shard_map/ppermute | solution.py:797
  24.3 7.3 %collective-permute-start.9 = (bf16[256,768]{1,0:T(8,128)(2,1)S(1)}, bf16[256,768]{1,0:T(8,128)(2,1)S(1)}, u32[]{:S(2)}, u32[]{:S(2)}) collective-permute-start(bf16[256,768]{1,0:T(8,128)(2,1)S(1)} %bitcast.12), channel_id=1, source_target_pairs={{0,8},{8,0},{16,24},{24,16},{1,9},{9,1},{17,25},{25,17},{2,10},{10... | collective-permute-start | bytes 1179656 | tf_op jit(solution)/shard_map/ppermute | solution.py:797
  24.3 8.9 %copy-start = (bf16[768,768]{1,0:T(8,128)(2,1)S(1)}, bf16[768,768]{1,0:T(8,128)(2,1)}, u32[]{:S(2)}) copy-start(bf16[768,768]{1,0:T(8,128)(2,1)} %w_out.5) | copy-start | bytes 3538948
  24.3 8.9 %copy-start.3 = (f32[4,768]{1,0:T(4,128)S(1)}, f32[4,768]{1,0:T(4,128)}, u32[]{:S(2)}) copy-start(f32[4,768]{1,0:T(4,128)} %bias.3) | copy-start | bytes 36868
  29.5 2.1 %collective-permute-start.6 = (bf16[576,192]{1,0:T(8,128)(2,1)S(1)}, bf16[576,192]{1,0:T(8,128)(2,1)S(1)}, u32[]{:S(2)}, u32[]{:S(2)}) collective-permute-start(bf16[576,192]{1,0:T(8,128)(2,1)S(1)} %get-tuple-element.164.a0), channel_id=1, source_target_pairs={{0,8},{8,0},{16,24},{24,16},{1,9},{9,1},{17,25},{25,17},{2,10},{10... | collective-permute-start | bytes 663560 | tf_op jit(solution)/shard_map/ppermute | solution.py:797
  31.6 1.6 %collective-permute-start.8 = (bf16[576,192]{1,0:T(8,128)(2,1)S(1)}, bf16[576,192]{1,0:T(8,128)(2,1)S(1)}, u32[]{:S(2)}, u32[]{:S(2)}) collective-permute-start(bf16[576,192]{1,0:T(8,128)(2,1)S(1)} %collective-permute-done.7.a2), channel_id=1, source_target_pairs={{0,8},{8,0},{16,24},{24,16},{1,9},{9,1},{17,25},{25,17},{2,10},{10... | collective-permute-start | bytes 663560 | tf_op jit(solution)/shard_map/ppermute | solution.py:797
  33.2 1.8 %copy-start.6 = (f32[3072]{0:T(1024)S(1)}, f32[3072]{0:T(1024)}, u32[]{:S(2)}) copy-start(f32[3072]{0:T(1024)} %param.26) | copy-start | bytes 36868
  40.2 12.3 %collective-permute-start.11 = (bf16[12,24,768]{2,1,0:T(8,128)(2,1)S(1)}, bf16[12,24,768]{2,1,0:T(8,128)(2,1)S(1)}, u32[]{:S(2)}, u32[]{:S(2)}) collective-permute-start(bf16[12,24,768]{2,1,0:T(8,128)(2,1)S(1)} %get-tuple-element.183), channel_id=1, source_target_pairs={{0,1},{1,0},{2,3},{3,2},{4,5},{5,4},{6,7},{7,6},{8,9},{9,8},{10,11... | collective-permute-start | bytes 1327112 | tf_op jit(solution)/shard_map/ppermute | solution.py:797
  42.1 8.8 %collective-permute-start.10 = (bf16[8,24,768]{2,1,0:T(8,128)(2,1)S(1)}, bf16[8,24,768]{2,1,0:T(8,128)(2,1)S(1)}, u32[]{:S(2)}, u32[]{:S(2)}) collective-permute-start(bf16[8,24,768]{2,1,0:T(8,128)(2,1)S(1)} %get-tuple-element.182), channel_id=1, source_target_pairs={{0,16},{8,24},{16,0},{24,8},{1,17},{9,25},{17,1},{25,9},{2,18},{10... | collective-permute-start | bytes 884744 | tf_op jit(solution)/shard_map/ppermute | solution.py:797
  43.5 8.5 %collective-permute-start.12 = (bf16[4,48,768]{2,1,0:T(8,128)(2,1)S(1)}, bf16[4,48,768]{2,1,0:T(8,128)(2,1)S(1)}, u32[]{:S(2)}, u32[]{:S(2)}) collective-permute-start(bf16[4,48,768]{2,1,0:T(8,128)(2,1)S(1)} %get-tuple-element.184), channel_id=1, source_target_pairs={{0,2},{1,3},{2,0},{3,1},{4,6},{5,7},{6,4},{7,5},{8,10},{9,11},{10,... | collective-permute-start | bytes 884744 | tf_op jit(solution)/shard_map/ppermute | solution.py:797
  52.5 3.8 %collective-permute-start.13 = (bf16[576,768]{1,0:T(8,128)(2,1)S(1)}, bf16[576,768]{1,0:T(8,128)(2,1)S(1)}, u32[]{:S(2)}, u32[]{:S(2)}) collective-permute-start(bf16[576,768]{1,0:T(8,128)(2,1)S(1)} %get-tuple-element.185), channel_id=1, source_target_pairs={{0,8},{8,0},{16,24},{24,16},{1,9},{9,1},{17,25},{25,17},{2,10},{10... | collective-permute-start | bytes 2654216 | tf_op jit(solution)/shard_map/ppermute | solution.py:797
  52.5 7.4 %collective-permute-start.14 = (bf16[288,768]{1,0:T(8,128)(2,1)S(1)}, bf16[288,768]{1,0:T(8,128)(2,1)S(1)}, u32[]{:S(2)}, u32[]{:S(2)}) collective-permute-start(bf16[288,768]{1,0:T(8,128)(2,1)S(1)} %get-tuple-element.189), channel_id=1, source_target_pairs={{0,8},{8,0},{16,24},{24,16},{1,9},{9,1},{17,25},{25,17},{2,10},{10... | collective-permute-start | bytes 1327112 | tf_op jit(solution)/shard_map/ppermute | solution.py:797
  53.0 26.6 %collective-permute-start.17 = (bf16[20,24,768]{2,1,0:T(8,128)(2,1)S(1)}, bf16[20,24,768]{2,1,0:T(8,128)(2,1)S(1)}, u32[]{:S(2)}, u32[]{:S(2)}) collective-permute-start(bf16[20,24,768]{2,1,0:T(8,128)(2,1)S(1)} %get-tuple-element.216), channel_id=1, source_target_pairs={{0,1},{1,0},{2,3},{3,2},{4,5},{5,4},{6,7},{7,6},{8,9},{9,8},{10,11... | collective-permute-start | bytes 2211848 | tf_op jit(solution)/shard_map/ppermute | solution.py:797
  54.8 8.6 %collective-permute-start.16 = (bf16[4,48,768]{2,1,0:T(8,128)(2,1)S(1)}, bf16[4,48,768]{2,1,0:T(8,128)(2,1)S(1)}, u32[]{:S(2)}, u32[]{:S(2)}) collective-permute-start(bf16[4,48,768]{2,1,0:T(8,128)(2,1)S(1)} %get-tuple-element.201), channel_id=1, source_target_pairs={{0,2},{1,3},{2,0},{3,1},{4,6},{5,7},{6,4},{7,5},{8,10},{9,11},{10,... | collective-permute-start | bytes 884744 | tf_op jit(solution)/shard_map/ppermute | solution.py:797
  58.4 8.4 %collective-permute-start.15 = (bf16[576,192]{1,0:T(8,128)(2,1)S(1)}, bf16[576,192]{1,0:T(8,128)(2,1)S(1)}, u32[]{:S(2)}, u32[]{:S(2)}) collective-permute-start(bf16[576,192]{1,0:T(8,128)(2,1)S(1)} %get-tuple-element.199), channel_id=1, source_target_pairs={{0,16},{8,24},{16,0},{24,8},{1,17},{9,25},{17,1},{25,9},{2,18},{10... | collective-permute-start | bytes 663560 | tf_op jit(solution)/shard_map/ppermute | solution.py:797
  61.6 18.1 %collective-permute-start.19 = (bf16[2,4,24,768]{3,2,1,0:T(8,128)(2,1)S(1)}, bf16[2,4,24,768]{3,2,1,0:T(8,128)(2,1)S(1)}, u32[]{:S(2)}, u32[]{:S(2)}) collective-permute-start(bf16[2,4,24,768]{3,2,1,0:T(8,128)(2,1)S(1)} %get-tuple-element.202), channel_id=1, source_target_pairs={{0,1},{1,0},{2,3},{3,2},{4,5},{5,4},{6,7},{7,6},{8,9},{9,8},{10,11... | collective-permute-start | bytes 884744 | tf_op jit(solution)/shard_map/ppermute | solution.py:797
  63.5 16.1 %collective-permute-start.20 = (bf16[4,48,768]{2,1,0:T(8,128)(2,1)S(1)}, bf16[4,48,768]{2,1,0:T(8,128)(2,1)S(1)}, u32[]{:S(2)}, u32[]{:S(2)}) collective-permute-start(bf16[4,48,768]{2,1,0:T(8,128)(2,1)S(1)} %get-tuple-element.206), channel_id=1, source_target_pairs={{0,4},{1,5},{2,6},{3,7},{4,0},{5,1},{6,2},{7,3},{8,12},{9,13},{10,... | collective-permute-start | bytes 884744 | tf_op jit(solution)/shard_map/ppermute | solution.py:797
  66.8 12.9 %collective-permute-start.18 = (bf16[8,24,768]{2,1,0:T(8,128)(2,1)S(1)}, bf16[8,24,768]{2,1,0:T(8,128)(2,1)S(1)}, u32[]{:S(2)}, u32[]{:S(2)}) collective-permute-start(bf16[8,24,768]{2,1,0:T(8,128)(2,1)S(1)} %get-tuple-element.217), channel_id=1, source_target_pairs={{0,16},{8,24},{16,0},{24,8},{1,17},{9,25},{17,1},{25,9},{2,18},{10... | collective-permute-start | bytes 884744 | tf_op jit(solution)/shard_map/ppermute | solution.py:797
  80.2 13.5 %collective-permute-start.22 = (bf16[16,24,768]{2,1,0:T(8,128)(2,1)S(1)}, bf16[16,24,768]{2,1,0:T(8,128)(2,1)S(1)}, u32[]{:S(2)}, u32[]{:S(2)}) collective-permute-start(bf16[16,24,768]{2,1,0:T(8,128)(2,1)S(1)} %get-tuple-element.237), channel_id=1, source_target_pairs={{0,1},{1,0},{2,3},{3,2},{4,5},{5,4},{6,7},{7,6},{8,9},{9,8},{10,11... | collective-permute-start | bytes 1769480 | tf_op jit(solution)/shard_map/ppermute | solution.py:797
  81.3 13.8 %collective-permute-start.23 = (bf16[16,24,768]{2,1,0:T(8,128)(2,1)S(1)}, bf16[16,24,768]{2,1,0:T(8,128)(2,1)S(1)}, u32[]{:S(2)}, u32[]{:S(2)}) collective-permute-start(bf16[16,24,768]{2,1,0:T(8,128)(2,1)S(1)} %get-tuple-element.238), channel_id=1, source_target_pairs={{0,2},{1,3},{2,0},{3,1},{4,6},{5,7},{6,4},{7,5},{8,10},{9,11},{10,... | collective-permute-start | bytes 1769480 | tf_op jit(solution)/shard_map/ppermute | solution.py:797
  82.9 8.7 %collective-permute-start.21 = (bf16[8,24,768]{2,1,0:T(8,128)(2,1)S(1)}, bf16[8,24,768]{2,1,0:T(8,128)(2,1)S(1)}, u32[]{:S(2)}, u32[]{:S(2)}) collective-permute-start(bf16[8,24,768]{2,1,0:T(8,128)(2,1)S(1)} %get-tuple-element.236), channel_id=1, source_target_pairs={{0,16},{8,24},{16,0},{24,8},{1,17},{9,25},{17,1},{25,9},{2,18},{10... | collective-permute-start | bytes 884744 | tf_op jit(solution)/shard_map/ppermute | solution.py:797
  95.1 3.5 %collective-permute-start.24 = (bf16[576,768]{1,0:T(8,128)(2,1)S(1)}, bf16[576,768]{1,0:T(8,128)(2,1)S(1)}, u32[]{:S(2)}, u32[]{:S(2)}) collective-permute-start(bf16[576,768]{1,0:T(8,128)(2,1)S(1)} %get-tuple-element.239), channel_id=1, source_target_pairs={{0,8},{8,0},{16,24},{24,16},{1,9},{9,1},{17,25},{25,17},{2,10},{10... | collective-permute-start | bytes 2654216 | tf_op jit(solution)/shard_map/ppermute | solution.py:797
  95.4 11.7 %collective-permute-start.27 = (bf16[10,24,768]{2,1,0:T(8,128)(2,1)S(1)}, bf16[10,24,768]{2,1,0:T(8,128)(2,1)S(1)}, u32[]{:S(2)}, u32[]{:S(2)}) collective-permute-start(bf16[10,24,768]{2,1,0:T(8,128)(2,1)S(1)} %get-tuple-element.254), channel_id=1, source_target_pairs={{0,2},{1,3},{2,0},{3,1},{4,6},{5,7},{6,4},{7,5},{8,10},{9,11},{10,... | collective-permute-start | bytes 1105928 | tf_op jit(solution)/shard_map/ppermute | solution.py:797
  97.2 9.8 %collective-permute-start.26 = (bf16[8,24,768]{2,1,0:T(8,128)(2,1)S(1)}, bf16[8,24,768]{2,1,0:T(8,128)(2,1)S(1)}, u32[]{:S(2)}, u32[]{:S(2)}) collective-permute-start(bf16[8,24,768]{2,1,0:T(8,128)(2,1)S(1)} %get-tuple-element.249), channel_id=1, source_target_pairs={{0,16},{8,24},{16,0},{24,8},{1,17},{9,25},{17,1},{25,9},{2,18},{10... | collective-permute-start | bytes 884744 | tf_op jit(solution)/shard_map/ppermute | solution.py:797
  97.8 9.3 %collective-permute-start.28 = (bf16[22,24,256]{2,1,0:T(8,128)(2,1)S(1)}, bf16[22,24,256]{2,1,0:T(8,128)(2,1)S(1)}, u32[]{:S(2)}, u32[]{:S(2)}) collective-permute-start(bf16[22,24,256]{2,1,0:T(8,128)(2,1)S(1)} %get-tuple-element.256), channel_id=1, source_target_pairs={{0,1},{1,0},{2,3},{3,2},{4,5},{5,4},{6,7},{7,6},{8,9},{9,8},{10,11... | collective-permute-start | bytes 811016 | tf_op jit(solution)/shard_map/ppermute | solution.py:797
  98.8 17.1 %collective-permute-start.25 = (bf16[288,768]{1,0:T(8,128)(2,1)S(1)}, bf16[288,768]{1,0:T(8,128)(2,1)S(1)}, u32[]{:S(2)}, u32[]{:S(2)}) collective-permute-start(bf16[288,768]{1,0:T(8,128)(2,1)S(1)} %shard_map.253), channel_id=1, source_target_pairs={{0,16},{8,24},{16,0},{24,8},{1,17},{9,25},{17,1},{25,9},{2,18},{10... | collective-permute-start | bytes 1327112 | tf_op jit(solution)/shard_map/ppermute | solution.py:797
  107.3 20.1 %collective-permute-start.29 = (bf16[9,24,768]{2,1,0:T(8,128)(2,1)S(1)}, bf16[9,24,768]{2,1,0:T(8,128)(2,1)S(1)}, u32[]{:S(2)}, u32[]{:S(2)}) collective-permute-start(bf16[9,24,768]{2,1,0:T(8,128)(2,1)S(1)} %get-tuple-element.263), channel_id=1, source_target_pairs={{0,4},{1,5},{2,6},{3,7},{4,0},{5,1},{6,2},{7,3},{8,12},{9,13},{10,... | collective-permute-start | bytes 995336 | tf_op jit(solution)/shard_map/ppermute | solution.py:797
  109.9 17.9 %collective-permute-start.31 = (bf16[4,24,256]{2,1,0:T(8,128)(2,1)S(1)}, bf16[4,24,256]{2,1,0:T(8,128)(2,1)S(1)}, u32[]{:S(2)}, u32[]{:S(2)}) collective-permute-start(bf16[4,24,256]{2,1,0:T(8,128)(2,1)S(1)} %get-tuple-element.266), channel_id=1, source_target_pairs={{0,4},{1,5},{2,6},{3,7},{4,0},{5,1},{6,2},{7,3},{8,12},{9,13},{10,... | collective-permute-start | bytes 147464 | tf_op jit(solution)/shard_map/ppermute | solution.py:797
  110.3 17.6 %collective-permute-start.32 = (bf16[4,24,256]{2,1,0:T(8,128)(2,1)S(1)}, bf16[4,24,256]{2,1,0:T(8,128)(2,1)S(1)}, u32[]{:S(2)}, u32[]{:S(2)}) collective-permute-start(bf16[4,24,256]{2,1,0:T(8,128)(2,1)S(1)} %get-tuple-element.267), channel_id=1, source_target_pairs={{0,6},{1,7},{2,4},{3,5},{4,2},{5,3},{6,0},{7,1},{8,14},{9,15},{10,... | collective-permute-start | bytes 147464 | tf_op jit(solution)/shard_map/ppermute | solution.py:797
  113.4 14.4 %collective-permute-start.30 = (bf16[4,24,256]{2,1,0:T(8,128)(2,1)S(1)}, bf16[4,24,256]{2,1,0:T(8,128)(2,1)S(1)}, u32[]{:S(2)}, u32[]{:S(2)}) collective-permute-start(bf16[4,24,256]{2,1,0:T(8,128)(2,1)S(1)} %get-tuple-element.257), channel_id=1, source_target_pairs={{0,2},{1,3},{2,0},{3,1},{4,6},{5,7},{6,4},{7,5},{8,10},{9,11},{10,... | collective-permute-start | bytes 147464 | tf_op jit(solution)/shard_map/ppermute | solution.py:797
  128.7 4.3 %collective-permute-start.36 = (bf16[48,768]{1,0:T(8,128)(2,1)S(1)}, bf16[48,768]{1,0:T(8,128)(2,1)S(1)}, u32[]{:S(2)}, u32[]{:S(2)}) collective-permute-start(bf16[48,768]{1,0:T(8,128)(2,1)S(1)} %get-tuple-element.275), channel_id=1, source_target_pairs={{0,8},{8,0},{16,24},{24,16},{1,9},{9,1},{17,25},{25,17},{2,10},{10... | collective-permute-start | bytes 221192 | tf_op jit(solution)/shard_map/ppermute | solution.py:797
  128.7 4.1 %collective-permute-start.34 = (bf16[24,640]{1,0:T(8,128)(2,1)S(1)}, bf16[24,640]{1,0:T(8,128)(2,1)S(1)}, u32[]{:S(2)}, u32[]{:S(2)}) collective-permute-start(bf16[24,640]{1,0:T(8,128)(2,1)S(1)} %get-tuple-element.270), channel_id=1, source_target_pairs={{0,16},{8,24},{16,0},{24,8},{1,17},{9,25},{17,1},{25,9},{2,18},{10... | collective-permute-start | bytes 92168 | tf_op jit(solution)/shard_map/ppermute | solution.py:797
  129.4 3.6 %collective-permute-start.35 = (bf16[24,640]{1,0:T(8,128)(2,1)S(1)}, bf16[24,640]{1,0:T(8,128)(2,1)S(1)}, u32[]{:S(2)}, u32[]{:S(2)}) collective-permute-start(bf16[24,640]{1,0:T(8,128)(2,1)S(1)} %get-tuple-element.271), channel_id=1, source_target_pairs={{0,24},{8,16},{16,8},{24,0},{1,25},{9,17},{17,9},{25,1},{2,26},{10... | collective-permute-start | bytes 92168 | tf_op jit(solution)/shard_map/ppermute | solution.py:797
  130.6 2.5 %collective-permute-start.33 = (bf16[24,640]{1,0:T(8,128)(2,1)S(1)}, bf16[24,640]{1,0:T(8,128)(2,1)S(1)}, u32[]{:S(2)}, u32[]{:S(2)}) collective-permute-start(bf16[24,640]{1,0:T(8,128)(2,1)S(1)} %get-tuple-element.269), channel_id=1, source_target_pairs={{0,8},{8,0},{16,24},{24,16},{1,9},{9,1},{17,25},{25,17},{2,10},{10... | collective-permute-start | bytes 92168 | tf_op jit(solution)/shard_map/ppermute | solution.py:797

commit v9 on v8

--- a/solution.py
+++ b/solution.py
@@ -125,7 +125,7 @@
         bias_own[:, t * LANES : (t + 1) * LANES] = bias
 
 
-def small_kernel(specials_in, segments_in, order_in, cots_in, small, specials, segments, order, cots, wide, sems):
+def small_kernel(specials_in, segments_in, order_in, cots_in, small, head, specials, segments, order, cots, wide, sems):
     pairs = ((specials_in, specials), (segments_in, segments), (order_in, order), (cots_in, cots))
     copies = [pltpu.make_async_copy(src, dst, sems.at[i]) for i, (src, dst) in enumerate(pairs)]
     for copy in copies:
@@ -141,6 +141,7 @@
     wide[extra : extra + 1, :count] = segments[...].astype(F32)
     wide[extra : extra + 1, count : count + extra] = (order[...] >> 1).astype(F32)
     small[...] = wide[...].astype(BF16)
+    head[...] = wide[:16, :].astype(BF16)
 
 
 def tokens_of(patches, small):
@@ -205,19 +206,22 @@
     return mark
 
 
+def project_one_kernel(p, small, gain, shift, w, bias, qa, ka, va, normed):
+    project(p, small, gain, shift, w, bias, pl.ds(0, normed.shape[0]), qa, ka, va, normed)
+
+
 def attend_first_kernel(
-    q0, k0, v0, n0, p2, s2, p3, s3, gain, shift, w, bias, qa, ka, va, send, oacc, normed
+    q0, k0, v0, n0, q2, k2, v2, n2, p3, s3, gain, shift, w, bias, qa, ka, va, send, oacc, normed
 ):
     half = n0.shape[0]
     rows = half // 2
-    own = pl.ds(0, half)
-    for h in range(OWN):
-        qa[h, own, :] = q0[h]
-        ka[h, own, :] = k0[h]
-        va[h, own, :] = v0[h]
-    normed[own, :] = n0[...]
-    for i, (p, small) in enumerate(((p2, s2), (p3, s3))):
-        project(p, small, gain, shift, w, bias, pl.ds(half + i * rows, rows), qa, ka, va, normed)
+    for at, qs, ks, vs, ns in ((pl.ds(0, half), q0, k0, v0, n0), (pl.ds(half, rows), q2, k2, v2, n2)):
+        for h in range(OWN):
+            qa[h, at, :] = qs[h]
+            ka[h, at, :] = ks[h]
+            va[h, at, :] = vs[h]
+        normed[at, :] = ns[...]
+    project(p3, s3, gain, shift, w, bias, pl.ds(half + rows, rows), qa, ka, va, normed)
 
     def block(i, carry):
         h, b = i // 2, i % 2
@@ -880,15 +884,15 @@
     own_p, own_cot = patches[0], cot_patches[0]
     got_px = swap_seq(own_p, 2)
     got_pc = swap_seq(own_p, 1)
-    (small,) = call(
+    small, small_head = call(
         small_kernel,
-        [SDS((32, width), BF16)],
+        [SDS((32, width), BF16), SDS((16, width), BF16)],
         (specials[0], segment_ids, special_order, cot_specials[0]),
         [pltpu.VMEM((extra, width), BF16), pltpu.VMEM((1, count), jnp.int32), pltpu.VMEM((1, extra), jnp.int32)]
         + [pltpu.VMEM((extra, width), BF16), pltpu.VMEM((32, width), F32), pltpu.SemaphoreType.DMA((4,))],
         far=(0, 1, 2, 3),
     )
-    got_sx = swap_seq(small, 2)
+    got_sx = swap_seq(small_head, 2)
     got_sc = swap_seq(small, 1)
     cot_c = swap_seq(own_cot, 1)
     fb = fc1_bias.reshape(1, -1)
@@ -914,12 +918,19 @@
     got_pd = swap_seq(got_px, 1)
     got_sd = swap_seq(got_sx, 1)
 
+    headed = SDS((OWN, block, LANES), BF16)
+    q2, k2, v2, n2 = call(
+        project_one_kernel,
+        [headed] * 3 + [SDS((block, width), BF16)],
+        (got_px, got_sx, norm_gains, norm_shifts, w_own, bias_own),
+        flops=2 * block * width * 3 * cols,
+    )
     headed = SDS((OWN, whole, LANES), BF16)
     heads32 = SDS((OWN, chip, LANES), F32)
     qa, ka, va, att_send, other, normed = call(
         attend_first_kernel,
         [headed] * 3 + [SDS((chip, cols), BF16), heads32, SDS((whole, width), BF16)],
-        (q0, k0, v0, n0, got_px, got_sx, got_pd, got_sd, norm_gains, norm_shifts, w_own, bias_own),
+        (q0, k0, v0, n0, q2, k2, v2, n2, got_pd, got_sd, norm_gains, norm_shifts, w_own, bias_own),
         flops=2 * chip * width * 3 * cols + 2 * OWN * whole * whole * LANES,
     )
     a2 = swap_seq(att_send, 2)

time: 134 us -> 133 us (level)
    ppermute x37, waiting for transfers between devices: 39.7 us -> 38.4 us  [swap(): lax.ppermute(v, kind, [(i, i ^ mask) for i in range(lax.axis_size(kind))])]
    pallas_call x21 -> x22, Pallas kernels: 56 us -> 56.4 us  [call(): pl.pallas_call(kernel, out_shape=outs, in_specs=[smem() if i < scalars el...]
  transfers between devices with their start and end apart: 37 -> 37, of which waited for: 17 -> 17; matrix products, arithmetic and copies ran while one was open for 0% -> 0% of each run, Pallas kernels for 30% -> 31%
where the time goes in v9:
time: 133 us
  Pallas kernels  56.4 us (42%)
  waiting for transfers between devices  38.4 us (29%)
  starting transfers between devices  37.3 us (28%)
    pallas_call x22, Pallas kernels, call(): pl.pallas_call(kernel, out_shape=outs, in_specs=[smem() if i < scalars el...  56.4 us
    ppermute x37, waiting for transfers between devices, swap(): lax.ppermute(v, kind, [(i, i ^ mask) for i in range(lax.axis_size(kind))])  38.4 us
    ppermute x37, starting transfers between devices, swap(): lax.ppermute(v, kind, [(i, i ^ mask) for i in range(lax.axis_size(kind))])  37.3 us
  transfers between devices with their start and end apart: 37, of which 17 were waited for; matrix products, arithmetic and copies ran while one was open for 0% of the time, Pallas kernels for 31%

profile of v9, /device:TPU:0, one launch (start us, length us, event | category | flops | bytes accessed | tf_op | source)
XLA Modules:
  0.0 133.0 jit_solution(18225824583676080850)
XLA Ops:
  0.6 0.5 collective-permute-start
  1.2 2.6 %collective-permute-start.2 = (bf16[256,768]{1,0:T(8,128)(2,1)}, bf16[256,768]{1,0:T(8,128)(2,1)S(1)}, u32[]{:S(2)}, u32[]{:S(2)}) collective-permute-start(bf16[256,768]{1,0:T(8,128)(2,1)} %bitcast.16), channel_id=1, source_target_pairs={{0,16},{8,24},{16,0},{24,8},{1,17},{9,25},{17,1},{25,9},{2,18},{10... | collective-permute-start | bytes 1179656 | tf_op jit(solution)/shard_map/ppermute | solution.py:801
  3.7 0.8 shard_map.238
  4.5 0.2 collective-permute-start.1
  4.8 0.3 collective-permute-start.3
  5.0 2.2 %shard_map.239 = (bf16[768,640]{1,0:T(8,128)(2,1)S(1)}, f32[1,640]{1,0:T(1,128)S(1)}) custom-call(s32[1]{0:T(128)} %bitcast.sref, bf16[768,2304]{1,0:T(8,128)(2,1)} %w.1, f32[4,768]{1,0:T(4,128)} %bias.3), custom_call_target="tpu_custom_call" | custom-call | bytes 4536836 | tf_op jit(solution)/shard_map/pallas_call | solution.py:78
  7.3 2.0 %shard_map.240 = (bf16[3,576,128]{2,1,0:T(8,128)(2,1)S(1)}, bf16[3,576,128]{2,1,0:T(8,128)(2,1)S(1)}, bf16[3,576,128]{2,1,0:T(8,128)(2,1)S(1)}, bf16[576,768]{1,...) custom-call(s32[1,16]{1,0:T(1,128)S(1)} %copy-done.7, bf16[256,768]{1,0:T(8,128)(2,1)S(1)} %bitcast.17, ...), custom_call_target="tpu_custom_call" | custom-call | flops 509607936 | bytes 5274176 | tf_op jit(solution)/shard_map/pallas_call | solution.py:78
  9.3 4.9 %collective-permute-done.3.small = bf16[16,768]{1,0:T(8,128)(2,1)S(1)} collective-permute-done((bf16[16,768]{1,0:T(8,128)(2,1)S(1)}, bf16[16,768]{1,0:T(8,128)(2,1)S(1)}, u32[]{:S(2)}, u32[]{:S(2)}) %collective-permute-start.3) | collective-permute-done | bytes 24608 | tf_op jit(solution)/shard_map/ppermute | solution.py:801
  14.2 0.5 collective-permute-start.5
  14.7 0.8 shard_map.241
  15.5 0.4 collective-permute-done.5.s3
  15.9 5.6 %shard_map.242 = (bf16[3,1152,128]{2,1,0:T(8,128)(2,1)S(1)}, bf16[3,1152,128]{2,1,0:T(8,128)(2,1)S(1)}, bf16[3,1152,128]{2,1,0:T(8,128)(2,1)S(1)}, bf16[576,192]...) custom-call(bf16[3,576,128]{2,1,0:T(8,128)(2,1)S(1)} %get-tuple-element.160.q0, ...), custom_call_target="tpu_custom_call" | custom-call | flops 1528823808 | bytes 10263040 | tf_op jit(solution)/shard_map/pallas_call | solution.py:78
  21.5 1.8 %collective-permute-start.7 = (bf16[576,192]{1,0:T(8,128)(2,1)S(1)}, bf16[576,192]{1,0:T(8,128)(2,1)S(1)}, u32[]{:S(2)}, u32[]{:S(2)}) collective-permute-start(bf16[576,192]{1,0:T(8,128)(2,1)S(1)} %get-tuple-element.177), channel_id=1, source_target_pairs={{0,16},{8,24},{16,0},{24,8},{1,17},{9,25},{17,1},{25,9},{2,18},{10... | collective-permute-start | bytes 663560 | tf_op jit(solution)/shard_map/ppermute | solution.py:801
  23.4 5.1 %shard_map.243 = (bf16[576,192]{1,0:T(8,128)(2,1)S(1)}, f32[3,3,8,384]{3,2,1,0:T(8,128)S(1)}, bf16[768,768]{1,0:T(8,128)(2,1)S(1)}, bf16[768,768]{1,0:T(8,128)(2...) custom-call(s32[1]{0:T(128)} %bitcast.sref, bf16[3,1152,128]{2,1,0:T(8,128)(2,1)S(1)} %get-tuple-element.172.qa, ...), custom_call_target="tpu_custom_call" | custom-call | flops 1019215872 | bytes 18026500 | tf_op jit(solution)/shard_map/pallas_call | solution.py:78
  28.5 0.5 collective-permute-start.6
  29.1 1.6 %collective-permute-done.7.a2 = bf16[576,192]{1,0:T(8,128)(2,1)S(1)} collective-permute-done((bf16[576,192]{1,0:T(8,128)(2,1)S(1)}, bf16[576,192]{1,0:T(8,128)(2,1)S(1)}, u32[]{:S(2)}, u32[]{:S(2)}) %collective-permute-start.7) | collective-permute-done | bytes 221216 | tf_op jit(solution)/shard_map/ppermute | solution.py:801
  30.7 1.6 %collective-permute-done.8.a3 = bf16[576,192]{1,0:T(8,128)(2,1)S(1)} collective-permute-done((bf16[576,192]{1,0:T(8,128)(2,1)S(1)}, bf16[576,192]{1,0:T(8,128)(2,1)S(1)}, u32[]{:S(2)}, u32[]{:S(2)}) %collective-permute-start.8) | collective-permute-done | bytes 221216 | tf_op jit(solution)/shard_map/ppermute | solution.py:801
  32.3 1.8 %shard_map.244 = (f32[576,768]{1,0:T(8,128)S(1)}, bf16[576,768]{1,0:T(8,128)(2,1)S(1)}, bf16[576,768]{1,0:T(8,128)(2,1)S(1)}) custom-call(s32[1]{0:T(128)} %bitcast.sref, bf16[576,192]{1,0:T(8,128)(2,1)S(1)} %get-tuple-element.176.a0, bf16[576,192]{1,0:T(8,128)(2,1)S(1)} %collective-permute-done.6.a1, bf16[576,192]{1,0:T(8,128)(2,1)S(1)} %collective-permute-done.7.a2, ...), custom_call_target="tpu_custom_call" | custom-call | flops 679477248 | bytes 7692292 | tf_op jit(solution)/shard_map/pallas_call | solution.py:78
  34.1 5.2 %shard_map.245 = (bf16[8,24,768]{2,1,0:T(8,128)(2,1)S(1)}, bf16[8,24,768]{2,1,0:T(8,128)(2,1)S(1)}, bf16[4,48,768]{2,1,0:T(8,128)(2,1)S(1)}, bf16[4,48,768]{2,1,...) custom-call(s32[1]{0:T(128)} %bitcast.sref, ...), custom_call_target="tpu_custom_call" | custom-call | flops 4076863488 | bytes 10042376 | tf_op jit(solution)/shard_map/pallas_call | solution.py:78
  39.3 1.8 %collective-permute-start.11 = (bf16[12,24,768]{2,1,0:T(8,128)(2,1)S(1)}, bf16[12,24,768]{2,1,0:T(8,128)(2,1)S(1)}, u32[]{:S(2)}, u32[]{:S(2)}) collective-permute-start(bf16[12,24,768]{2,1,0:T(8,128)(2,1)S(1)} %get-tuple-element.195), channel_id=1, source_target_pairs={{0,1},{1,0},{2,3},{3,2},{4,5},{5,4},{6,7},{7,6},{8,9},{9,8},{10,11... | collective-permute-start | bytes 1327112 | tf_op jit(solution)/shard_map/ppermute | solution.py:801
  41.1 1.5 %collective-permute-start.10 = (bf16[8,24,768]{2,1,0:T(8,128)(2,1)S(1)}, bf16[8,24,768]{2,1,0:T(8,128)(2,1)S(1)}, u32[]{:S(2)}, u32[]{:S(2)}) collective-permute-start(bf16[8,24,768]{2,1,0:T(8,128)(2,1)S(1)} %get-tuple-element.194), channel_id=1, source_target_pairs={{0,16},{8,24},{16,0},{24,8},{1,17},{9,25},{17,1},{25,9},{2,18},{10... | collective-permute-start | bytes 884744 | tf_op jit(solution)/shard_map/ppermute | solution.py:801
  42.6 1.6 %collective-permute-start.12 = (bf16[4,48,768]{2,1,0:T(8,128)(2,1)S(1)}, bf16[4,48,768]{2,1,0:T(8,128)(2,1)S(1)}, u32[]{:S(2)}, u32[]{:S(2)}) collective-permute-start(bf16[4,48,768]{2,1,0:T(8,128)(2,1)S(1)} %get-tuple-element.196), channel_id=1, source_target_pairs={{0,2},{1,3},{2,0},{3,1},{4,6},{5,7},{6,4},{7,5},{8,10},{9,11},{10,... | collective-permute-start | bytes 884744 | tf_op jit(solution)/shard_map/ppermute | solution.py:801
  44.2 5.2 %shard_map.246 = (bf16[8,48,768]{2,1,0:T(8,128)(2,1)S(1)}, bf16[4,48,768]{2,1,0:T(8,128)(2,1)S(1)}, bf16[4,48,768]{2,1,0:T(8,128)(2,1)S(1)}, bf16[20,24,768]{2,1...) custom-call(s32[1]{0:T(128)} %bitcast.sref, ...), custom_call_target="tpu_custom_call" | custom-call | flops 4076863488 | bytes 14318600 | tf_op jit(solution)/shard_map/pallas_call | solution.py:78
  49.4 0.5 collective-permute-done.10.g2a
  49.9 1.2 collective-permute-done.12.oth_got
  51.1 0.5 collective-permute-done.11.y1
  51.6 0.5 collective-permute-start.14
  52.1 1.7 %collective-permute-start.17 = (bf16[20,24,768]{2,1,0:T(8,128)(2,1)S(1)}, bf16[20,24,768]{2,1,0:T(8,128)(2,1)S(1)}, u32[]{:S(2)}, u32[]{:S(2)}) collective-permute-start(bf16[20,24,768]{2,1,0:T(8,128)(2,1)S(1)} %get-tuple-element.228), channel_id=1, source_target_pairs={{0,1},{1,0},{2,3},{3,2},{4,5},{5,4},{6,7},{7,6},{8,9},{9,8},{10,11... | collective-permute-start | bytes 2211848 | tf_op jit(solution)/shard_map/ppermute | solution.py:801
  53.8 1.6 %collective-permute-start.16 = (bf16[4,48,768]{2,1,0:T(8,128)(2,1)S(1)}, bf16[4,48,768]{2,1,0:T(8,128)(2,1)S(1)}, u32[]{:S(2)}, u32[]{:S(2)}) collective-permute-start(bf16[4,48,768]{2,1,0:T(8,128)(2,1)S(1)} %get-tuple-element.213), channel_id=1, source_target_pairs={{0,2},{1,3},{2,0},{3,1},{4,6},{5,7},{6,4},{7,5},{8,10},{9,11},{10,... | collective-permute-start | bytes 884744 | tf_op jit(solution)/shard_map/ppermute | solution.py:801
  55.4 2.0 %shard_map.247 = (f32[288,768]{1,0:T(8,128)S(1)}, bf16[576,768]{1,0:T(8,128)(2,1)S(1)}, bf16[576,192]{1,0:T(8,128)(2,1)S(1)}, f32[8,768]{1,0:T(8,128)S(1)}) custom-call(s32[1]{0:T(128)} %bitcast.sref, f32[576,768]{1,0:T(8,128)S(1)} %get-tuple-element.189.gn_keep, bf16[576,768]{1,0:T(8,128)(2,1)S(1)} %collective-permute-done.13.gn_got, ...), custom_call_target="tpu_custom_call" | custom-call | flops 169869312 | bytes 9689092 | tf_op jit(solution)/shard_map/pallas_call | solution.py:78
  57.4 1.6 %collective-permute-start.15 = (bf16[576,192]{1,0:T(8,128)(2,1)S(1)}, bf16[576,192]{1,0:T(8,128)(2,1)S(1)}, u32[]{:S(2)}, u32[]{:S(2)}) collective-permute-start(bf16[576,192]{1,0:T(8,128)(2,1)S(1)} %get-tuple-element.211), channel_id=1, source_target_pairs={{0,16},{8,24},{16,0},{24,8},{1,17},{9,25},{17,1},{25,9},{2,18},{10... | collective-permute-start | bytes 663560 | tf_op jit(solution)/shard_map/ppermute | solution.py:801
  59.0 1.6 %shard_map.248 = (bf16[576,192]{1,0:T(8,128)(2,1)S(1)}, bf16[2,4,24,768]{3,2,1,0:T(8,128)(2,1)S(1)}, bf16[2,4,24,768]{3,2,1,0:T(8,128)(2,1)S(1)}, f32[768,128]{1...) custom-call(s32[1]{0:T(128)} %bitcast.sref, s32[1]{0:T(128)} %bitcast.1.bref, ...), custom_call_target="tpu_custom_call" | custom-call | flops 509607936 | bytes 7557128 | tf_op jit(solution)/shard_map/pallas_call | solution.py:78
  60.6 0.5 collective-permute-start.19
  61.1 1.3 %collective-permute-done.16.own_got = bf16[4,48,768]{2,1,0:T(8,128)(2,1)S(1)} collective-permute-done((bf16[4,48,768]{2,1,0:T(8,128)(2,1)S(1)}, bf16[4,48,768]{2,1,0:T(8,128)(2,1)S(1)}, u32[]{:S(2)}, u32[]{:S(2)}) %collective-permute-start.16) | collective-permute-done | bytes 294944 | tf_op jit(solution)/shard_map/ppermute | solution.py:801
  62.6 2.6 %collective-permute-start.20 = (bf16[4,48,768]{2,1,0:T(8,128)(2,1)S(1)}, bf16[4,48,768]{2,1,0:T(8,128)(2,1)S(1)}, u32[]{:S(2)}, u32[]{:S(2)}) collective-permute-start(bf16[4,48,768]{2,1,0:T(8,128)(2,1)S(1)} %get-tuple-element.218), channel_id=1, source_target_pairs={{0,4},{1,5},{2,6},{3,7},{4,0},{5,1},{6,2},{7,3},{8,12},{9,13},{10,... | collective-permute-start | bytes 884744 | tf_op jit(solution)/shard_map/ppermute | solution.py:801
  65.2 0.6 collective-permute-done.15.gx
  65.9 1.5 %collective-permute-start.18 = (bf16[8,24,768]{2,1,0:T(8,128)(2,1)S(1)}, bf16[8,24,768]{2,1,0:T(8,128)(2,1)S(1)}, u32[]{:S(2)}, u32[]{:S(2)}) collective-permute-start(bf16[8,24,768]{2,1,0:T(8,128)(2,1)S(1)} %get-tuple-element.229), channel_id=1, source_target_pairs={{0,16},{8,24},{16,0},{24,8},{1,17},{9,25},{17,1},{25,9},{2,18},{10... | collective-permute-start | bytes 884744 | tf_op jit(solution)/shard_map/ppermute | solution.py:801
  67.4 11.4 %shard_map.250 = (bf16[2,1152,192]{2,1,0:T(8,128)(2,1)S(1)}, bf16[8,24,768]{2,1,0:T(8,128)(2,1)S(1)}, bf16[8,24,768]{2,1,0:T(8,128)(2,1)S(1)}, f32[768,128]{1,0:T(8,128)S(1)}) custom-call(s32[1]{0:T(128)} %bitcast.sref, s32[1]{0:T(128)} %bitcast.1.bref, bf16[3,1152,128]{2,1,0:T(8,128)(2,1)S(1)} %get-tuple-element.172.qa, ...), custom_call_target="tpu_custom_call" | custom-call | flops 3397386240 | bytes 8220680 | tf_op jit(solution)/shard_map/pallas_call | solution.py:78
  78.8 0.5 shard_map.251
  79.3 1.1 collective-permute-start.22
  80.4 1.6 %collective-permute-start.23 = (bf16[16,24,768]{2,1,0:T(8,128)(2,1)S(1)}, bf16[16,24,768]{2,1,0:T(8,128)(2,1)S(1)}, u32[]{:S(2)}, u32[]{:S(2)}) collective-permute-start(bf16[16,24,768]{2,1,0:T(8,128)(2,1)S(1)} %get-tuple-element.250), channel_id=1, source_target_pairs={{0,2},{1,3},{2,0},{3,1},{4,6},{5,7},{6,4},{7,5},{8,10},{9,11},{10,... | collective-permute-start | bytes 1769480 | tf_op jit(solution)/shard_map/ppermute | solution.py:801
  81.9 0.5 collective-permute-start.21
  82.5 8.2 %shard_map.252 = (f32[576,768]{1,0:T(8,128)S(1)}, bf16[576,768]{1,0:T(8,128)(2,1)S(1)}, bf16[16,24,256]{2,1,0:T(8,128)(2,1)S(1)}, bf16[16,24,256]{2,1,0:T(8,128)(2,1)S(1)}) custom-call(s32[1]{0:T(128)} %bitcast.sref, s32[1]{0:T(128)} %bitcast.1.bref, bf16[3,1152,128]{2,1,0:T(8,128)(2,1)S(1)} %get-tuple-element.172.qa, ...), custom_call_target="tpu_custom_call" | custom-call | flops 1698693120 | bytes 10285064 | tf_op jit(solution)/shard_map/pallas_call | solution.py:78
  90.7 2.1 %collective-permute-done.22.got_y = bf16[16,24,768]{2,1,0:T(8,128)(2,1)S(1)} collective-permute-done((bf16[16,24,768]{2,1,0:T(8,128)(2,1)S(1)}, bf16[16,24,768]{2,1,0:T(8,128)(2,1)S(1)}, u32[]{:S(2)}, u32[]{:S(2)}) %collective-permute-start.22) | collective-permute-done | bytes 589856 | tf_op jit(solution)/shard_map/ppermute | solution.py:801
  92.8 1.4 %collective-permute-done.23.got_z = bf16[16,24,768]{2,1,0:T(8,128)(2,1)S(1)} collective-permute-done((bf16[16,24,768]{2,1,0:T(8,128)(2,1)S(1)}, bf16[16,24,768]{2,1,0:T(8,128)(2,1)S(1)}, u32[]{:S(2)}, u32[]{:S(2)}) %collective-permute-start.23) | collective-permute-done | bytes 589856 | tf_op jit(solution)/shard_map/ppermute | solution.py:801
  94.2 0.3 shard_map.253
  94.5 1.8 %collective-permute-start.27 = (bf16[10,24,768]{2,1,0:T(8,128)(2,1)S(1)}, bf16[10,24,768]{2,1,0:T(8,128)(2,1)S(1)}, u32[]{:S(2)}, u32[]{:S(2)}) collective-permute-start(bf16[10,24,768]{2,1,0:T(8,128)(2,1)S(1)} %get-tuple-element.266), channel_id=1, source_target_pairs={{0,2},{1,3},{2,0},{3,1},{4,6},{5,7},{6,4},{7,5},{8,10},{9,11},{10,... | collective-permute-start | bytes 1105928 | tf_op jit(solution)/shard_map/ppermute | solution.py:801
  96.3 0.5 collective-permute-start.26
  96.8 0.9 collective-permute-start.28
  97.8 1.1 collective-permute-start.25
  98.9 7.2 %collective-permute-done.26.got_x = bf16[8,24,768]{2,1,0:T(8,128)(2,1)S(1)} collective-permute-done((bf16[8,24,768]{2,1,0:T(8,128)(2,1)S(1)}, bf16[8,24,768]{2,1,0:T(8,128)(2,1)S(1)}, u32[]{:S(2)}, u32[]{:S(2)}) %collective-permute-start.26) | collective-permute-done | bytes 294944 | tf_op jit(solution)/shard_map/ppermute | solution.py:801
  106.3 2.6 %collective-permute-start.29 = (bf16[9,24,768]{2,1,0:T(8,128)(2,1)S(1)}, bf16[9,24,768]{2,1,0:T(8,128)(2,1)S(1)}, u32[]{:S(2)}, u32[]{:S(2)}) collective-permute-start(bf16[9,24,768]{2,1,0:T(8,128)(2,1)S(1)} %get-tuple-element.275), channel_id=1, source_target_pairs={{0,4},{1,5},{2,6},{3,7},{4,0},{5,1},{6,2},{7,3},{8,12},{9,13},{10,... | collective-permute-start | bytes 995336 | tf_op jit(solution)/shard_map/ppermute | solution.py:801
  108.9 0.3 collective-permute-start.31
  109.3 3.2 %collective-permute-start.32 = (bf16[4,24,256]{2,1,0:T(8,128)(2,1)S(1)}, bf16[4,24,256]{2,1,0:T(8,128)(2,1)S(1)}, u32[]{:S(2)}, u32[]{:S(2)}) collective-permute-start(bf16[4,24,256]{2,1,0:T(8,128)(2,1)S(1)} %get-tuple-element.279), channel_id=1, source_target_pairs={{0,6},{1,7},{2,4},{3,5},{4,2},{5,3},{6,0},{7,1},{8,14},{9,15},{10,... | collective-permute-start | bytes 147464 | tf_op jit(solution)/shard_map/ppermute | solution.py:801
  112.5 2.4 %collective-permute-done.25.x0 = bf16[288,768]{1,0:T(8,128)(2,1)S(1)} collective-permute-done((bf16[288,768]{1,0:T(8,128)(2,1)S(1)}, bf16[288,768]{1,0:T(8,128)(2,1)S(1)}, u32[]{:S(2)}, u32[]{:S(2)}) %collective-permute-start.25) | collective-permute-done | bytes 442400 | tf_op jit(solution)/shard_map/ppermute | solution.py:801
  114.9 1.5 %shard_map.256 = (f32[256,768]{1,0:T(8,128)}, f32[4,768]{1,0:T(4,128)}) custom-call(f32[576,768]{1,0:T(8,128)S(1)} %get-tuple-element.262.keep.k0, bf16[576,768]{1,0:T(8,128)(2,1)S(1)} %collective-permute-done.24.got.c0, bf16[288,768]{1,0:T(8,128)(2,1)S(1)} %collective-permute-done.25.x0, bf16[256,768]{1,0:T(8,128)(2,1)S(1)} %bitcast.18, ...), custom_call_target="tpu_custom_call" | custom-call | bytes 5228544 | tf_op jit(solution)/shard_map/pallas_call | solution.py:78
  116.4 10.0 %collective-permute-done.29.got = bf16[9,24,768]{2,1,0:T(8,128)(2,1)S(1)} collective-permute-done((bf16[9,24,768]{2,1,0:T(8,128)(2,1)S(1)}, bf16[9,24,768]{2,1,0:T(8,128)(2,1)S(1)}, u32[]{:S(2)}, u32[]{:S(2)}) %collective-permute-start.29) | collective-permute-done | bytes 331808 | tf_op jit(solution)/shard_map/ppermute | solution.py:801
  126.4 0.5 collective-permute-done.31.z2
  127.0 0.8 shard_map.258
  127.8 0.7 collective-permute-start.34
  128.4 1.2 collective-permute-start.35
  129.6 0.3 collective-permute-start.33
  129.9 2.0 %collective-permute-done.34.g2 = bf16[24,640]{1,0:T(8,128)(2,1)S(1)} collective-permute-done((bf16[24,640]{1,0:T(8,128)(2,1)S(1)}, bf16[24,640]{1,0:T(8,128)(2,1)S(1)}, u32[]{:S(2)}, u32[]{:S(2)}) %collective-permute-start.34) | collective-permute-done | bytes 30752 | tf_op jit(solution)/shard_map/ppermute | solution.py:801
  132.1 0.9 shard_map.259
  (48 shorter events, 0.7 us)
Async XLA Ops:
  0.6 6.7 %collective-permute-start = (bf16[256,768]{1,0:T(8,128)(2,1)}, bf16[256,768]{1,0:T(8,128)(2,1)S(1)}, u32[]{:S(2)}, u32[]{:S(2)}) collective-permute-start(bf16[256,768]{1,0:T(8,128)(2,1)} %bitcast.15), channel_id=1, source_target_pairs={{0,8},{8,0},{16,24},{24,16},{1,9},{9,1},{17,25},{25,17},{2,10},{10... | collective-permute-start | bytes 1179656 | tf_op jit(solution)/shard_map/ppermute | solution.py:801
  1.2 13.0 %collective-permute-start.2 = (bf16[256,768]{1,0:T(8,128)(2,1)}, bf16[256,768]{1,0:T(8,128)(2,1)S(1)}, u32[]{:S(2)}, u32[]{:S(2)}) collective-permute-start(bf16[256,768]{1,0:T(8,128)(2,1)} %bitcast.16), channel_id=1, source_target_pairs={{0,16},{8,24},{16,0},{24,8},{1,17},{9,25},{17,1},{25,9},{2,18},{10... | collective-permute-start | bytes 1179656 | tf_op jit(solution)/shard_map/ppermute | solution.py:801
  4.5 2.8 %collective-permute-start.1 = (bf16[32,768]{1,0:T(8,128)(2,1)S(1)}, bf16[32,768]{1,0:T(8,128)(2,1)S(1)}, u32[]{:S(2)}, u32[]{:S(2)}) collective-permute-start(bf16[32,768]{1,0:T(8,128)(2,1)S(1)} %get-tuple-element.157.s0.c0), channel_id=1, source_target_pairs={{0,8},{8,0},{16,24},{24,16},{1,9},{9,1},{17,25},{25,17},{2,10},{10... | collective-permute-start | bytes 147464 | tf_op jit(solution)/shard_map/ppermute | solution.py:801
  4.8 9.4 %collective-permute-start.3 = (bf16[16,768]{1,0:T(8,128)(2,1)S(1)}, bf16[16,768]{1,0:T(8,128)(2,1)S(1)}, u32[]{:S(2)}, u32[]{:S(2)}) collective-permute-start(bf16[16,768]{1,0:T(8,128)(2,1)S(1)} %get-tuple-element.163), channel_id=1, source_target_pairs={{0,16},{8,24},{16,0},{24,8},{1,17},{9,25},{17,1},{25,9},{2,18},{10... | collective-permute-start | bytes 73736 | tf_op jit(solution)/shard_map/ppermute | solution.py:801
  5.0 2.3 %copy-start.2 = (bf16[1,256,768]{2,1,0:T(8,128)(2,1)S(1)}, bf16[1,256,768]{2,1,0:T(8,128)(2,1)}, u32[]{:S(2)}) copy-start(bf16[1,256,768]{2,1,0:T(8,128)(2,1)} %param.15) | copy-start | bytes 1179652
  5.0 2.3 %copy-start.3 = (f32[2,768]{1,0:T(2,128)S(1)}, f32[2,768]{1,0:T(2,128)}, u32[]{:S(2)}) copy-start(f32[2,768]{1,0:T(2,128)} %gain.11) | copy-start | bytes 18436
  5.0 2.3 %copy-start.5 = (f32[2,768]{1,0:T(2,128)S(1)}, f32[2,768]{1,0:T(2,128)}, u32[]{:S(2)}) copy-start(f32[2,768]{1,0:T(2,128)} %shift1.1) | copy-start | bytes 18436
  5.0 2.3 %copy-start.7 = (s32[1,16]{1,0:T(1,128)S(1)}, s32[1,16]{1,0:T(1,128)}, u32[]{:S(2)}) copy-start(s32[1,16]{1,0:T(1,128)} %flags.1) | copy-start | bytes 196
  14.2 1.8 %collective-permute-start.4 = (bf16[256,768]{1,0:T(8,128)(2,1)S(1)}, bf16[256,768]{1,0:T(8,128)(2,1)S(1)}, u32[]{:S(2)}, u32[]{:S(2)}) collective-permute-start(bf16[256,768]{1,0:T(8,128)(2,1)S(1)} %collective-permute-done.2.p), channel_id=1, source_target_pairs={{0,8},{8,0},{16,24},{24,16},{1,9},{9,1},{17,25},{25,17},{2,10},{10... | collective-permute-start | bytes 1179656 | tf_op jit(solution)/shard_map/ppermute | solution.py:801
  14.2 1.8 %collective-permute-start.5 = (bf16[16,768]{1,0:T(8,128)(2,1)S(1)}, bf16[16,768]{1,0:T(8,128)(2,1)S(1)}, u32[]{:S(2)}, u32[]{:S(2)}) collective-permute-start(bf16[16,768]{1,0:T(8,128)(2,1)S(1)} %collective-permute-done.3.small), channel_id=1, source_target_pairs={{0,8},{8,0},{16,24},{24,16},{1,9},{9,1},{17,25},{25,17},{2,10},{10... | collective-permute-start | bytes 73736 | tf_op jit(solution)/shard_map/ppermute | solution.py:801
  15.9 7.4 %copy-start.1 = (bf16[1,256,768]{2,1,0:T(8,128)(2,1)S(1)}, bf16[1,256,768]{2,1,0:T(8,128)(2,1)}, u32[]{:S(2)}) copy-start(bf16[1,256,768]{2,1,0:T(8,128)(2,1)} %param.28) | copy-start | bytes 1179652
  21.5 9.1 %collective-permute-start.7 = (bf16[576,192]{1,0:T(8,128)(2,1)S(1)}, bf16[576,192]{1,0:T(8,128)(2,1)S(1)}, u32[]{:S(2)}, u32[]{:S(2)}) collective-permute-start(bf16[576,192]{1,0:T(8,128)(2,1)S(1)} %get-tuple-element.177), channel_id=1, source_target_pairs={{0,16},{8,24},{16,0},{24,8},{1,17},{9,25},{17,1},{25,9},{2,18},{10... | collective-permute-start | bytes 663560 | tf_op jit(solution)/shard_map/ppermute | solution.py:801
  23.4 7.3 %collective-permute-start.9 = (bf16[256,768]{1,0:T(8,128)(2,1)S(1)}, bf16[256,768]{1,0:T(8,128)(2,1)S(1)}, u32[]{:S(2)}, u32[]{:S(2)}) collective-permute-start(bf16[256,768]{1,0:T(8,128)(2,1)S(1)} %bitcast.12), channel_id=1, source_target_pairs={{0,8},{8,0},{16,24},{24,16},{1,9},{9,1},{17,25},{25,17},{2,10},{10... | collective-permute-start | bytes 1179656 | tf_op jit(solution)/shard_map/ppermute | solution.py:801
  23.4 8.9 %copy-start = (bf16[768,768]{1,0:T(8,128)(2,1)S(1)}, bf16[768,768]{1,0:T(8,128)(2,1)}, u32[]{:S(2)}) copy-start(bf16[768,768]{1,0:T(8,128)(2,1)} %w_out.5) | copy-start | bytes 3538948
  23.4 8.9 %copy-start.4 = (f32[4,768]{1,0:T(4,128)S(1)}, f32[4,768]{1,0:T(4,128)}, u32[]{:S(2)}) copy-start(f32[4,768]{1,0:T(4,128)} %bias.3) | copy-start | bytes 36868
  28.5 2.1 %collective-permute-start.6 = (bf16[576,192]{1,0:T(8,128)(2,1)S(1)}, bf16[576,192]{1,0:T(8,128)(2,1)S(1)}, u32[]{:S(2)}, u32[]{:S(2)}) collective-permute-start(bf16[576,192]{1,0:T(8,128)(2,1)S(1)} %get-tuple-element.176.a0), channel_id=1, source_target_pairs={{0,8},{8,0},{16,24},{24,16},{1,9},{9,1},{17,25},{25,17},{2,10},{10... | collective-permute-start | bytes 663560 | tf_op jit(solution)/shard_map/ppermute | solution.py:801
  30.7 1.6 %collective-permute-start.8 = (bf16[576,192]{1,0:T(8,128)(2,1)S(1)}, bf16[576,192]{1,0:T(8,128)(2,1)S(1)}, u32[]{:S(2)}, u32[]{:S(2)}) collective-permute-start(bf16[576,192]{1,0:T(8,128)(2,1)S(1)} %collective-permute-done.7.a2), channel_id=1, source_target_pairs={{0,8},{8,0},{16,24},{24,16},{1,9},{9,1},{17,25},{25,17},{2,10},{10... | collective-permute-start | bytes 663560 | tf_op jit(solution)/shard_map/ppermute | solution.py:801
  32.3 1.8 %copy-start.6 = (f32[3072]{0:T(1024)S(1)}, f32[3072]{0:T(1024)}, u32[]{:S(2)}) copy-start(f32[3072]{0:T(1024)} %param.26) | copy-start | bytes 36868
  39.3 12.3 %collective-permute-start.11 = (bf16[12,24,768]{2,1,0:T(8,128)(2,1)S(1)}, bf16[12,24,768]{2,1,0:T(8,128)(2,1)S(1)}, u32[]{:S(2)}, u32[]{:S(2)}) collective-permute-start(bf16[12,24,768]{2,1,0:T(8,128)(2,1)S(1)} %get-tuple-element.195), channel_id=1, source_target_pairs={{0,1},{1,0},{2,3},{3,2},{4,5},{5,4},{6,7},{7,6},{8,9},{9,8},{10,11... | collective-permute-start | bytes 1327112 | tf_op jit(solution)/shard_map/ppermute | solution.py:801
  41.1 8.8 %collective-permute-start.10 = (bf16[8,24,768]{2,1,0:T(8,128)(2,1)S(1)}, bf16[8,24,768]{2,1,0:T(8,128)(2,1)S(1)}, u32[]{:S(2)}, u32[]{:S(2)}) collective-permute-start(bf16[8,24,768]{2,1,0:T(8,128)(2,1)S(1)} %get-tuple-element.194), channel_id=1, source_target_pairs={{0,16},{8,24},{16,0},{24,8},{1,17},{9,25},{17,1},{25,9},{2,18},{10... | collective-permute-start | bytes 884744 | tf_op jit(solution)/shard_map/ppermute | solution.py:801
  42.6 8.5 %collective-permute-start.12 = (bf16[4,48,768]{2,1,0:T(8,128)(2,1)S(1)}, bf16[4,48,768]{2,1,0:T(8,128)(2,1)S(1)}, u32[]{:S(2)}, u32[]{:S(2)}) collective-permute-start(bf16[4,48,768]{2,1,0:T(8,128)(2,1)S(1)} %get-tuple-element.196), channel_id=1, source_target_pairs={{0,2},{1,3},{2,0},{3,1},{4,6},{5,7},{6,4},{7,5},{8,10},{9,11},{10,... | collective-permute-start | bytes 884744 | tf_op jit(solution)/shard_map/ppermute | solution.py:801
  51.6 3.8 %collective-permute-start.13 = (bf16[576,768]{1,0:T(8,128)(2,1)S(1)}, bf16[576,768]{1,0:T(8,128)(2,1)S(1)}, u32[]{:S(2)}, u32[]{:S(2)}) collective-permute-start(bf16[576,768]{1,0:T(8,128)(2,1)S(1)} %get-tuple-element.197), channel_id=1, source_target_pairs={{0,8},{8,0},{16,24},{24,16},{1,9},{9,1},{17,25},{25,17},{2,10},{10... | collective-permute-start | bytes 2654216 | tf_op jit(solution)/shard_map/ppermute | solution.py:801
  51.6 7.4 %collective-permute-start.14 = (bf16[288,768]{1,0:T(8,128)(2,1)S(1)}, bf16[288,768]{1,0:T(8,128)(2,1)S(1)}, u32[]{:S(2)}, u32[]{:S(2)}) collective-permute-start(bf16[288,768]{1,0:T(8,128)(2,1)S(1)} %get-tuple-element.201), channel_id=1, source_target_pairs={{0,8},{8,0},{16,24},{24,16},{1,9},{9,1},{17,25},{25,17},{2,10},{10... | collective-permute-start | bytes 1327112 | tf_op jit(solution)/shard_map/ppermute | solution.py:801
  52.1 26.6 %collective-permute-start.17 = (bf16[20,24,768]{2,1,0:T(8,128)(2,1)S(1)}, bf16[20,24,768]{2,1,0:T(8,128)(2,1)S(1)}, u32[]{:S(2)}, u32[]{:S(2)}) collective-permute-start(bf16[20,24,768]{2,1,0:T(8,128)(2,1)S(1)} %get-tuple-element.228), channel_id=1, source_target_pairs={{0,1},{1,0},{2,3},{3,2},{4,5},{5,4},{6,7},{7,6},{8,9},{9,8},{10,11... | collective-permute-start | bytes 2211848 | tf_op jit(solution)/shard_map/ppermute | solution.py:801
  53.8 8.6 %collective-permute-start.16 = (bf16[4,48,768]{2,1,0:T(8,128)(2,1)S(1)}, bf16[4,48,768]{2,1,0:T(8,128)(2,1)S(1)}, u32[]{:S(2)}, u32[]{:S(2)}) collective-permute-start(bf16[4,48,768]{2,1,0:T(8,128)(2,1)S(1)} %get-tuple-element.213), channel_id=1, source_target_pairs={{0,2},{1,3},{2,0},{3,1},{4,6},{5,7},{6,4},{7,5},{8,10},{9,11},{10,... | collective-permute-start | bytes 884744 | tf_op jit(solution)/shard_map/ppermute | solution.py:801
  57.4 8.4 %collective-permute-start.15 = (bf16[576,192]{1,0:T(8,128)(2,1)S(1)}, bf16[576,192]{1,0:T(8,128)(2,1)S(1)}, u32[]{:S(2)}, u32[]{:S(2)}) collective-permute-start(bf16[576,192]{1,0:T(8,128)(2,1)S(1)} %get-tuple-element.211), channel_id=1, source_target_pairs={{0,16},{8,24},{16,0},{24,8},{1,17},{9,25},{17,1},{25,9},{2,18},{10... | collective-permute-start | bytes 663560 | tf_op jit(solution)/shard_map/ppermute | solution.py:801
  60.6 18.1 %collective-permute-start.19 = (bf16[2,4,24,768]{3,2,1,0:T(8,128)(2,1)S(1)}, bf16[2,4,24,768]{3,2,1,0:T(8,128)(2,1)S(1)}, u32[]{:S(2)}, u32[]{:S(2)}) collective-permute-start(bf16[2,4,24,768]{3,2,1,0:T(8,128)(2,1)S(1)} %get-tuple-element.214), channel_id=1, source_target_pairs={{0,1},{1,0},{2,3},{3,2},{4,5},{5,4},{6,7},{7,6},{8,9},{9,8},{10,11... | collective-permute-start | bytes 884744 | tf_op jit(solution)/shard_map/ppermute | solution.py:801
  62.6 16.1 %collective-permute-start.20 = (bf16[4,48,768]{2,1,0:T(8,128)(2,1)S(1)}, bf16[4,48,768]{2,1,0:T(8,128)(2,1)S(1)}, u32[]{:S(2)}, u32[]{:S(2)}) collective-permute-start(bf16[4,48,768]{2,1,0:T(8,128)(2,1)S(1)} %get-tuple-element.218), channel_id=1, source_target_pairs={{0,4},{1,5},{2,6},{3,7},{4,0},{5,1},{6,2},{7,3},{8,12},{9,13},{10,... | collective-permute-start | bytes 884744 | tf_op jit(solution)/shard_map/ppermute | solution.py:801
  65.9 12.9 %collective-permute-start.18 = (bf16[8,24,768]{2,1,0:T(8,128)(2,1)S(1)}, bf16[8,24,768]{2,1,0:T(8,128)(2,1)S(1)}, u32[]{:S(2)}, u32[]{:S(2)}) collective-permute-start(bf16[8,24,768]{2,1,0:T(8,128)(2,1)S(1)} %get-tuple-element.229), channel_id=1, source_target_pairs={{0,16},{8,24},{16,0},{24,8},{1,17},{9,25},{17,1},{25,9},{2,18},{10... | collective-permute-start | bytes 884744 | tf_op jit(solution)/shard_map/ppermute | solution.py:801
  79.3 13.5 %collective-permute-start.22 = (bf16[16,24,768]{2,1,0:T(8,128)(2,1)S(1)}, bf16[16,24,768]{2,1,0:T(8,128)(2,1)S(1)}, u32[]{:S(2)}, u32[]{:S(2)}) collective-permute-start(bf16[16,24,768]{2,1,0:T(8,128)(2,1)S(1)} %get-tuple-element.249), channel_id=1, source_target_pairs={{0,1},{1,0},{2,3},{3,2},{4,5},{5,4},{6,7},{7,6},{8,9},{9,8},{10,11... | collective-permute-start | bytes 1769480 | tf_op jit(solution)/shard_map/ppermute | solution.py:801
  80.4 13.8 %collective-permute-start.23 = (bf16[16,24,768]{2,1,0:T(8,128)(2,1)S(1)}, bf16[16,24,768]{2,1,0:T(8,128)(2,1)S(1)}, u32[]{:S(2)}, u32[]{:S(2)}) collective-permute-start(bf16[16,24,768]{2,1,0:T(8,128)(2,1)S(1)} %get-tuple-element.250), channel_id=1, source_target_pairs={{0,2},{1,3},{2,0},{3,1},{4,6},{5,7},{6,4},{7,5},{8,10},{9,11},{10,... | collective-permute-start | bytes 1769480 | tf_op jit(solution)/shard_map/ppermute | solution.py:801
  81.9 8.7 %collective-permute-start.21 = (bf16[8,24,768]{2,1,0:T(8,128)(2,1)S(1)}, bf16[8,24,768]{2,1,0:T(8,128)(2,1)S(1)}, u32[]{:S(2)}, u32[]{:S(2)}) collective-permute-start(bf16[8,24,768]{2,1,0:T(8,128)(2,1)S(1)} %get-tuple-element.248), channel_id=1, source_target_pairs={{0,16},{8,24},{16,0},{24,8},{1,17},{9,25},{17,1},{25,9},{2,18},{10... | collective-permute-start | bytes 884744 | tf_op jit(solution)/shard_map/ppermute | solution.py:801
  94.2 3.5 %collective-permute-start.24 = (bf16[576,768]{1,0:T(8,128)(2,1)S(1)}, bf16[576,768]{1,0:T(8,128)(2,1)S(1)}, u32[]{:S(2)}, u32[]{:S(2)}) collective-permute-start(bf16[576,768]{1,0:T(8,128)(2,1)S(1)} %get-tuple-element.251), channel_id=1, source_target_pairs={{0,8},{8,0},{16,24},{24,16},{1,9},{9,1},{17,25},{25,17},{2,10},{10... | collective-permute-start | bytes 2654216 | tf_op jit(solution)/shard_map/ppermute | solution.py:801
  94.5 11.7 %collective-permute-start.27 = (bf16[10,24,768]{2,1,0:T(8,128)(2,1)S(1)}, bf16[10,24,768]{2,1,0:T(8,128)(2,1)S(1)}, u32[]{:S(2)}, u32[]{:S(2)}) collective-permute-start(bf16[10,24,768]{2,1,0:T(8,128)(2,1)S(1)} %get-tuple-element.266), channel_id=1, source_target_pairs={{0,2},{1,3},{2,0},{3,1},{4,6},{5,7},{6,4},{7,5},{8,10},{9,11},{10,... | collective-permute-start | bytes 1105928 | tf_op jit(solution)/shard_map/ppermute | solution.py:801
  96.3 9.8 %collective-permute-start.26 = (bf16[8,24,768]{2,1,0:T(8,128)(2,1)S(1)}, bf16[8,24,768]{2,1,0:T(8,128)(2,1)S(1)}, u32[]{:S(2)}, u32[]{:S(2)}) collective-permute-start(bf16[8,24,768]{2,1,0:T(8,128)(2,1)S(1)} %get-tuple-element.261), channel_id=1, source_target_pairs={{0,16},{8,24},{16,0},{24,8},{1,17},{9,25},{17,1},{25,9},{2,18},{10... | collective-permute-start | bytes 884744 | tf_op jit(solution)/shard_map/ppermute | solution.py:801
  96.8 9.3 %collective-permute-start.28 = (bf16[22,24,256]{2,1,0:T(8,128)(2,1)S(1)}, bf16[22,24,256]{2,1,0:T(8,128)(2,1)S(1)}, u32[]{:S(2)}, u32[]{:S(2)}) collective-permute-start(bf16[22,24,256]{2,1,0:T(8,128)(2,1)S(1)} %get-tuple-element.268), channel_id=1, source_target_pairs={{0,1},{1,0},{2,3},{3,2},{4,5},{5,4},{6,7},{7,6},{8,9},{9,8},{10,11... | collective-permute-start | bytes 811016 | tf_op jit(solution)/shard_map/ppermute | solution.py:801
  97.8 17.1 %collective-permute-start.25 = (bf16[288,768]{1,0:T(8,128)(2,1)S(1)}, bf16[288,768]{1,0:T(8,128)(2,1)S(1)}, u32[]{:S(2)}, u32[]{:S(2)}) collective-permute-start(bf16[288,768]{1,0:T(8,128)(2,1)S(1)} %shard_map.254), channel_id=1, source_target_pairs={{0,16},{8,24},{16,0},{24,8},{1,17},{9,25},{17,1},{25,9},{2,18},{10... | collective-permute-start | bytes 1327112 | tf_op jit(solution)/shard_map/ppermute | solution.py:801
  106.3 20.1 %collective-permute-start.29 = (bf16[9,24,768]{2,1,0:T(8,128)(2,1)S(1)}, bf16[9,24,768]{2,1,0:T(8,128)(2,1)S(1)}, u32[]{:S(2)}, u32[]{:S(2)}) collective-permute-start(bf16[9,24,768]{2,1,0:T(8,128)(2,1)S(1)} %get-tuple-element.275), channel_id=1, source_target_pairs={{0,4},{1,5},{2,6},{3,7},{4,0},{5,1},{6,2},{7,3},{8,12},{9,13},{10,... | collective-permute-start | bytes 995336 | tf_op jit(solution)/shard_map/ppermute | solution.py:801
  108.9 18.0 %collective-permute-start.31 = (bf16[4,24,256]{2,1,0:T(8,128)(2,1)S(1)}, bf16[4,24,256]{2,1,0:T(8,128)(2,1)S(1)}, u32[]{:S(2)}, u32[]{:S(2)}) collective-permute-start(bf16[4,24,256]{2,1,0:T(8,128)(2,1)S(1)} %get-tuple-element.278), channel_id=1, source_target_pairs={{0,4},{1,5},{2,6},{3,7},{4,0},{5,1},{6,2},{7,3},{8,12},{9,13},{10,... | collective-permute-start | bytes 147464 | tf_op jit(solution)/shard_map/ppermute | solution.py:801
  109.3 17.6 %collective-permute-start.32 = (bf16[4,24,256]{2,1,0:T(8,128)(2,1)S(1)}, bf16[4,24,256]{2,1,0:T(8,128)(2,1)S(1)}, u32[]{:S(2)}, u32[]{:S(2)}) collective-permute-start(bf16[4,24,256]{2,1,0:T(8,128)(2,1)S(1)} %get-tuple-element.279), channel_id=1, source_target_pairs={{0,6},{1,7},{2,4},{3,5},{4,2},{5,3},{6,0},{7,1},{8,14},{9,15},{10,... | collective-permute-start | bytes 147464 | tf_op jit(solution)/shard_map/ppermute | solution.py:801
  112.5 14.4 %collective-permute-start.30 = (bf16[4,24,256]{2,1,0:T(8,128)(2,1)S(1)}, bf16[4,24,256]{2,1,0:T(8,128)(2,1)S(1)}, u32[]{:S(2)}, u32[]{:S(2)}) collective-permute-start(bf16[4,24,256]{2,1,0:T(8,128)(2,1)S(1)} %get-tuple-element.269), channel_id=1, source_target_pairs={{0,2},{1,3},{2,0},{3,1},{4,6},{5,7},{6,4},{7,5},{8,10},{9,11},{10,... | collective-permute-start | bytes 147464 | tf_op jit(solution)/shard_map/ppermute | solution.py:801
  127.8 4.3 %collective-permute-start.36 = (bf16[48,768]{1,0:T(8,128)(2,1)S(1)}, bf16[48,768]{1,0:T(8,128)(2,1)S(1)}, u32[]{:S(2)}, u32[]{:S(2)}) collective-permute-start(bf16[48,768]{1,0:T(8,128)(2,1)S(1)} %get-tuple-element.287), channel_id=1, source_target_pairs={{0,8},{8,0},{16,24},{24,16},{1,9},{9,1},{17,25},{25,17},{2,10},{10... | collective-permute-start | bytes 221192 | tf_op jit(solution)/shard_map/ppermute | solution.py:801
  127.8 4.1 %collective-permute-start.34 = (bf16[24,640]{1,0:T(8,128)(2,1)S(1)}, bf16[24,640]{1,0:T(8,128)(2,1)S(1)}, u32[]{:S(2)}, u32[]{:S(2)}) collective-permute-start(bf16[24,640]{1,0:T(8,128)(2,1)S(1)} %get-tuple-element.282), channel_id=1, source_target_pairs={{0,16},{8,24},{16,0},{24,8},{1,17},{9,25},{17,1},{25,9},{2,18},{10... | collective-permute-start | bytes 92168 | tf_op jit(solution)/shard_map/ppermute | solution.py:801
  128.4 3.6 %collective-permute-start.35 = (bf16[24,640]{1,0:T(8,128)(2,1)S(1)}, bf16[24,640]{1,0:T(8,128)(2,1)S(1)}, u32[]{:S(2)}, u32[]{:S(2)}) collective-permute-start(bf16[24,640]{1,0:T(8,128)(2,1)S(1)} %get-tuple-element.283), channel_id=1, source_target_pairs={{0,24},{8,16},{16,8},{24,0},{1,25},{9,17},{17,9},{25,1},{2,26},{10... | collective-permute-start | bytes 92168 | tf_op jit(solution)/shard_map/ppermute | solution.py:801
  129.6 2.4 %collective-permute-start.33 = (bf16[24,640]{1,0:T(8,128)(2,1)S(1)}, bf16[24,640]{1,0:T(8,128)(2,1)S(1)}, u32[]{:S(2)}, u32[]{:S(2)}) collective-permute-start(bf16[24,640]{1,0:T(8,128)(2,1)S(1)} %get-tuple-element.281), channel_id=1, source_target_pairs={{0,8},{8,0},{16,24},{24,16},{1,9},{9,1},{17,25},{25,17},{2,10},{10... | collective-permute-start | bytes 92168 | tf_op jit(solution)/shard_map/ppermute | solution.py:801
